TPU v7x, 128 devices: a whole 4x4x4 slice. The times are simulated.
128 devices in a mesh: gx: 4 (over z), gy: 8 (over y_lo, x), gz: 4 (over y_hi, core).
Axes of the slice: x: 4, y: 4 (y_hi: 2, y_lo: 2; y = y_hi * 2 + y_lo), z: 4, core: 2. Of those that a mesh axis runs over, the one named last changes fastest.
Arguments:
- images: float32 [2, 64, 256, 512], P(None, 'gx', 'gy', 'gz'), may hold values from -6 to 6
- velocity: float32 [2, 3, 8, 32, 64], P(None, None, 'gx', None, 'gz'), may hold values from -2 to 2
Outputs:
- new_velocity: float32 [2, 3, 8, 32, 64], P(None, None, 'gx', None, 'gz')
- velocity_field: bfloat16 [2, 3, 64, 256, 512], P(None, None, 'gx', 'gy', 'gz')
All inputs are finite; a program needn't handle non-finite values.
Results may differ from a plain program's by a relative error of at most 0.001.
Values sent between devices are 32-bit elements; how exact they have to be, the bound alone decides.
No kernel may reach another device: no remote copies, remote signals or barrier semaphores. Data moves between devices by JAX's collectives and lax.ppermute only.
A program may use at most 64 MiB of HBM per device.

v0:
```python
import jax
import jax.numpy as jnp
from jax import lax
from jax.sharding import PartitionSpec as P

epsilon_value = 1e-05
step_size = 0.5


def extended_2(cells, sides, width):
    for axis, dim in sides:
        count = lax.axis_size(axis)
        ends = count - 1
        head = lax.slice_in_dim(cells, 0, width, axis=dim)
        tail = lax.slice_in_dim(cells, cells.shape[dim] - width, cells.shape[dim], axis=dim)
        cells = jnp.concatenate(
            [
                lax.ppermute(tail, axis, [(i, (i + 1) % count) for i in range(ends)]),
                cells,
                lax.ppermute(head, axis, [((i + 1) % count, i) for i in range(ends)]),
            ],
            axis=dim,
        )
    return cells


def copy_for_each(value, axis):
    peers = lax.axis_size(axis)
    return lax.all_to_all(
        jnp.broadcast_to(value[None], (peers, *value.shape)), axis, 0, 0, tiled=True
    )


def taken_together(value, axis):
    everything = copy_for_each(value, axis)
    return jnp.sum(everything, axis=0)


def spline_weight(offset):
    magnitude = jnp.abs(offset)
    interior = 2.0 / 3.0 - magnitude * magnitude + 0.5 * magnitude * magnitude * magnitude
    outside = jnp.maximum(2.0 - magnitude, 0.0)
    outside = outside * outside * outside / 6.0
    return jnp.where(magnitude < 1.0, interior, outside)


def spline_table(voxels, points, first_point):
    positions = jnp.arange(voxels, dtype=jnp.float32)[:, None]
    centres = 8.0 * (jnp.arange(points, dtype=jnp.float32)[None, :] + first_point) + 3.5
    return spline_weight((positions - centres) / 8.0)


def fold_matrix(length):
    table_rows = jnp.arange(length, dtype=jnp.int32)[:, None]
    columns = jnp.arange(length - 8, dtype=jnp.int32)[None, :]
    matches = (
        (table_rows == columns + 4)
        | (table_rows < 2) & (columns == table_rows)
        | (table_rows >= length - 2) & (columns == table_rows - 8)
    )
    return matches.astype(jnp.float32)


def window_sum(values, which_axis, keep_count):
    running = lax.slice_in_dim(values, 0, keep_count, axis=which_axis)
    for offset in range(1, 9):
        running = running + lax.slice_in_dim(values, offset, offset + keep_count, axis=which_axis)
    return running


def gradient(volume, count_x, count_y, count_z):
    along_x = (
        volume[5 : 5 + count_x, 4 : 4 + count_y, 4 : 4 + count_z]
        - volume[3 : 3 + count_x, 4 : 4 + count_y, 4 : 4 + count_z]
    )
    along_y = (
        volume[4 : 4 + count_x, 5 : 5 + count_y, 4 : 4 + count_z]
        - volume[4 : 4 + count_x, 3 : 3 + count_y, 4 : 4 + count_z]
    )
    along_z = (
        volume[4 : 4 + count_x, 4 : 4 + count_y, 5 : 5 + count_z]
        - volume[4 : 4 + count_x, 4 : 4 + count_y, 3 : 3 + count_z]
    )
    return 0.5 * jnp.stack([along_x, along_y, along_z])


def local_forces(padded):
    count_x = padded.shape[1] - 8
    count_y = padded.shape[2] - 8
    count_z = padded.shape[3] - 8
    fixed_side = padded[0]
    moving_side = padded[1]
    products = jnp.stack(
        [
            fixed_side,
            moving_side,
            fixed_side * fixed_side,
            moving_side * moving_side,
            fixed_side * moving_side,
        ]
    )
    window_sums = window_sum(window_sum(window_sum(products, 1, count_x), 2, count_y), 3, count_z)
    averages = window_sums / 729.0
    mean_fixed = averages[0]
    mean_moving = averages[1]
    var_fixed = averages[2] - mean_fixed * mean_fixed + epsilon_value
    var_moving = averages[3] - mean_moving * mean_moving + epsilon_value
    covariance = averages[4] - mean_fixed * mean_moving
    centre_fixed = fixed_side[4 : 4 + count_x, 4 : 4 + count_y, 4 : 4 + count_z] - mean_fixed
    centre_moving = moving_side[4 : 4 + count_x, 4 : 4 + count_y, 4 : 4 + count_z] - mean_moving
    factor = 2.0 * covariance / (var_fixed * var_moving)
    pull_fixed = factor * (centre_moving - covariance / var_fixed * centre_fixed)
    pull_moving = factor * (centre_fixed - covariance / var_moving * centre_moving)
    return jnp.stack(
        [
            pull_fixed[None] * gradient(fixed_side, count_x, count_y, count_z),
            pull_moving[None] * gradient(moving_side, count_x, count_y, count_z),
        ]
    )


def shards(images, velocity):
    highest = lax.Precision.HIGHEST
    count_x = images.shape[1]
    count_y = images.shape[2]
    count_z = images.shape[3]
    block_x = count_x // 8
    block_y = count_y // 8
    block_z = count_z // 8
    padded = extended_2(images, (("gx", 1), ("gy", 2), ("gz", 3)), 4)
    pushes = local_forces(padded)
    table_x = spline_table(count_x, block_x + 4, -2.0)
    table_y = spline_table(count_y, block_y + 4, -2.0)
    table_z = spline_table(count_z, block_z + 4, -2.0)
    along_z = jnp.einsum("hcxyz,zk->hcxyk", pushes, table_z, precision=highest)
    along_y = jnp.einsum("hcxyk,yj->hcxjk", along_z, table_y, precision=highest)
    partial_value = jnp.einsum("hcxjk,xi->hcijk", along_y, table_x, precision=highest)
    fold_x = fold_matrix(block_x + 8)
    fold_z = fold_matrix(block_z + 8)
    extended = extended_2(partial_value, (("gx", 2), ("gz", 4)), 2)
    folded = jnp.einsum("hcpqr,pi->hciqr", extended, fold_x, precision=highest)
    folded = jnp.einsum("hciqr,rk->hciqk", folded, fold_z, precision=highest)
    whole_rows = block_y * lax.axis_size("gy") + 4
    canvas = jnp.zeros((2, 3, block_x, whole_rows, block_z), jnp.float32)
    canvas = lax.dynamic_update_slice_in_dim(canvas, folded, lax.axis_index("gy") * block_y, 3)
    summed = taken_together(canvas, "gy")
    descent = summed[:, :, :, 2 : whole_rows - 2, :]
    new_velocity = velocity + step_size * descent
    beside_all = extended_2(new_velocity, (("gx", 2), ("gz", 4)), 2)
    rows_padded = jnp.pad(beside_all, ((0, 0), (0, 0), (0, 0), (2, 2), (0, 0)))
    window = lax.dynamic_slice_in_dim(rows_padded, lax.axis_index("gy") * block_y, block_y + 4, 3)
    field_x = jnp.einsum("hcijk,xi->hcxjk", window, table_x, precision=highest)
    field_y = jnp.einsum("hcxjk,yj->hcxyk", field_x, table_y, precision=highest)
    velocity_field = jnp.einsum("hcxyk,zk->hcxyz", field_y, table_z, precision=highest).astype(
        jnp.bfloat16
    )
    return (new_velocity, velocity_field)


def solution(mesh):
    placed = (P(None, "gx", "gy", "gz"), P(None, None, "gx", None, "gz"))
    return jax.shard_map(
        shards,
        mesh=mesh,
        in_specs=placed,
        out_specs=(P(None, None, "gx", None, "gz"), P(None, None, "gx", "gy", "gz")),
        check_vma=False,
    )
```

profile of v0, /device:TPU:1, one launch (start us, length us, event | category | flops | bytes accessed | tf_op | source)
XLA Modules:
  0.0 130.2 jit_solution(12191270260960985314)
XLA Ops:
  0.6 1.0 fusion.195
  1.6 4.4 %collective-permute-start = (f32[2,4,32,128]{3,2,1,0:T(8,128)S(1)}, f32[2,4,32,128]{3,2,1,0:T(8,128)S(1)}, u32[]{:S(2)}, u32[]{:S(2)}) collective-permute-start(f32[2,4,32,128]{3,2,1,0:T(8,128)S(1)} %get-tuple-element.21), channel_id=1, source_target_pairs={{0,32},{32,64},{64,96},{1,33},{33,65},{65,97},{2,34},{34,66},{66,9... | collective-permute-start | bytes 393224 | tf_op jit(solution)/shard_map/ppermute | solution.py:18
  6.0 1.3 collective-permute-start.1
  7.4 0.8 collective-permute-done
  8.2 1.1 constant_dynamic-update-slice_fusion.1
  9.2 3.1 %collective-permute-done.1 = f32[2,4,32,128]{3,2,1,0:T(8,128)S(1)} collective-permute-done((f32[2,4,32,128]{3,2,1,0:T(8,128)S(1)}, f32[2,4,32,128]{3,2,1,0:T(8,128)S(1)}, u32[]{:S(2)}, u32[]{:S(2)}) %collective-permute-start.1) | collective-permute-done | bytes 131104 | tf_op jit(solution)/shard_map/ppermute | solution.py:20
  12.4 3.1 %collective-permute-start.2 = (f32[2,24,4,128]{3,1,2,0:T(8,128)S(1)}, f32[2,24,4,128]{3,1,2,0:T(8,128)S(1)}, u32[]{:S(2)}, u32[]{:S(2)}) collective-permute-start(f32[2,24,4,128]{3,1,2,0:T(8,128)S(1)} %copy.79), channel_id=1, source_target_pairs={{0,4},{4,8},{8,12},{12,16},{16,20},{20,24},{24,28},{1,5},{5,9},{9,... | collective-permute-start | bytes 294920 | tf_op jit(solution)/shard_map/ppermute | solution.py:18
  15.6 1.3 collective-permute-start.3
  16.9 0.3 collective-permute-done.2
  17.2 3.7 %collective-permute-done.3 = f32[2,24,4,128]{3,1,2,0:T(8,128)S(1)} collective-permute-done((f32[2,24,4,128]{3,1,2,0:T(8,128)S(1)}, f32[2,24,4,128]{3,1,2,0:T(8,128)S(1)}, u32[]{:S(2)}, u32[]{:S(2)}) %collective-permute-start.3) | collective-permute-done | bytes 98336 | tf_op jit(solution)/shard_map/ppermute | solution.py:20
  20.9 0.1 pad_maximum_fusion.2
  21.1 0.3 fusion.193
  21.4 0.4 copy.62
  21.8 7.8 %collective-permute-start.4 = (f32[2,24,40,4]{2,1,3,0:T(8,128)S(1)}, f32[2,24,40,4]{2,1,3,0:T(8,128)S(1)}, u32[]{:S(2)}, u32[]{:S(2)}) collective-permute-start(f32[2,24,40,4]{2,1,3,0:T(8,128)S(1)} %copy.62), channel_id=1, source_target_pairs={{0,1},{1,2},{2,3},{4,5},{5,6},{6,7},{8,9},{9,10},{10,11},{12,13},{... | collective-permute-start | bytes 92168 | tf_op jit(solution)/shard_map/ppermute | solution.py:18
  29.6 0.4 copy.63
  30.0 1.9 %collective-permute-start.5 = (f32[2,24,40,4]{2,1,3,0:T(8,128)S(1)}, f32[2,24,40,4]{2,1,3,0:T(8,128)S(1)}, u32[]{:S(2)}, u32[]{:S(2)}) collective-permute-start(f32[2,24,40,4]{2,1,3,0:T(8,128)S(1)} %copy.63), channel_id=1, source_target_pairs={{1,0},{2,1},{3,2},{5,4},{6,5},{7,6},{9,8},{10,9},{11,10},{13,12},{... | collective-permute-start | bytes 92168 | tf_op jit(solution)/shard_map/ppermute | solution.py:20
  32.0 0.4 copy.64
  32.4 5.1 %collective-permute-done.5 = f32[2,24,40,4]{2,1,3,0:T(8,128)S(1)} collective-permute-done((f32[2,24,40,4]{2,1,3,0:T(8,128)S(1)}, f32[2,24,40,4]{2,1,3,0:T(8,128)S(1)}, u32[]{:S(2)}, u32[]{:S(2)}) %collective-permute-start.5) | collective-permute-done | bytes 30752 | tf_op jit(solution)/shard_map/ppermute | solution.py:20
  37.4 0.4 copy.65
  37.9 1.0 pad_maximum_fusion.1
  38.9 0.4 slice_bitcast_fusion.1
  39.3 1.8 %pad_maximum_fusion = f32[5,24,40,136]{3,2,1,0:T(8,128)S(1)} fusion(f32[1,24,40,136]{3,2,1,0:T(8,128)S(1)} %get-tuple-element.8, f32[1,24,40,136]{3,2,1,0:T(8,128)S(1)} %get-tuple-element.10, f32[1,24,40,136]{3,2,1,0:T(8,128)S(1)} %get-tuple-element.7, f32[2,24,40,4]{3,2,1,0:T(8,128)S(1)} %copy.65, f32[2,24,4,128]{3,2,1,0:T(4,128)S(1)} %copy.61, ...), kind=kLoop, calls=%fused_computation | loop fusion | flops 4569600 | bytes 5222400 | tf_op jit(solution)/shard_map/stack | solution.py:93
  41.1 3.0 %slice_add_fusion = f32[5,16,40,136]{3,2,1,0:T(8,128)S(1)} fusion(f32[5,24,40,136]{3,2,1,0:T(8,128)S(1)} %pad_maximum_fusion), kind=kLoop, calls=%fused_computation.1 | loop fusion | flops 3481600 | bytes 17408000 | tf_op jit(solution)/shard_map/add | solution.py:67
  44.2 2.0 %slice_add_fusion.8 = f32[5,16,32,136]{3,2,1,0:T(8,128)S(1)} fusion(f32[5,16,40,136]{3,2,1,0:T(8,128)S(1)} %slice_add_fusion), kind=kLoop, calls=%fused_computation.9 | loop fusion | flops 2785280 | bytes 13926400 | tf_op jit(solution)/shard_map/add | solution.py:67
  46.1 2.8 %fusion.4 = f32[5,16,32,128]{3,2,1,0:T(8,128)S(1)} fusion(f32[5,16,32,136]{3,2,1,0:T(8,128)S(1)} %slice_add_fusion.8), kind=kLoop, calls=%fused_computation.25 | loop fusion | flops 2949120 | bytes 13107200 | tf_op jit(solution)/shard_map/div | solution.py:103
  48.9 0.6 fusion.18
  49.5 0.5 multiply_multiply_fusion.1
  50.0 0.1 maximum_multiply_fusion
  50.1 0.1 maximum_multiply_fusion.1
  50.2 6.2 %fusion = f32[2,3,16,32,20]{3,4,2,1,0:T(8,128)S(1)} fusion(f32[1,3,16,32,128]{4,3,2,1,0:T(8,128)S(1)} %maximum_multiply_fusion.1, f32[1,3,16,32,128]{4,3,2,1,0:T(8,128)S(1)} %maximum_multiply_fusion, f32[20]{0:T(128)S(1)} %multiply_add_fusion), kind=kOutput, calls=%fused_computation.18 | convolution fusion | flops 94806016 | bytes 1818704 | tf_op jit(solution)/shard_map/hcxyz,zk->hcxyk/dot_general | solution.py:135
  56.4 5.9 %convolution_bitcast_fusion.2 = f32[2,3,16,8,20]{4,3,2,1,0:T(8,128)S(1)} fusion(f32[2,3,16,32,20]{3,4,2,1,0:T(8,128)S(1)} %fusion, f32[8]{0:T(128)S(1)} %multiply_add_fusion.1), kind=kOutput, calls=%fused_computation.34 | convolution fusion | flops 5902336 | bytes 307232 | tf_op jit(solution)/shard_map/hcxyk,yj->hcxjk/dot_general | solution.py:136
  62.3 0.4 convolution_bitcast_fusion.3
  62.8 3.4 %collective-permute-start.6 = (f32[2,3,2,8,20]{4,2,3,1,0:T(2,128)S(1)}, f32[2,3,2,8,20]{4,2,3,1,0:T(2,128)S(1)}, u32[]{:S(2)}, u32[]{:S(2)}) collective-permute-start(f32[2,3,2,8,20]{4,2,3,1,0:T(2,128)S(1)} %get-tuple-element.26), channel_id=1, source_target_pairs={{0,32},{32,64},{64,96},{1,33},{33,65},{65,97},{2,34},{34,66},{66,9... | collective-permute-start | bytes 23048 | tf_op jit(solution)/shard_map/ppermute | solution.py:18
  66.1 1.5 %collective-permute-start.7 = (f32[2,3,2,8,20]{4,2,3,1,0:T(2,128)S(1)}, f32[2,3,2,8,20]{4,2,3,1,0:T(2,128)S(1)}, u32[]{:S(2)}, u32[]{:S(2)}) collective-permute-start(f32[2,3,2,8,20]{4,2,3,1,0:T(2,128)S(1)} %get-tuple-element.27), channel_id=1, source_target_pairs={{32,0},{64,32},{96,64},{33,1},{65,33},{97,65},{34,2},{66,34},{98,6... | collective-permute-start | bytes 23048 | tf_op jit(solution)/shard_map/ppermute | solution.py:20
  67.7 3.3 %collective-permute-done.7 = f32[2,3,2,8,20]{4,2,3,1,0:T(2,128)S(1)} collective-permute-done((f32[2,3,2,8,20]{4,2,3,1,0:T(2,128)S(1)}, f32[2,3,2,8,20]{4,2,3,1,0:T(2,128)S(1)}, u32[]{:S(2)}, u32[]{:S(2)}) %collective-permute-start.7) | collective-permute-done | bytes 7712 | tf_op jit(solution)/shard_map/ppermute | solution.py:20
  71.0 0.1 pad_maximum_fusion.3
  71.1 0.2 fusion.196
  71.2 3.3 %collective-permute-start.8 = (f32[2,3,10,8,2]{4,2,3,1,0:T(8,128)S(1)}, f32[2,3,10,8,2]{4,2,3,1,0:T(8,128)S(1)}, u32[]{:S(2)}, u32[]{:S(2)}) collective-permute-start(f32[2,3,10,8,2]{4,2,3,1,0:T(8,128)S(1)} %get-tuple-element.22), channel_id=1, source_target_pairs={{0,1},{1,2},{2,3},{4,5},{5,6},{6,7},{8,9},{9,10},{10,11},{12,13},{... | collective-permute-start | bytes 11528 | tf_op jit(solution)/shard_map/ppermute | solution.py:18
  74.5 1.9 %collective-permute-start.9 = (f32[2,3,10,8,2]{4,2,3,1,0:T(8,128)S(1)}, f32[2,3,10,8,2]{4,2,3,1,0:T(8,128)S(1)}, u32[]{:S(2)}, u32[]{:S(2)}) collective-permute-start(f32[2,3,10,8,2]{4,2,3,1,0:T(8,128)S(1)} %get-tuple-element.23), channel_id=1, source_target_pairs={{1,0},{2,1},{3,2},{5,4},{6,5},{7,6},{9,8},{10,9},{11,10},{13,12},{... | collective-permute-start | bytes 11528 | tf_op jit(solution)/shard_map/ppermute | solution.py:20
  76.4 2.8 %collective-permute-done.8 = f32[2,3,10,8,2]{4,2,3,1,0:T(8,128)S(1)} collective-permute-done((f32[2,3,10,8,2]{4,2,3,1,0:T(8,128)S(1)}, f32[2,3,10,8,2]{4,2,3,1,0:T(8,128)S(1)}, u32[]{:S(2)}, u32[]{:S(2)}) %collective-permute-start.8) | collective-permute-done | bytes 3872 | tf_op jit(solution)/shard_map/ppermute | solution.py:18
  79.2 5.9 %collective-permute-done.9 = f32[2,3,10,8,2]{4,2,3,1,0:T(8,128)S(1)} collective-permute-done((f32[2,3,10,8,2]{4,2,3,1,0:T(8,128)S(1)}, f32[2,3,10,8,2]{4,2,3,1,0:T(8,128)S(1)}, u32[]{:S(2)}, u32[]{:S(2)}) %collective-permute-start.9) | collective-permute-done | bytes 3872 | tf_op jit(solution)/shard_map/ppermute | solution.py:20
  85.1 0.6 convolution_bitcast_fusion.4
  85.7 0.5 fusion.45
  86.2 0.3 dynamic_update_slice.5
  86.5 0.1 broadcast_bitcast_fusion
  86.6 0.9 reshape.173
  87.5 12.9 %all_to_all.5 = f32[8,1,6912]{2,1,0:T(1,128)S(1)} all-to-all(f32[8,1,6912]{2,1,0:T(1,128)S(1)} %reshape.173), channel_id=1, replica_groups=mesh['gx'=4,'gy'=8,'gz'=4] {'gy'}, dimensions={0} | all-to-all | bytes 442368 | tf_op jit(solution)/shard_map/all_to_all | solution.py:29
  100.4 0.5 broadcast.253
  100.9 1.2 reduce
  102.1 1.0 reshape.174
  103.2 0.1 fusion.44
  103.3 3.3 %collective-permute-start.10 = (f32[2,3,2,32,16]{3,4,2,1,0:T(8,128)S(1)}, f32[2,3,2,32,16]{3,4,2,1,0:T(8,128)S(1)}, u32[]{:S(2)}, u32[]{:S(2)}) collective-permute-start(f32[2,3,2,32,16]{3,4,2,1,0:T(8,128)S(1)} %fusion.44), channel_id=1, source_target_pairs={{0,32},{32,64},{64,96},{1,33},{33,65},{65,97},{2,34},{34,66},{66,9... | collective-permute-start | bytes 73736 | tf_op jit(solution)/shard_map/ppermute | solution.py:18
  106.6 1.3 collective-permute-start.11
  107.9 0.3 collective-permute-done.10
  108.2 3.7 %collective-permute-done.11 = f32[2,3,2,32,16]{3,4,2,1,0:T(8,128)S(1)} collective-permute-done((f32[2,3,2,32,16]{3,4,2,1,0:T(8,128)S(1)}, f32[2,3,2,32,16]{3,4,2,1,0:T(8,128)S(1)}, u32[]{:S(2)}, u32[]{:S(2)}) %collective-permute-start.11) | collective-permute-done | bytes 24608 | tf_op jit(solution)/shard_map/ppermute | solution.py:20
  112.0 4.6 %collective-permute-start.12 = (f32[2,3,6,32,2]{3,4,2,1,0:T(2,128)S(1)}, f32[2,3,6,32,2]{3,4,2,1,0:T(2,128)S(1)}, u32[]{:S(2)}, u32[]{:S(2)}) collective-permute-start(f32[2,3,6,32,2]{3,4,2,1,0:T(2,128)S(1)} %get-tuple-element.25), channel_id=1, source_target_pairs={{0,1},{1,2},{2,3},{4,5},{5,6},{6,7},{8,9},{9,10},{10,11},{12,13},{... | collective-permute-start | bytes 27656 | tf_op jit(solution)/shard_map/ppermute | solution.py:18
  116.6 1.9 %collective-permute-start.13 = (f32[2,3,6,32,2]{3,4,2,1,0:T(2,128)S(1)}, f32[2,3,6,32,2]{3,4,2,1,0:T(2,128)S(1)}, u32[]{:S(2)}, u32[]{:S(2)}) collective-permute-start(f32[2,3,6,32,2]{3,4,2,1,0:T(2,128)S(1)} %get-tuple-element.24), channel_id=1, source_target_pairs={{1,0},{2,1},{3,2},{5,4},{6,5},{7,6},{9,8},{10,9},{11,10},{13,12},{... | collective-permute-start | bytes 27656 | tf_op jit(solution)/shard_map/ppermute | solution.py:20
  118.5 0.3 copy.70
  118.9 0.4 copy.69
  119.2 4.1 %collective-permute-done.13 = f32[2,3,6,32,2]{3,4,2,1,0:T(2,128)S(1)} collective-permute-done((f32[2,3,6,32,2]{3,4,2,1,0:T(2,128)S(1)}, f32[2,3,6,32,2]{3,4,2,1,0:T(2,128)S(1)}, u32[]{:S(2)}, u32[]{:S(2)}) %collective-permute-start.13) | collective-permute-done | bytes 9248 | tf_op jit(solution)/shard_map/ppermute | solution.py:20
  123.4 0.4 copy.71
  123.7 0.8 convolution_bitcast_fusion.1
  124.6 2.1 %convolution_bitcast_fusion = f32[2,3,16,32,20]{3,4,2,1,0:T(8,128)S(1)} fusion(f32[2,3,16,8,20]{4,2,3,1,0:T(8,128)S(1)} %convolution_bitcast_fusion.1, f32[8]{0:T(128)S(1)} %multiply_add_fusion.1), kind=kOutput, calls=%fused_computation.23 | convolution fusion | flops 5902336 | bytes 307232 | tf_op jit(solution)/shard_map/hcxjk,yj->hcxyk/dot_general | solution.py:153
  126.6 3.6 %convolution_convert_fusion = bf16[2,3,16,32,128]{4,3,2,1,0:T(8,128)(2,1)} fusion(f32[2,3,16,32,20]{3,4,2,1,0:T(8,128)S(1)} %convolution_bitcast_fusion, f32[20]{0:T(128)S(1)} %multiply_add_fusion), kind=kOutput, calls=%fused_computation.22 | convolution fusion | flops 94806016 | bytes 1032272 | tf_op jit(solution)/shard_map/hcxyk,zk->hcxyz/dot_general | solution.py:154
  (28 shorter events, 0.4 us)
Async XLA Ops:
  1.6 6.5 %collective-permute-start = (f32[2,4,32,128]{3,2,1,0:T(8,128)S(1)}, f32[2,4,32,128]{3,2,1,0:T(8,128)S(1)}, u32[]{:S(2)}, u32[]{:S(2)}) collective-permute-start(f32[2,4,32,128]{3,2,1,0:T(8,128)S(1)} %get-tuple-element.21), channel_id=1, source_target_pairs={{0,32},{32,64},{64,96},{1,33},{33,65},{65,97},{2,34},{34,66},{66,9... | collective-permute-start | bytes 393224 | tf_op jit(solution)/shard_map/ppermute | solution.py:18
  6.0 6.3 %collective-permute-start.1 = (f32[2,4,32,128]{3,2,1,0:T(8,128)S(1)}, f32[2,4,32,128]{3,2,1,0:T(8,128)S(1)}, u32[]{:S(2)}, u32[]{:S(2)}) collective-permute-start(f32[2,4,32,128]{3,2,1,0:T(8,128)S(1)} %get-tuple-element.20), channel_id=1, source_target_pairs={{32,0},{64,32},{96,64},{33,1},{65,33},{97,65},{34,2},{66,34},{98,6... | collective-permute-start | bytes 393224 | tf_op jit(solution)/shard_map/ppermute | solution.py:20
  12.4 4.7 %collective-permute-start.2 = (f32[2,24,4,128]{3,1,2,0:T(8,128)S(1)}, f32[2,24,4,128]{3,1,2,0:T(8,128)S(1)}, u32[]{:S(2)}, u32[]{:S(2)}) collective-permute-start(f32[2,24,4,128]{3,1,2,0:T(8,128)S(1)} %copy.79), channel_id=1, source_target_pairs={{0,4},{4,8},{8,12},{12,16},{16,20},{20,24},{24,28},{1,5},{5,9},{9,... | collective-permute-start | bytes 294920 | tf_op jit(solution)/shard_map/ppermute | solution.py:18
  15.6 5.4 %collective-permute-start.3 = (f32[2,24,4,128]{3,1,2,0:T(8,128)S(1)}, f32[2,24,4,128]{3,1,2,0:T(8,128)S(1)}, u32[]{:S(2)}, u32[]{:S(2)}) collective-permute-start(f32[2,24,4,128]{3,1,2,0:T(8,128)S(1)} %copy.80), channel_id=1, source_target_pairs={{4,0},{8,4},{12,8},{16,12},{20,16},{24,20},{28,24},{5,1},{9,5},{13... | collective-permute-start | bytes 294920 | tf_op jit(solution)/shard_map/ppermute | solution.py:20
  21.8 10.2 %collective-permute-start.4 = (f32[2,24,40,4]{2,1,3,0:T(8,128)S(1)}, f32[2,24,40,4]{2,1,3,0:T(8,128)S(1)}, u32[]{:S(2)}, u32[]{:S(2)}) collective-permute-start(f32[2,24,40,4]{2,1,3,0:T(8,128)S(1)} %copy.62), channel_id=1, source_target_pairs={{0,1},{1,2},{2,3},{4,5},{5,6},{6,7},{8,9},{9,10},{10,11},{12,13},{... | collective-permute-start | bytes 92168 | tf_op jit(solution)/shard_map/ppermute | solution.py:18
  30.0 7.5 %collective-permute-start.5 = (f32[2,24,40,4]{2,1,3,0:T(8,128)S(1)}, f32[2,24,40,4]{2,1,3,0:T(8,128)S(1)}, u32[]{:S(2)}, u32[]{:S(2)}) collective-permute-start(f32[2,24,40,4]{2,1,3,0:T(8,128)S(1)} %copy.63), channel_id=1, source_target_pairs={{1,0},{2,1},{3,2},{5,4},{6,5},{7,6},{9,8},{10,9},{11,10},{13,12},{... | collective-permute-start | bytes 92168 | tf_op jit(solution)/shard_map/ppermute | solution.py:20
  62.8 4.9 %collective-permute-start.6 = (f32[2,3,2,8,20]{4,2,3,1,0:T(2,128)S(1)}, f32[2,3,2,8,20]{4,2,3,1,0:T(2,128)S(1)}, u32[]{:S(2)}, u32[]{:S(2)}) collective-permute-start(f32[2,3,2,8,20]{4,2,3,1,0:T(2,128)S(1)} %get-tuple-element.26), channel_id=1, source_target_pairs={{0,32},{32,64},{64,96},{1,33},{33,65},{65,97},{2,34},{34,66},{66,9... | collective-permute-start | bytes 23048 | tf_op jit(solution)/shard_map/ppermute | solution.py:18
  66.1 4.8 %collective-permute-start.7 = (f32[2,3,2,8,20]{4,2,3,1,0:T(2,128)S(1)}, f32[2,3,2,8,20]{4,2,3,1,0:T(2,128)S(1)}, u32[]{:S(2)}, u32[]{:S(2)}) collective-permute-start(f32[2,3,2,8,20]{4,2,3,1,0:T(2,128)S(1)} %get-tuple-element.27), channel_id=1, source_target_pairs={{32,0},{64,32},{96,64},{33,1},{65,33},{97,65},{34,2},{66,34},{98,6... | collective-permute-start | bytes 23048 | tf_op jit(solution)/shard_map/ppermute | solution.py:20
  71.2 8.0 %collective-permute-start.8 = (f32[2,3,10,8,2]{4,2,3,1,0:T(8,128)S(1)}, f32[2,3,10,8,2]{4,2,3,1,0:T(8,128)S(1)}, u32[]{:S(2)}, u32[]{:S(2)}) collective-permute-start(f32[2,3,10,8,2]{4,2,3,1,0:T(8,128)S(1)} %get-tuple-element.22), channel_id=1, source_target_pairs={{0,1},{1,2},{2,3},{4,5},{5,6},{6,7},{8,9},{9,10},{10,11},{12,13},{... | collective-permute-start | bytes 11528 | tf_op jit(solution)/shard_map/ppermute | solution.py:18
  74.5 10.6 %collective-permute-start.9 = (f32[2,3,10,8,2]{4,2,3,1,0:T(8,128)S(1)}, f32[2,3,10,8,2]{4,2,3,1,0:T(8,128)S(1)}, u32[]{:S(2)}, u32[]{:S(2)}) collective-permute-start(f32[2,3,10,8,2]{4,2,3,1,0:T(8,128)S(1)} %get-tuple-element.23), channel_id=1, source_target_pairs={{1,0},{2,1},{3,2},{5,4},{6,5},{7,6},{9,8},{10,9},{11,10},{13,12},{... | collective-permute-start | bytes 11528 | tf_op jit(solution)/shard_map/ppermute | solution.py:20
  85.7 17.5 %copy-start.1 = (f32[2,3,2,32,16]{3,4,2,1,0:T(8,128)S(1)}, f32[2,3,2,32,16]{3,4,2,1,0:T(8,128)}, u32[]{:S(2)}) copy-start(f32[2,3,2,32,16]{3,4,2,1,0:T(8,128)} %param.3) | copy-start | bytes 73732
  103.3 21.3 %copy-start = (f32[2,3,2,32,16]{3,4,2,1,0:T(8,128)}, f32[2,3,2,32,16]{3,4,2,1,0:T(8,128)S(1)}, u32[]{:S(2)}) copy-start(f32[2,3,2,32,16]{3,4,2,1,0:T(8,128)S(1)} %fusion.44) | copy-start | bytes 73732
  103.3 4.9 %collective-permute-start.10 = (f32[2,3,2,32,16]{3,4,2,1,0:T(8,128)S(1)}, f32[2,3,2,32,16]{3,4,2,1,0:T(8,128)S(1)}, u32[]{:S(2)}, u32[]{:S(2)}) collective-permute-start(f32[2,3,2,32,16]{3,4,2,1,0:T(8,128)S(1)} %fusion.44), channel_id=1, source_target_pairs={{0,32},{32,64},{64,96},{1,33},{33,65},{65,97},{2,34},{34,66},{66,9... | collective-permute-start | bytes 73736 | tf_op jit(solution)/shard_map/ppermute | solution.py:18
  106.6 5.4 %collective-permute-start.11 = (f32[2,3,2,32,16]{3,4,2,1,0:T(8,128)S(1)}, f32[2,3,2,32,16]{3,4,2,1,0:T(8,128)S(1)}, u32[]{:S(2)}, u32[]{:S(2)}) collective-permute-start(f32[2,3,2,32,16]{3,4,2,1,0:T(8,128)S(1)} %fusion.44), channel_id=1, source_target_pairs={{32,0},{64,32},{96,64},{33,1},{65,33},{97,65},{34,2},{66,34},{98,6... | collective-permute-start | bytes 73736 | tf_op jit(solution)/shard_map/ppermute | solution.py:20
  112.0 6.9 %collective-permute-start.12 = (f32[2,3,6,32,2]{3,4,2,1,0:T(2,128)S(1)}, f32[2,3,6,32,2]{3,4,2,1,0:T(2,128)S(1)}, u32[]{:S(2)}, u32[]{:S(2)}) collective-permute-start(f32[2,3,6,32,2]{3,4,2,1,0:T(2,128)S(1)} %get-tuple-element.25), channel_id=1, source_target_pairs={{0,1},{1,2},{2,3},{4,5},{5,6},{6,7},{8,9},{9,10},{10,11},{12,13},{... | collective-permute-start | bytes 27656 | tf_op jit(solution)/shard_map/ppermute | solution.py:18
  116.6 6.8 %collective-permute-start.13 = (f32[2,3,6,32,2]{3,4,2,1,0:T(2,128)S(1)}, f32[2,3,6,32,2]{3,4,2,1,0:T(2,128)S(1)}, u32[]{:S(2)}, u32[]{:S(2)}) collective-permute-start(f32[2,3,6,32,2]{3,4,2,1,0:T(2,128)S(1)} %get-tuple-element.24), channel_id=1, source_target_pairs={{1,0},{2,1},{3,2},{5,4},{6,5},{7,6},{9,8},{10,9},{11,10},{13,12},{... | collective-permute-start | bytes 27656 | tf_op jit(solution)/shard_map/ppermute | solution.py:20
where the time goes:
time: 131 us; the launch traced here: 130 us
  starting transfers between devices  41 us (31%)
  waiting for transfers between devices  33.1 us (25%)
  matrix products  20 us (15%)
  other arithmetic  13.9 us (11%)
  blocking collectives  12.9 us (10%)
  local copies, waits for them, and re-layouts  8.26 us (6%)
    ppermute x7, starting transfers between devices, extended_2(): lax.ppermute(tail, axis, [(i, (i + 1) % count) for i in range(ends)])  29.8 us
    ppermute x7, waiting for transfers between devices, extended_2(): lax.ppermute(head, axis, [((i + 1) % count, i) for i in range(ends)])  29 us
    all_to_all x1, blocking collectives, copy_for_each(): lax.all_to_all(jnp.broadcast_to(value[None], (peers, *value.shape)), axis...  12.9 us
    ppermute x7, starting transfers between devices, extended_2(): lax.ppermute(head, axis, [((i + 1) % count, i) for i in range(ends)])  11.2 us
    dot_general x1, matrix products, shards(): along_z = jnp.einsum('hcxyz,zk->hcxyk', pushes, table_z, precision=highest)  6.22 us
    dot_general x1, matrix products, shards(): along_y = jnp.einsum('hcxyk,yj->hcxjk', along_z, table_y, precision=highest)  5.91 us
    add x2, other arithmetic, window_sum(): running + lax.slice_in_dim(values, offset, offset + keep_count, axis=whic...  5 us
    ppermute x7, waiting for transfers between devices, extended_2(): lax.ppermute(tail, axis, [(i, (i + 1) % count) for i in range(ends)])  4.14 us
  transfers between devices with their start and end apart: 14, of which 11 were waited for; matrix products, arithmetic and copies ran while one was open for 2% of the time, Pallas kernels for 0%

commit v1 on v0

v1 whole, which is shorter than its diff:
```python
import functools

import jax
import jax.numpy as jnp
import numpy as np
from jax import lax
from jax.experimental import pallas as pl
from jax.experimental.pallas import tpu as pltpu
from jax.sharding import PartitionSpec as P

epsilon_value = 1e-05
step_size = 0.5
f32 = jnp.float32
bf16 = jnp.bfloat16


def spline(t):
    m = np.abs(t)
    inside = 2.0 / 3.0 - m * m + 0.5 * m * m * m
    out = np.maximum(2.0 - m, 0.0)
    return np.where(m < 1.0, inside, out * out * out / 6.0)


def split_two(w):
    hi = w.astype(np.float32).astype(jnp.bfloat16)
    lo = (w - hi.astype(np.float64)).astype(np.float32).astype(jnp.bfloat16)
    return hi, lo


def seam_table(size, points, fold_from):
    idx = np.arange(size)
    pos = np.where(idx >= fold_from, idx - size, idx) if fold_from else idx - 4
    pts = np.arange(points) - 2
    w = spline((pos[None, :] - 8.0 * pts[:, None] - 3.5) / 8.0)
    same = (pos[None, :] < 0) == (pts[:, None] < 0)
    return w, w * same


def projection_tables(nx, ny, nz):
    bx, by, bz = nx // 8, ny // 8, nz // 8
    return bx, by, bz


def pack_kernel(img_ref, out_ref):
    lane = lax.broadcasted_iota(jnp.int32, (32, 128), 1)
    for h in range(2):
        acc = jnp.zeros((32, 128), f32)
        for t in range(16):
            moved = pltpu.roll(img_ref[h, t], (8 * t + 8) % 128, 1)
            acc = jnp.where((lane >= 8 * t) & (lane < 8 * t + 8), moved, acc)
        out_ref[h] = acc


def split3(v):
    hi = v.astype(bf16)
    r = v - hi.astype(f32)
    mid = r.astype(bf16)
    lo = (r - mid.astype(f32)).astype(bf16)
    return hi, mid, lo


def split2(v):
    hi = v.astype(bf16)
    return hi, (v - hi.astype(f32)).astype(bf16)


def dot(a, b):
    return jnp.dot(a, b, preferred_element_type=f32)


def up_by(v, n, row):
    size = v.shape[0]
    return jnp.where(row < size - n, pltpu.roll(v, size - n, 0), 0.0)


def rows_window(v, head, tail, row8, row40):
    first = v[0:8]
    own = jnp.concatenate([jnp.zeros((8, 128), f32), v[8:40]], axis=0)
    s = first + up_by(first, 1, row8)
    s = s + up_by(s, 2, row8)
    s = s + up_by(s, 4, row8)
    w = own + pltpu.roll(own, 39, 0)
    w = w + pltpu.roll(w, 38, 0)
    w = w + pltpu.roll(w, 36, 0)
    w = w[0:32] + own[8:40]
    top = head * s + tail * w[0:8]
    return jnp.concatenate([top, w[8:32]], axis=0)


def force_kernel(
    edge_ref,
    own_ref,
    zr_ref,
    xr_ref,
    yr_ref,
    xyr_ref,
    vel_ref,
    wxy_ref,
    wz_ref,
    out_ref,
    a_ref,
    h_ref,
    v_ref,
    dz_ref,
    xs_ref,
    hs_ref,
    fh_ref,
    fl_ref,
):
    ex = edge_ref[0]
    ey = edge_ref[1]
    ez = edge_ref[2]
    lane8 = lax.broadcasted_iota(jnp.int32, (8, 128), 1)
    row8 = lax.broadcasted_iota(jnp.int32, (8, 128), 0)
    lane32 = lax.broadcasted_iota(jnp.int32, (32, 128), 1)
    row32 = lax.broadcasted_iota(jnp.int32, (32, 128), 0)
    lane40 = lax.broadcasted_iota(jnp.int32, (40, 128), 1)
    row40 = lax.broadcasted_iota(jnp.int32, (40, 128), 0)
    head = jnp.where(row8 < 4, 1.0, ey)
    tail = jnp.where(row8 < 4, ey, 1.0)

    for h in range(2):
        for t in range(16):
            a_ref[h, 8 + t, 8:40] = own_ref[h, t]
            a_ref[h, 8 + t, 0:8] = yr_ref[h, t]
        for t in range(8):
            a_ref[h, t, 8:40] = xr_ref[h, t]
            a_ref[h, t, 0:8] = xyr_ref[h, t]
        h_ref[h, 0, 8:40] = zr_ref[h]
        h_ref[h, 0, 0:8] = yr_ref[h, 16]
        h_ref[h, 1, 8:40] = xr_ref[h, 8]
        h_ref[h, 1, 0:8] = xyr_ref[h, 8]

    plus_z = jnp.where(lane40 == 127, ez, 1.0)
    minus_z = jnp.where(lane40 == 0, ez, 1.0)
    for h in range(2):
        for l in range(3, 21):
            a = a_ref[h, l]
            if l >= 8:
                halo = pltpu.roll(h_ref[h, 0], (120 - 8 * (l - 8)) % 128, 1)
            else:
                halo = pltpu.roll(h_ref[h, 1], (120 - 8 * (l + 8)) % 128, 1)
            v_ref[h, l - 3] = jnp.where(lane40 >= 124, halo, a)
            if 4 <= l < 20:
                up = pltpu.roll(jnp.where(lane40 >= 125, halo, a), 127, 1)
                down = pltpu.roll(jnp.where(lane40 >= 123, halo, a), 1, 1)
                dz_ref[h, l - 4] = plus_z * up - minus_z * down

    def products(f, m):
        return (f, m, f * f, m * m, f * m)

    def x_step(tile, carry):
        rows = pl.ds(pl.multiple_of(tile * 8, 8), 8)
        for q in range(5):
            p = []
            for l in range(24):
                if q == 0:
                    p.append(a_ref[0, l, rows])
                elif q == 1:
                    p.append(a_ref[1, l, rows])
                elif q == 2:
                    f = a_ref[0, l, rows]
                    p.append(f * f)
                elif q == 3:
                    m = a_ref[1, l, rows]
                    p.append(m * m)
                else:
                    p.append(a_ref[0, l, rows] * a_ref[1, l, rows])
            left = [None] * 8
            left[7] = p[7]
            for o in range(6, -1, -1):
                left[o] = left[o + 1] + p[o]
            right = [None] * 8
            right[0] = p[8]
            for o in range(1, 8):
                right[o] = right[o - 1] + p[o + 8]
            for o in range(8):
                xs_ref[q, o, rows] = left[o] + ex * right[o] if o < 4 else ex * left[o] + right[o]
            s = p[8:24]
            b = [s[n] + s[n + 1] for n in range(15)]
            b = [b[n] + b[n + 2] for n in range(13)]
            b = [b[n] + b[n + 4] for n in range(9)]
            for o in range(8):
                xs_ref[q, 8 + o, rows] = b[o] + s[o + 8]
        return carry

    lax.fori_loop(0, 5, x_step, 0)

    src = lax.broadcasted_iota(jnp.int32, (256, 128), 0)
    dst = lax.broadcasted_iota(jnp.int32, (256, 128), 1)
    plane = jnp.where(src < 128, lax.shift_right_logical(src, 3) + 8, lax.shift_right_logical(src - 128, 3) - 8)
    goal = lax.shift_right_logical(dst, 3)
    near = (plane >= goal) & (plane <= goal + 8) & ((src & 7) == (dst & 7)) & (plane >= 0)
    across = (plane < 8) != (goal < 4)
    x_sum = jnp.where(near, jnp.where(across, ex, 1.0), 0.0).astype(bf16)
    for q in range(5):
        parts = []
        for side in range(2):
            f = h_ref[0, side]
            m = h_ref[1, side]
            parts.append(rows_window(products(f, m)[q], head, tail, row8, row40))
        both = jnp.concatenate(parts, axis=1)
        total = jnp.zeros((32, 128), f32)
        for piece in split3(both):
            total = total + dot(piece, x_sum)
        for n, piece in enumerate(split3(total)):
            hs_ref[q, n] = piece

    centre = jnp.where(dst < 124, dst, dst - 128)
    below = src >= 128
    place = jnp.where(below, (src & 7) - 8, src)
    gap = place - centre
    inside = (gap <= 4) & (gap >= -4)
    crossing = below != (dst >= 124)
    z_sum = jnp.where(inside, jnp.where(crossing, ez, 1.0), 0.0).astype(bf16)

    plus_y = jnp.where(row32 == 3, ey, 1.0)
    minus_y = jnp.where(row32 == 4, ey, 1.0)
    group = lax.shift_right_logical(lane32, 3)

    def o_step(o, carry):
        pieces = [[], [], []]
        mine = group == o
        for q in range(5):
            y = rows_window(xs_ref[q, o], head, tail, row8, row40)
            for n, piece in enumerate(split3(y)):
                halo = jnp.where(mine, hs_ref[q, n].astype(f32), 0.0).astype(bf16)
                pieces[n].append(jnp.concatenate([piece, halo], axis=1))
        sums = dot(jnp.concatenate(pieces[0], axis=0), z_sum)
        sums = sums + dot(jnp.concatenate(pieces[1], axis=0), z_sum)
        sums = sums + dot(jnp.concatenate(pieces[2], axis=0), z_sum)
        sums = sums * (1.0 / 729.0)
        mean_f = sums[0:32]
        mean_m = sums[32:64]
        var_f = sums[64:96] - mean_f * mean_f + epsilon_value
        var_m = sums[96:128] - mean_m * mean_m + epsilon_value
        cov = sums[128:160] - mean_f * mean_m
        off_f = v_ref[0, o + 1, 4:36] - mean_f
        off_m = v_ref[1, o + 1, 4:36] - mean_m
        inv = 1.0 / (var_f * var_m)
        factor = cov * inv
        pulls = (
            factor * (off_m - factor * var_m * off_f),
            factor * (off_f - factor * var_f * off_m),
        )
        plus_x = jnp.where(o == 3, ex, 1.0)
        minus_x = jnp.where(o == 4, ex, 1.0)
        where_to = pl.ds(pl.multiple_of(o * 32, 32), 32)
        for h in range(2):
            dx = plus_x * v_ref[h, o + 2, 4:36] - minus_x * v_ref[h, o, 4:36]
            dy = plus_y * v_ref[h, o + 1, 5:37] - minus_y * v_ref[h, o + 1, 3:35]
            dz = dz_ref[h, o, 4:36]
            for c, d in enumerate((dx, dy, dz)):
                hi, lo = split2(pulls[h] * d)
                fh_ref[3 * h + c, where_to] = hi
                fl_ref[3 * h + c, where_to] = lo
        return carry

    lax.fori_loop(0, 16, o_step, 0)

    total = jnp.zeros((40, 128), f32)
    for c in range(6):
        first = dot(wxy_ref[...], fh_ref[c])
        second = dot(wxy_ref[0:40], fl_ref[c])
        xy = first[0:40] + first[40:80] + second
        hi, lo = split2(xy)
        total = total + dot(hi, wz_ref[0, c]) + dot(hi, wz_ref[1, c]) + dot(lo, wz_ref[0, c])
    total = step_size * total
    out_ref[0:16] = total[0:16]
    out_ref[16:32] = total[16:32] + vel_ref[...]
    out_ref[32:40] = total[32:40]


def fold_kernel(mine_ref, low_ref, high_ref, out_ref):
    lane = lax.broadcasted_iota(jnp.int32, (40, 128), 1)
    spot = lax.rem(lane, 20)
    live = lane < 120
    low = pltpu.roll(low_ref[...], 112, 1)
    high = pltpu.roll(high_ref[...], 16, 1)
    total = mine_ref[...]
    total = total + jnp.where(live & (spot < 3), low, 0.0)
    total = total + jnp.where(live & (spot >= 16), high, 0.0)
    for n in range(32):
        out_ref[n] = total


def field_kernel(at_ref, g_ref, wxy_ref, wz_ref, nv_ref, field_ref, rows_ref):
    me_i = at_ref[0]
    me_j = at_ref[1]
    row8 = lax.broadcasted_iota(jnp.int32, (8, 128), 0)
    slot = [lax.rem(me_i + d, 4) * 8 for d in range(4)]

    def piece(d, j, p):
        return g_ref[slot[d] + j, 8 * p : 8 * p + 8]

    for side in range(2):
        cols = []
        for j in range(8):
            if side == 0:
                cols.append(piece(0, j, 2) + piece(3, j, 4) + piece(1, j, 0))
            else:
                cols.append(piece(0, j, 3) + piece(1, j, 1))
        turned = [pltpu.roll(c, 4, 0) for c in cols]
        tiles = []
        for n in range(5):
            zero = jnp.zeros((8, 128), f32)
            even = cols[2 * n] if n < 4 else zero
            high = turned[2 * n + 1] if n < 4 else zero
            low = turned[2 * n - 1] if n > 0 else zero
            tiles.append(even + jnp.where(row8 < 4, low, high))
        tiles[4] = tiles[4] + tiles[0]
        for n in range(5):
            rows_ref[8 * n : 8 * n + 8] = tiles[n]
        block = rows_ref[2:34]
        for c in range(6):
            nv_ref[c, side] = block[:, 20 * c + 2 : 20 * c + 18]

    window = []
    js = [lax.rem(me_j + 7, 8), me_j, lax.rem(me_j + 1, 8)]
    for w in range(6):
        sums = []
        for j in js:
            terms = []
            if w <= 4:
                terms.append(piece(0, j, w))
            if w <= 2:
                terms.append(piece(3, j, w + 2))
            if w >= 2:
                terms.append(piece(1, j, w - 2))
            if w == 0:
                terms.append(piece(2, j, 4))
            if w >= 4:
                terms.append(piece(2, j, w - 4))
            total = terms[0]
            for t in terms[1:]:
                total = total + t
            sums.append(total)
        before = pltpu.roll(sums[0], 4, 0)
        after = pltpu.roll(sums[2], 4, 0)
        window.append(sums[1] + jnp.where(row8 < 4, before, after))
    coefs = jnp.concatenate(window, axis=0)
    hi, lo = split2(coefs)
    for c in range(6):
        along = dot(hi, wz_ref[0, c]) + dot(hi, wz_ref[1, c]) + dot(lo, wz_ref[0, c])
        ch, cl = split2(along)
        rhs = jnp.concatenate([ch, cl, ch], axis=0)
        field_ref[c] = dot(wxy_ref[...], rhs).astype(bf16)


VMEM = pl.BlockSpec(memory_space=pltpu.VMEM)
SMEM = pl.BlockSpec(memory_space=pltpu.SMEM)


def call(body, out_shape, in_specs, scratch=(), flops=0, bytes_accessed=0):
    many = isinstance(out_shape, (list, tuple))
    return pl.pallas_call(
        body,
        out_shape=out_shape,
        in_specs=in_specs,
        out_specs=[VMEM] * len(out_shape) if many else VMEM,
        scratch_shapes=list(scratch),
        compiler_params=pltpu.CompilerParams(vmem_limit_bytes=48 << 20),
        cost_estimate=pl.CostEstimate(flops=flops, bytes_accessed=bytes_accessed, transcendentals=0),
    )


def pairs(mesh_sizes, di, dj, dk):
    ni, nj, nk = mesh_sizes
    out = []
    for i in range(ni):
        for j in range(nj):
            for k in range(nk):
                to = (((i + di) % ni) * nj + (j + dj) % nj) * nk + (k + dk) % nk
                out.append(((i * nj + j) * nk + k, to))
    return out


def at_edge(table, first, edge, is_first):
    return jnp.where(is_first, first, table) * edge


def shards(images, velocity):
    axes = ("gx", "gy", "gz")
    sizes = tuple(lax.axis_size(a) for a in axes)
    i, j, k = (lax.axis_index(a) for a in axes)
    ni, nj, nk = sizes

    def send(v, di, dj, dk):
        return lax.ppermute(v, axes, pairs(sizes, di, dj, dk))

    pack = call(pack_kernel, jax.ShapeDtypeStruct((2, 32, 128), f32), [VMEM])(images)
    zr = lax.ppermute(pack, "gz", [(n, (n + 1) % nk) for n in range(nk)])
    to_x = jnp.concatenate([images[:, 8:], zr[:, None]], axis=1)
    to_y = jnp.concatenate([images[:, :, 24:], zr[:, None, 24:]], axis=1)
    to_xy = jnp.concatenate([images[:, 8:, 24:], zr[:, None, 24:]], axis=1)
    xr = send(to_x, 1, 0, 0)
    yr = send(to_y, 0, 1, 0)
    xyr = send(to_xy, 1, 1, 0)

    def parts(size, points, fold_from, at, count):
        plain, first = seam_table(size, points, fold_from)
        keep = np.ones((points, 1))
        keep[-1] = 0.0
        return plain, first, keep

    wx, wx0, kx = parts(16, 5, 0, i, ni)
    wy, wy0, ky = parts(32, 7, 0, j, nj)
    pad = lambda t: np.concatenate([t, np.zeros((1,) + t.shape[1:])], axis=0)
    wy, wy0, ky = pad(wy), pad(wy0), pad(ky)
    ky[7] = 1.0
    flat = (np.einsum("po,qr->pqor", wx, wy)).reshape(40, 512)
    hi, lo = split_two(flat)
    side_x = np.broadcast_to(((wx0 != 0) | (wx == 0))[:, None, :, None], (5, 8, 16, 32)).reshape(40, 512)
    side_y = np.broadcast_to(((wy0 != 0) | (wy == 0))[None, :, None, :], (5, 8, 16, 32)).reshape(40, 512)
    last_x = np.broadcast_to(kx[:, None], (5, 8, 1)).reshape(40, 1)
    last_y = np.broadcast_to(ky[None], (5, 8, 1)).reshape(40, 1)
    mask = (
        jnp.where(i == 0, side_x.astype(jnp.bfloat16), bf16(1))
        * jnp.where(j == 0, side_y.astype(jnp.bfloat16), bf16(1))
        * jnp.where(i == ni - 1, last_x.astype(jnp.bfloat16), bf16(1))
        * jnp.where(j == nj - 1, last_y.astype(jnp.bfloat16), bf16(1))
    )
    wxy = jnp.concatenate([hi * mask, lo * mask], axis=0)
    wz, wz0, kz = parts(128, 19, 124, k, nk)
    canvas = np.zeros((3, 6, 128, 128))
    for c in range(6):
        canvas[0, c, :, 20 * c : 20 * c + 19] = wz.T
        canvas[1, c, :, 20 * c : 20 * c + 19] = (wz0 != 0).T | (wz == 0).T
        canvas[2, c, :, 20 * c : 20 * c + 19] = kz.T
    zhi, zlo = split_two(canvas[0])
    zmask = jnp.where(k == 0, canvas[1].astype(jnp.bfloat16), bf16(1)) * jnp.where(
        k == nk - 1, canvas[2].astype(jnp.bfloat16), bf16(1)
    )
    wzs = jnp.stack([zhi * zmask, zlo * zmask])

    rows = lax.dynamic_slice_in_dim(velocity, j * 4, 4, 3)
    vel = jnp.transpose(rows, (2, 3, 0, 1, 4)).reshape(2, 4, 6, 16)
    vel = jnp.pad(vel, ((0, 0), (2, 2), (0, 0), (2, 2))).reshape(16, 120)
    vel = jnp.pad(vel, ((0, 0), (0, 8)))

    edges = jnp.stack([i != 0, j != 0, k != 0]).astype(f32)
    part = call(
        force_kernel,
        jax.ShapeDtypeStruct((40, 128), f32),
        [SMEM] + [VMEM] * 8,
        [
            pltpu.VMEM((2, 24, 40, 128), f32),
            pltpu.VMEM((2, 2, 40, 128), f32),
            pltpu.VMEM((2, 18, 40, 128), f32),
            pltpu.VMEM((2, 16, 40, 128), f32),
            pltpu.VMEM((5, 16, 40, 128), f32),
            pltpu.VMEM((5, 3, 32, 128), bf16),
            pltpu.VMEM((6, 512, 128), bf16),
            pltpu.VMEM((6, 512, 128), bf16),
        ],
        flops=10**9,
        bytes_accessed=2 * 10**6,
    )(edges, images, zr, xr, yr, xyr, vel, wxy, wzs)

    low = lax.ppermute(part, "gz", [(n, (n + 1) % nk) for n in range(nk)])
    high = lax.ppermute(part, "gz", [((n + 1) % nk, n) for n in range(nk)])
    copies = call(fold_kernel, jax.ShapeDtypeStruct((32, 40, 128), f32), [VMEM] * 3)(part, low, high)
    everything = lax.all_to_all(copies, ("gx", "gy"), 0, 0, tiled=True)

    pos = lambda n: np.arange(n)[:, None]
    ex = spline((pos(16) - 8.0 * (np.arange(6)[None] - 2) - 3.5) / 8.0)
    ey = spline((pos(32) - 8.0 * (np.arange(8)[None] - 2) - 3.5) / 8.0)
    ez = spline((pos(128) - 8.0 * (np.arange(20)[None] - 2) - 3.5) / 8.0)
    ehi, elo = split_two(np.einsum("xp,yq->xypq", ex, ey).reshape(512, 48))
    pt_x = 2 * i - 2 + np.arange(48) // 8
    pt_y = 4 * j - 2 + np.arange(48) % 8
    real = ((pt_x >= 0) & (pt_x < 2 * ni) & (pt_y >= 0) & (pt_y < 4 * nj)).astype(bf16)[None]
    exy = jnp.concatenate([ehi * real, ehi * real, elo * real], axis=1)
    zc = np.zeros((6, 128, 128))
    for c in range(6):
        zc[c, 20 * c : 20 * c + 20] = ez.T
    chi, clo = split_two(zc)
    pt_z = 16 * k - 2 + np.arange(128) % 20
    zreal = ((pt_z >= 0) & (pt_z < 16 * nk)).astype(bf16)[:, None]
    ezs = jnp.stack([chi * zreal, clo * zreal])
    at = jnp.stack([i, j]).astype(jnp.int32)
    nv, field = call(
        field_kernel,
        [jax.ShapeDtypeStruct((6, 2, 32, 16), f32), jax.ShapeDtypeStruct((6, 512, 128), bf16)],
        [SMEM] + [VMEM] * 3,
        [pltpu.VMEM((40, 128), f32)],
        flops=10**8,
        bytes_accessed=10**6,
    )(at, everything, exy, ezs)
    return nv.reshape(2, 3, 2, 32, 16), field.reshape(2, 3, 16, 32, 128)


def solution(mesh):
    placed = (P(None, "gx", "gy", "gz"), P(None, None, "gx", None, "gz"))
    return jax.shard_map(
        shards,
        mesh=mesh,
        in_specs=placed,
        out_specs=(P(None, None, "gx", None, "gz"), P(None, None, "gx", "gy", "gz")),
        check_vma=False,
    )
```

time: 131 us -> 58.5 us (0.45)
  the two profiles are of different devices: /device:TPU:1 before, /device:TPU:0 now
where the time goes in v1:
time: 58.5 us; the launch traced here: 58.2 us
  waiting for transfers between devices  25.5 us (44%)
  starting transfers between devices  13.4 us (23%)
  Pallas kernels  12.3 us (21%)
  local copies, waits for them, and re-layouts  5.33 us (9%)
  between operations  0.94 us (2%)
  other arithmetic  0.77 us (1%)
    all_to_all x1, waiting for transfers between devices, shards(): everything = lax.all_to_all(copies, ('gx', 'gy'), 0, 0, tiled=True)  12.1 us
    pallas_call x1, Pallas kernels, shards(): call(force_kernel, jax.ShapeDtypeStruct((40, 128), f32), [SMEM] + [VMEM]...  8.62 us
    ppermute x3, waiting for transfers between devices, send(): return lax.ppermute(v, axes, pairs(sizes, di, dj, dk))  7.74 us
    ppermute x3, starting transfers between devices, send(): return lax.ppermute(v, axes, pairs(sizes, di, dj, dk))  6.48 us
    all_to_all x1, starting transfers between devices, shards(): everything = lax.all_to_all(copies, ('gx', 'gy'), 0, 0, tiled=True)  6.3 us
    unnamed x43, local copies, waits for them, and re-layouts  4.89 us
    ppermute x1, waiting for transfers between devices, shards(): low = lax.ppermute(part, 'gz', [(n, (n + 1) % nk) for n in range(nk)])  3.31 us
    pallas_call x1, Pallas kernels, shards(): call(field_kernel, [jax.ShapeDtypeStruct((6, 2, 32, 16), f32), jax.ShapeD...  2.55 us
  transfers between devices with their start and end apart: 7, of which 5 were waited for; matrix products, arithmetic and copies ran while one was open for 2% of the time, Pallas kernels for 0%

profile of v1, /device:TPU:0, one launch (start us, length us, event | category | flops | bytes accessed | tf_op | source)
XLA Modules:
  0.0 58.2 jit_solution(14030082809549274392)
XLA Ops:
  0.6 0.0 copy-start
  0.6 0.0 copy-start.1
  0.7 1.1 %copy-done.1 = f32[2,16,32,128]{3,2,1,0:T(8,128)S(1)} copy-done((f32[2,16,32,128]{3,2,1,0:T(8,128)S(1)}, f32[2,16,32,128]{3,2,1,0:T(8,128)}, u32[]{:S(2)}) %copy-start.1) | copy-done | bytes 524312
  1.7 0.0 copy-start.7
  1.7 0.2 shard_map.194
  1.9 0.0 copy-start.6
  1.9 0.1 collective-permute-start
  2.0 0.0 copy-done
  2.1 0.1 constant_dynamic-slice_fusion
  2.1 0.5 copy-done.7
  2.6 0.1 copy-done.8
  2.7 0.1 copy-done.9
  2.8 0.2 copy-done.6
  3.0 0.0 copy-start.16
  3.1 0.0 copy-start.17
  3.1 0.0 copy-start.10
  3.1 0.0 copy-start.11
  3.1 0.0 copy-start.12
  3.1 0.0 copy-start.13
  3.1 0.0 copy-start.14
  3.1 0.0 copy-start.15
  3.2 0.5 copy-done.16
  3.7 0.0 copy-done.17
  3.7 0.3 copy-done.10
  4.0 0.1 copy-done.11
  4.1 0.6 %copy-done.18 = bf16[40,1]{0,1:T(2,128)(2,1)S(1)} copy-done((bf16[40,1]{0,1:T(2,128)(2,1)S(1)}, bf16[40,1]{0,1:T(2,128)(2,1)}, u32[]{:S(2)}) %copy-start.18) | copy-done | bytes 104
  4.7 0.0 copy-done.19
  4.7 0.0 copy-done.12
  4.7 0.0 copy-done.13
  4.7 0.0 copy-done.14
  4.7 0.0 copy-done.15
  4.8 0.1 fusion.1
  4.9 0.0 copy-done.2
  4.9 0.0 slice-start.1
  4.9 0.2 copy.25
  5.1 0.1 pad.8
  5.2 0.1 reshape.19
  5.3 1.6 %collective-permute-done.zr_ref = f32[2,32,128]{2,1,0:T(8,128)S(1)} collective-permute-done((f32[2,32,128]{2,1,0:T(8,128)S(1)}, f32[2,32,128]{2,1,0:T(8,128)S(1)}, u32[]{:S(2)}, u32[]{:S(2)}) %collective-permute-start) | collective-permute-done | bytes 32800 | tf_op jit(solution)/shard_map/ppermute | solution.py:392
  6.8 0.0 slice-done.1
  6.9 2.1 %collective-permute-start.1 = (f32[2,9,32,128]{3,2,1,0:T(8,128)S(1)}, f32[2,9,32,128]{3,2,1,0:T(8,128)S(1)}, u32[]{:S(2)}, u32[]{:S(2)}) collective-permute-start(f32[2,9,32,128]{3,2,1,0:T(8,128)S(1)} %pad_maximum_fusion.2), channel_id=1, source_target_pairs={{0,32},{1,33},{2,34},{3,35},{4,36},{5,37},{6,38},{7,39},{8,40},{9,... | collective-permute-start | bytes 884744 | tf_op jit(solution)/shard_map/ppermute | solution.py:389
  8.9 0.0 slice-done
  9.0 1.6 %collective-permute-start.2 = (f32[2,17,8,128]{3,2,1,0:T(8,128)S(1)}, f32[2,17,8,128]{3,2,1,0:T(8,128)S(1)}, u32[]{:S(2)}, u32[]{:S(2)}) collective-permute-start(f32[2,17,8,128]{3,2,1,0:T(8,128)S(1)} %pad_maximum_fusion.4), channel_id=1, source_target_pairs={{0,4},{1,5},{2,6},{3,7},{4,8},{5,9},{6,10},{7,11},{8,12},{9,13},{1... | collective-permute-start | bytes 417800 | tf_op jit(solution)/shard_map/ppermute | solution.py:389
  10.5 2.8 %collective-permute-start.3 = (f32[2,9,8,128]{3,2,1,0:T(8,128)S(1)}, f32[2,9,8,128]{3,2,1,0:T(8,128)S(1)}, u32[]{:S(2)}, u32[]{:S(2)}) collective-permute-start(f32[2,9,8,128]{3,2,1,0:T(8,128)S(1)} %pad_maximum_fusion.6), channel_id=1, source_target_pairs={{0,36},{1,37},{2,38},{3,39},{4,40},{5,41},{6,42},{7,43},{8,44},{9,... | collective-permute-start | bytes 221192 | tf_op jit(solution)/shard_map/ppermute | solution.py:389
  13.4 0.1 add_convert_fusion.edge_ref
  13.5 7.7 %collective-permute-done.3.xyr_ref = f32[2,9,8,128]{3,2,1,0:T(8,128)S(1)} collective-permute-done((f32[2,9,8,128]{3,2,1,0:T(8,128)S(1)}, f32[2,9,8,128]{3,2,1,0:T(8,128)S(1)}, u32[]{:S(2)}, u32[]{:S(2)}) %collective-permute-start.3) | collective-permute-done | bytes 73760 | tf_op jit(solution)/shard_map/ppermute | solution.py:389
  21.2 0.0 collective-permute-done.2.yr_ref
  21.2 0.0 collective-permute-done.1.xr_ref
  21.2 0.0 copy-done.3
  21.2 8.6 %shard_map.195.mine_ref = f32[40,128]{1,0:T(8,128)S(1)} custom-call(f32[3]{0:T(128)S(1)} %add_convert_fusion.edge_ref, f32[2,16,32,128]{3,2,1,0:T(8,128)S(1)} %copy-done.3, f32[2,32,128]{2,1,0:T(8,128)S(1)} %collective-permute-done.zr_ref, f32[2,9,32,128]{3,2,1,0:T(8,128)S(1)} %collective-permute-done.1.xr_ref, ...), custom_call_target="tpu_custom_call" | custom-call | flops 1000000000 | bytes 2000000 | tf_op jit(solution)/shard_map/pallas_call | solution.py:442
  29.8 0.1 collective-permute-start.5
  29.9 0.5 collective-permute-start.4
  30.4 0.2 pad_maximum_fusion.3.wxy_ref
  30.6 0.8 %collective-permute-done.5.high_ref = f32[40,128]{1,0:T(8,128)S(1)} collective-permute-done((f32[40,128]{1,0:T(8,128)S(1)}, f32[40,128]{1,0:T(8,128)S(1)}, u32[]{:S(2)}, u32[]{:S(2)}) %collective-permute-start.5) | collective-permute-done | bytes 20512 | tf_op jit(solution)/shard_map/ppermute | solution.py:461
  31.4 3.3 %collective-permute-done.4.low_ref = f32[40,128]{1,0:T(8,128)S(1)} collective-permute-done((f32[40,128]{1,0:T(8,128)S(1)}, f32[40,128]{1,0:T(8,128)S(1)}, u32[]{:S(2)}, u32[]{:S(2)}) %collective-permute-start.4) | collective-permute-done | bytes 20512 | tf_op jit(solution)/shard_map/ppermute | solution.py:460
  34.7 1.0 %shard_map.196 = f32[32,40,128]{2,1,0:T(8,128)} custom-call(f32[40,128]{1,0:T(8,128)S(1)} %shard_map.195.mine_ref, f32[40,128]{1,0:T(8,128)S(1)} %collective-permute-done.4.low_ref, f32[40,128]{1,0:T(8,128)S(1)} %collective-permute-done.5.high_ref), custom_call_target="tpu_custom_call" | custom-call | tf_op jit(solution)/shard_map/pallas_call | solution.py:462
  35.7 6.3 %all-to-all-start = ((f32[32,40,128]{2,1,0:T(8,128)}), f32[32,40,128]{2,1,0:T(8,128)S(1)}, u32[]{:S(2)}, u32[]{:S(2)}) async-start(f32[32,40,128]{2,1,0:T(8,128)} %shard_map.196), calls=%async_computation | async-start | bytes 1310720 | tf_op jit(solution)/shard_map/all_to_all | solution.py:463
  42.0 0.1 pad_add_fusion.at_ref
  42.0 0.7 %copy-done.20 = s32[128]{0:T(128)S(1)} copy-done((s32[128]{0:T(128)S(1)}, s32[128]{0:T(128)}, u32[]{:S(2)}) %copy-start.20) | copy-done | bytes 536
  42.7 0.0 copy-done.4
  42.7 0.0 copy-done.5
  42.7 0.1 multiply_bitcast_fusion.1
  42.9 12.1 %all-to-all-done.g_ref = f32[32,40,128]{2,1,0:T(8,128)S(1)} async-done(((f32[32,40,128]{2,1,0:T(8,128)}), f32[32,40,128]{2,1,0:T(8,128)S(1)}, u32[]{:S(2)}, u32[]{:S(2)}) %all-to-all-start) | async-done | bytes 655392 | tf_op jit(solution)/shard_map/all_to_all | solution.py:463
  54.9 2.5 %shard_map.197 = (f32[6,2,32,16]{3,2,1,0:T(8,128)S(1)}, bf16[6,512,128]{2,1,0:T(8,128)(2,1)}) custom-call(s32[2]{0:T(128)S(1)} %pad_add_fusion.at_ref, f32[32,40,128]{2,1,0:T(8,128)S(1)} %all-to-all-done.g_ref, bf16[512,144]{1,0:T(8,128)(2,1)S(1)} %pad_maximum_fusion.3.wxy_ref, bf16[2,6,128,128]{3,2,1,0:T(8,128)(2,1)S(1)} %pad_maximum_fusion.1.wz_ref), custom_call_target="tpu_custom_call" | custom-call | flops 100000000 | bytes 1000000 | tf_op jit(solution)/shard_map/pallas_call | solution.py:482
  57.5 0.8 %copy.26 = f32[2,3,2,32,16]{3,4,2,1,0:T(8,128)} copy(f32[2,3,2,32,16]{4,3,2,1,0:T(8,128)S(1)} %bitcast.27) | data formatting | bytes 49152
  (24 shorter events, 0.3 us)
Async XLA Ops:
  0.6 1.4 %copy-start = (f32[2,3,2,32,16]{3,4,2,1,0:T(8,128)S(1)}, f32[2,3,2,32,16]{3,4,2,1,0:T(8,128)}, u32[]{:S(2)}) copy-start(f32[2,3,2,32,16]{3,4,2,1,0:T(8,128)} %param.20) | copy-start | bytes 73732
  0.6 1.1 %copy-start.1 = (f32[2,16,32,128]{3,2,1,0:T(8,128)S(1)}, f32[2,16,32,128]{3,2,1,0:T(8,128)}, u32[]{:S(2)}) copy-start(f32[2,16,32,128]{3,2,1,0:T(8,128)} %own_ref.1) | copy-start | bytes 1572868
  1.7 0.9 %copy-start.7 = (bf16[6,128,128]{2,1,0:T(8,128)(2,1)S(1)}, bf16[6,128,128]{2,1,0:T(8,128)(2,1)}, u32[]{:S(2)}) copy-start(bf16[6,128,128]{2,1,0:T(8,128)(2,1)} %constant.84.clone) | copy-start | bytes 589828
  1.7 1.0 %copy-start.8 = (bf16[6,128,128]{2,1,0:T(8,128)(2,1)S(1)}, bf16[6,128,128]{2,1,0:T(8,128)(2,1)}, u32[]{:S(2)}) copy-start(bf16[6,128,128]{2,1,0:T(8,128)(2,1)} %constant.83.clone) | copy-start | bytes 589828
  1.7 1.1 %copy-start.9 = (bf16[6,128,128]{2,1,0:T(8,128)(2,1)S(1)}, bf16[6,128,128]{2,1,0:T(8,128)(2,1)}, u32[]{:S(2)}) copy-start(bf16[6,128,128]{2,1,0:T(8,128)(2,1)} %constant.82.clone) | copy-start | bytes 589828
  1.9 1.1 %copy-start.6 = (bf16[6,128,128]{2,1,0:T(8,128)(2,1)S(1)}, bf16[6,128,128]{2,1,0:T(8,128)(2,1)}, u32[]{:S(2)}) copy-start(bf16[6,128,128]{2,1,0:T(8,128)(2,1)} %constant.85.clone) | copy-start | bytes 589828
  1.9 4.9 %collective-permute-start = (f32[2,32,128]{2,1,0:T(8,128)S(1)}, f32[2,32,128]{2,1,0:T(8,128)S(1)}, u32[]{:S(2)}, u32[]{:S(2)}) collective-permute-start(f32[2,32,128]{2,1,0:T(8,128)S(1)} %shard_map.194), channel_id=1, source_target_pairs={{0,1},{1,2},{2,3},{3,0},{4,5},{5,6},{6,7},{7,4},{8,9},{9,10},{10,1... | collective-permute-start | bytes 98312 | tf_op jit(solution)/shard_map/ppermute | solution.py:392
  3.0 0.7 %copy-start.16 = (s32[48]{0:T(128)S(1)}, s32[48]{0:T(128)}, u32[]{:S(2)}) copy-start(s32[48]{0:T(128)} %constant.87.clone) | copy-start | bytes 580
  3.1 0.7 %copy-start.17 = (s32[48]{0:T(128)S(1)}, s32[48]{0:T(128)}, u32[]{:S(2)}) copy-start(s32[48]{0:T(128)} %constant.86.clone) | copy-start | bytes 580
  3.1 0.9 %copy-start.10 = (bf16[512,48]{1,0:T(8,128)(2,1)S(1)}, bf16[512,48]{1,0:T(8,128)(2,1)}, u32[]{:S(2)}) copy-start(bf16[512,48]{1,0:T(8,128)(2,1)} %constant.89.clone) | copy-start | bytes 147460
  3.1 1.0 %copy-start.11 = (bf16[512,48]{1,0:T(8,128)(2,1)S(1)}, bf16[512,48]{1,0:T(8,128)(2,1)}, u32[]{:S(2)}) copy-start(bf16[512,48]{1,0:T(8,128)(2,1)} %constant.88.clone) | copy-start | bytes 147460
  3.1 1.6 %copy-start.12 = (bf16[40,512]{1,0:T(8,128)(2,1)S(1)}, bf16[40,512]{1,0:T(8,128)(2,1)}, u32[]{:S(2)}) copy-start(bf16[40,512]{1,0:T(8,128)(2,1)} %constant.81.clone) | copy-start | bytes 122884
  3.1 1.6 %copy-start.13 = (bf16[40,512]{1,0:T(8,128)(2,1)S(1)}, bf16[40,512]{1,0:T(8,128)(2,1)}, u32[]{:S(2)}) copy-start(bf16[40,512]{1,0:T(8,128)(2,1)} %constant.80.clone) | copy-start | bytes 122884
  3.1 1.6 %copy-start.14 = (bf16[40,512]{1,0:T(8,128)(2,1)S(1)}, bf16[40,512]{1,0:T(8,128)(2,1)}, u32[]{:S(2)}) copy-start(bf16[40,512]{1,0:T(8,128)(2,1)} %constant.77.clone) | copy-start | bytes 122884
  3.1 1.6 %copy-start.15 = (bf16[40,512]{1,0:T(8,128)(2,1)S(1)}, bf16[40,512]{1,0:T(8,128)(2,1)}, u32[]{:S(2)}) copy-start(bf16[40,512]{1,0:T(8,128)(2,1)} %constant.76.clone) | copy-start | bytes 122884
  3.7 1.2 %copy-start.2 = (f32[2,16,32,128]{3,2,1,0:T(8,128)S(1)}, f32[2,16,32,128]{3,2,1,0:T(8,128)}, u32[]{:S(2)}) copy-start(f32[2,16,32,128]{3,2,1,0:T(8,128)} %own_ref.1) | copy-start | bytes 1572868
  4.0 0.7 %copy-start.18 = (bf16[40,1]{0,1:T(2,128)(2,1)S(1)}, bf16[40,1]{0,1:T(2,128)(2,1)}, u32[]{:S(2)}) copy-start(bf16[40,1]{0,1:T(2,128)(2,1)} %constant.79.clone) | copy-start | bytes 244
  4.0 0.7 %copy-start.19 = (bf16[40,1]{0,1:T(2,128)(2,1)S(1)}, bf16[40,1]{0,1:T(2,128)(2,1)}, u32[]{:S(2)}) copy-start(bf16[40,1]{0,1:T(2,128)(2,1)} %constant.78.clone) | copy-start | bytes 244
  4.9 1.9 %slice-start.1 = ((f32[2,16,32,128]{3,2,1,0:T(8,128)}), f32[2,8,32,128]{3,2,1,0:T(8,128)S(1)}, s32[]{:S(2)}) async-start(f32[2,16,32,128]{3,2,1,0:T(8,128)} %own_ref.1), calls=%async_computation.2 | async-start | bytes 524288 | tf_op jit(solution)/shard_map/slice | solution.py:393
  6.8 2.1 %slice-start = ((f32[2,16,32,128]{3,2,1,0:T(8,128)}), f32[2,16,8,128]{3,2,1,0:T(8,128)S(1)}, s32[]{:S(2)}) async-start(f32[2,16,32,128]{3,2,1,0:T(8,128)} %own_ref.1), calls=%async_computation.1 | async-start | bytes 262144 | tf_op jit(solution)/shard_map/slice | solution.py:394
  6.9 14.4 %copy-start.3 = (f32[2,16,32,128]{3,2,1,0:T(8,128)S(1)}, f32[2,16,32,128]{3,2,1,0:T(8,128)}, u32[]{:S(2)}) copy-start(f32[2,16,32,128]{3,2,1,0:T(8,128)} %own_ref.1) | copy-start | bytes 1572868
  6.9 14.3 %collective-permute-start.1 = (f32[2,9,32,128]{3,2,1,0:T(8,128)S(1)}, f32[2,9,32,128]{3,2,1,0:T(8,128)S(1)}, u32[]{:S(2)}, u32[]{:S(2)}) collective-permute-start(f32[2,9,32,128]{3,2,1,0:T(8,128)S(1)} %pad_maximum_fusion.2), channel_id=1, source_target_pairs={{0,32},{1,33},{2,34},{3,35},{4,36},{5,37},{6,38},{7,39},{8,40},{9,... | collective-permute-start | bytes 884744 | tf_op jit(solution)/shard_map/ppermute | solution.py:389
  9.0 12.2 %collective-permute-start.2 = (f32[2,17,8,128]{3,2,1,0:T(8,128)S(1)}, f32[2,17,8,128]{3,2,1,0:T(8,128)S(1)}, u32[]{:S(2)}, u32[]{:S(2)}) collective-permute-start(f32[2,17,8,128]{3,2,1,0:T(8,128)S(1)} %pad_maximum_fusion.4), channel_id=1, source_target_pairs={{0,4},{1,5},{2,6},{3,7},{4,8},{5,9},{6,10},{7,11},{8,12},{9,13},{1... | collective-permute-start | bytes 417800 | tf_op jit(solution)/shard_map/ppermute | solution.py:389
  10.5 10.7 %collective-permute-start.3 = (f32[2,9,8,128]{3,2,1,0:T(8,128)S(1)}, f32[2,9,8,128]{3,2,1,0:T(8,128)S(1)}, u32[]{:S(2)}, u32[]{:S(2)}) collective-permute-start(f32[2,9,8,128]{3,2,1,0:T(8,128)S(1)} %pad_maximum_fusion.6), channel_id=1, source_target_pairs={{0,36},{1,37},{2,38},{3,39},{4,40},{5,41},{6,42},{7,43},{8,44},{9,... | collective-permute-start | bytes 221192 | tf_op jit(solution)/shard_map/ppermute | solution.py:389
  29.8 1.6 %collective-permute-start.5 = (f32[40,128]{1,0:T(8,128)S(1)}, f32[40,128]{1,0:T(8,128)S(1)}, u32[]{:S(2)}, u32[]{:S(2)}) collective-permute-start(f32[40,128]{1,0:T(8,128)S(1)} %shard_map.195.mine_ref), channel_id=1, source_target_pairs={{1,0},{2,1},{3,2},{0,3},{5,4},{6,5},{7,6},{4,7},{9,8},{10,9},{11,1... | collective-permute-start | bytes 61448 | tf_op jit(solution)/shard_map/ppermute | solution.py:461
  29.9 4.8 %collective-permute-start.4 = (f32[40,128]{1,0:T(8,128)S(1)}, f32[40,128]{1,0:T(8,128)S(1)}, u32[]{:S(2)}, u32[]{:S(2)}) collective-permute-start(f32[40,128]{1,0:T(8,128)S(1)} %shard_map.195.mine_ref), channel_id=1, source_target_pairs={{0,1},{1,2},{2,3},{3,0},{4,5},{5,6},{6,7},{7,4},{8,9},{9,10},{10,1... | collective-permute-start | bytes 61448 | tf_op jit(solution)/shard_map/ppermute | solution.py:460
  35.7 7.1 %copy-start.4 = (bf16[6,128,128]{2,1,0:T(8,128)(2,1)S(1)}, bf16[6,128,128]{2,1,0:T(8,128)(2,1)}, u32[]{:S(2)}) copy-start(bf16[6,128,128]{2,1,0:T(8,128)(2,1)} %constant.92.clone) | copy-start | bytes 589828
  35.7 7.1 %copy-start.5 = (bf16[6,128,128]{2,1,0:T(8,128)(2,1)S(1)}, bf16[6,128,128]{2,1,0:T(8,128)(2,1)}, u32[]{:S(2)}) copy-start(bf16[6,128,128]{2,1,0:T(8,128)(2,1)} %constant.91.clone) | copy-start | bytes 589828
  35.7 19.3 %all-to-all-start = ((f32[32,40,128]{2,1,0:T(8,128)}), f32[32,40,128]{2,1,0:T(8,128)S(1)}, u32[]{:S(2)}, u32[]{:S(2)}) async-start(f32[32,40,128]{2,1,0:T(8,128)} %shard_map.196), calls=%async_computation | async-start | bytes 1310720 | tf_op jit(solution)/shard_map/all_to_all | solution.py:463
  42.0 0.7 %copy-start.20 = (s32[128]{0:T(128)S(1)}, s32[128]{0:T(128)}, u32[]{:S(2)}) copy-start(s32[128]{0:T(128)} %constant.90.clone) | copy-start | bytes 1540

commit v2 on v1

v2 whole, which is shorter than its diff:
```python
import jax
import jax.numpy as jnp
import numpy as np
from jax import lax
from jax.experimental import pallas as pl
from jax.experimental.pallas import tpu as pltpu
from jax.sharding import PartitionSpec as P

epsilon_value = 1e-05
step_size = 0.5
f32 = jnp.float32
bf16 = jnp.bfloat16


def spline(t):
    m = np.abs(t)
    inside = 2.0 / 3.0 - m * m + 0.5 * m * m * m
    out = np.maximum(2.0 - m, 0.0)
    return np.where(m < 1.0, inside, out * out * out / 6.0)


def split_two(w):
    hi = w.astype(np.float32).astype(jnp.bfloat16)
    lo = (w - hi.astype(np.float64)).astype(np.float32).astype(jnp.bfloat16)
    return hi, lo


def pack_kernel(img_ref, out_ref, x_ref, y_ref, xy_ref, buf_ref, sems):
    lane = lax.broadcasted_iota(jnp.int32, (32, 128), 1)
    copies = []
    for n in range(4):
        for h in range(2):
            planes = pl.ds(4 * n, 4)
            copy = pltpu.make_async_copy(img_ref.at[h, planes], buf_ref.at[h, planes], sems.at[2 * n + h])
            copy.start()
            copies.append(copy)
    packed = [jnp.zeros((32, 128), f32) for _ in range(2)]
    for n in range(4):
        for h in range(2):
            copies[2 * n + h].wait()
            for t in range(4 * n, 4 * n + 4):
                moved = pltpu.roll(buf_ref[h, t], (8 * t + 8) % 128, 1)
                packed[h] = jnp.where((lane >= 8 * t) & (lane < 8 * t + 8), moved, packed[h])
                y_ref[h, t] = buf_ref[h, t, 24:32]
                if t >= 8:
                    x_ref[h, t - 8] = buf_ref[h, t]
                    xy_ref[h, t - 8] = buf_ref[h, t, 24:32]
    for h in range(2):
        out_ref[h] = packed[h]
        y_ref[h, 16] = jnp.zeros((8, 128), f32)
        xy_ref[h, 8] = jnp.zeros((8, 128), f32)


def prep_kernel(at_ref, vel_ref, wxy_ref, wz_ref, vel_out, wxy_out, wz_out, xsum_out, zsum_out, rows_ref):
    i = at_ref[0]
    j = at_ref[1]
    k = at_ref[2]
    ex = jnp.where(i == 0, 0.0, 1.0)
    ez = jnp.where(k == 0, 0.0, 1.0)
    row = lax.broadcasted_iota(jnp.int32, (40, 512), 0)
    col = lax.broadcasted_iota(jnp.int32, (40, 512), 1)
    p = lax.shift_right_logical(row, 3)
    q = row & 7
    o = lax.shift_right_logical(col, 5)
    r = col & 31
    ok = ((p < 2) == (o < 4)) | (i != 0)
    ok = ok & (((q < 2) == (r < 4)) | (j != 0))
    ok = ok & ((p < 4) | (i != at_ref[3] - 1)) & ((q < 6) | (j != at_ref[4] - 1))
    keep = jnp.where(ok, 1.0, 0.0)
    for n in range(2):
        rows = pl.ds(40 * n, 40)
        wxy_out[rows] = wxy_ref[rows] * keep
    lane = lax.broadcasted_iota(jnp.int32, (128, 128), 1)
    sub = lax.broadcasted_iota(jnp.int32, (128, 128), 0)
    spot = lax.rem(lane, 20)
    ok = ((spot < 2) == (sub >= 124)) | (k != 0)
    ok = ok & ((spot < 18) | (k != at_ref[5] - 1))
    keep = jnp.where(ok, 1.0, 0.0)
    for n in range(2):
        for c in range(6):
            wz_out[n, c] = (wz_ref[n, c].astype(f32) * keep).astype(bf16)

    src = lax.broadcasted_iota(jnp.int32, (256, 128), 0)
    dst = lax.broadcasted_iota(jnp.int32, (256, 128), 1)
    plane = jnp.where(src < 128, lax.shift_right_logical(src, 3) + 8, lax.shift_right_logical(src - 128, 3) - 8)
    goal = lax.shift_right_logical(dst, 3)
    near = (plane >= goal) & (plane <= goal + 8) & ((src & 7) == (dst & 7)) & (plane >= 0)
    across = (plane < 8) != (goal < 4)
    xsum_out[...] = jnp.where(near, jnp.where(across, ex, 1.0), 0.0).astype(bf16)
    centre = jnp.where(dst < 124, dst, dst - 128)
    below = src >= 128
    place = jnp.where(below, (src & 7) - 8, src)
    gap = place - centre
    inside = (gap <= 4) & (gap >= -4)
    crossing = below != (dst >= 124)
    zsum_out[...] = jnp.where(inside, jnp.where(crossing, ez, 1.0), 0.0)

    pick_q = lax.broadcasted_iota(jnp.int32, (8, 32), 0)
    pick_y = lax.broadcasted_iota(jnp.int32, (8, 32), 1)
    pick = ((pick_y == 4 * j + pick_q - 2) & (pick_q >= 2) & (pick_q < 6)).astype(f32).astype(bf16)
    for side in range(2):
        rows_ref[...] = jnp.zeros((128, 32), f32)
        for c in range(6):
            rows_ref[20 * c + 2 : 20 * c + 18] = vel_ref[c, side]
        turned = jnp.transpose(rows_ref[...])
        total = jnp.zeros((8, 128), f32)
        for piece in split3(turned):
            total = total + dot(pick, piece)
        vel_out[8 * side : 8 * side + 8] = total


def split3(v):
    hi = v.astype(bf16)
    r = v - hi.astype(f32)
    mid = r.astype(bf16)
    lo = (r - mid.astype(f32)).astype(bf16)
    return hi, mid, lo


def split2(v):
    hi = v.astype(bf16)
    return hi, (v - hi.astype(f32)).astype(bf16)


def dot(a, b):
    return jnp.dot(a, b, preferred_element_type=f32)


def up_by(v, n, row):
    size = v.shape[0]
    return jnp.where(row < size - n, pltpu.roll(v, size - n, 0), 0.0)


def rows_window(v, head, tail, row8, row40):
    first = v[0:8]
    own = jnp.concatenate([jnp.zeros((8, 128), f32), v[8:40]], axis=0)
    s = first + up_by(first, 1, row8)
    s = s + up_by(s, 2, row8)
    s = s + up_by(s, 4, row8)
    w = own + pltpu.roll(own, 39, 0)
    w = w + pltpu.roll(w, 38, 0)
    w = w + pltpu.roll(w, 36, 0)
    w = w[0:32] + own[8:40]
    top = head * s + tail * w[0:8]
    return jnp.concatenate([top, w[8:32]], axis=0)


def force_kernel(
    edge_ref,
    own_ref,
    zr_ref,
    xr_ref,
    xzr_ref,
    yr_ref,
    xyr_ref,
    vel_ref,
    wxy_ref,
    wz_ref,
    xsum_ref,
    zsum_ref,
    out_ref,
    a_ref,
    h_ref,
    v_ref,
    dz_ref,
    xs_ref,
    hs_ref,
    fh_ref,
    fl_ref,
):
    ex = edge_ref[0]
    ey = edge_ref[1]
    ez = edge_ref[2]
    lane8 = lax.broadcasted_iota(jnp.int32, (8, 128), 1)
    row8 = lax.broadcasted_iota(jnp.int32, (8, 128), 0)
    lane32 = lax.broadcasted_iota(jnp.int32, (32, 128), 1)
    row32 = lax.broadcasted_iota(jnp.int32, (32, 128), 0)
    lane40 = lax.broadcasted_iota(jnp.int32, (40, 128), 1)
    row40 = lax.broadcasted_iota(jnp.int32, (40, 128), 0)
    head = jnp.where(row8 < 4, 1.0, ey)
    tail = jnp.where(row8 < 4, ey, 1.0)

    for h in range(2):
        for t in range(16):
            a_ref[h, 8 + t, 8:40] = own_ref[h, t]
            a_ref[h, 8 + t, 0:8] = yr_ref[h, t]
        for t in range(8):
            a_ref[h, t, 8:40] = xr_ref[h, t]
            a_ref[h, t, 0:8] = xyr_ref[h, t]
        h_ref[h, 0, 8:40] = zr_ref[h]
        h_ref[h, 0, 0:8] = yr_ref[h, 16]
        h_ref[h, 1, 8:40] = xzr_ref[h]
        h_ref[h, 1, 0:8] = xyr_ref[h, 8]

    plus_z = jnp.where(lane40 == 127, ez, 1.0)
    minus_z = jnp.where(lane40 == 0, ez, 1.0)
    for h in range(2):
        for l in range(3, 21):
            if l >= 8:
                halo = pltpu.roll(h_ref[h, 0], (120 - 8 * (l - 8)) % 128, 1)
            else:
                halo = pltpu.roll(h_ref[h, 1], (120 - 8 * (l + 8)) % 128, 1)
            v_ref[h, l - 3] = jnp.where(lane40 >= 124, halo, a_ref[h, l])
            if 4 <= l < 20:
                dz_ref[h, l - 4] = halo
    for h in range(2):
        for l in range(4, 20):
            a = a_ref[h, l]
            halo = dz_ref[h, l - 4]
            up = pltpu.roll(jnp.where(lane40 >= 125, halo, a), 127, 1)
            down = pltpu.roll(jnp.where(lane40 >= 123, halo, a), 1, 1)
            dz_ref[h, l - 4] = plus_z * up - minus_z * down

    def products(f, m):
        return (f, m, f * f, m * m, f * m)

    def x_step(tile, carry):
        rows = pl.ds(pl.multiple_of(tile * 8, 8), 8)
        for q in range(5):
            p = []
            for l in range(24):
                if q == 0:
                    p.append(a_ref[0, l, rows])
                elif q == 1:
                    p.append(a_ref[1, l, rows])
                elif q == 2:
                    f = a_ref[0, l, rows]
                    p.append(f * f)
                elif q == 3:
                    m = a_ref[1, l, rows]
                    p.append(m * m)
                else:
                    p.append(a_ref[0, l, rows] * a_ref[1, l, rows])
            left = [None] * 8
            left[7] = p[7]
            for o in range(6, -1, -1):
                left[o] = left[o + 1] + p[o]
            right = [None] * 8
            right[0] = p[8]
            for o in range(1, 8):
                right[o] = right[o - 1] + p[o + 8]
            for o in range(8):
                xs_ref[q, o, rows] = left[o] + ex * right[o] if o < 4 else ex * left[o] + right[o]
            s = p[8:24]
            b = [s[n] + s[n + 1] for n in range(15)]
            b = [b[n] + b[n + 2] for n in range(13)]
            b = [b[n] + b[n + 4] for n in range(9)]
            for o in range(8):
                xs_ref[q, 8 + o, rows] = b[o] + s[o + 8]
        return carry

    lax.fori_loop(0, 5, x_step, 0)

    x_sum = xsum_ref[...]
    for q in range(5):
        parts = []
        for side in range(2):
            f = h_ref[0, side]
            m = h_ref[1, side]
            parts.append(rows_window(products(f, m)[q], head, tail, row8, row40))
        both = jnp.concatenate(parts, axis=1)
        total = jnp.zeros((32, 128), f32)
        for piece in split3(both):
            total = total + dot(piece, x_sum)
        for n, piece in enumerate(split3(total)):
            hs_ref[q, n] = piece

    from_row = lax.broadcasted_iota(jnp.int32, (256, 128), 0)
    plus_y = jnp.where(row32 == 3, ey, 1.0)
    minus_y = jnp.where(row32 == 4, ey, 1.0)

    def o_step(o, carry):
        mine = (from_row < 128) | (lax.shift_right_logical(from_row - 128, 3) == o)
        z_sum = jnp.where(mine, zsum_ref[...], 0.0).astype(bf16)
        pieces = [[], [], []]
        for q in range(5):
            y = rows_window(xs_ref[q, o], head, tail, row8, row40)
            for n, piece in enumerate(split3(y)):
                pieces[n].append(jnp.concatenate([piece, hs_ref[q, n]], axis=1))
        big = dot(jnp.concatenate(pieces[0] + pieces[1] + pieces[2], axis=0), z_sum)
        sums = (big[0:160] + big[160:320]) + big[320:480]
        sums = sums * (1.0 / 729.0)
        mean_f = sums[0:32]
        mean_m = sums[32:64]
        var_f = sums[64:96] - mean_f * mean_f + epsilon_value
        var_m = sums[96:128] - mean_m * mean_m + epsilon_value
        cov = sums[128:160] - mean_f * mean_m
        off_f = v_ref[0, o + 1, 4:36] - mean_f
        off_m = v_ref[1, o + 1, 4:36] - mean_m
        inv = 1.0 / (var_f * var_m)
        factor = cov * inv
        pulls = (
            factor * (off_m - factor * var_m * off_f),
            factor * (off_f - factor * var_f * off_m),
        )
        plus_x = jnp.where(o == 3, ex, 1.0)
        minus_x = jnp.where(o == 4, ex, 1.0)
        where_to = pl.ds(pl.multiple_of(o * 32, 32), 32)
        for h in range(2):
            dx = plus_x * v_ref[h, o + 2, 4:36] - minus_x * v_ref[h, o, 4:36]
            dy = plus_y * v_ref[h, o + 1, 5:37] - minus_y * v_ref[h, o + 1, 3:35]
            dz = dz_ref[h, o, 4:36]
            for c, d in enumerate((dx, dy, dz)):
                hi, lo = split2(pulls[h] * d)
                fh_ref[3 * h + c, where_to] = hi
                fl_ref[3 * h + c, where_to] = lo
        return carry

    lax.fori_loop(0, 16, o_step, 0, unroll=8)

    total = jnp.zeros((40, 128), f32)
    wxy = wxy_ref[...].astype(bf16)
    wxy_hi = wxy_ref[0:40].astype(bf16)
    for c in range(6):
        first = dot(wxy, fh_ref[c])
        second = dot(wxy_hi, fl_ref[c])
        xy = first[0:40] + first[40:80] + second
        hi, lo = split2(xy)
        total = total + dot(hi, wz_ref[0, c]) + dot(hi, wz_ref[1, c]) + dot(lo, wz_ref[0, c])
    total = step_size * total
    out_ref[0:16] = total[0:16]
    out_ref[16:32] = total[16:32] + vel_ref[...]
    out_ref[32:40] = total[32:40]


def fold_kernel(mine_ref, low_ref, high_ref, out_ref):
    lane = lax.broadcasted_iota(jnp.int32, (40, 128), 1)
    spot = lax.rem(lane, 20)
    live = lane < 120
    low = pltpu.roll(low_ref[...], 112, 1)
    high = pltpu.roll(high_ref[...], 16, 1)
    total = mine_ref[...]
    total = total + jnp.where(live & (spot < 3), low, 0.0)
    out_ref[...] = total + jnp.where(live & (spot >= 16), high, 0.0)


def across_kernel(own_ref, below_ref, above_ref, far_ref, out_ref):
    tiles = lambda ref: [ref[8 * p : 8 * p + 8] for p in range(5)]
    own, below, above, far = tiles(own_ref), tiles(below_ref), tiles(above_ref), tiles(far_ref)
    window = [
        own[0] + below[2] + far[4],
        own[1] + below[3],
        own[2] + below[4] + above[0],
        own[3] + above[1],
        own[4] + above[2] + far[0],
        above[3] + far[1],
    ]
    for n in range(8):
        for w in range(6):
            out_ref[n, 8 * w : 8 * w + 8] = window[w]


def field_kernel(at_ref, g_ref, wxy_ref, wz_ref, nv_ref, field_ref, rows_ref, buf_ref, sems):
    me_j = at_ref[1]
    row8 = lax.broadcasted_iota(jnp.int32, (8, 128), 0)

    window = []
    js = [lax.rem(me_j + 7, 8), me_j, lax.rem(me_j + 1, 8)]
    for w in range(6):
        before, own, after = (g_ref[j, 8 * w : 8 * w + 8] for j in js)
        window.append(own + jnp.where(row8 < 4, pltpu.roll(before, 4, 0), pltpu.roll(after, 4, 0)))
    coefs = jnp.concatenate(window, axis=0)
    row = lax.broadcasted_iota(jnp.int32, (48, 128), 0)
    lane = lax.broadcasted_iota(jnp.int32, (48, 128), 1)
    at_x = 2 * at_ref[0] - 2 + lax.shift_right_logical(row, 3)
    at_y = 4 * me_j - 2 + (row & 7)
    at_z = 16 * at_ref[2] - 2 + lax.rem(lane, 20)
    real = (at_x >= 0) & (at_x < 2 * at_ref[3]) & (at_y >= 0) & (at_y < 4 * at_ref[4])
    real = real & (at_z >= 0) & (at_z < 16 * at_ref[5]) & (lane < 120)
    coefs = jnp.where(real, coefs, 0.0)
    hi, lo = split2(coefs)
    copies = []
    for pair in range(3):
        rhs = []
        for c in (2 * pair, 2 * pair + 1):
            along = dot(hi, wz_ref[0, c]) + dot(hi, wz_ref[1, c]) + dot(lo, wz_ref[0, c])
            ch, cl = split2(along)
            rhs.append(jnp.concatenate([ch, cl, ch], axis=0))
        both = dot(wxy_ref[...], jnp.concatenate(rhs, axis=1)).astype(bf16)
        for n in range(2):
            buf_ref[2 * pair + n] = both[:, 128 * n : 128 * n + 128]
        there = pl.ds(2 * pair, 2)
        copy = pltpu.make_async_copy(buf_ref.at[there], field_ref.at[there], sems.at[pair])
        copy.start()
        copies.append(copy)

    for side in range(2):
        cols = [g_ref[j, 16 + 8 * side : 24 + 8 * side] for j in range(8)]
        turned = [pltpu.roll(c, 4, 0) for c in cols]
        tiles = []
        zero = jnp.zeros((8, 128), f32)
        for n in range(5):
            even = cols[2 * n] if n < 4 else zero
            high = turned[2 * n + 1] if n < 4 else zero
            low = turned[2 * n - 1] if n > 0 else zero
            tiles.append(even + jnp.where(row8 < 4, low, high))
        tiles[4] = tiles[4] + tiles[0]
        for n in range(5):
            rows_ref[side, 8 * n : 8 * n + 8] = tiles[n]
        block = jnp.transpose(rows_ref[side, 2:34])
        for c in range(6):
            nv_ref[c, side] = block[20 * c + 2 : 20 * c + 18]
    for copy in copies:
        copy.wait()


VMEM = pl.BlockSpec(memory_space=pltpu.VMEM)
SMEM = pl.BlockSpec(memory_space=pltpu.SMEM)


HBM = pl.BlockSpec(memory_space=pltpu.HBM)


def call(body, out_shape, in_specs, scratch=(), out_specs=None, flops=0, bytes_accessed=0):
    return pl.pallas_call(
        body,
        out_shape=[jax.ShapeDtypeStruct(shape, dtype) for shape, dtype in out_shape],
        in_specs=in_specs,
        out_specs=out_specs or [VMEM] * len(out_shape),
        scratch_shapes=list(scratch),
        compiler_params=pltpu.CompilerParams(vmem_limit_bytes=48 << 20),
        cost_estimate=pl.CostEstimate(flops=flops, bytes_accessed=bytes_accessed, transcendentals=0),
    )


def pairs(mesh_sizes, di, dj, dk):
    ni, nj, nk = mesh_sizes
    out = []
    for i in range(ni):
        for j in range(nj):
            for k in range(nk):
                to = (((i + di) % ni) * nj + (j + dj) % nj) * nk + (k + dk) % nk
                out.append(((i * nj + j) * nk + k, to))
    return out


def fixed_tables():
    position = lambda n: np.arange(n) - 4
    weight = lambda pos, points: spline((pos[None, :] - 8.0 * (np.arange(points) - 2)[:, None] - 3.5) / 8.0)
    wx = weight(position(16), 5)
    wy = np.concatenate([weight(position(32), 7), np.zeros((1, 32))])
    hi, lo = split_two(np.einsum("po,qr->pqor", wx, wy).reshape(40, 512))
    wxy = np.concatenate([hi, lo]).astype(np.float32)
    lanes = np.arange(128)
    wz = weight(np.where(lanes >= 124, lanes - 128, lanes), 19)
    canvas = np.zeros((6, 128, 128))
    for c in range(6):
        canvas[c, :, 20 * c : 20 * c + 19] = wz.T
    wzs = np.stack(split_two(canvas))
    ex, ey, ez = (weight(np.arange(n), points) for n, points in ((16, 6), (32, 8), (128, 20)))
    hi, lo = split_two(np.einsum("px,qy->xypq", ex, ey).reshape(512, 48))
    exy = np.concatenate([hi, hi, lo], axis=1)
    canvas = np.zeros((6, 128, 128))
    for c in range(6):
        canvas[c, 20 * c : 20 * c + 20] = ez
    ezs = np.stack(split_two(canvas))
    return wxy, wzs, exy, ezs


def shards(images, velocity):
    axes = ("gx", "gy", "gz")
    sizes = tuple(lax.axis_size(a) for a in axes)
    spot = [lax.axis_index(a) for a in axes]
    nk = sizes[2]
    at = jnp.stack([jnp.int32(v) for v in (*spot, *sizes)])
    wxy, wzs, exy, ezs = fixed_tables()

    def send(v, di, dj, dk):
        return lax.ppermute(v, axes, pairs(sizes, di, dj, dk))

    pack, to_x, to_y, to_xy = call(
        pack_kernel,
        [((2, 32, 128), f32), ((2, 8, 32, 128), f32), ((2, 17, 8, 128), f32), ((2, 9, 8, 128), f32)],
        [HBM],
        [pltpu.VMEM((2, 16, 32, 128), f32), pltpu.SemaphoreType.DMA((8,))],
        bytes_accessed=10**6,
    )(images)
    zr = lax.ppermute(pack, "gz", [(n, (n + 1) % nk) for n in range(nk)])
    xr = send(to_x, 1, 0, 0)
    yr = send(to_y.at[:, 16].set(zr[:, 24:]), 0, 1, 0)
    xyr = send(to_xy.at[:, 8].set(zr[:, 24:]), 1, 1, 0)
    xzr = send(zr, 1, 0, 0)

    velocity = jnp.swapaxes(velocity, 3, 4).reshape(6, 2, 16, 32)
    vel, wxy, wzs, xsum, zsum = call(
        prep_kernel,
        [((16, 128), f32), ((80, 512), f32), ((2, 6, 128, 128), bf16), ((256, 128), bf16), ((256, 128), f32)],
        [SMEM] + [VMEM] * 3,
        [pltpu.VMEM((128, 32), f32)],
        bytes_accessed=10**6,
    )(at, velocity, wxy, wzs)

    edges = jnp.minimum(at, 1).astype(f32)
    (part,) = call(
        force_kernel,
        [((40, 128), f32)],
        [SMEM] + [VMEM] * 11,
        [
            pltpu.VMEM((2, 24, 40, 128), f32),
            pltpu.VMEM((2, 2, 40, 128), f32),
            pltpu.VMEM((2, 18, 40, 128), f32),
            pltpu.VMEM((2, 16, 40, 128), f32),
            pltpu.VMEM((5, 16, 40, 128), f32),
            pltpu.VMEM((5, 3, 32, 128), bf16),
            pltpu.VMEM((6, 512, 128), bf16),
            pltpu.VMEM((6, 512, 128), bf16),
        ],
        flops=10**9,
        bytes_accessed=2 * 10**6,
    )(edges, images, zr, xr, xzr, yr, xyr, vel, wxy, wzs, xsum, zsum)

    low = lax.ppermute(part, "gz", [(n, (n + 1) % nk) for n in range(nk)])
    high = lax.ppermute(part, "gz", [((n + 1) % nk, n) for n in range(nk)])
    (own,) = call(fold_kernel, [((40, 128), f32)], [VMEM] * 3)(part, low, high)
    below = send(own, 1, 0, 0)
    above = send(own, -1, 0, 0)
    far = send(own, 2, 0, 0)
    (copies,) = call(across_kernel, [((8, 48, 128), f32)], [VMEM] * 4)(own, below, above, far)
    everything = lax.all_to_all(copies, "gy", 0, 0, tiled=True)

    nv, field = call(
        field_kernel,
        [((6, 2, 16, 32), f32), ((6, 512, 128), bf16)],
        [SMEM] + [VMEM] * 3,
        [pltpu.VMEM((2, 40, 128), f32), pltpu.VMEM((6, 512, 128), bf16), pltpu.SemaphoreType.DMA((3,))],
        out_specs=[VMEM, HBM],
        flops=10**8,
        bytes_accessed=10**6,
    )(at, everything, exy, ezs)
    nv = jnp.swapaxes(nv.reshape(2, 3, 2, 16, 32), 3, 4)
    return nv, field.reshape(2, 3, 16, 32, 128)


def solution(mesh):
    placed = (P(None, "gx", "gy", "gz"), P(None, None, "gx", None, "gz"))
    return jax.shard_map(
        shards,
        mesh=mesh,
        in_specs=placed,
        out_specs=(P(None, None, "gx", None, "gz"), P(None, None, "gx", "gy", "gz")),
        check_vma=False,
    )
```

time: 58.5 us -> 51.1 us (0.87)
  waiting for transfers between devices: 25.5 us -> 12.2 us
  blocking collectives: 0 us -> 9.8 us
  Pallas kernels: 12.3 us -> 9.78 us
  local copies, waits for them, and re-layouts: 5.33 us -> 3.95 us
  starting transfers between devices: 13.4 us -> 14.4 us
  other arithmetic: 0.77 us -> 0.01 us
    all_to_all x1 -> x0, waiting for transfers between devices: 12.1 us -> none  [shards(): everything = lax.all_to_all(copies, ('gx', 'gy'), 0, 0, tiled=True)]
    all_to_all x0 -> x1, blocking collectives: none -> 9.8 us  [shards(): everything = lax.all_to_all(copies, 'gy', 0, 0, tiled=True)]
    ppermute x3 -> x7, starting transfers between devices: 6.48 us -> 13.7 us  [send(): return lax.ppermute(v, axes, pairs(sizes, di, dj, dk))]
    all_to_all x1 -> x0, starting transfers between devices: 6.3 us -> none  [shards(): everything = lax.all_to_all(copies, ('gx', 'gy'), 0, 0, tiled=True)]
    pallas_call x4 -> x6, Pallas kernels: 12.3 us -> 9.78 us  [the longest x1 4.7 us: shards(): call(force_kernel, [((40, 128), f32)], [SMEM] + [VMEM] * 11, [pltpu.VMEM(...]
    ppermute x3 -> x7, waiting for transfers between devices: 7.74 us -> 5.26 us  [send(): return lax.ppermute(v, axes, pairs(sizes, di, dj, dk))]
    ppermute x1, waiting for transfers between devices: 1.58 us -> 2.68 us  [shards(): zr = lax.ppermute(pack, 'gz', [(n, (n + 1) % nk) for n in range(nk)])]
    unnamed x43 -> x14, local copies, waits for them, and re-layouts: 4.89 us -> 3.86 us
  transfers between devices with their start and end apart: 7 -> 10, of which waited for: 5 -> 7; matrix products, arithmetic and copies ran while one was open for 2% -> 0% of each run, Pallas kernels for 0% -> 2%
where the time goes in v2:
time: 51.1 us; the launch traced here: 50.8 us
  starting transfers between devices  14.4 us (28%)
  waiting for transfers between devices  12.2 us (24%)
  blocking collectives  9.8 us (19%)
  Pallas kernels  9.78 us (19%)
  local copies, waits for them, and re-layouts  3.95 us (8%)
  between operations  0.72 us (1%)
    ppermute x7, starting transfers between devices, send(): return lax.ppermute(v, axes, pairs(sizes, di, dj, dk))  13.7 us
    all_to_all x1, blocking collectives, shards(): everything = lax.all_to_all(copies, 'gy', 0, 0, tiled=True)  9.8 us
    ppermute x7, waiting for transfers between devices, send(): return lax.ppermute(v, axes, pairs(sizes, di, dj, dk))  5.26 us
    pallas_call x1, Pallas kernels, shards(): call(force_kernel, [((40, 128), f32)], [SMEM] + [VMEM] * 11, [pltpu.VMEM(...  4.7 us
    unnamed x14, local copies, waits for them, and re-layouts  3.86 us
    ppermute x1, waiting for transfers between devices, shards(): low = lax.ppermute(part, 'gz', [(n, (n + 1) % nk) for n in range(nk)])  3.31 us
    pallas_call x1, Pallas kernels, shards(): call(field_kernel, [((6, 2, 16, 32), f32), ((6, 512, 128), bf16)], [SMEM]...  2.8 us
    ppermute x1, waiting for transfers between devices, shards(): zr = lax.ppermute(pack, 'gz', [(n, (n + 1) % nk) for n in range(nk)])  2.68 us
  transfers between devices with their start and end apart: 10, of which 7 were waited for; matrix products, arithmetic and copies ran while one was open for 0% of the time, Pallas kernels for 2%

profile of v2, /device:TPU:0, one launch (start us, length us, event | category | flops | bytes accessed | tf_op | source)
XLA Modules:
  0.0 50.8 jit_solution(6978895591176733308)
XLA Ops:
  0.6 0.0 copy-start
  0.6 1.0 %copy-done = f32[2,16,32,128]{3,2,1,0:T(8,128)S(1)} copy-done((f32[2,16,32,128]{3,2,1,0:T(8,128)S(1)}, f32[2,16,32,128]{3,2,1,0:T(8,128)}, u32[]{:S(2)}) %copy-start) | copy-done | bytes 524312
  1.7 0.0 copy-start.1
  1.7 1.4 %shard_map.77 = (f32[2,32,128]{2,1,0:T(8,128)S(1)}, f32[2,8,32,128]{3,2,1,0:T(8,128)S(1)}, f32[2,17,8,128]{3,2,1,0:T(8,128)S(1)}, f32[2,9,8,128]{3,2,1,0:T(8,128)S(1)}) custom-call(f32[2,16,32,128]{3,2,1,0:T(8,128)S(1)} %copy-done), custom_call_target="tpu_custom_call" | custom-call | bytes 1000000 | tf_op jit(solution)/shard_map/pallas_call | solution.py:471
  3.1 0.1 collective-permute-start
  3.2 2.1 %collective-permute-start.1 = (f32[2,8,32,128]{3,2,1,0:T(8,128)S(1)}, f32[2,8,32,128]{3,2,1,0:T(8,128)S(1)}, u32[]{:S(2)}, u32[]{:S(2)}) collective-permute-start(f32[2,8,32,128]{3,2,1,0:T(8,128)S(1)} %get-tuple-element.38), channel_id=1, source_target_pairs={{0,32},{1,33},{2,34},{3,35},{4,36},{5,37},{6,38},{7,39},{8,40},{9,... | collective-permute-start | bytes 786440 | tf_op jit(solution)/shard_map/ppermute | solution.py:469
  5.2 0.1 stack.15.at_ref
  5.3 2.7 %collective-permute-done.zr_ref = f32[2,32,128]{2,1,0:T(8,128)S(1)} collective-permute-done((f32[2,32,128]{2,1,0:T(8,128)S(1)}, f32[2,32,128]{2,1,0:T(8,128)S(1)}, u32[]{:S(2)}, u32[]{:S(2)}) %collective-permute-start) | collective-permute-done | bytes 32800 | tf_op jit(solution)/shard_map/ppermute | solution.py:478
  8.0 2.9 %collective-permute-start.4 = (f32[2,9,8,128]{3,2,1,0:T(8,128)S(1)}, f32[2,9,8,128]{3,2,1,0:T(8,128)S(1)}, u32[]{:S(2)}, u32[]{:S(2)}) collective-permute-start(f32[2,9,8,128]{3,2,1,0:T(8,128)S(1)} %get-tuple-element.48), channel_id=1, source_target_pairs={{0,36},{1,37},{2,38},{3,39},{4,40},{5,41},{6,42},{7,43},{8,44},{9,... | collective-permute-start | bytes 221192 | tf_op jit(solution)/shard_map/ppermute | solution.py:469
  10.9 1.5 %collective-permute-start.3 = (f32[2,17,8,128]{3,2,1,0:T(8,128)S(1)}, f32[2,17,8,128]{3,2,1,0:T(8,128)S(1)}, u32[]{:S(2)}, u32[]{:S(2)}) collective-permute-start(f32[2,17,8,128]{3,2,1,0:T(8,128)S(1)} %get-tuple-element.49), channel_id=1, source_target_pairs={{0,4},{1,5},{2,6},{3,7},{4,8},{5,9},{6,10},{7,11},{8,12},{9,13},{1... | collective-permute-start | bytes 417800 | tf_op jit(solution)/shard_map/ppermute | solution.py:469
  12.4 1.9 %collective-permute-start.2 = (f32[2,32,128]{2,1,0:T(8,128)S(1)}, f32[2,32,128]{2,1,0:T(8,128)S(1)}, u32[]{:S(2)}, u32[]{:S(2)}) collective-permute-start(f32[2,32,128]{2,1,0:T(8,128)S(1)} %collective-permute-done.zr_ref), channel_id=1, source_target_pairs={{0,32},{1,33},{2,34},{3,35},{4,36},{5,37},{6,38},{7,39},{8,40},{9,... | collective-permute-start | bytes 98312 | tf_op jit(solution)/shard_map/ppermute | solution.py:469
  14.3 0.0 copy-start.3
  14.3 1.0 %copy-done.3 = bf16[2,6,128,128]{3,2,1,0:T(8,128)(2,1)S(1)} copy-done((bf16[2,6,128,128]{3,2,1,0:T(8,128)(2,1)S(1)}, bf16[2,6,128,128]{3,2,1,0:T(8,128)(2,1)}, u32[]{:S(2)}) %copy-start.3) | copy-done | bytes 393240
  15.3 0.0 copy-start.5
  15.3 0.9 %copy-done.5 = f32[80,512]{1,0:T(8,128)S(1)} copy-done((f32[80,512]{1,0:T(8,128)S(1)}, f32[80,512]{1,0:T(8,128)}, u32[]{:S(2)}) %copy-start.5) | copy-done | bytes 163864
  16.2 0.0 copy-start.6
  16.3 0.9 %copy-done.6 = f32[2,3,2,32,16]{3,4,2,1,0:T(8,128)S(1)} copy-done((f32[2,3,2,32,16]{3,4,2,1,0:T(8,128)S(1)}, f32[2,3,2,32,16]{3,4,2,1,0:T(8,128)}, u32[]{:S(2)}) %copy-start.6) | copy-done | bytes 24600
  17.1 0.8 %shard_map.78 = (f32[16,128]{1,0:T(8,128)S(1)}, f32[80,512]{1,0:T(8,128)S(1)}, bf16[2,6,128,128]{3,2,1,0:T(8,128)(2,1)S(1)}, bf16[256,128]{1,0:T(8,128)(2,1)S(1)}, f32[256,128]{1,0:T(8,128)S(1)}) custom-call(s32[6]{0:T(128)S(1)} %stack.15.at_ref, f32[6,2,16,32]{3,2,1,0:T(8,128)S(1)} %bitcast.16, f32[80,512]{1,0:T(8,128)S(1)} %copy-done.5, ...), custom_call_target="tpu_custom_call" | custom-call | bytes 1000000 | tf_op jit(solution)/shard_map/pallas_call | solution.py:485
  17.9 0.0 collective-permute-done.2.xzr_ref
  18.0 0.4 collective-permute-done.4.xyr_ref
  18.4 0.6 %collective-permute-done.3.yr_ref = f32[2,17,8,128]{3,2,1,0:T(8,128)S(1)} collective-permute-done((f32[2,17,8,128]{3,2,1,0:T(8,128)S(1)}, f32[2,17,8,128]{3,2,1,0:T(8,128)S(1)}, u32[]{:S(2)}, u32[]{:S(2)}) %collective-permute-start.3) | collective-permute-done | bytes 139296 | tf_op jit(solution)/shard_map/ppermute | solution.py:469
  19.0 0.0 collective-permute-done.1.xr_ref
  19.0 0.0 copy-done.1
  19.0 4.7 %shard_map.79.mine_ref = f32[40,128]{1,0:T(8,128)S(1)} custom-call(f32[6]{0:T(128)S(1)} %minimum_convert_fusion.edge_ref, f32[2,16,32,128]{3,2,1,0:T(8,128)S(1)} %copy-done.1, f32[2,32,128]{2,1,0:T(8,128)S(1)} %collective-permute-done.zr_ref, f32[2,8,32,128]{3,2,1,0:T(8,128)S(1)} %collective-permute-done.1.xr_ref, ...), custom_call_target="tpu_custom_call" | custom-call | flops 1000000000 | bytes 2000000 | tf_op jit(solution)/shard_map/pallas_call | solution.py:494
  23.7 0.0 copy-start.2
  23.7 0.1 collective-permute-start.6
  23.8 0.5 collective-permute-start.5
  24.3 1.0 %collective-permute-done.6.high_ref = f32[40,128]{1,0:T(8,128)S(1)} collective-permute-done((f32[40,128]{1,0:T(8,128)S(1)}, f32[40,128]{1,0:T(8,128)S(1)}, u32[]{:S(2)}, u32[]{:S(2)}) %collective-permute-start.6) | collective-permute-done | bytes 20512 | tf_op jit(solution)/shard_map/ppermute | solution.py:513
  25.2 3.3 %collective-permute-done.5.low_ref = f32[40,128]{1,0:T(8,128)S(1)} collective-permute-done((f32[40,128]{1,0:T(8,128)S(1)}, f32[40,128]{1,0:T(8,128)S(1)}, u32[]{:S(2)}, u32[]{:S(2)}) %collective-permute-start.5) | collective-permute-done | bytes 20512 | tf_op jit(solution)/shard_map/ppermute | solution.py:512
  28.6 0.1 shard_map.80.own_ref
  28.6 3.3 %collective-permute-start.9 = (f32[40,128]{1,0:T(8,128)S(1)}, f32[40,128]{1,0:T(8,128)S(1)}, u32[]{:S(2)}, u32[]{:S(2)}) collective-permute-start(f32[40,128]{1,0:T(8,128)S(1)} %shard_map.80.own_ref), channel_id=1, source_target_pairs={{0,64},{1,65},{2,66},{3,67},{4,68},{5,69},{6,70},{7,71},{8,72},{9,... | collective-permute-start | bytes 61448 | tf_op jit(solution)/shard_map/ppermute | solution.py:469
  31.9 1.3 %collective-permute-start.8 = (f32[40,128]{1,0:T(8,128)S(1)}, f32[40,128]{1,0:T(8,128)S(1)}, u32[]{:S(2)}, u32[]{:S(2)}) collective-permute-start(f32[40,128]{1,0:T(8,128)S(1)} %shard_map.80.own_ref), channel_id=1, source_target_pairs={{0,96},{1,97},{2,98},{3,99},{4,100},{5,101},{6,102},{7,103},{8,104... | collective-permute-start | bytes 61448 | tf_op jit(solution)/shard_map/ppermute | solution.py:469
  33.2 0.7 %collective-permute-start.7 = (f32[40,128]{1,0:T(8,128)S(1)}, f32[40,128]{1,0:T(8,128)S(1)}, u32[]{:S(2)}, u32[]{:S(2)}) collective-permute-start(f32[40,128]{1,0:T(8,128)S(1)} %shard_map.80.own_ref), channel_id=1, source_target_pairs={{0,32},{1,33},{2,34},{3,35},{4,36},{5,37},{6,38},{7,39},{8,40},{9,... | collective-permute-start | bytes 61448 | tf_op jit(solution)/shard_map/ppermute | solution.py:469
  33.9 0.0 collective-permute-done.9.far_ref
  34.0 1.7 %collective-permute-done.8.above_ref = f32[40,128]{1,0:T(8,128)S(1)} collective-permute-done((f32[40,128]{1,0:T(8,128)S(1)}, f32[40,128]{1,0:T(8,128)S(1)}, u32[]{:S(2)}, u32[]{:S(2)}) %collective-permute-start.8) | collective-permute-done | bytes 20512 | tf_op jit(solution)/shard_map/ppermute | solution.py:469
  35.7 2.5 %collective-permute-done.7.below_ref = f32[40,128]{1,0:T(8,128)S(1)} collective-permute-done((f32[40,128]{1,0:T(8,128)S(1)}, f32[40,128]{1,0:T(8,128)S(1)}, u32[]{:S(2)}, u32[]{:S(2)}) %collective-permute-start.7) | collective-permute-done | bytes 20512 | tf_op jit(solution)/shard_map/ppermute | solution.py:469
  38.2 0.0 copy-start.4
  38.2 9.8 %all_to_all.5.g_ref = f32[8,48,128]{2,1,0:T(8,128)S(1)} all-to-all(f32[8,48,128]{2,1,0:T(8,128)S(1)} %shard_map.81), channel_id=1, replica_groups=mesh['gx'=4,'gy'=8,'gz'=4] {'gy'}, dimensions={0} | all-to-all | bytes 393216 | tf_op jit(solution)/shard_map/all_to_all | solution.py:519
  48.0 0.0 copy-done.2
  48.0 0.0 copy-done.4
  48.0 2.8 %shard_map.82 = (f32[6,2,16,32]{3,2,1,0:T(8,128)}, bf16[6,512,128]{2,1,0:T(8,128)(2,1)}) custom-call(s32[6]{0:T(128)S(1)} %stack.15.at_ref, f32[8,48,128]{2,1,0:T(8,128)S(1)} %all_to_all.5.g_ref, bf16[512,144]{1,0:T(8,128)(2,1)S(1)} %copy-done.4, bf16[2,6,128,128]{3,2,1,0:T(8,128)(2,1)S(1)} %copy-done.2), custom_call_target="tpu_custom_call" | custom-call | flops 100000000 | bytes 1000000 | tf_op jit(solution)/shard_map/pallas_call | solution.py:521
  (3 shorter events, 0.0 us)
Async XLA Ops:
  0.6 1.0 %copy-start = (f32[2,16,32,128]{3,2,1,0:T(8,128)S(1)}, f32[2,16,32,128]{3,2,1,0:T(8,128)}, u32[]{:S(2)}) copy-start(f32[2,16,32,128]{3,2,1,0:T(8,128)} %own_ref.1) | copy-start | bytes 1572868
  1.7 17.3 %copy-start.1 = (f32[2,16,32,128]{3,2,1,0:T(8,128)S(1)}, f32[2,16,32,128]{3,2,1,0:T(8,128)}, u32[]{:S(2)}) copy-start(f32[2,16,32,128]{3,2,1,0:T(8,128)} %own_ref.1) | copy-start | bytes 1572868
  3.1 4.9 %collective-permute-start = (f32[2,32,128]{2,1,0:T(8,128)S(1)}, f32[2,32,128]{2,1,0:T(8,128)S(1)}, u32[]{:S(2)}, u32[]{:S(2)}) collective-permute-start(f32[2,32,128]{2,1,0:T(8,128)S(1)} %get-tuple-element.37), channel_id=1, source_target_pairs={{0,1},{1,2},{2,3},{3,0},{4,5},{5,6},{6,7},{7,4},{8,9},{9,10},{10,1... | collective-permute-start | bytes 98312 | tf_op jit(solution)/shard_map/ppermute | solution.py:478
  3.2 15.8 %collective-permute-start.1 = (f32[2,8,32,128]{3,2,1,0:T(8,128)S(1)}, f32[2,8,32,128]{3,2,1,0:T(8,128)S(1)}, u32[]{:S(2)}, u32[]{:S(2)}) collective-permute-start(f32[2,8,32,128]{3,2,1,0:T(8,128)S(1)} %get-tuple-element.38), channel_id=1, source_target_pairs={{0,32},{1,33},{2,34},{3,35},{4,36},{5,37},{6,38},{7,39},{8,40},{9,... | collective-permute-start | bytes 786440 | tf_op jit(solution)/shard_map/ppermute | solution.py:469
  8.0 10.4 %collective-permute-start.4 = (f32[2,9,8,128]{3,2,1,0:T(8,128)S(1)}, f32[2,9,8,128]{3,2,1,0:T(8,128)S(1)}, u32[]{:S(2)}, u32[]{:S(2)}) collective-permute-start(f32[2,9,8,128]{3,2,1,0:T(8,128)S(1)} %get-tuple-element.48), channel_id=1, source_target_pairs={{0,36},{1,37},{2,38},{3,39},{4,40},{5,41},{6,42},{7,43},{8,44},{9,... | collective-permute-start | bytes 221192 | tf_op jit(solution)/shard_map/ppermute | solution.py:469
  10.9 8.0 %collective-permute-start.3 = (f32[2,17,8,128]{3,2,1,0:T(8,128)S(1)}, f32[2,17,8,128]{3,2,1,0:T(8,128)S(1)}, u32[]{:S(2)}, u32[]{:S(2)}) collective-permute-start(f32[2,17,8,128]{3,2,1,0:T(8,128)S(1)} %get-tuple-element.49), channel_id=1, source_target_pairs={{0,4},{1,5},{2,6},{3,7},{4,8},{5,9},{6,10},{7,11},{8,12},{9,13},{1... | collective-permute-start | bytes 417800 | tf_op jit(solution)/shard_map/ppermute | solution.py:469
  12.4 5.5 %collective-permute-start.2 = (f32[2,32,128]{2,1,0:T(8,128)S(1)}, f32[2,32,128]{2,1,0:T(8,128)S(1)}, u32[]{:S(2)}, u32[]{:S(2)}) collective-permute-start(f32[2,32,128]{2,1,0:T(8,128)S(1)} %collective-permute-done.zr_ref), channel_id=1, source_target_pairs={{0,32},{1,33},{2,34},{3,35},{4,36},{5,37},{6,38},{7,39},{8,40},{9,... | collective-permute-start | bytes 98312 | tf_op jit(solution)/shard_map/ppermute | solution.py:469
  14.3 1.0 %copy-start.3 = (bf16[2,6,128,128]{3,2,1,0:T(8,128)(2,1)S(1)}, bf16[2,6,128,128]{3,2,1,0:T(8,128)(2,1)}, u32[]{:S(2)}) copy-start(bf16[2,6,128,128]{3,2,1,0:T(8,128)(2,1)} %constant.84.clone.wz_ref) | copy-start | bytes 1179652
  15.3 0.9 %copy-start.5 = (f32[80,512]{1,0:T(8,128)S(1)}, f32[80,512]{1,0:T(8,128)}, u32[]{:S(2)}) copy-start(f32[80,512]{1,0:T(8,128)} %constant.83.clone.wxy_ref) | copy-start | bytes 491524
  16.2 0.9 %copy-start.6 = (f32[2,3,2,32,16]{3,4,2,1,0:T(8,128)S(1)}, f32[2,3,2,32,16]{3,4,2,1,0:T(8,128)}, u32[]{:S(2)}) copy-start(f32[2,3,2,32,16]{3,4,2,1,0:T(8,128)} %param.11) | copy-start | bytes 73732
  23.7 24.4 %copy-start.2 = (bf16[2,6,128,128]{3,2,1,0:T(8,128)(2,1)S(1)}, bf16[2,6,128,128]{3,2,1,0:T(8,128)(2,1)}, u32[]{:S(2)}) copy-start(bf16[2,6,128,128]{3,2,1,0:T(8,128)(2,1)} %constant.86.clone.wz_ref) | copy-start | bytes 1179652
  23.7 1.6 %collective-permute-start.6 = (f32[40,128]{1,0:T(8,128)S(1)}, f32[40,128]{1,0:T(8,128)S(1)}, u32[]{:S(2)}, u32[]{:S(2)}) collective-permute-start(f32[40,128]{1,0:T(8,128)S(1)} %shard_map.79.mine_ref), channel_id=1, source_target_pairs={{1,0},{2,1},{3,2},{0,3},{5,4},{6,5},{7,6},{4,7},{9,8},{10,9},{11,1... | collective-permute-start | bytes 61448 | tf_op jit(solution)/shard_map/ppermute | solution.py:513
  23.8 4.8 %collective-permute-start.5 = (f32[40,128]{1,0:T(8,128)S(1)}, f32[40,128]{1,0:T(8,128)S(1)}, u32[]{:S(2)}, u32[]{:S(2)}) collective-permute-start(f32[40,128]{1,0:T(8,128)S(1)} %shard_map.79.mine_ref), channel_id=1, source_target_pairs={{0,1},{1,2},{2,3},{3,0},{4,5},{5,6},{6,7},{7,4},{8,9},{9,10},{10,1... | collective-permute-start | bytes 61448 | tf_op jit(solution)/shard_map/ppermute | solution.py:512
  28.6 5.3 %collective-permute-start.9 = (f32[40,128]{1,0:T(8,128)S(1)}, f32[40,128]{1,0:T(8,128)S(1)}, u32[]{:S(2)}, u32[]{:S(2)}) collective-permute-start(f32[40,128]{1,0:T(8,128)S(1)} %shard_map.80.own_ref), channel_id=1, source_target_pairs={{0,64},{1,65},{2,66},{3,67},{4,68},{5,69},{6,70},{7,71},{8,72},{9,... | collective-permute-start | bytes 61448 | tf_op jit(solution)/shard_map/ppermute | solution.py:469
  31.9 3.8 %collective-permute-start.8 = (f32[40,128]{1,0:T(8,128)S(1)}, f32[40,128]{1,0:T(8,128)S(1)}, u32[]{:S(2)}, u32[]{:S(2)}) collective-permute-start(f32[40,128]{1,0:T(8,128)S(1)} %shard_map.80.own_ref), channel_id=1, source_target_pairs={{0,96},{1,97},{2,98},{3,99},{4,100},{5,101},{6,102},{7,103},{8,104... | collective-permute-start | bytes 61448 | tf_op jit(solution)/shard_map/ppermute | solution.py:469
  33.2 5.0 %collective-permute-start.7 = (f32[40,128]{1,0:T(8,128)S(1)}, f32[40,128]{1,0:T(8,128)S(1)}, u32[]{:S(2)}, u32[]{:S(2)}) collective-permute-start(f32[40,128]{1,0:T(8,128)S(1)} %shard_map.80.own_ref), channel_id=1, source_target_pairs={{0,32},{1,33},{2,34},{3,35},{4,36},{5,37},{6,38},{7,39},{8,40},{9,... | collective-permute-start | bytes 61448 | tf_op jit(solution)/shard_map/ppermute | solution.py:469
  38.2 9.8 %copy-start.4 = (bf16[512,144]{1,0:T(8,128)(2,1)S(1)}, bf16[512,144]{1,0:T(8,128)(2,1)}, u32[]{:S(2)}) copy-start(bf16[512,144]{1,0:T(8,128)(2,1)} %constant.85.clone.wxy_ref) | copy-start | bytes 442372

commit v3 on v2

--- a/solution.py
+++ b/solution.py
@@ -1,3 +1,5 @@
+import functools
+
 import jax
 import jax.numpy as jnp
 import numpy as np
@@ -25,33 +27,39 @@
     return hi, lo
 
 
-def pack_kernel(img_ref, out_ref, x_ref, y_ref, xy_ref, buf_ref, sems):
+def pack_kernel(img_ref, out_ref):
     lane = lax.broadcasted_iota(jnp.int32, (32, 128), 1)
-    copies = []
-    for n in range(4):
-        for h in range(2):
-            planes = pl.ds(4 * n, 4)
-            copy = pltpu.make_async_copy(img_ref.at[h, planes], buf_ref.at[h, planes], sems.at[2 * n + h])
-            copy.start()
-            copies.append(copy)
-    packed = [jnp.zeros((32, 128), f32) for _ in range(2)]
-    for n in range(4):
-        for h in range(2):
-            copies[2 * n + h].wait()
-            for t in range(4 * n, 4 * n + 4):
-                moved = pltpu.roll(buf_ref[h, t], (8 * t + 8) % 128, 1)
-                packed[h] = jnp.where((lane >= 8 * t) & (lane < 8 * t + 8), moved, packed[h])
-                y_ref[h, t] = buf_ref[h, t, 24:32]
-                if t >= 8:
-                    x_ref[h, t - 8] = buf_ref[h, t]
-                    xy_ref[h, t - 8] = buf_ref[h, t, 24:32]
     for h in range(2):
-        out_ref[h] = packed[h]
+        packed = jnp.zeros((32, 128), f32)
+        for t in range(16):
+            moved = pltpu.roll(img_ref[h, t], (8 * t + 8) % 128, 1)
+            packed = jnp.where((lane >= 8 * t) & (lane < 8 * t + 8), moved, packed)
+        out_ref[h] = packed
+
+
+def slab_kernel(img_ref, x_ref, y_ref, xy_ref):
+    for h in range(2):
+        for t in range(16):
+            y_ref[h, t] = img_ref[h, t, 24:32]
+            if t >= 8:
+                x_ref[h, t - 8] = img_ref[h, t]
+                xy_ref[h, t - 8] = img_ref[h, t, 24:32]
         y_ref[h, 16] = jnp.zeros((8, 128), f32)
         xy_ref[h, 8] = jnp.zeros((8, 128), f32)
 
 
-def prep_kernel(at_ref, vel_ref, wxy_ref, wz_ref, vel_out, wxy_out, wz_out, xsum_out, zsum_out, rows_ref):
+def spline_at(t):
+    m = jnp.abs(t)
+    inside = 2.0 / 3.0 - m * m + 0.5 * m * m * m
+    out = jnp.maximum(2.0 - m, 0.0)
+    return jnp.where(m < 1.0, inside, out * out * out / 6.0)
+
+
+def weights(voxel, point):
+    return spline_at((voxel.astype(f32) - 8.0 * point.astype(f32) - 3.5) * 0.125)
+
+
+def prep_kernel(at_ref, vel_ref, vel_out, wxy_out, wz_out, xsum_out, zsum_out, rows_ref):
     i = at_ref[0]
     j = at_ref[1]
     k = at_ref[2]
@@ -64,21 +72,19 @@
     o = lax.shift_right_logical(col, 5)
     r = col & 31
     ok = ((p < 2) == (o < 4)) | (i != 0)
-    ok = ok & (((q < 2) == (r < 4)) | (j != 0))
+    ok = ok & (((q < 2) == (r < 4)) | (j != 0)) & (q < 7)
     ok = ok & ((p < 4) | (i != at_ref[3] - 1)) & ((q < 6) | (j != at_ref[4] - 1))
-    keep = jnp.where(ok, 1.0, 0.0)
-    for n in range(2):
-        rows = pl.ds(40 * n, 40)
-        wxy_out[rows] = wxy_ref[rows] * keep
+    table = jnp.where(ok, weights(o - 4, p - 2) * weights(r - 4, q - 2), 0.0)
+    hi, lo = split2(table)
+    wxy_out[...] = jnp.concatenate([hi.astype(f32), lo.astype(f32)], axis=0).astype(bf16)
     lane = lax.broadcasted_iota(jnp.int32, (128, 128), 1)
     sub = lax.broadcasted_iota(jnp.int32, (128, 128), 0)
     spot = lax.rem(lane, 20)
     ok = ((spot < 2) == (sub >= 124)) | (k != 0)
-    ok = ok & ((spot < 18) | (k != at_ref[5] - 1))
-    keep = jnp.where(ok, 1.0, 0.0)
-    for n in range(2):
-        for c in range(6):
-            wz_out[n, c] = (wz_ref[n, c].astype(f32) * keep).astype(bf16)
+    ok = ok & (spot < 19) & ((spot < 18) | (k != at_ref[5] - 1))
+    voxel = jnp.where(sub >= 124, sub - 128, sub)
+    hi, lo = split2(jnp.where(ok, weights(voxel, spot - 2), 0.0))
+    wz_out[...] = jnp.concatenate([hi, lo], axis=1)
 
     src = lax.broadcasted_iota(jnp.int32, (256, 128), 0)
     dst = lax.broadcasted_iota(jnp.int32, (256, 128), 1)
@@ -131,7 +137,7 @@
     return jnp.where(row < size - n, pltpu.roll(v, size - n, 0), 0.0)
 
 
-def rows_window(v, head, tail, row8, row40):
+def rows_window(v, head, tail, row8):
     first = v[0:8]
     own = jnp.concatenate([jnp.zeros((8, 128), f32), v[8:40]], axis=0)
     s = first + up_by(first, 1, row8)
@@ -145,122 +151,96 @@
     return jnp.concatenate([top, w[8:32]], axis=0)
 
 
-def force_kernel(
-    edge_ref,
-    own_ref,
-    zr_ref,
-    xr_ref,
-    xzr_ref,
-    yr_ref,
-    xyr_ref,
-    vel_ref,
-    wxy_ref,
-    wz_ref,
-    xsum_ref,
-    zsum_ref,
-    out_ref,
-    a_ref,
-    h_ref,
-    v_ref,
-    dz_ref,
-    xs_ref,
-    hs_ref,
-    fh_ref,
-    fl_ref,
-):
-    ex = edge_ref[0]
-    ey = edge_ref[1]
-    ez = edge_ref[2]
-    lane8 = lax.broadcasted_iota(jnp.int32, (8, 128), 1)
+def force_kernel(upper, at_ref, own_ref, zr_ref, yr_ref, *refs):
+    if upper:
+        base_ref, *refs = refs
+    else:
+        xr_ref, xzr_ref, xyr_ref, base_ref, *refs = refs
+    wxy_ref, wz_ref, xsum_ref, zsum_ref, out_ref, a_ref, h_ref, v_ref, dz_ref, xs_ref, hs_ref, fh_ref, fl_ref = refs
+    first = 8 if upper else 0
+    ex, ey, ez = (jnp.where(at_ref[n] == 0, 0.0, 1.0) for n in range(3))
     row8 = lax.broadcasted_iota(jnp.int32, (8, 128), 0)
-    lane32 = lax.broadcasted_iota(jnp.int32, (32, 128), 1)
     row32 = lax.broadcasted_iota(jnp.int32, (32, 128), 0)
     lane40 = lax.broadcasted_iota(jnp.int32, (40, 128), 1)
-    row40 = lax.broadcasted_iota(jnp.int32, (40, 128), 0)
     head = jnp.where(row8 < 4, 1.0, ey)
     tail = jnp.where(row8 < 4, ey, 1.0)
 
     for h in range(2):
-        for t in range(16):
-            a_ref[h, 8 + t, 8:40] = own_ref[h, t]
-            a_ref[h, 8 + t, 0:8] = yr_ref[h, t]
-        for t in range(8):
-            a_ref[h, t, 8:40] = xr_ref[h, t]
-            a_ref[h, t, 0:8] = xyr_ref[h, t]
+        for n in range(16):
+            if upper or n >= 8:
+                t = n if upper else n - 8
+                a_ref[h, n, 8:40] = own_ref[h, t]
+                a_ref[h, n, 0:8] = yr_ref[h, t]
+            else:
+                a_ref[h, n, 8:40] = xr_ref[h, n]
+                a_ref[h, n, 0:8] = xyr_ref[h, n]
         h_ref[h, 0, 8:40] = zr_ref[h]
         h_ref[h, 0, 0:8] = yr_ref[h, 16]
-        h_ref[h, 1, 8:40] = xzr_ref[h]
-        h_ref[h, 1, 0:8] = xyr_ref[h, 8]
+        if not upper:
+            h_ref[h, 1, 8:40] = xzr_ref[h]
+            h_ref[h, 1, 0:8] = xyr_ref[h, 8]
 
     plus_z = jnp.where(lane40 == 127, ez, 1.0)
     minus_z = jnp.where(lane40 == 0, ez, 1.0)
     for h in range(2):
-        for l in range(3, 21):
+        for n in range(3, 13):
+            l = n + first
             if l >= 8:
                 halo = pltpu.roll(h_ref[h, 0], (120 - 8 * (l - 8)) % 128, 1)
             else:
                 halo = pltpu.roll(h_ref[h, 1], (120 - 8 * (l + 8)) % 128, 1)
-            v_ref[h, l - 3] = jnp.where(lane40 >= 124, halo, a_ref[h, l])
-            if 4 <= l < 20:
-                dz_ref[h, l - 4] = halo
+            v_ref[h, n - 3] = jnp.where(lane40 >= 124, halo, a_ref[h, n])
+            if 4 <= n < 12:
+                dz_ref[h, n - 4] = halo
     for h in range(2):
-        for l in range(4, 20):
-            a = a_ref[h, l]
-            halo = dz_ref[h, l - 4]
+        for n in range(4, 12):
+            a = a_ref[h, n]
+            halo = dz_ref[h, n - 4]
             up = pltpu.roll(jnp.where(lane40 >= 125, halo, a), 127, 1)
             down = pltpu.roll(jnp.where(lane40 >= 123, halo, a), 1, 1)
-            dz_ref[h, l - 4] = plus_z * up - minus_z * down
-
-    def products(f, m):
-        return (f, m, f * f, m * m, f * m)
+            dz_ref[h, n - 4] = plus_z * up - minus_z * down
 
     def x_step(tile, carry):
         rows = pl.ds(pl.multiple_of(tile * 8, 8), 8)
         for q in range(5):
             p = []
-            for l in range(24):
-                if q == 0:
-                    p.append(a_ref[0, l, rows])
-                elif q == 1:
-                    p.append(a_ref[1, l, rows])
-                elif q == 2:
-                    f = a_ref[0, l, rows]
-                    p.append(f * f)
-                elif q == 3:
-                    m = a_ref[1, l, rows]
-                    p.append(m * m)
+            for n in range(16):
+                if q == 4:
+                    p.append(a_ref[0, n, rows] * a_ref[1, n, rows])
                 else:
-                    p.append(a_ref[0, l, rows] * a_ref[1, l, rows])
+                    value = a_ref[q % 2, n, rows]
+                    p.append(value if q < 2 else value * value)
+            if upper:
+                b = [p[n] + p[n + 1] for n in range(15)]
+                b = [b[n] + b[n + 2] for n in range(13)]
+                b = [b[n] + b[n + 4] for n in range(9)]
+                for o in range(8):
+                    xs_ref[q, o, rows] = b[o] + p[o + 8]
+                continue
             left = [None] * 8
             left[7] = p[7]
             for o in range(6, -1, -1):
                 left[o] = left[o + 1] + p[o]
-            right = [None] * 8
-            right[0] = p[8]
-            for o in range(1, 8):
-                right[o] = right[o - 1] + p[o + 8]
+            right = p[8]
             for o in range(8):
-                xs_ref[q, o, rows] = left[o] + ex * right[o] if o < 4 else ex * left[o] + right[o]
-            s = p[8:24]
-            b = [s[n] + s[n + 1] for n in range(15)]
-            b = [b[n] + b[n + 2] for n in range(13)]
-            b = [b[n] + b[n + 4] for n in range(9)]
-            for o in range(8):
-                xs_ref[q, 8 + o, rows] = b[o] + s[o + 8]
+                if o > 0:
+                    right = right + p[o + 8]
+                xs_ref[q, o, rows] = left[o] + ex * right if o < 4 else ex * left[o] + right
         return carry
 
     lax.fori_loop(0, 5, x_step, 0)
 
-    x_sum = xsum_ref[...]
+    sides = 1 if upper else 2
+    x_sum = xsum_ref[0 : 128 * sides]
     for q in range(5):
         parts = []
-        for side in range(2):
+        for side in range(sides):
             f = h_ref[0, side]
             m = h_ref[1, side]
-            parts.append(rows_window(products(f, m)[q], head, tail, row8, row40))
-        both = jnp.concatenate(parts, axis=1)
+            value = (f, m, f * f, m * m, f * m)[q]
+            parts.append(rows_window(value, head, tail, row8))
         total = jnp.zeros((32, 128), f32)
-        for piece in split3(both):
+        for piece in split3(jnp.concatenate(parts, axis=1)):
             total = total + dot(piece, x_sum)
         for n, piece in enumerate(split3(total)):
             hs_ref[q, n] = piece
@@ -270,11 +250,11 @@
     minus_y = jnp.where(row32 == 4, ey, 1.0)
 
     def o_step(o, carry):
-        mine = (from_row < 128) | (lax.shift_right_logical(from_row - 128, 3) == o)
+        mine = (from_row < 128) | (lax.shift_right_logical(from_row - 128, 3) == o + first)
         z_sum = jnp.where(mine, zsum_ref[...], 0.0).astype(bf16)
         pieces = [[], [], []]
         for q in range(5):
-            y = rows_window(xs_ref[q, o], head, tail, row8, row40)
+            y = rows_window(xs_ref[q, o], head, tail, row8)
             for n, piece in enumerate(split3(y)):
                 pieces[n].append(jnp.concatenate([piece, hs_ref[q, n]], axis=1))
         big = dot(jnp.concatenate(pieces[0] + pieces[1] + pieces[2], axis=0), z_sum)
@@ -293,8 +273,8 @@
             factor * (off_m - factor * var_m * off_f),
             factor * (off_f - factor * var_f * off_m),
         )
-        plus_x = jnp.where(o == 3, ex, 1.0)
-        minus_x = jnp.where(o == 4, ex, 1.0)
+        plus_x = jnp.where(o + first == 3, ex, 1.0)
+        minus_x = jnp.where(o + first == 4, ex, 1.0)
         where_to = pl.ds(pl.multiple_of(o * 32, 32), 32)
         for h in range(2):
             dx = plus_x * v_ref[h, o + 2, 4:36] - minus_x * v_ref[h, o, 4:36]
@@ -306,21 +286,29 @@
                 fl_ref[3 * h + c, where_to] = lo
         return carry
 
-    lax.fori_loop(0, 16, o_step, 0, unroll=8)
-
+    lax.fori_loop(0, 8, o_step, 0, unroll=8)
+
+    cols = slice(32 * first, 32 * first + 256)
+    wxy = wxy_ref[:, cols]
+    wxy_hi = wxy_ref[0:40, cols]
+    planes = []
+    for c in range(6):
+        one = dot(wxy, fh_ref[c])
+        planes.append(one[0:40] + one[40:80] + dot(wxy_hi, fl_ref[c]))
+    hi, lo = split2(jnp.concatenate(planes, axis=0))
+    along = dot(jnp.concatenate([hi, lo], axis=0), wz_ref[...])
+    along = (along[0:240, 0:128] + along[0:240, 128:256]) + along[240:480, 0:128]
+    which = lax.div(lax.broadcasted_iota(jnp.int32, (40, 128), 1), 20)
     total = jnp.zeros((40, 128), f32)
-    wxy = wxy_ref[...].astype(bf16)
-    wxy_hi = wxy_ref[0:40].astype(bf16)
     for c in range(6):
-        first = dot(wxy, fh_ref[c])
-        second = dot(wxy_hi, fl_ref[c])
-        xy = first[0:40] + first[40:80] + second
-        hi, lo = split2(xy)
-        total = total + dot(hi, wz_ref[0, c]) + dot(hi, wz_ref[1, c]) + dot(lo, wz_ref[0, c])
+        total = total + jnp.where(which == c, along[40 * c : 40 * c + 40], 0.0)
     total = step_size * total
-    out_ref[0:16] = total[0:16]
-    out_ref[16:32] = total[16:32] + vel_ref[...]
-    out_ref[32:40] = total[32:40]
+    if upper:
+        out_ref[0:16] = total[0:16]
+        out_ref[16:32] = total[16:32] + base_ref[...]
+        out_ref[32:40] = total[32:40]
+    else:
+        out_ref[...] = total + base_ref[...]
 
 
 def fold_kernel(mine_ref, low_ref, high_ref, out_ref):
@@ -367,15 +355,18 @@
     at_z = 16 * at_ref[2] - 2 + lax.rem(lane, 20)
     real = (at_x >= 0) & (at_x < 2 * at_ref[3]) & (at_y >= 0) & (at_y < 4 * at_ref[4])
     real = real & (at_z >= 0) & (at_z < 16 * at_ref[5]) & (lane < 120)
+    part = lax.div(lane, 20)
     coefs = jnp.where(real, coefs, 0.0)
-    hi, lo = split2(coefs)
+    hi, lo = split2(jnp.concatenate([jnp.where(part == c, coefs, 0.0) for c in range(6)], axis=0))
+    along = dot(jnp.concatenate([hi, lo], axis=0), wz_ref[...])
+    along = (along[0:288, 0:128] + along[0:288, 128:256]) + along[288:576, 0:128]
+    ch, cl = split2(along)
     copies = []
     for pair in range(3):
         rhs = []
         for c in (2 * pair, 2 * pair + 1):
-            along = dot(hi, wz_ref[0, c]) + dot(hi, wz_ref[1, c]) + dot(lo, wz_ref[0, c])
-            ch, cl = split2(along)
-            rhs.append(jnp.concatenate([ch, cl, ch], axis=0))
+            rows = slice(48 * c, 48 * c + 48)
+            rhs.append(jnp.concatenate([ch[rows], cl[rows], ch[rows]], axis=0))
         both = dot(wxy_ref[...], jnp.concatenate(rhs, axis=1)).astype(bf16)
         for n in range(2):
             buf_ref[2 * pair + n] = both[:, 128 * n : 128 * n + 128]
@@ -435,26 +426,12 @@
 
 
 def fixed_tables():
-    position = lambda n: np.arange(n) - 4
-    weight = lambda pos, points: spline((pos[None, :] - 8.0 * (np.arange(points) - 2)[:, None] - 3.5) / 8.0)
-    wx = weight(position(16), 5)
-    wy = np.concatenate([weight(position(32), 7), np.zeros((1, 32))])
-    hi, lo = split_two(np.einsum("po,qr->pqor", wx, wy).reshape(40, 512))
-    wxy = np.concatenate([hi, lo]).astype(np.float32)
-    lanes = np.arange(128)
-    wz = weight(np.where(lanes >= 124, lanes - 128, lanes), 19)
-    canvas = np.zeros((6, 128, 128))
-    for c in range(6):
-        canvas[c, :, 20 * c : 20 * c + 19] = wz.T
-    wzs = np.stack(split_two(canvas))
-    ex, ey, ez = (weight(np.arange(n), points) for n, points in ((16, 6), (32, 8), (128, 20)))
+    weight = lambda n, points: spline((np.arange(n)[None, :] - 8.0 * (np.arange(points) - 2)[:, None] - 3.5) / 8.0)
+    ex, ey, ez = (weight(n, points) for n, points in ((16, 6), (32, 8), (128, 20)))
     hi, lo = split_two(np.einsum("px,qy->xypq", ex, ey).reshape(512, 48))
     exy = np.concatenate([hi, hi, lo], axis=1)
-    canvas = np.zeros((6, 128, 128))
-    for c in range(6):
-        canvas[c, 20 * c : 20 * c + 20] = ez
-    ezs = np.stack(split_two(canvas))
-    return wxy, wzs, exy, ezs
+    padded = lambda part: np.concatenate([np.tile(part, (6, 1)), np.zeros((8, 128), part.dtype)])
+    return exy, np.concatenate([padded(part) for part in split_two(ez)], axis=1)
 
 
 def shards(images, velocity):
@@ -463,16 +440,16 @@
     spot = [lax.axis_index(a) for a in axes]
     nk = sizes[2]
     at = jnp.stack([jnp.int32(v) for v in (*spot, *sizes)])
-    wxy, wzs, exy, ezs = fixed_tables()
+    exy, ezs = fixed_tables()
 
     def send(v, di, dj, dk):
         return lax.ppermute(v, axes, pairs(sizes, di, dj, dk))
 
-    pack, to_x, to_y, to_xy = call(
-        pack_kernel,
-        [((2, 32, 128), f32), ((2, 8, 32, 128), f32), ((2, 17, 8, 128), f32), ((2, 9, 8, 128), f32)],
-        [HBM],
-        [pltpu.VMEM((2, 16, 32, 128), f32), pltpu.SemaphoreType.DMA((8,))],
+    (pack,) = call(pack_kernel, [((2, 32, 128), f32)], [VMEM], bytes_accessed=6 * 10**5)(images)
+    to_x, to_y, to_xy = call(
+        slab_kernel,
+        [((2, 8, 32, 128), f32), ((2, 17, 8, 128), f32), ((2, 9, 8, 128), f32)],
+        [VMEM],
         bytes_accessed=10**6,
     )(images)
     zr = lax.ppermute(pack, "gz", [(n, (n + 1) % nk) for n in range(nk)])
@@ -484,30 +461,33 @@
     velocity = jnp.swapaxes(velocity, 3, 4).reshape(6, 2, 16, 32)
     vel, wxy, wzs, xsum, zsum = call(
         prep_kernel,
-        [((16, 128), f32), ((80, 512), f32), ((2, 6, 128, 128), bf16), ((256, 128), bf16), ((256, 128), f32)],
-        [SMEM] + [VMEM] * 3,
+        [((16, 128), f32), ((80, 512), bf16), ((128, 256), bf16), ((256, 128), bf16), ((256, 128), f32)],
+        [SMEM, VMEM],
         [pltpu.VMEM((128, 32), f32)],
         bytes_accessed=10**6,
-    )(at, velocity, wxy, wzs)
-
-    edges = jnp.minimum(at, 1).astype(f32)
-    (part,) = call(
-        force_kernel,
-        [((40, 128), f32)],
-        [SMEM] + [VMEM] * 11,
-        [
-            pltpu.VMEM((2, 24, 40, 128), f32),
-            pltpu.VMEM((2, 2, 40, 128), f32),
-            pltpu.VMEM((2, 18, 40, 128), f32),
-            pltpu.VMEM((2, 16, 40, 128), f32),
-            pltpu.VMEM((5, 16, 40, 128), f32),
-            pltpu.VMEM((5, 3, 32, 128), bf16),
-            pltpu.VMEM((6, 512, 128), bf16),
-            pltpu.VMEM((6, 512, 128), bf16),
-        ],
-        flops=10**9,
-        bytes_accessed=2 * 10**6,
-    )(edges, images, zr, xr, xzr, yr, xyr, vel, wxy, wzs, xsum, zsum)
+    )(at, velocity)
+
+    def forces(upper, *arrays):
+        return call(
+            functools.partial(force_kernel, upper),
+            [((40, 128), f32)],
+            [SMEM] + [VMEM] * (len(arrays) + 4),
+            [
+                pltpu.VMEM((2, 16, 40, 128), f32),
+                pltpu.VMEM((2, 2, 40, 128), f32),
+                pltpu.VMEM((2, 10, 40, 128), f32),
+                pltpu.VMEM((2, 8, 40, 128), f32),
+                pltpu.VMEM((5, 8, 40, 128), f32),
+                pltpu.VMEM((5, 3, 32, 128), bf16),
+                pltpu.VMEM((6, 256, 128), bf16),
+                pltpu.VMEM((6, 256, 128), bf16),
+            ],
+            flops=5 * 10**8,
+            bytes_accessed=10**6,
+        )(at, *arrays, wxy, wzs, xsum, zsum)[0]
+
+    part = forces(True, images, zr, yr, vel)
+    part = forces(False, images, zr, yr, xr, xzr, xyr, part)
 
     low = lax.ppermute(part, "gz", [(n, (n + 1) % nk) for n in range(nk)])
     high = lax.ppermute(part, "gz", [((n + 1) % nk, n) for n in range(nk)])

time: 51.1 us -> 48.9 us (0.957)
  local copies, waits for them, and re-layouts: 3.95 us -> 1.14 us
  starting transfers between devices: 14.4 us -> 16.6 us
  waiting for transfers between devices: 12.2 us -> 10.1 us
  Pallas kernels: 9.78 us -> 9.24 us
    ppermute x1, starting transfers between devices: 0.07 us -> 3.24 us  [shards(): high = lax.ppermute(part, 'gz', [((n + 1) % nk, n) for n in range(nk)])]
    unnamed x14 -> x10, local copies, waits for them, and re-layouts: 3.86 us -> 1.06 us
    ppermute x1, waiting for transfers between devices: 3.31 us -> 1.46 us  [shards(): low = lax.ppermute(part, 'gz', [(n, (n + 1) % nk) for n in range(nk)])]
    ppermute x1, waiting for transfers between devices: 0.98 us -> 0.02 us  [shards(): high = lax.ppermute(part, 'gz', [((n + 1) % nk, n) for n in range(nk)])]
    ppermute x7, waiting for transfers between devices: 5.26 us -> 5.91 us  [send(): return lax.ppermute(v, axes, pairs(sizes, di, dj, dk))]
    all_to_all x1, blocking collectives: 9.8 us -> 10.3 us  [shards(): everything = lax.all_to_all(copies, 'gy', 0, 0, tiled=True)]
    pallas_call x3 -> x5, Pallas kernels: 6.88 us -> 6.51 us  [the longest x2 5.28 us: forces(): call(functools.partial(force_kernel, upper), [((40, 128), f32)], [SMEM] +...]
  transfers between devices with their start and end apart: 10 -> 10, of which waited for: 7 -> 6; matrix products, arithmetic and copies ran while one was open for 0% -> 0% of each run, Pallas kernels for 2% -> 8%
where the time goes in v3:
time: 48.9 us; the launch traced here: 48.2 us
  starting transfers between devices  16.6 us (34%)
  blocking collectives  10.3 us (21%)
  waiting for transfers between devices  10.1 us (21%)
  Pallas kernels  9.24 us (19%)
  local copies, waits for them, and re-layouts  1.14 us (2%)
  between operations  0.73 us (1%)
    ppermute x7, starting transfers between devices, send(): return lax.ppermute(v, axes, pairs(sizes, di, dj, dk))  13.2 us
    all_to_all x1, blocking collectives, shards(): everything = lax.all_to_all(copies, 'gy', 0, 0, tiled=True)  10.3 us
    ppermute x7, waiting for transfers between devices, send(): return lax.ppermute(v, axes, pairs(sizes, di, dj, dk))  5.91 us
    pallas_call x2, Pallas kernels, forces(): call(functools.partial(force_kernel, upper), [((40, 128), f32)], [SMEM] +...  5.28 us
    ppermute x1, starting transfers between devices, shards(): high = lax.ppermute(part, 'gz', [((n + 1) % nk, n) for n in range(nk)])  3.24 us
    ppermute x1, waiting for transfers between devices, shards(): zr = lax.ppermute(pack, 'gz', [(n, (n + 1) % nk) for n in range(nk)])  2.71 us
    pallas_call x1, Pallas kernels, shards(): call(field_kernel, [((6, 2, 16, 32), f32), ((6, 512, 128), bf16)], [SMEM]...  2.64 us
    ppermute x1, waiting for transfers between devices, shards(): low = lax.ppermute(part, 'gz', [(n, (n + 1) % nk) for n in range(nk)])  1.46 us
  transfers between devices with their start and end apart: 10, of which 6 were waited for; matrix products, arithmetic and copies ran while one was open for 0% of the time, Pallas kernels for 8%

profile of v3, /device:TPU:0, one launch (start us, length us, event | category | flops | bytes accessed | tf_op | source)
XLA Modules:
  0.0 48.2 jit_solution(16991217162814627081)
XLA Ops:
  0.6 0.0 copy-start
  0.6 1.0 %copy-done = f32[2,16,32,128]{3,2,1,0:T(8,128)S(1)} copy-done((f32[2,16,32,128]{3,2,1,0:T(8,128)S(1)}, f32[2,16,32,128]{3,2,1,0:T(8,128)}, u32[]{:S(2)}) %copy-start) | copy-done | bytes 524312
  1.7 0.0 copy-start.1
  1.7 0.2 shard_map.59
  1.9 0.1 collective-permute-start
  1.9 0.0 copy-start.3
  2.0 2.1 %collective-permute-start.2 = (f32[2,8,32,128]{3,2,1,0:T(8,128)S(1)}, f32[2,8,32,128]{3,2,1,0:T(8,128)S(1)}, u32[]{:S(2)}, u32[]{:S(2)}) collective-permute-start(f32[2,8,32,128]{3,2,1,0:T(8,128)S(1)} %get-tuple-element.37), channel_id=1, source_target_pairs={{0,32},{1,33},{2,34},{3,35},{4,36},{5,37},{6,38},{7,39},{8,40},{9,... | collective-permute-start | bytes 786440 | tf_op jit(solution)/shard_map/ppermute | solution.py:446
  4.1 2.7 %collective-permute-done.zr_ref = f32[2,32,128]{2,1,0:T(8,128)S(1)} collective-permute-done((f32[2,32,128]{2,1,0:T(8,128)S(1)}, f32[2,32,128]{2,1,0:T(8,128)S(1)}, u32[]{:S(2)}, u32[]{:S(2)}) %collective-permute-start) | collective-permute-done | bytes 32800 | tf_op jit(solution)/shard_map/ppermute | solution.py:455
  6.8 1.6 %collective-permute-start.1 = (f32[2,17,8,128]{3,2,1,0:T(8,128)S(1)}, f32[2,17,8,128]{3,2,1,0:T(8,128)S(1)}, u32[]{:S(2)}, u32[]{:S(2)}) collective-permute-start(f32[2,17,8,128]{3,2,1,0:T(8,128)S(1)} %get-tuple-element.47), channel_id=1, source_target_pairs={{0,4},{1,5},{2,6},{3,7},{4,8},{5,9},{6,10},{7,11},{8,12},{9,13},{1... | collective-permute-start | bytes 417800 | tf_op jit(solution)/shard_map/ppermute | solution.py:446
  8.4 2.8 %collective-permute-start.4 = (f32[2,9,8,128]{3,2,1,0:T(8,128)S(1)}, f32[2,9,8,128]{3,2,1,0:T(8,128)S(1)}, u32[]{:S(2)}, u32[]{:S(2)}) collective-permute-start(f32[2,9,8,128]{3,2,1,0:T(8,128)S(1)} %get-tuple-element.46), channel_id=1, source_target_pairs={{0,36},{1,37},{2,38},{3,39},{4,40},{5,41},{6,42},{7,43},{8,44},{9,... | collective-permute-start | bytes 221192 | tf_op jit(solution)/shard_map/ppermute | solution.py:446
  11.2 0.1 stack.15.at_ref
  11.3 0.0 copy-done.3
  11.3 1.0 %shard_map.61 = (f32[16,128]{1,0:T(8,128)S(1)}, bf16[80,512]{1,0:T(8,128)(2,1)S(1)}, bf16[128,256]{1,0:T(8,128)(2,1)S(1)}, bf16[256,128]{1,0:T(8,128)(2,1)S(1)}, f32[256,128]{1,0:T(8,128)S(1)}) custom-call(s32[6]{0:T(128)S(1)} %stack.15.at_ref, f32[6,2,16,32]{3,2,1,0:T(8,128)S(1)} %bitcast.16), custom_call_target="tpu_custom_call" | custom-call | bytes 1000000 | tf_op jit(solution)/shard_map/pallas_call | solution.py:462
  12.3 1.9 %collective-permute-start.3 = (f32[2,32,128]{2,1,0:T(8,128)S(1)}, f32[2,32,128]{2,1,0:T(8,128)S(1)}, u32[]{:S(2)}, u32[]{:S(2)}) collective-permute-start(f32[2,32,128]{2,1,0:T(8,128)S(1)} %collective-permute-done.zr_ref), channel_id=1, source_target_pairs={{0,32},{1,33},{2,34},{3,35},{4,36},{5,37},{6,38},{7,39},{8,40},{9,... | collective-permute-start | bytes 98312 | tf_op jit(solution)/shard_map/ppermute | solution.py:446
  14.2 0.9 %collective-permute-done.1.yr_ref = f32[2,17,8,128]{3,2,1,0:T(8,128)S(1)} collective-permute-done((f32[2,17,8,128]{3,2,1,0:T(8,128)S(1)}, f32[2,17,8,128]{3,2,1,0:T(8,128)S(1)}, u32[]{:S(2)}, u32[]{:S(2)}) %collective-permute-start.1) | collective-permute-done | bytes 139296 | tf_op jit(solution)/shard_map/ppermute | solution.py:446
  15.1 0.0 copy-done.1
  15.1 2.7 %shard_map.62.refs_3_ = f32[40,128]{1,0:T(8,128)S(1)} custom-call(s32[6]{0:T(128)S(1)} %stack.15.at_ref, f32[2,16,32,128]{3,2,1,0:T(8,128)S(1)} %copy-done.1, f32[2,32,128]{2,1,0:T(8,128)S(1)} %collective-permute-done.zr_ref, f32[2,17,8,128]{3,2,1,0:T(8,128)S(1)} %collective-permute-done.1.yr_ref, f32[16,128]{1,0:T(8,128)S(1)} %get-tuple-element.39.refs_0_, ...), custom_call_target="tpu_custom_call" | custom-call | flops 500000000 | bytes 1000000 | tf_op jit(solution)/shard_map/pallas_call | solution.py:471
  17.8 0.0 collective-permute-done.3.refs_1_
  17.8 1.3 %collective-permute-done.4.refs_2_ = f32[2,9,8,128]{3,2,1,0:T(8,128)S(1)} collective-permute-done((f32[2,9,8,128]{3,2,1,0:T(8,128)S(1)}, f32[2,9,8,128]{3,2,1,0:T(8,128)S(1)}, u32[]{:S(2)}, u32[]{:S(2)}) %collective-permute-start.4) | collective-permute-done | bytes 73760 | tf_op jit(solution)/shard_map/ppermute | solution.py:446
  19.1 0.0 collective-permute-done.2.refs_0_
  19.1 2.6 %shard_map.63.mine_ref = f32[40,128]{1,0:T(8,128)S(1)} custom-call(s32[6]{0:T(128)S(1)} %stack.15.at_ref, f32[2,16,32,128]{3,2,1,0:T(8,128)S(1)} %copy-done.1, f32[2,32,128]{2,1,0:T(8,128)S(1)} %collective-permute-done.zr_ref, f32[2,17,8,128]{3,2,1,0:T(8,128)S(1)} %collective-permute-done.1.yr_ref, f32[2,8,32,128]{3,2,1,0:T(8,128)S(1)} %collective-permute-done.2.refs_0_, ...), custom_call_target="tpu_custom_call" | custom-call | flops 500000000 | bytes 1000000 | tf_op jit(solution)/shard_map/pallas_call | solution.py:471
  21.7 0.1 collective-permute-start.5
  21.8 3.2 %collective-permute-start.6 = (f32[40,128]{1,0:T(8,128)S(1)}, f32[40,128]{1,0:T(8,128)S(1)}, u32[]{:S(2)}, u32[]{:S(2)}) collective-permute-start(f32[40,128]{1,0:T(8,128)S(1)} %shard_map.63.mine_ref), channel_id=1, source_target_pairs={{1,0},{2,1},{3,2},{0,3},{5,4},{6,5},{7,6},{4,7},{9,8},{10,9},{11,1... | collective-permute-start | bytes 61448 | tf_op jit(solution)/shard_map/ppermute | solution.py:493
  25.0 1.5 %collective-permute-done.5.low_ref = f32[40,128]{1,0:T(8,128)S(1)} collective-permute-done((f32[40,128]{1,0:T(8,128)S(1)}, f32[40,128]{1,0:T(8,128)S(1)}, u32[]{:S(2)}, u32[]{:S(2)}) %collective-permute-start.5) | collective-permute-done | bytes 20512 | tf_op jit(solution)/shard_map/ppermute | solution.py:492
  26.5 0.0 collective-permute-done.6.high_ref
  26.5 0.1 shard_map.64.own_ref
  26.6 1.0 %collective-permute-start.7 = (f32[40,128]{1,0:T(8,128)S(1)}, f32[40,128]{1,0:T(8,128)S(1)}, u32[]{:S(2)}, u32[]{:S(2)}) collective-permute-start(f32[40,128]{1,0:T(8,128)S(1)} %shard_map.64.own_ref), channel_id=1, source_target_pairs={{0,32},{1,33},{2,34},{3,35},{4,36},{5,37},{6,38},{7,39},{8,40},{9,... | collective-permute-start | bytes 61448 | tf_op jit(solution)/shard_map/ppermute | solution.py:446
  27.6 2.3 %collective-permute-start.8 = (f32[40,128]{1,0:T(8,128)S(1)}, f32[40,128]{1,0:T(8,128)S(1)}, u32[]{:S(2)}, u32[]{:S(2)}) collective-permute-start(f32[40,128]{1,0:T(8,128)S(1)} %shard_map.64.own_ref), channel_id=1, source_target_pairs={{0,96},{1,97},{2,98},{3,99},{4,100},{5,101},{6,102},{7,103},{8,104... | collective-permute-start | bytes 61448 | tf_op jit(solution)/shard_map/ppermute | solution.py:446
  29.9 1.5 %collective-permute-start.9 = (f32[40,128]{1,0:T(8,128)S(1)}, f32[40,128]{1,0:T(8,128)S(1)}, u32[]{:S(2)}, u32[]{:S(2)}) collective-permute-start(f32[40,128]{1,0:T(8,128)S(1)} %shard_map.64.own_ref), channel_id=1, source_target_pairs={{0,64},{1,65},{2,66},{3,67},{4,68},{5,69},{6,70},{7,71},{8,72},{9,... | collective-permute-start | bytes 61448 | tf_op jit(solution)/shard_map/ppermute | solution.py:446
  31.4 0.2 collective-permute-done.7.below_ref
  31.6 0.0 collective-permute-done.8.above_ref
  31.6 3.5 %collective-permute-done.9.far_ref = f32[40,128]{1,0:T(8,128)S(1)} collective-permute-done((f32[40,128]{1,0:T(8,128)S(1)}, f32[40,128]{1,0:T(8,128)S(1)}, u32[]{:S(2)}, u32[]{:S(2)}) %collective-permute-start.9) | collective-permute-done | bytes 20512 | tf_op jit(solution)/shard_map/ppermute | solution.py:446
  35.2 0.0 copy-start.2
  35.2 0.0 copy-start.4
  35.2 10.3 %all_to_all.5.g_ref = f32[8,48,128]{2,1,0:T(8,128)S(1)} all-to-all(f32[8,48,128]{2,1,0:T(8,128)S(1)} %shard_map.65), channel_id=1, replica_groups=mesh['gx'=4,'gy'=8,'gz'=4] {'gy'}, dimensions={0} | all-to-all | bytes 393216 | tf_op jit(solution)/shard_map/all_to_all | solution.py:499
  45.5 0.0 copy-done.2
  45.5 0.0 copy-done.4
  45.5 2.6 %shard_map.66 = (f32[6,2,16,32]{3,2,1,0:T(8,128)}, bf16[6,512,128]{2,1,0:T(8,128)(2,1)}) custom-call(s32[6]{0:T(128)S(1)} %stack.15.at_ref, f32[8,48,128]{2,1,0:T(8,128)S(1)} %all_to_all.5.g_ref, bf16[512,144]{1,0:T(8,128)(2,1)S(1)} %copy-done.2, bf16[128,256]{1,0:T(8,128)(2,1)S(1)} %copy-done.4), custom_call_target="tpu_custom_call" | custom-call | flops 100000000 | bytes 1000000 | tf_op jit(solution)/shard_map/pallas_call | solution.py:501
  (3 shorter events, 0.1 us)
Async XLA Ops:
  0.6 1.0 %copy-start = (f32[2,16,32,128]{3,2,1,0:T(8,128)S(1)}, f32[2,16,32,128]{3,2,1,0:T(8,128)}, u32[]{:S(2)}) copy-start(f32[2,16,32,128]{3,2,1,0:T(8,128)} %own_ref.3) | copy-start | bytes 1572868
  1.7 13.4 %copy-start.1 = (f32[2,16,32,128]{3,2,1,0:T(8,128)S(1)}, f32[2,16,32,128]{3,2,1,0:T(8,128)}, u32[]{:S(2)}) copy-start(f32[2,16,32,128]{3,2,1,0:T(8,128)} %own_ref.3) | copy-start | bytes 1572868
  1.9 4.9 %collective-permute-start = (f32[2,32,128]{2,1,0:T(8,128)S(1)}, f32[2,32,128]{2,1,0:T(8,128)S(1)}, u32[]{:S(2)}, u32[]{:S(2)}) collective-permute-start(f32[2,32,128]{2,1,0:T(8,128)S(1)} %shard_map.59), channel_id=1, source_target_pairs={{0,1},{1,2},{2,3},{3,0},{4,5},{5,6},{6,7},{7,4},{8,9},{9,10},{10,1... | collective-permute-start | bytes 98312 | tf_op jit(solution)/shard_map/ppermute | solution.py:455
  1.9 9.3 %copy-start.3 = (f32[2,3,2,32,16]{3,4,2,1,0:T(8,128)S(1)}, f32[2,3,2,32,16]{3,4,2,1,0:T(8,128)}, u32[]{:S(2)}) copy-start(f32[2,3,2,32,16]{3,4,2,1,0:T(8,128)} %param.9) | copy-start | bytes 73732
  2.0 17.1 %collective-permute-start.2 = (f32[2,8,32,128]{3,2,1,0:T(8,128)S(1)}, f32[2,8,32,128]{3,2,1,0:T(8,128)S(1)}, u32[]{:S(2)}, u32[]{:S(2)}) collective-permute-start(f32[2,8,32,128]{3,2,1,0:T(8,128)S(1)} %get-tuple-element.37), channel_id=1, source_target_pairs={{0,32},{1,33},{2,34},{3,35},{4,36},{5,37},{6,38},{7,39},{8,40},{9,... | collective-permute-start | bytes 786440 | tf_op jit(solution)/shard_map/ppermute | solution.py:446
  6.8 8.3 %collective-permute-start.1 = (f32[2,17,8,128]{3,2,1,0:T(8,128)S(1)}, f32[2,17,8,128]{3,2,1,0:T(8,128)S(1)}, u32[]{:S(2)}, u32[]{:S(2)}) collective-permute-start(f32[2,17,8,128]{3,2,1,0:T(8,128)S(1)} %get-tuple-element.47), channel_id=1, source_target_pairs={{0,4},{1,5},{2,6},{3,7},{4,8},{5,9},{6,10},{7,11},{8,12},{9,13},{1... | collective-permute-start | bytes 417800 | tf_op jit(solution)/shard_map/ppermute | solution.py:446
  8.4 10.7 %collective-permute-start.4 = (f32[2,9,8,128]{3,2,1,0:T(8,128)S(1)}, f32[2,9,8,128]{3,2,1,0:T(8,128)S(1)}, u32[]{:S(2)}, u32[]{:S(2)}) collective-permute-start(f32[2,9,8,128]{3,2,1,0:T(8,128)S(1)} %get-tuple-element.46), channel_id=1, source_target_pairs={{0,36},{1,37},{2,38},{3,39},{4,40},{5,41},{6,42},{7,43},{8,44},{9,... | collective-permute-start | bytes 221192 | tf_op jit(solution)/shard_map/ppermute | solution.py:446
  12.3 5.5 %collective-permute-start.3 = (f32[2,32,128]{2,1,0:T(8,128)S(1)}, f32[2,32,128]{2,1,0:T(8,128)S(1)}, u32[]{:S(2)}, u32[]{:S(2)}) collective-permute-start(f32[2,32,128]{2,1,0:T(8,128)S(1)} %collective-permute-done.zr_ref), channel_id=1, source_target_pairs={{0,32},{1,33},{2,34},{3,35},{4,36},{5,37},{6,38},{7,39},{8,40},{9,... | collective-permute-start | bytes 98312 | tf_op jit(solution)/shard_map/ppermute | solution.py:446
  21.7 4.8 %collective-permute-start.5 = (f32[40,128]{1,0:T(8,128)S(1)}, f32[40,128]{1,0:T(8,128)S(1)}, u32[]{:S(2)}, u32[]{:S(2)}) collective-permute-start(f32[40,128]{1,0:T(8,128)S(1)} %shard_map.63.mine_ref), channel_id=1, source_target_pairs={{0,1},{1,2},{2,3},{3,0},{4,5},{5,6},{6,7},{7,4},{8,9},{9,10},{10,1... | collective-permute-start | bytes 61448 | tf_op jit(solution)/shard_map/ppermute | solution.py:492
  21.8 4.7 %collective-permute-start.6 = (f32[40,128]{1,0:T(8,128)S(1)}, f32[40,128]{1,0:T(8,128)S(1)}, u32[]{:S(2)}, u32[]{:S(2)}) collective-permute-start(f32[40,128]{1,0:T(8,128)S(1)} %shard_map.63.mine_ref), channel_id=1, source_target_pairs={{1,0},{2,1},{3,2},{0,3},{5,4},{6,5},{7,6},{4,7},{9,8},{10,9},{11,1... | collective-permute-start | bytes 61448 | tf_op jit(solution)/shard_map/ppermute | solution.py:493
  26.6 5.0 %collective-permute-start.7 = (f32[40,128]{1,0:T(8,128)S(1)}, f32[40,128]{1,0:T(8,128)S(1)}, u32[]{:S(2)}, u32[]{:S(2)}) collective-permute-start(f32[40,128]{1,0:T(8,128)S(1)} %shard_map.64.own_ref), channel_id=1, source_target_pairs={{0,32},{1,33},{2,34},{3,35},{4,36},{5,37},{6,38},{7,39},{8,40},{9,... | collective-permute-start | bytes 61448 | tf_op jit(solution)/shard_map/ppermute | solution.py:446
  27.6 4.0 %collective-permute-start.8 = (f32[40,128]{1,0:T(8,128)S(1)}, f32[40,128]{1,0:T(8,128)S(1)}, u32[]{:S(2)}, u32[]{:S(2)}) collective-permute-start(f32[40,128]{1,0:T(8,128)S(1)} %shard_map.64.own_ref), channel_id=1, source_target_pairs={{0,96},{1,97},{2,98},{3,99},{4,100},{5,101},{6,102},{7,103},{8,104... | collective-permute-start | bytes 61448 | tf_op jit(solution)/shard_map/ppermute | solution.py:446
  29.9 5.3 %collective-permute-start.9 = (f32[40,128]{1,0:T(8,128)S(1)}, f32[40,128]{1,0:T(8,128)S(1)}, u32[]{:S(2)}, u32[]{:S(2)}) collective-permute-start(f32[40,128]{1,0:T(8,128)S(1)} %shard_map.64.own_ref), channel_id=1, source_target_pairs={{0,64},{1,65},{2,66},{3,67},{4,68},{5,69},{6,70},{7,71},{8,72},{9,... | collective-permute-start | bytes 61448 | tf_op jit(solution)/shard_map/ppermute | solution.py:446
  35.2 10.4 %copy-start.2 = (bf16[512,144]{1,0:T(8,128)(2,1)S(1)}, bf16[512,144]{1,0:T(8,128)(2,1)}, u32[]{:S(2)}) copy-start(bf16[512,144]{1,0:T(8,128)(2,1)} %constant.77.clone.wxy_ref) | copy-start | bytes 442372
  35.2 10.3 %copy-start.4 = (bf16[128,256]{1,0:T(8,128)(2,1)S(1)}, bf16[128,256]{1,0:T(8,128)(2,1)}, u32[]{:S(2)}) copy-start(bf16[128,256]{1,0:T(8,128)(2,1)} %constant.78.clone.wz_ref) | copy-start | bytes 196612

commit v4 on v3

--- a/solution.py
+++ b/solution.py
@@ -27,14 +27,24 @@
     return hi, lo
 
 
-def pack_kernel(img_ref, out_ref):
+def pack_kernel(img_ref, out_ref, buf_ref, sems):
     lane = lax.broadcasted_iota(jnp.int32, (32, 128), 1)
+    copies = []
+    for n in range(4):
+        for h in range(2):
+            planes = pl.ds(4 * n, 4)
+            copy = pltpu.make_async_copy(img_ref.at[h, planes], buf_ref.at[h, planes], sems.at[2 * n + h])
+            copy.start()
+            copies.append(copy)
+    packed = [jnp.zeros((32, 128), f32) for _ in range(2)]
+    for n in range(4):
+        for h in range(2):
+            copies[2 * n + h].wait()
+            for t in range(4 * n, 4 * n + 4):
+                moved = pltpu.roll(buf_ref[h, t], (8 * t + 8) % 128, 1)
+                packed[h] = jnp.where((lane >= 8 * t) & (lane < 8 * t + 8), moved, packed[h])
     for h in range(2):
-        packed = jnp.zeros((32, 128), f32)
-        for t in range(16):
-            moved = pltpu.roll(img_ref[h, t], (8 * t + 8) % 128, 1)
-            packed = jnp.where((lane >= 8 * t) & (lane < 8 * t + 8), moved, packed)
-        out_ref[h] = packed
+        out_ref[h] = packed[h]
 
 
 def slab_kernel(img_ref, x_ref, y_ref, xy_ref):
@@ -311,20 +321,25 @@
         out_ref[...] = total + base_ref[...]
 
 
-def fold_kernel(mine_ref, low_ref, high_ref, out_ref):
+def fold_kernel(at_ref, mine_ref, chip_ref, core_ref, out_ref):
     lane = lax.broadcasted_iota(jnp.int32, (40, 128), 1)
     spot = lax.rem(lane, 20)
     live = lane < 120
-    low = pltpu.roll(low_ref[...], 112, 1)
-    high = pltpu.roll(high_ref[...], 16, 1)
+    odd = (at_ref[2] & 1) == 1
+    chip, core = chip_ref[...], core_ref[...]
+    low = pltpu.roll(jnp.where(odd, core, chip), 112, 1)
+    high = pltpu.roll(jnp.where(odd, chip, core), 16, 1)
     total = mine_ref[...]
     total = total + jnp.where(live & (spot < 3), low, 0.0)
     out_ref[...] = total + jnp.where(live & (spot >= 16), high, 0.0)
 
 
-def across_kernel(own_ref, below_ref, above_ref, far_ref, out_ref):
+def across_kernel(at_ref, own_ref, one_ref, two_ref, far_ref, out_ref):
+    odd = (at_ref[0] & 1) == 1
     tiles = lambda ref: [ref[8 * p : 8 * p + 8] for p in range(5)]
-    own, below, above, far = tiles(own_ref), tiles(below_ref), tiles(above_ref), tiles(far_ref)
+    own, one, two, far = tiles(own_ref), tiles(one_ref), tiles(two_ref), tiles(far_ref)
+    below = [jnp.where(odd, a, b) for a, b in zip(one, two)]
+    above = [jnp.where(odd, b, a) for a, b in zip(one, two)]
     window = [
         own[0] + below[2] + far[4],
         own[1] + below[3],
@@ -402,14 +417,14 @@
 HBM = pl.BlockSpec(memory_space=pltpu.HBM)
 
 
-def call(body, out_shape, in_specs, scratch=(), out_specs=None, flops=0, bytes_accessed=0):
+def call(body, out_shape, in_specs, scratch=(), out_specs=None, vmem=48 << 20, flops=0, bytes_accessed=0):
     return pl.pallas_call(
         body,
         out_shape=[jax.ShapeDtypeStruct(shape, dtype) for shape, dtype in out_shape],
         in_specs=in_specs,
         out_specs=out_specs or [VMEM] * len(out_shape),
         scratch_shapes=list(scratch),
-        compiler_params=pltpu.CompilerParams(vmem_limit_bytes=48 << 20),
+        compiler_params=pltpu.CompilerParams(vmem_limit_bytes=vmem),
         cost_estimate=pl.CostEstimate(flops=flops, bytes_accessed=bytes_accessed, transcendentals=0),
     )
 
@@ -445,7 +460,14 @@
     def send(v, di, dj, dk):
         return lax.ppermute(v, axes, pairs(sizes, di, dj, dk))
 
-    (pack,) = call(pack_kernel, [((2, 32, 128), f32)], [VMEM], bytes_accessed=6 * 10**5)(images)
+    (pack,) = call(
+        pack_kernel,
+        [((2, 32, 128), f32)],
+        [HBM],
+        [pltpu.VMEM((2, 16, 32, 128), f32), pltpu.SemaphoreType.DMA((8,))],
+        vmem=60 << 20,
+        bytes_accessed=6 * 10**5,
+    )(images)
     to_x, to_y, to_xy = call(
         slab_kernel,
         [((2, 8, 32, 128), f32), ((2, 17, 8, 128), f32), ((2, 9, 8, 128), f32)],
@@ -453,11 +475,6 @@
         bytes_accessed=10**6,
     )(images)
     zr = lax.ppermute(pack, "gz", [(n, (n + 1) % nk) for n in range(nk)])
-    xr = send(to_x, 1, 0, 0)
-    yr = send(to_y.at[:, 16].set(zr[:, 24:]), 0, 1, 0)
-    xyr = send(to_xy.at[:, 8].set(zr[:, 24:]), 1, 1, 0)
-    xzr = send(zr, 1, 0, 0)
-
     velocity = jnp.swapaxes(velocity, 3, 4).reshape(6, 2, 16, 32)
     vel, wxy, wzs, xsum, zsum = call(
         prep_kernel,
@@ -466,6 +483,11 @@
         [pltpu.VMEM((128, 32), f32)],
         bytes_accessed=10**6,
     )(at, velocity)
+    zr, vel = lax.optimization_barrier((zr, vel))
+    xr = send(to_x, 1, 0, 0)
+    yr = send(to_y.at[:, 16].set(zr[:, 24:]), 0, 1, 0)
+    xyr = send(to_xy.at[:, 8].set(zr[:, 24:]), 1, 1, 0)
+    xzr = send(zr, 1, 0, 0)
 
     def forces(upper, *arrays):
         return call(
@@ -489,13 +511,14 @@
     part = forces(True, images, zr, yr, vel)
     part = forces(False, images, zr, yr, xr, xzr, xyr, part)
 
-    low = lax.ppermute(part, "gz", [(n, (n + 1) % nk) for n in range(nk)])
-    high = lax.ppermute(part, "gz", [((n + 1) % nk, n) for n in range(nk)])
-    (own,) = call(fold_kernel, [((40, 128), f32)], [VMEM] * 3)(part, low, high)
-    below = send(own, 1, 0, 0)
-    above = send(own, -1, 0, 0)
-    far = send(own, 2, 0, 0)
-    (copies,) = call(across_kernel, [((8, 48, 128), f32)], [VMEM] * 4)(own, below, above, far)
+    swap = lambda v, axis, couples: lax.ppermute(v, axis, couples + [(b, a) for a, b in couples])
+    chip = swap(part, "gz", [(1, 2), (3, 0)])
+    core = swap(part, "gz", [(0, 1), (2, 3)])
+    (own,) = call(fold_kernel, [((40, 128), f32)], [SMEM] + [VMEM] * 3)(at, part, chip, core)
+    far = swap(own, "gx", [(0, 2), (1, 3)])
+    one = swap(own, "gx", [(0, 1), (2, 3)])
+    two = swap(own, "gx", [(1, 2), (3, 0)])
+    (copies,) = call(across_kernel, [((8, 48, 128), f32)], [SMEM] + [VMEM] * 4)(at, own, one, two, far)
     everything = lax.all_to_all(copies, "gy", 0, 0, tiled=True)
 
     nv, field = call(

time: 48.9 us -> 50.5 us (1.033); the launches traced: 48.2 us -> 50.4 us
  Pallas kernels: 9.24 us -> 12.4 us
  waiting for transfers between devices: 10.1 us -> 13 us
  starting transfers between devices: 16.6 us -> 14.5 us
  local copies, waits for them, and re-layouts: 1.14 us -> 0.11 us
  blocking collectives: 10.3 us -> 9.64 us
    ppermute x2 -> x5, waiting for transfers between devices: 1.48 us -> 7.15 us  [shards(): lax.ppermute(v, axis, couples + [(b, a) for a, b in couples])]
    ppermute x7 -> x4, starting transfers between devices: 13.2 us -> 8.41 us  [send(): return lax.ppermute(v, axes, pairs(sizes, di, dj, dk))]
    pallas_call x3, Pallas kernels: 0.28 us -> 3.44 us  [the longest x1 2.25 us: shards(): call(pack_kernel, [((2, 32, 128), f32)], [HBM], [pltpu.VMEM((2, 16, 32, 1...]
    ppermute x2 -> x5, starting transfers between devices: 3.31 us -> 6.03 us  [shards(): lax.ppermute(v, axis, couples + [(b, a) for a, b in couples])]
    ppermute x7 -> x4, waiting for transfers between devices: 5.91 us -> 3.99 us  [send(): return lax.ppermute(v, axes, pairs(sizes, di, dj, dk))]
    unnamed x10 -> x8, local copies, waits for them, and re-layouts: 1.06 us -> 0.02 us
    ppermute x1, waiting for transfers between devices: 2.71 us -> 1.82 us  [shards(): zr = lax.ppermute(pack, 'gz', [(n, (n + 1) % nk) for n in range(nk)])]
    all_to_all x1, blocking collectives: 10.3 us -> 9.64 us  [shards(): everything = lax.all_to_all(copies, 'gy', 0, 0, tiled=True)]
  transfers between devices with their start and end apart: 10 -> 10, of which waited for: 6 -> 6; matrix products, arithmetic and copies ran while one was open for 0% -> 0% of each run, Pallas kernels for 8% -> 7%
where the time goes in v4:
time: 50.5 us; the launch traced here: 50.4 us
  starting transfers between devices  14.5 us (29%)
  waiting for transfers between devices  13 us (26%)
  Pallas kernels  12.4 us (25%)
  blocking collectives  9.64 us (19%)
  between operations  0.74 us (1%)
    all_to_all x1, blocking collectives, shards(): everything = lax.all_to_all(copies, 'gy', 0, 0, tiled=True)  9.64 us
    ppermute x4, starting transfers between devices, send(): return lax.ppermute(v, axes, pairs(sizes, di, dj, dk))  8.41 us
    ppermute x5, waiting for transfers between devices, shards(): lax.ppermute(v, axis, couples + [(b, a) for a, b in couples])  7.15 us
    ppermute x5, starting transfers between devices, shards(): lax.ppermute(v, axis, couples + [(b, a) for a, b in couples])  6.03 us
    pallas_call x2, Pallas kernels, forces(): call(functools.partial(force_kernel, upper), [((40, 128), f32)], [SMEM] +...  5.28 us
    ppermute x4, waiting for transfers between devices, send(): return lax.ppermute(v, axes, pairs(sizes, di, dj, dk))  3.99 us
    pallas_call x1, Pallas kernels, shards(): call(field_kernel, [((6, 2, 16, 32), f32), ((6, 512, 128), bf16)], [SMEM]...  2.64 us
    pallas_call x1, Pallas kernels, shards(): call(pack_kernel, [((2, 32, 128), f32)], [HBM], [pltpu.VMEM((2, 16, 32, 1...  2.25 us
  transfers between devices with their start and end apart: 10, of which 6 were waited for; matrix products, arithmetic and copies ran while one was open for 0% of the time, Pallas kernels for 7%

profile of v4, /device:TPU:0, one launch (start us, length us, event | category | flops | bytes accessed | tf_op | source)
XLA Modules:
  0.0 50.4 jit_solution(17926423482938284598)
XLA Ops:
  0.6 0.0 copy-start
  0.6 2.3 %shard_map.59 = f32[2,32,128]{2,1,0:T(8,128)} custom-call(f32[2,16,32,128]{3,2,1,0:T(8,128)} %own_ref.3), custom_call_target="tpu_custom_call" | custom-call | bytes 600000 | tf_op jit(solution)/shard_map/pallas_call | solution.py:463
  2.9 0.1 collective-permute-start
  3.0 0.0 copy-done
  3.0 0.0 copy-start.2
  3.0 2.1 %collective-permute-start.2 = (f32[2,8,32,128]{3,2,1,0:T(8,128)S(1)}, f32[2,8,32,128]{3,2,1,0:T(8,128)S(1)}, u32[]{:S(2)}, u32[]{:S(2)}) collective-permute-start(f32[2,8,32,128]{3,2,1,0:T(8,128)S(1)} %get-tuple-element.41), channel_id=1, source_target_pairs={{0,32},{1,33},{2,34},{3,35},{4,36},{5,37},{6,38},{7,39},{8,40},{9,... | collective-permute-start | bytes 786440 | tf_op jit(solution)/shard_map/ppermute | solution.py:461
  5.1 0.1 stack.15.at_ref
  5.2 0.0 copy-done.2
  5.2 1.0 %shard_map.60 = (f32[16,128]{1,0:T(8,128)S(1)}, bf16[80,512]{1,0:T(8,128)(2,1)S(1)}, bf16[128,256]{1,0:T(8,128)(2,1)S(1)}, bf16[256,128]{1,0:T(8,128)(2,1)S(1)}, f32[256,128]{1,0:T(8,128)S(1)}) custom-call(s32[6]{0:T(128)S(1)} %stack.15.at_ref, f32[6,2,16,32]{3,2,1,0:T(8,128)S(1)} %bitcast.13), custom_call_target="tpu_custom_call" | custom-call | bytes 1000000 | tf_op jit(solution)/shard_map/pallas_call | solution.py:479
  6.2 1.8 %collective-permute-done.zr_ref = f32[2,32,128]{2,1,0:T(8,128)S(1)} collective-permute-done((f32[2,32,128]{2,1,0:T(8,128)}, f32[2,32,128]{2,1,0:T(8,128)S(1)}, u32[]{:S(2)}, u32[]{:S(2)}) %collective-permute-start) | collective-permute-done | bytes 32800 | tf_op jit(solution)/shard_map/ppermute | solution.py:477
  8.0 1.6 %collective-permute-start.1 = (f32[2,17,8,128]{3,2,1,0:T(8,128)S(1)}, f32[2,17,8,128]{3,2,1,0:T(8,128)S(1)}, u32[]{:S(2)}, u32[]{:S(2)}) collective-permute-start(f32[2,17,8,128]{3,2,1,0:T(8,128)S(1)} %get-tuple-element.51), channel_id=1, source_target_pairs={{0,4},{1,5},{2,6},{3,7},{4,8},{5,9},{6,10},{7,11},{8,12},{9,13},{1... | collective-permute-start | bytes 417800 | tf_op jit(solution)/shard_map/ppermute | solution.py:461
  9.6 2.8 %collective-permute-start.4 = (f32[2,9,8,128]{3,2,1,0:T(8,128)S(1)}, f32[2,9,8,128]{3,2,1,0:T(8,128)S(1)}, u32[]{:S(2)}, u32[]{:S(2)}) collective-permute-start(f32[2,9,8,128]{3,2,1,0:T(8,128)S(1)} %get-tuple-element.50), channel_id=1, source_target_pairs={{0,36},{1,37},{2,38},{3,39},{4,40},{5,41},{6,42},{7,43},{8,44},{9,... | collective-permute-start | bytes 221192 | tf_op jit(solution)/shard_map/ppermute | solution.py:461
  12.4 1.9 %collective-permute-start.3 = (f32[2,32,128]{2,1,0:T(8,128)S(1)}, f32[2,32,128]{2,1,0:T(8,128)S(1)}, u32[]{:S(2)}, u32[]{:S(2)}) collective-permute-start(f32[2,32,128]{2,1,0:T(8,128)S(1)} %collective-permute-done.zr_ref), channel_id=1, source_target_pairs={{0,32},{1,33},{2,34},{3,35},{4,36},{5,37},{6,38},{7,39},{8,40},{9,... | collective-permute-start | bytes 98312 | tf_op jit(solution)/shard_map/ppermute | solution.py:461
  14.4 2.1 %collective-permute-done.1.yr_ref = f32[2,17,8,128]{3,2,1,0:T(8,128)S(1)} collective-permute-done((f32[2,17,8,128]{3,2,1,0:T(8,128)S(1)}, f32[2,17,8,128]{3,2,1,0:T(8,128)S(1)}, u32[]{:S(2)}, u32[]{:S(2)}) %collective-permute-start.1) | collective-permute-done | bytes 139296 | tf_op jit(solution)/shard_map/ppermute | solution.py:461
  16.4 2.7 %shard_map.62.refs_3_ = f32[40,128]{1,0:T(8,128)S(1)} custom-call(s32[6]{0:T(128)S(1)} %stack.15.at_ref, f32[2,16,32,128]{3,2,1,0:T(8,128)S(1)} %copy-done, f32[2,32,128]{2,1,0:T(8,128)S(1)} %collective-permute-done.zr_ref, f32[2,17,8,128]{3,2,1,0:T(8,128)S(1)} %collective-permute-done.1.yr_ref, f32[16,128]{1,0:T(8,128)S(1)} %get-tuple-element.43.refs_0_, ...), custom_call_target="tpu_custom_call" | custom-call | flops 500000000 | bytes 1000000 | tf_op jit(solution)/shard_map/pallas_call | solution.py:493
  19.1 0.0 collective-permute-done.3.refs_1_
  19.1 1.9 %collective-permute-done.4.refs_2_ = f32[2,9,8,128]{3,2,1,0:T(8,128)S(1)} collective-permute-done((f32[2,9,8,128]{3,2,1,0:T(8,128)S(1)}, f32[2,9,8,128]{3,2,1,0:T(8,128)S(1)}, u32[]{:S(2)}, u32[]{:S(2)}) %collective-permute-start.4) | collective-permute-done | bytes 73760 | tf_op jit(solution)/shard_map/ppermute | solution.py:461
  21.0 0.0 collective-permute-done.2.refs_0_
  21.0 2.6 %shard_map.63.mine_ref = f32[40,128]{1,0:T(8,128)S(1)} custom-call(s32[6]{0:T(128)S(1)} %stack.15.at_ref, f32[2,16,32,128]{3,2,1,0:T(8,128)S(1)} %copy-done, f32[2,32,128]{2,1,0:T(8,128)S(1)} %collective-permute-done.zr_ref, f32[2,17,8,128]{3,2,1,0:T(8,128)S(1)} %collective-permute-done.1.yr_ref, f32[2,8,32,128]{3,2,1,0:T(8,128)S(1)} %collective-permute-done.2.refs_0_, ...), custom_call_target="tpu_custom_call" | custom-call | flops 500000000 | bytes 1000000 | tf_op jit(solution)/shard_map/pallas_call | solution.py:493
  23.7 0.1 collective-permute-start.5
  23.8 1.8 %collective-permute-start.6 = (f32[40,128]{1,0:T(8,128)S(1)}, f32[40,128]{1,0:T(8,128)S(1)}, u32[]{:S(2)}, u32[]{:S(2)}) collective-permute-start(f32[40,128]{1,0:T(8,128)S(1)} %shard_map.63.mine_ref), channel_id=1, source_target_pairs={{0,1},{2,3},{1,0},{3,2},{4,5},{6,7},{5,4},{7,6},{8,9},{10,11},{9,8... | collective-permute-start | bytes 61448 | tf_op jit(solution)/shard_map/ppermute | solution.py:514
  25.5 2.9 %collective-permute-done.5.chip_ref = f32[40,128]{1,0:T(8,128)S(1)} collective-permute-done((f32[40,128]{1,0:T(8,128)S(1)}, f32[40,128]{1,0:T(8,128)S(1)}, u32[]{:S(2)}, u32[]{:S(2)}) %collective-permute-start.5) | collective-permute-done | bytes 20512 | tf_op jit(solution)/shard_map/ppermute | solution.py:514
  28.5 0.0 collective-permute-done.6.core_ref
  28.5 0.6 %shard_map.64.own_ref = f32[40,128]{1,0:T(8,128)S(1)} custom-call(s32[6]{0:T(128)S(1)} %stack.15.at_ref, f32[40,128]{1,0:T(8,128)S(1)} %shard_map.63.mine_ref, f32[40,128]{1,0:T(8,128)S(1)} %collective-permute-done.5.chip_ref, f32[40,128]{1,0:T(8,128)S(1)} %collective-permute-done.6.core_ref), custom_call_target="tpu_custom_call" | custom-call | tf_op jit(solution)/shard_map/pallas_call | solution.py:517
  29.1 0.2 collective-permute-start.7
  29.3 2.9 %collective-permute-start.8 = (f32[40,128]{1,0:T(8,128)S(1)}, f32[40,128]{1,0:T(8,128)S(1)}, u32[]{:S(2)}, u32[]{:S(2)}) collective-permute-start(f32[40,128]{1,0:T(8,128)S(1)} %shard_map.64.own_ref), channel_id=1, source_target_pairs={{32,64},{96,0},{64,32},{0,96},{33,65},{97,1},{65,33},{1,97},{34,66... | collective-permute-start | bytes 61448 | tf_op jit(solution)/shard_map/ppermute | solution.py:514
  32.2 1.0 %collective-permute-start.9 = (f32[40,128]{1,0:T(8,128)S(1)}, f32[40,128]{1,0:T(8,128)S(1)}, u32[]{:S(2)}, u32[]{:S(2)}) collective-permute-start(f32[40,128]{1,0:T(8,128)S(1)} %shard_map.64.own_ref), channel_id=1, source_target_pairs={{0,64},{32,96},{64,0},{96,32},{1,65},{33,97},{65,1},{97,33},{2,66}... | collective-permute-start | bytes 61448 | tf_op jit(solution)/shard_map/ppermute | solution.py:514
  33.2 0.0 collective-permute-done.7.one_ref
  33.2 1.1 %collective-permute-done.8.two_ref = f32[40,128]{1,0:T(8,128)S(1)} collective-permute-done((f32[40,128]{1,0:T(8,128)S(1)}, f32[40,128]{1,0:T(8,128)S(1)}, u32[]{:S(2)}, u32[]{:S(2)}) %collective-permute-start.8) | collective-permute-done | bytes 20512 | tf_op jit(solution)/shard_map/ppermute | solution.py:514
  34.3 3.2 %collective-permute-done.9.far_ref = f32[40,128]{1,0:T(8,128)S(1)} collective-permute-done((f32[40,128]{1,0:T(8,128)S(1)}, f32[40,128]{1,0:T(8,128)S(1)}, u32[]{:S(2)}, u32[]{:S(2)}) %collective-permute-start.9) | collective-permute-done | bytes 20512 | tf_op jit(solution)/shard_map/ppermute | solution.py:514
  37.5 0.6 %shard_map.65 = f32[8,48,128]{2,1,0:T(8,128)S(1)} custom-call(s32[6]{0:T(128)S(1)} %stack.15.at_ref, f32[40,128]{1,0:T(8,128)S(1)} %shard_map.64.own_ref, f32[40,128]{1,0:T(8,128)S(1)} %collective-permute-done.7.one_ref, f32[40,128]{1,0:T(8,128)S(1)} %collective-permute-done.8.two_ref, f32[40,128]{1,0:T(8,128)S(1)} %collective-permute-done.9.far_ref), custom_call_target="tpu_custom_call" | custom-call | tf_op jit(solution)/shard_map/pallas_call | solution.py:521
  38.0 0.0 copy-start.1
  38.1 0.0 copy-start.3
  38.1 9.6 %all_to_all.5.g_ref = f32[8,48,128]{2,1,0:T(8,128)S(1)} all-to-all(f32[8,48,128]{2,1,0:T(8,128)S(1)} %shard_map.65), channel_id=1, replica_groups=mesh['gx'=4,'gy'=8,'gz'=4] {'gy'}, dimensions={0} | all-to-all | bytes 393216 | tf_op jit(solution)/shard_map/all_to_all | solution.py:522
  47.7 0.0 copy-done.1
  47.7 0.0 copy-done.3
  47.7 2.6 %shard_map.66 = (f32[6,2,16,32]{3,2,1,0:T(8,128)}, bf16[6,512,128]{2,1,0:T(8,128)(2,1)}) custom-call(s32[6]{0:T(128)S(1)} %stack.15.at_ref, f32[8,48,128]{2,1,0:T(8,128)S(1)} %all_to_all.5.g_ref, bf16[512,144]{1,0:T(8,128)(2,1)S(1)} %copy-done.1, bf16[128,256]{1,0:T(8,128)(2,1)S(1)} %copy-done.3), custom_call_target="tpu_custom_call" | custom-call | flops 100000000 | bytes 1000000 | tf_op jit(solution)/shard_map/pallas_call | solution.py:524
  (2 shorter events, 0.0 us)
Async XLA Ops:
  0.6 2.4 %copy-start = (f32[2,16,32,128]{3,2,1,0:T(8,128)S(1)}, f32[2,16,32,128]{3,2,1,0:T(8,128)}, u32[]{:S(2)}) copy-start(f32[2,16,32,128]{3,2,1,0:T(8,128)} %own_ref.3) | copy-start | bytes 1572868
  2.9 5.1 %collective-permute-start = (f32[2,32,128]{2,1,0:T(8,128)}, f32[2,32,128]{2,1,0:T(8,128)S(1)}, u32[]{:S(2)}, u32[]{:S(2)}) collective-permute-start(f32[2,32,128]{2,1,0:T(8,128)} %shard_map.59), channel_id=1, source_target_pairs={{0,1},{1,2},{2,3},{3,0},{4,5},{5,6},{6,7},{7,4},{8,9},{9,10},{10,1... | collective-permute-start | bytes 98312 | tf_op jit(solution)/shard_map/ppermute | solution.py:477
  3.0 2.2 %copy-start.2 = (f32[2,3,2,32,16]{3,4,2,1,0:T(8,128)S(1)}, f32[2,3,2,32,16]{3,4,2,1,0:T(8,128)}, u32[]{:S(2)}) copy-start(f32[2,3,2,32,16]{3,4,2,1,0:T(8,128)} %param.9) | copy-start | bytes 73732
  3.0 18.0 %collective-permute-start.2 = (f32[2,8,32,128]{3,2,1,0:T(8,128)S(1)}, f32[2,8,32,128]{3,2,1,0:T(8,128)S(1)}, u32[]{:S(2)}, u32[]{:S(2)}) collective-permute-start(f32[2,8,32,128]{3,2,1,0:T(8,128)S(1)} %get-tuple-element.41), channel_id=1, source_target_pairs={{0,32},{1,33},{2,34},{3,35},{4,36},{5,37},{6,38},{7,39},{8,40},{9,... | collective-permute-start | bytes 786440 | tf_op jit(solution)/shard_map/ppermute | solution.py:461
  8.0 8.4 %collective-permute-start.1 = (f32[2,17,8,128]{3,2,1,0:T(8,128)S(1)}, f32[2,17,8,128]{3,2,1,0:T(8,128)S(1)}, u32[]{:S(2)}, u32[]{:S(2)}) collective-permute-start(f32[2,17,8,128]{3,2,1,0:T(8,128)S(1)} %get-tuple-element.51), channel_id=1, source_target_pairs={{0,4},{1,5},{2,6},{3,7},{4,8},{5,9},{6,10},{7,11},{8,12},{9,13},{1... | collective-permute-start | bytes 417800 | tf_op jit(solution)/shard_map/ppermute | solution.py:461
  9.6 11.4 %collective-permute-start.4 = (f32[2,9,8,128]{3,2,1,0:T(8,128)S(1)}, f32[2,9,8,128]{3,2,1,0:T(8,128)S(1)}, u32[]{:S(2)}, u32[]{:S(2)}) collective-permute-start(f32[2,9,8,128]{3,2,1,0:T(8,128)S(1)} %get-tuple-element.50), channel_id=1, source_target_pairs={{0,36},{1,37},{2,38},{3,39},{4,40},{5,41},{6,42},{7,43},{8,44},{9,... | collective-permute-start | bytes 221192 | tf_op jit(solution)/shard_map/ppermute | solution.py:461
  12.4 6.7 %collective-permute-start.3 = (f32[2,32,128]{2,1,0:T(8,128)S(1)}, f32[2,32,128]{2,1,0:T(8,128)S(1)}, u32[]{:S(2)}, u32[]{:S(2)}) collective-permute-start(f32[2,32,128]{2,1,0:T(8,128)S(1)} %collective-permute-done.zr_ref), channel_id=1, source_target_pairs={{0,32},{1,33},{2,34},{3,35},{4,36},{5,37},{6,38},{7,39},{8,40},{9,... | collective-permute-start | bytes 98312 | tf_op jit(solution)/shard_map/ppermute | solution.py:461
  23.7 4.8 %collective-permute-start.5 = (f32[40,128]{1,0:T(8,128)S(1)}, f32[40,128]{1,0:T(8,128)S(1)}, u32[]{:S(2)}, u32[]{:S(2)}) collective-permute-start(f32[40,128]{1,0:T(8,128)S(1)} %shard_map.63.mine_ref), channel_id=1, source_target_pairs={{1,2},{3,0},{2,1},{0,3},{5,6},{7,4},{6,5},{4,7},{9,10},{11,8},{10,... | collective-permute-start | bytes 61448 | tf_op jit(solution)/shard_map/ppermute | solution.py:514
  23.8 4.7 %collective-permute-start.6 = (f32[40,128]{1,0:T(8,128)S(1)}, f32[40,128]{1,0:T(8,128)S(1)}, u32[]{:S(2)}, u32[]{:S(2)}) collective-permute-start(f32[40,128]{1,0:T(8,128)S(1)} %shard_map.63.mine_ref), channel_id=1, source_target_pairs={{0,1},{2,3},{1,0},{3,2},{4,5},{6,7},{5,4},{7,6},{8,9},{10,11},{9,8... | collective-permute-start | bytes 61448 | tf_op jit(solution)/shard_map/ppermute | solution.py:514
  29.1 4.2 %collective-permute-start.7 = (f32[40,128]{1,0:T(8,128)S(1)}, f32[40,128]{1,0:T(8,128)S(1)}, u32[]{:S(2)}, u32[]{:S(2)}) collective-permute-start(f32[40,128]{1,0:T(8,128)S(1)} %shard_map.64.own_ref), channel_id=1, source_target_pairs={{0,32},{64,96},{32,0},{96,64},{1,33},{65,97},{33,1},{97,65},{2,34}... | collective-permute-start | bytes 61448 | tf_op jit(solution)/shard_map/ppermute | solution.py:514
  29.3 5.0 %collective-permute-start.8 = (f32[40,128]{1,0:T(8,128)S(1)}, f32[40,128]{1,0:T(8,128)S(1)}, u32[]{:S(2)}, u32[]{:S(2)}) collective-permute-start(f32[40,128]{1,0:T(8,128)S(1)} %shard_map.64.own_ref), channel_id=1, source_target_pairs={{32,64},{96,0},{64,32},{0,96},{33,65},{97,1},{65,33},{1,97},{34,66... | collective-permute-start | bytes 61448 | tf_op jit(solution)/shard_map/ppermute | solution.py:514
  32.2 5.3 %collective-permute-start.9 = (f32[40,128]{1,0:T(8,128)S(1)}, f32[40,128]{1,0:T(8,128)S(1)}, u32[]{:S(2)}, u32[]{:S(2)}) collective-permute-start(f32[40,128]{1,0:T(8,128)S(1)} %shard_map.64.own_ref), channel_id=1, source_target_pairs={{0,64},{32,96},{64,0},{96,32},{1,65},{33,97},{65,1},{97,33},{2,66}... | collective-permute-start | bytes 61448 | tf_op jit(solution)/shard_map/ppermute | solution.py:514
  38.0 9.7 %copy-start.1 = (bf16[512,144]{1,0:T(8,128)(2,1)S(1)}, bf16[512,144]{1,0:T(8,128)(2,1)}, u32[]{:S(2)}) copy-start(bf16[512,144]{1,0:T(8,128)(2,1)} %constant.77.clone.wxy_ref) | copy-start | bytes 442372
  38.1 9.7 %copy-start.3 = (bf16[128,256]{1,0:T(8,128)(2,1)S(1)}, bf16[128,256]{1,0:T(8,128)(2,1)}, u32[]{:S(2)}) copy-start(bf16[128,256]{1,0:T(8,128)(2,1)} %constant.78.clone.wz_ref) | copy-start | bytes 196612

commit v5 on v3

--- a/solution.py
+++ b/solution.py
@@ -10,6 +10,7 @@
 
 epsilon_value = 1e-05
 step_size = 0.5
+AXES = ("gx", "gy", "gz")
 f32 = jnp.float32
 bf16 = jnp.bfloat16
 
@@ -59,10 +60,9 @@
     return spline_at((voxel.astype(f32) - 8.0 * point.astype(f32) - 3.5) * 0.125)
 
 
-def prep_kernel(at_ref, vel_ref, vel_out, wxy_out, wz_out, xsum_out, zsum_out, rows_ref):
-    i = at_ref[0]
-    j = at_ref[1]
-    k = at_ref[2]
+def prep_kernel(vel_ref, vel_out, wxy_out, wz_out, xsum_out, zsum_out, rows_ref):
+    i, j, k = coords()
+    ni, nj, nk = (lax.axis_size(a) for a in AXES)
     ex = jnp.where(i == 0, 0.0, 1.0)
     ez = jnp.where(k == 0, 0.0, 1.0)
     row = lax.broadcasted_iota(jnp.int32, (40, 512), 0)
@@ -73,7 +73,7 @@
     r = col & 31
     ok = ((p < 2) == (o < 4)) | (i != 0)
     ok = ok & (((q < 2) == (r < 4)) | (j != 0)) & (q < 7)
-    ok = ok & ((p < 4) | (i != at_ref[3] - 1)) & ((q < 6) | (j != at_ref[4] - 1))
+    ok = ok & ((p < 4) | (i != ni - 1)) & ((q < 6) | (j != nj - 1))
     table = jnp.where(ok, weights(o - 4, p - 2) * weights(r - 4, q - 2), 0.0)
     hi, lo = split2(table)
     wxy_out[...] = jnp.concatenate([hi.astype(f32), lo.astype(f32)], axis=0).astype(bf16)
@@ -81,7 +81,7 @@
     sub = lax.broadcasted_iota(jnp.int32, (128, 128), 0)
     spot = lax.rem(lane, 20)
     ok = ((spot < 2) == (sub >= 124)) | (k != 0)
-    ok = ok & (spot < 19) & ((spot < 18) | (k != at_ref[5] - 1))
+    ok = ok & (spot < 19) & ((spot < 18) | (k != nk - 1))
     voxel = jnp.where(sub >= 124, sub - 128, sub)
     hi, lo = split2(jnp.where(ok, weights(voxel, spot - 2), 0.0))
     wz_out[...] = jnp.concatenate([hi, lo], axis=1)
@@ -115,6 +115,10 @@
         vel_out[8 * side : 8 * side + 8] = total
 
 
+def coords():
+    return tuple(lax.axis_index(a) for a in AXES)
+
+
 def split3(v):
     hi = v.astype(bf16)
     r = v - hi.astype(f32)
@@ -151,14 +155,14 @@
     return jnp.concatenate([top, w[8:32]], axis=0)
 
 
-def force_kernel(upper, at_ref, own_ref, zr_ref, yr_ref, *refs):
+def force_kernel(upper, own_ref, zr_ref, yr_ref, *refs):
     if upper:
         base_ref, *refs = refs
     else:
         xr_ref, xzr_ref, xyr_ref, base_ref, *refs = refs
     wxy_ref, wz_ref, xsum_ref, zsum_ref, out_ref, a_ref, h_ref, v_ref, dz_ref, xs_ref, hs_ref, fh_ref, fl_ref = refs
     first = 8 if upper else 0
-    ex, ey, ez = (jnp.where(at_ref[n] == 0, 0.0, 1.0) for n in range(3))
+    ex, ey, ez = (jnp.where(at == 0, 0.0, 1.0) for at in coords())
     row8 = lax.broadcasted_iota(jnp.int32, (8, 128), 0)
     row32 = lax.broadcasted_iota(jnp.int32, (32, 128), 0)
     lane40 = lax.broadcasted_iota(jnp.int32, (40, 128), 1)
@@ -311,20 +315,25 @@
         out_ref[...] = total + base_ref[...]
 
 
-def fold_kernel(mine_ref, low_ref, high_ref, out_ref):
+def fold_kernel(mine_ref, chip_ref, core_ref, out_ref):
     lane = lax.broadcasted_iota(jnp.int32, (40, 128), 1)
     spot = lax.rem(lane, 20)
     live = lane < 120
-    low = pltpu.roll(low_ref[...], 112, 1)
-    high = pltpu.roll(high_ref[...], 16, 1)
+    odd = (lax.axis_index("gz") & 1) == 1
+    chip, core = chip_ref[...], core_ref[...]
+    low = pltpu.roll(jnp.where(odd, core, chip), 112, 1)
+    high = pltpu.roll(jnp.where(odd, chip, core), 16, 1)
     total = mine_ref[...]
     total = total + jnp.where(live & (spot < 3), low, 0.0)
     out_ref[...] = total + jnp.where(live & (spot >= 16), high, 0.0)
 
 
-def across_kernel(own_ref, below_ref, above_ref, far_ref, out_ref):
+def across_kernel(own_ref, one_ref, two_ref, far_ref, out_ref):
+    odd = (lax.axis_index("gx") & 1) == 1
     tiles = lambda ref: [ref[8 * p : 8 * p + 8] for p in range(5)]
-    own, below, above, far = tiles(own_ref), tiles(below_ref), tiles(above_ref), tiles(far_ref)
+    own, one, two, far = tiles(own_ref), tiles(one_ref), tiles(two_ref), tiles(far_ref)
+    below = [jnp.where(odd, a, b) for a, b in zip(one, two)]
+    above = [jnp.where(odd, b, a) for a, b in zip(one, two)]
     window = [
         own[0] + below[2] + far[4],
         own[1] + below[3],
@@ -338,8 +347,9 @@
             out_ref[n, 8 * w : 8 * w + 8] = window[w]
 
 
-def field_kernel(at_ref, g_ref, wxy_ref, wz_ref, nv_ref, field_ref, rows_ref, buf_ref, sems):
-    me_j = at_ref[1]
+def field_kernel(g_ref, wxy_ref, wz_ref, nv_ref, field_ref, rows_ref, buf_ref, sems):
+    me_i, me_j, me_k = coords()
+    ni, nj, nk = (lax.axis_size(a) for a in AXES)
     row8 = lax.broadcasted_iota(jnp.int32, (8, 128), 0)
 
     window = []
@@ -350,11 +360,11 @@
     coefs = jnp.concatenate(window, axis=0)
     row = lax.broadcasted_iota(jnp.int32, (48, 128), 0)
     lane = lax.broadcasted_iota(jnp.int32, (48, 128), 1)
-    at_x = 2 * at_ref[0] - 2 + lax.shift_right_logical(row, 3)
+    at_x = 2 * me_i - 2 + lax.shift_right_logical(row, 3)
     at_y = 4 * me_j - 2 + (row & 7)
-    at_z = 16 * at_ref[2] - 2 + lax.rem(lane, 20)
-    real = (at_x >= 0) & (at_x < 2 * at_ref[3]) & (at_y >= 0) & (at_y < 4 * at_ref[4])
-    real = real & (at_z >= 0) & (at_z < 16 * at_ref[5]) & (lane < 120)
+    at_z = 16 * me_k - 2 + lax.rem(lane, 20)
+    real = (at_x >= 0) & (at_x < 2 * ni) & (at_y >= 0) & (at_y < 4 * nj)
+    real = real & (at_z >= 0) & (at_z < 16 * nk) & (lane < 120)
     part = lax.div(lane, 20)
     coefs = jnp.where(real, coefs, 0.0)
     hi, lo = split2(jnp.concatenate([jnp.where(part == c, coefs, 0.0) for c in range(6)], axis=0))
@@ -396,7 +406,6 @@
 
 
 VMEM = pl.BlockSpec(memory_space=pltpu.VMEM)
-SMEM = pl.BlockSpec(memory_space=pltpu.SMEM)
 
 
 HBM = pl.BlockSpec(memory_space=pltpu.HBM)
@@ -435,15 +444,12 @@
 
 
 def shards(images, velocity):
-    axes = ("gx", "gy", "gz")
-    sizes = tuple(lax.axis_size(a) for a in axes)
-    spot = [lax.axis_index(a) for a in axes]
+    sizes = tuple(lax.axis_size(a) for a in AXES)
     nk = sizes[2]
-    at = jnp.stack([jnp.int32(v) for v in (*spot, *sizes)])
     exy, ezs = fixed_tables()
 
     def send(v, di, dj, dk):
-        return lax.ppermute(v, axes, pairs(sizes, di, dj, dk))
+        return lax.ppermute(v, AXES, pairs(sizes, di, dj, dk))
 
     (pack,) = call(pack_kernel, [((2, 32, 128), f32)], [VMEM], bytes_accessed=6 * 10**5)(images)
     to_x, to_y, to_xy = call(
@@ -453,25 +459,25 @@
         bytes_accessed=10**6,
     )(images)
     zr = lax.ppermute(pack, "gz", [(n, (n + 1) % nk) for n in range(nk)])
+    velocity = jnp.swapaxes(velocity, 3, 4).reshape(6, 2, 16, 32)
+    vel, wxy, wzs, xsum, zsum = call(
+        prep_kernel,
+        [((16, 128), f32), ((80, 512), bf16), ((128, 256), bf16), ((256, 128), bf16), ((256, 128), f32)],
+        [VMEM],
+        [pltpu.VMEM((128, 32), f32)],
+        bytes_accessed=10**6,
+    )(velocity)
+    zr, vel = lax.optimization_barrier((zr, vel))
     xr = send(to_x, 1, 0, 0)
     yr = send(to_y.at[:, 16].set(zr[:, 24:]), 0, 1, 0)
     xyr = send(to_xy.at[:, 8].set(zr[:, 24:]), 1, 1, 0)
     xzr = send(zr, 1, 0, 0)
 
-    velocity = jnp.swapaxes(velocity, 3, 4).reshape(6, 2, 16, 32)
-    vel, wxy, wzs, xsum, zsum = call(
-        prep_kernel,
-        [((16, 128), f32), ((80, 512), bf16), ((128, 256), bf16), ((256, 128), bf16), ((256, 128), f32)],
-        [SMEM, VMEM],
-        [pltpu.VMEM((128, 32), f32)],
-        bytes_accessed=10**6,
-    )(at, velocity)
-
     def forces(upper, *arrays):
         return call(
             functools.partial(force_kernel, upper),
             [((40, 128), f32)],
-            [SMEM] + [VMEM] * (len(arrays) + 4),
+            [VMEM] * (len(arrays) + 4),
             [
                 pltpu.VMEM((2, 16, 40, 128), f32),
                 pltpu.VMEM((2, 2, 40, 128), f32),
@@ -484,29 +490,30 @@
             ],
             flops=5 * 10**8,
             bytes_accessed=10**6,
-        )(at, *arrays, wxy, wzs, xsum, zsum)[0]
+        )(*arrays, wxy, wzs, xsum, zsum)[0]
 
     part = forces(True, images, zr, yr, vel)
     part = forces(False, images, zr, yr, xr, xzr, xyr, part)
 
-    low = lax.ppermute(part, "gz", [(n, (n + 1) % nk) for n in range(nk)])
-    high = lax.ppermute(part, "gz", [((n + 1) % nk, n) for n in range(nk)])
-    (own,) = call(fold_kernel, [((40, 128), f32)], [VMEM] * 3)(part, low, high)
-    below = send(own, 1, 0, 0)
-    above = send(own, -1, 0, 0)
-    far = send(own, 2, 0, 0)
-    (copies,) = call(across_kernel, [((8, 48, 128), f32)], [VMEM] * 4)(own, below, above, far)
+    swap = lambda v, axis, couples: lax.ppermute(v, axis, couples + [(b, a) for a, b in couples])
+    chip = swap(part, "gz", [(1, 2), (3, 0)])
+    core = swap(part, "gz", [(0, 1), (2, 3)])
+    (own,) = call(fold_kernel, [((40, 128), f32)], [VMEM] * 3)(part, chip, core)
+    far = swap(own, "gx", [(0, 2), (1, 3)])
+    one = swap(own, "gx", [(0, 1), (2, 3)])
+    two = swap(own, "gx", [(1, 2), (3, 0)])
+    (copies,) = call(across_kernel, [((8, 48, 128), f32)], [VMEM] * 4)(own, one, two, far)
     everything = lax.all_to_all(copies, "gy", 0, 0, tiled=True)
 
     nv, field = call(
         field_kernel,
         [((6, 2, 16, 32), f32), ((6, 512, 128), bf16)],
-        [SMEM] + [VMEM] * 3,
+        [VMEM] * 3,
         [pltpu.VMEM((2, 40, 128), f32), pltpu.VMEM((6, 512, 128), bf16), pltpu.SemaphoreType.DMA((3,))],
         out_specs=[VMEM, HBM],
         flops=10**8,
         bytes_accessed=10**6,
-    )(at, everything, exy, ezs)
+    )(everything, exy, ezs)
     nv = jnp.swapaxes(nv.reshape(2, 3, 2, 16, 32), 3, 4)
     return nv, field.reshape(2, 3, 16, 32, 128)
 

time: 48.9 us -> 46.2 us (0.945); the launches traced: 48.2 us -> 46 us
  waiting for transfers between devices: 10.1 us -> 12.5 us
  Pallas kernels: 9.24 us -> 7.05 us
  starting transfers between devices: 16.6 us -> 15.2 us
  blocking collectives: 10.3 us -> 9.47 us
    ppermute x9, waiting for transfers between devices: 7.4 us -> 10.2 us  [the longest x5 6.39 us: shards(): lax.ppermute(v, axis, couples + [(b, a) for a, b in couples])]
    pallas_call x5, Pallas kernels: 8.01 us -> 6.37 us  [the longest x2 4.17 us: forces(): call(functools.partial(force_kernel, upper), [((40, 128), f32)], [VMEM] *...]
    ppermute x9, starting transfers between devices: 16.6 us -> 15.2 us  [the longest x4 8.44 us: send(): return lax.ppermute(v, AXES, pairs(sizes, di, dj, dk))]
    all_to_all x1, blocking collectives: 10.3 us -> 9.47 us  [shards(): everything = lax.all_to_all(copies, 'gy', 0, 0, tiled=True)]
    pallas_call x1, Pallas kernels: 1 us -> 0.46 us  [shards(): call(prep_kernel, [((16, 128), f32), ((80, 512), bf16), ((128, 256), bf16...]
  transfers between devices with their start and end apart: 10 -> 10, of which waited for: 6 -> 6; matrix products, arithmetic and copies ran while one was open for 0% -> 0% of each run, Pallas kernels for 8% -> 6%
where the time goes in v5:
time: 46.2 us; the launch traced here: 46 us
  starting transfers between devices  15.2 us (33%)
  waiting for transfers between devices  12.5 us (27%)
  blocking collectives  9.47 us (20%)
  Pallas kernels  7.05 us (15%)
  local copies, waits for them, and re-layouts  1.06 us (2%)
  between operations  0.72 us (2%)
    all_to_all x1, blocking collectives, shards(): everything = lax.all_to_all(copies, 'gy', 0, 0, tiled=True)  9.47 us
    ppermute x4, starting transfers between devices, send(): return lax.ppermute(v, AXES, pairs(sizes, di, dj, dk))  8.44 us
    ppermute x5, starting transfers between devices, shards(): lax.ppermute(v, axis, couples + [(b, a) for a, b in couples])  6.73 us
    ppermute x5, waiting for transfers between devices, shards(): lax.ppermute(v, axis, couples + [(b, a) for a, b in couples])  6.39 us
    pallas_call x2, Pallas kernels, forces(): call(functools.partial(force_kernel, upper), [((40, 128), f32)], [VMEM] *...  4.17 us
    ppermute x4, waiting for transfers between devices, send(): return lax.ppermute(v, AXES, pairs(sizes, di, dj, dk))  3.82 us
    ppermute x1, waiting for transfers between devices, shards(): zr = lax.ppermute(pack, 'gz', [(n, (n + 1) % nk) for n in range(nk)])  2.26 us
    pallas_call x1, Pallas kernels, shards(): call(field_kernel, [((6, 2, 16, 32), f32), ((6, 512, 128), bf16)], [VMEM]...  2.1 us
  transfers between devices with their start and end apart: 10, of which 6 were waited for; matrix products, arithmetic and copies ran while one was open for 0% of the time, Pallas kernels for 6%

profile of v5, /device:TPU:0, one launch (start us, length us, event | category | flops | bytes accessed | tf_op | source)
XLA Modules:
  0.0 46.0 jit_solution(2580952685037208833)
XLA Ops:
  0.6 0.0 copy-start
  0.6 1.0 %copy-done = f32[2,16,32,128]{3,2,1,0:T(8,128)S(1)} copy-done((f32[2,16,32,128]{3,2,1,0:T(8,128)S(1)}, f32[2,16,32,128]{3,2,1,0:T(8,128)}, u32[]{:S(2)}) %copy-start) | copy-done | bytes 524312
  1.7 0.0 copy-start.1
  1.7 0.2 shard_map.59
  1.9 0.0 copy-start.3
  1.9 0.1 collective-permute-start
  2.0 2.1 %collective-permute-start.2 = (f32[2,8,32,128]{3,2,1,0:T(8,128)S(1)}, f32[2,8,32,128]{3,2,1,0:T(8,128)S(1)}, u32[]{:S(2)}, u32[]{:S(2)}) collective-permute-start(f32[2,8,32,128]{3,2,1,0:T(8,128)S(1)} %get-tuple-element.41), channel_id=1, source_target_pairs={{0,32},{1,33},{2,34},{3,35},{4,36},{5,37},{6,38},{7,39},{8,40},{9,... | collective-permute-start | bytes 786440 | tf_op jit(solution)/shard_map/ppermute | solution.py:452
  4.1 0.0 copy-done.3
  4.1 0.5 %shard_map.60 = (f32[16,128]{1,0:T(8,128)S(1)}, bf16[80,512]{1,0:T(8,128)(2,1)S(1)}, bf16[128,256]{1,0:T(8,128)(2,1)S(1)}, bf16[256,128]{1,0:T(8,128)(2,1)S(1)}, f32[256,128]{1,0:T(8,128)S(1)}) custom-call(f32[6,2,16,32]{3,2,1,0:T(8,128)S(1)} %bitcast.10), custom_call_target="tpu_custom_call" | custom-call | bytes 1000000 | tf_op jit(solution)/shard_map/pallas_call | solution.py:463
  4.5 2.3 %collective-permute-done.zr_ref = f32[2,32,128]{2,1,0:T(8,128)S(1)} collective-permute-done((f32[2,32,128]{2,1,0:T(8,128)S(1)}, f32[2,32,128]{2,1,0:T(8,128)S(1)}, u32[]{:S(2)}, u32[]{:S(2)}) %collective-permute-start) | collective-permute-done | bytes 32800 | tf_op jit(solution)/shard_map/ppermute | solution.py:461
  6.8 1.6 %collective-permute-start.1 = (f32[2,17,8,128]{3,2,1,0:T(8,128)S(1)}, f32[2,17,8,128]{3,2,1,0:T(8,128)S(1)}, u32[]{:S(2)}, u32[]{:S(2)}) collective-permute-start(f32[2,17,8,128]{3,2,1,0:T(8,128)S(1)} %get-tuple-element.51), channel_id=1, source_target_pairs={{0,4},{1,5},{2,6},{3,7},{4,8},{5,9},{6,10},{7,11},{8,12},{9,13},{1... | collective-permute-start | bytes 417800 | tf_op jit(solution)/shard_map/ppermute | solution.py:452
  8.4 2.8 %collective-permute-start.4 = (f32[2,9,8,128]{3,2,1,0:T(8,128)S(1)}, f32[2,9,8,128]{3,2,1,0:T(8,128)S(1)}, u32[]{:S(2)}, u32[]{:S(2)}) collective-permute-start(f32[2,9,8,128]{3,2,1,0:T(8,128)S(1)} %get-tuple-element.50), channel_id=1, source_target_pairs={{0,36},{1,37},{2,38},{3,39},{4,40},{5,41},{6,42},{7,43},{8,44},{9,... | collective-permute-start | bytes 221192 | tf_op jit(solution)/shard_map/ppermute | solution.py:452
  11.2 1.9 %collective-permute-start.3 = (f32[2,32,128]{2,1,0:T(8,128)S(1)}, f32[2,32,128]{2,1,0:T(8,128)S(1)}, u32[]{:S(2)}, u32[]{:S(2)}) collective-permute-start(f32[2,32,128]{2,1,0:T(8,128)S(1)} %collective-permute-done.zr_ref), channel_id=1, source_target_pairs={{0,32},{1,33},{2,34},{3,35},{4,36},{5,37},{6,38},{7,39},{8,40},{9,... | collective-permute-start | bytes 98312 | tf_op jit(solution)/shard_map/ppermute | solution.py:452
  13.2 2.3 %collective-permute-done.1.yr_ref = f32[2,17,8,128]{3,2,1,0:T(8,128)S(1)} collective-permute-done((f32[2,17,8,128]{3,2,1,0:T(8,128)S(1)}, f32[2,17,8,128]{3,2,1,0:T(8,128)S(1)}, u32[]{:S(2)}, u32[]{:S(2)}) %collective-permute-start.1) | collective-permute-done | bytes 139296 | tf_op jit(solution)/shard_map/ppermute | solution.py:452
  15.4 0.0 copy-done.1
  15.5 2.1 %shard_map.62.refs_3_ = f32[40,128]{1,0:T(8,128)S(1)} custom-call(f32[2,16,32,128]{3,2,1,0:T(8,128)S(1)} %copy-done.1, f32[2,32,128]{2,1,0:T(8,128)S(1)} %collective-permute-done.zr_ref, f32[2,17,8,128]{3,2,1,0:T(8,128)S(1)} %collective-permute-done.1.yr_ref, f32[16,128]{1,0:T(8,128)S(1)} %get-tuple-element.43.refs_0_, ...), custom_call_target="tpu_custom_call" | custom-call | flops 500000000 | bytes 1000000 | tf_op jit(solution)/shard_map/pallas_call | solution.py:477
  17.6 0.0 collective-permute-done.3.refs_1_
  17.6 1.5 %collective-permute-done.4.refs_2_ = f32[2,9,8,128]{3,2,1,0:T(8,128)S(1)} collective-permute-done((f32[2,9,8,128]{3,2,1,0:T(8,128)S(1)}, f32[2,9,8,128]{3,2,1,0:T(8,128)S(1)}, u32[]{:S(2)}, u32[]{:S(2)}) %collective-permute-start.4) | collective-permute-done | bytes 73760 | tf_op jit(solution)/shard_map/ppermute | solution.py:452
  19.1 0.0 collective-permute-done.2.refs_0_
  19.1 2.1 %shard_map.63.mine_ref = f32[40,128]{1,0:T(8,128)S(1)} custom-call(f32[2,16,32,128]{3,2,1,0:T(8,128)S(1)} %copy-done.1, f32[2,32,128]{2,1,0:T(8,128)S(1)} %collective-permute-done.zr_ref, f32[2,17,8,128]{3,2,1,0:T(8,128)S(1)} %collective-permute-done.1.yr_ref, f32[2,8,32,128]{3,2,1,0:T(8,128)S(1)} %collective-permute-done.2.refs_0_, ...), custom_call_target="tpu_custom_call" | custom-call | flops 500000000 | bytes 1000000 | tf_op jit(solution)/shard_map/pallas_call | solution.py:477
  21.2 0.1 collective-permute-start.5
  21.3 2.5 %collective-permute-start.6 = (f32[40,128]{1,0:T(8,128)S(1)}, f32[40,128]{1,0:T(8,128)S(1)}, u32[]{:S(2)}, u32[]{:S(2)}) collective-permute-start(f32[40,128]{1,0:T(8,128)S(1)} %shard_map.63.mine_ref), channel_id=1, source_target_pairs={{0,1},{2,3},{1,0},{3,2},{4,5},{6,7},{5,4},{7,6},{8,9},{10,11},{9,8... | collective-permute-start | bytes 61448 | tf_op jit(solution)/shard_map/ppermute | solution.py:498
  23.8 2.2 %collective-permute-done.5.chip_ref = f32[40,128]{1,0:T(8,128)S(1)} collective-permute-done((f32[40,128]{1,0:T(8,128)S(1)}, f32[40,128]{1,0:T(8,128)S(1)}, u32[]{:S(2)}, u32[]{:S(2)}) %collective-permute-start.5) | collective-permute-done | bytes 20512 | tf_op jit(solution)/shard_map/ppermute | solution.py:498
  26.0 0.0 collective-permute-done.6.core_ref
  26.0 0.1 shard_map.64.own_ref
  26.0 0.5 %collective-permute-start.7 = (f32[40,128]{1,0:T(8,128)S(1)}, f32[40,128]{1,0:T(8,128)S(1)}, u32[]{:S(2)}, u32[]{:S(2)}) collective-permute-start(f32[40,128]{1,0:T(8,128)S(1)} %shard_map.64.own_ref), channel_id=1, source_target_pairs={{0,32},{64,96},{32,0},{96,64},{1,33},{65,97},{33,1},{97,65},{2,34}... | collective-permute-start | bytes 61448 | tf_op jit(solution)/shard_map/ppermute | solution.py:498
  26.6 2.5 %collective-permute-start.8 = (f32[40,128]{1,0:T(8,128)S(1)}, f32[40,128]{1,0:T(8,128)S(1)}, u32[]{:S(2)}, u32[]{:S(2)}) collective-permute-start(f32[40,128]{1,0:T(8,128)S(1)} %shard_map.64.own_ref), channel_id=1, source_target_pairs={{32,64},{96,0},{64,32},{0,96},{33,65},{97,1},{65,33},{1,97},{34,66... | collective-permute-start | bytes 61448 | tf_op jit(solution)/shard_map/ppermute | solution.py:498
  29.1 1.1 %collective-permute-start.9 = (f32[40,128]{1,0:T(8,128)S(1)}, f32[40,128]{1,0:T(8,128)S(1)}, u32[]{:S(2)}, u32[]{:S(2)}) collective-permute-start(f32[40,128]{1,0:T(8,128)S(1)} %shard_map.64.own_ref), channel_id=1, source_target_pairs={{0,64},{32,96},{64,0},{96,32},{1,65},{33,97},{65,1},{97,33},{2,66}... | collective-permute-start | bytes 61448 | tf_op jit(solution)/shard_map/ppermute | solution.py:498
  30.2 0.0 collective-permute-done.7.one_ref
  30.2 1.4 %collective-permute-done.8.two_ref = f32[40,128]{1,0:T(8,128)S(1)} collective-permute-done((f32[40,128]{1,0:T(8,128)S(1)}, f32[40,128]{1,0:T(8,128)S(1)}, u32[]{:S(2)}, u32[]{:S(2)}) %collective-permute-start.8) | collective-permute-done | bytes 20512 | tf_op jit(solution)/shard_map/ppermute | solution.py:498
  31.6 2.8 %collective-permute-done.9.far_ref = f32[40,128]{1,0:T(8,128)S(1)} collective-permute-done((f32[40,128]{1,0:T(8,128)S(1)}, f32[40,128]{1,0:T(8,128)S(1)}, u32[]{:S(2)}, u32[]{:S(2)}) %collective-permute-start.9) | collective-permute-done | bytes 20512 | tf_op jit(solution)/shard_map/ppermute | solution.py:498
  34.4 0.0 copy-start.2
  34.4 0.0 copy-start.4
  34.4 9.5 %all_to_all.5.g_ref = f32[8,48,128]{2,1,0:T(8,128)S(1)} all-to-all(f32[8,48,128]{2,1,0:T(8,128)S(1)} %shard_map.65), channel_id=1, replica_groups=mesh['gx'=4,'gy'=8,'gz'=4] {'gy'}, dimensions={0} | all-to-all | bytes 393216 | tf_op jit(solution)/shard_map/all_to_all | solution.py:506
  43.9 0.0 copy-done.2
  43.9 0.0 copy-done.4
  43.9 2.1 %shard_map.66 = (f32[6,2,16,32]{3,2,1,0:T(8,128)}, bf16[6,512,128]{2,1,0:T(8,128)(2,1)}) custom-call(f32[8,48,128]{2,1,0:T(8,128)S(1)} %all_to_all.5.g_ref, bf16[512,144]{1,0:T(8,128)(2,1)S(1)} %copy-done.2, bf16[128,256]{1,0:T(8,128)(2,1)S(1)} %copy-done.4), custom_call_target="tpu_custom_call" | custom-call | flops 100000000 | bytes 1000000 | tf_op jit(solution)/shard_map/pallas_call | solution.py:508
  (3 shorter events, 0.1 us)
Async XLA Ops:
  0.6 1.0 %copy-start = (f32[2,16,32,128]{3,2,1,0:T(8,128)S(1)}, f32[2,16,32,128]{3,2,1,0:T(8,128)}, u32[]{:S(2)}) copy-start(f32[2,16,32,128]{3,2,1,0:T(8,128)} %own_ref.3) | copy-start | bytes 1572868
  1.7 13.8 %copy-start.1 = (f32[2,16,32,128]{3,2,1,0:T(8,128)S(1)}, f32[2,16,32,128]{3,2,1,0:T(8,128)}, u32[]{:S(2)}) copy-start(f32[2,16,32,128]{3,2,1,0:T(8,128)} %own_ref.3) | copy-start | bytes 1572868
  1.9 2.2 %copy-start.3 = (f32[2,3,2,32,16]{3,4,2,1,0:T(8,128)S(1)}, f32[2,3,2,32,16]{3,4,2,1,0:T(8,128)}, u32[]{:S(2)}) copy-start(f32[2,3,2,32,16]{3,4,2,1,0:T(8,128)} %param.9) | copy-start | bytes 73732
  1.9 4.9 %collective-permute-start = (f32[2,32,128]{2,1,0:T(8,128)S(1)}, f32[2,32,128]{2,1,0:T(8,128)S(1)}, u32[]{:S(2)}, u32[]{:S(2)}) collective-permute-start(f32[2,32,128]{2,1,0:T(8,128)S(1)} %shard_map.59), channel_id=1, source_target_pairs={{0,1},{1,2},{2,3},{3,0},{4,5},{5,6},{6,7},{7,4},{8,9},{9,10},{10,1... | collective-permute-start | bytes 98312 | tf_op jit(solution)/shard_map/ppermute | solution.py:461
  2.0 17.1 %collective-permute-start.2 = (f32[2,8,32,128]{3,2,1,0:T(8,128)S(1)}, f32[2,8,32,128]{3,2,1,0:T(8,128)S(1)}, u32[]{:S(2)}, u32[]{:S(2)}) collective-permute-start(f32[2,8,32,128]{3,2,1,0:T(8,128)S(1)} %get-tuple-element.41), channel_id=1, source_target_pairs={{0,32},{1,33},{2,34},{3,35},{4,36},{5,37},{6,38},{7,39},{8,40},{9,... | collective-permute-start | bytes 786440 | tf_op jit(solution)/shard_map/ppermute | solution.py:452
  6.8 8.7 %collective-permute-start.1 = (f32[2,17,8,128]{3,2,1,0:T(8,128)S(1)}, f32[2,17,8,128]{3,2,1,0:T(8,128)S(1)}, u32[]{:S(2)}, u32[]{:S(2)}) collective-permute-start(f32[2,17,8,128]{3,2,1,0:T(8,128)S(1)} %get-tuple-element.51), channel_id=1, source_target_pairs={{0,4},{1,5},{2,6},{3,7},{4,8},{5,9},{6,10},{7,11},{8,12},{9,13},{1... | collective-permute-start | bytes 417800 | tf_op jit(solution)/shard_map/ppermute | solution.py:452
  8.4 10.7 %collective-permute-start.4 = (f32[2,9,8,128]{3,2,1,0:T(8,128)S(1)}, f32[2,9,8,128]{3,2,1,0:T(8,128)S(1)}, u32[]{:S(2)}, u32[]{:S(2)}) collective-permute-start(f32[2,9,8,128]{3,2,1,0:T(8,128)S(1)} %get-tuple-element.50), channel_id=1, source_target_pairs={{0,36},{1,37},{2,38},{3,39},{4,40},{5,41},{6,42},{7,43},{8,44},{9,... | collective-permute-start | bytes 221192 | tf_op jit(solution)/shard_map/ppermute | solution.py:452
  11.2 6.4 %collective-permute-start.3 = (f32[2,32,128]{2,1,0:T(8,128)S(1)}, f32[2,32,128]{2,1,0:T(8,128)S(1)}, u32[]{:S(2)}, u32[]{:S(2)}) collective-permute-start(f32[2,32,128]{2,1,0:T(8,128)S(1)} %collective-permute-done.zr_ref), channel_id=1, source_target_pairs={{0,32},{1,33},{2,34},{3,35},{4,36},{5,37},{6,38},{7,39},{8,40},{9,... | collective-permute-start | bytes 98312 | tf_op jit(solution)/shard_map/ppermute | solution.py:452
  21.2 4.8 %collective-permute-start.5 = (f32[40,128]{1,0:T(8,128)S(1)}, f32[40,128]{1,0:T(8,128)S(1)}, u32[]{:S(2)}, u32[]{:S(2)}) collective-permute-start(f32[40,128]{1,0:T(8,128)S(1)} %shard_map.63.mine_ref), channel_id=1, source_target_pairs={{1,2},{3,0},{2,1},{0,3},{5,6},{7,4},{6,5},{4,7},{9,10},{11,8},{10,... | collective-permute-start | bytes 61448 | tf_op jit(solution)/shard_map/ppermute | solution.py:498
  21.3 4.7 %collective-permute-start.6 = (f32[40,128]{1,0:T(8,128)S(1)}, f32[40,128]{1,0:T(8,128)S(1)}, u32[]{:S(2)}, u32[]{:S(2)}) collective-permute-start(f32[40,128]{1,0:T(8,128)S(1)} %shard_map.63.mine_ref), channel_id=1, source_target_pairs={{0,1},{2,3},{1,0},{3,2},{4,5},{6,7},{5,4},{7,6},{8,9},{10,11},{9,8... | collective-permute-start | bytes 61448 | tf_op jit(solution)/shard_map/ppermute | solution.py:498
  26.0 4.1 %collective-permute-start.7 = (f32[40,128]{1,0:T(8,128)S(1)}, f32[40,128]{1,0:T(8,128)S(1)}, u32[]{:S(2)}, u32[]{:S(2)}) collective-permute-start(f32[40,128]{1,0:T(8,128)S(1)} %shard_map.64.own_ref), channel_id=1, source_target_pairs={{0,32},{64,96},{32,0},{96,64},{1,33},{65,97},{33,1},{97,65},{2,34}... | collective-permute-start | bytes 61448 | tf_op jit(solution)/shard_map/ppermute | solution.py:498
  26.6 5.0 %collective-permute-start.8 = (f32[40,128]{1,0:T(8,128)S(1)}, f32[40,128]{1,0:T(8,128)S(1)}, u32[]{:S(2)}, u32[]{:S(2)}) collective-permute-start(f32[40,128]{1,0:T(8,128)S(1)} %shard_map.64.own_ref), channel_id=1, source_target_pairs={{32,64},{96,0},{64,32},{0,96},{33,65},{97,1},{65,33},{1,97},{34,66... | collective-permute-start | bytes 61448 | tf_op jit(solution)/shard_map/ppermute | solution.py:498
  29.1 5.3 %collective-permute-start.9 = (f32[40,128]{1,0:T(8,128)S(1)}, f32[40,128]{1,0:T(8,128)S(1)}, u32[]{:S(2)}, u32[]{:S(2)}) collective-permute-start(f32[40,128]{1,0:T(8,128)S(1)} %shard_map.64.own_ref), channel_id=1, source_target_pairs={{0,64},{32,96},{64,0},{96,32},{1,65},{33,97},{65,1},{97,33},{2,66}... | collective-permute-start | bytes 61448 | tf_op jit(solution)/shard_map/ppermute | solution.py:498
  34.4 9.5 %copy-start.2 = (bf16[512,144]{1,0:T(8,128)(2,1)S(1)}, bf16[512,144]{1,0:T(8,128)(2,1)}, u32[]{:S(2)}) copy-start(bf16[512,144]{1,0:T(8,128)(2,1)} %constant.61.clone.wxy_ref) | copy-start | bytes 442372
  34.4 9.5 %copy-start.4 = (bf16[128,256]{1,0:T(8,128)(2,1)S(1)}, bf16[128,256]{1,0:T(8,128)(2,1)}, u32[]{:S(2)}) copy-start(bf16[128,256]{1,0:T(8,128)(2,1)} %constant.62.clone.wz_ref) | copy-start | bytes 196612

commit v6 on v5

--- a/solution.py
+++ b/solution.py
@@ -38,14 +38,13 @@
         out_ref[h] = packed
 
 
-def slab_kernel(img_ref, x_ref, y_ref, xy_ref):
+def slab_kernel(after_ref, img_ref, x_ref, y_ref, xy_ref):
     for h in range(2):
         for t in range(16):
             y_ref[h, t] = img_ref[h, t, 24:32]
             if t >= 8:
                 x_ref[h, t - 8] = img_ref[h, t]
                 xy_ref[h, t - 8] = img_ref[h, t, 24:32]
-        y_ref[h, 16] = jnp.zeros((8, 128), f32)
         xy_ref[h, 8] = jnp.zeros((8, 128), f32)
 
 
@@ -155,11 +154,11 @@
     return jnp.concatenate([top, w[8:32]], axis=0)
 
 
-def force_kernel(upper, own_ref, zr_ref, yr_ref, *refs):
+def force_kernel(upper, own_ref, zr_ref, yr_ref, yzr_ref, *refs):
     if upper:
         base_ref, *refs = refs
     else:
-        xr_ref, xzr_ref, xyr_ref, base_ref, *refs = refs
+        xr_ref, xyr_ref, xzr_ref, base_ref, *refs = refs
     wxy_ref, wz_ref, xsum_ref, zsum_ref, out_ref, a_ref, h_ref, v_ref, dz_ref, xs_ref, hs_ref, fh_ref, fl_ref = refs
     first = 8 if upper else 0
     ex, ey, ez = (jnp.where(at == 0, 0.0, 1.0) for at in coords())
@@ -179,7 +178,7 @@
                 a_ref[h, n, 8:40] = xr_ref[h, n]
                 a_ref[h, n, 0:8] = xyr_ref[h, n]
         h_ref[h, 0, 8:40] = zr_ref[h]
-        h_ref[h, 0, 0:8] = yr_ref[h, 16]
+        h_ref[h, 0, 0:8] = yzr_ref[h]
         if not upper:
             h_ref[h, 1, 8:40] = xzr_ref[h]
             h_ref[h, 1, 0:8] = xyr_ref[h, 8]
@@ -328,7 +327,7 @@
     out_ref[...] = total + jnp.where(live & (spot >= 16), high, 0.0)
 
 
-def across_kernel(own_ref, one_ref, two_ref, far_ref, out_ref):
+def across_kernel(own_ref, far_ref, one_ref, two_ref, out_ref):
     odd = (lax.axis_index("gx") & 1) == 1
     tiles = lambda ref: [ref[8 * p : 8 * p + 8] for p in range(5)]
     own, one, two, far = tiles(own_ref), tiles(one_ref), tiles(two_ref), tiles(far_ref)
@@ -454,11 +453,14 @@
     (pack,) = call(pack_kernel, [((2, 32, 128), f32)], [VMEM], bytes_accessed=6 * 10**5)(images)
     to_x, to_y, to_xy = call(
         slab_kernel,
-        [((2, 8, 32, 128), f32), ((2, 17, 8, 128), f32), ((2, 9, 8, 128), f32)],
-        [VMEM],
+        [((2, 8, 32, 128), f32), ((2, 16, 8, 128), f32), ((2, 9, 8, 128), f32)],
+        [pl.BlockSpec(memory_space=pl.ANY), VMEM],
         bytes_accessed=10**6,
-    )(images)
+    )(pack, images)
     zr = lax.ppermute(pack, "gz", [(n, (n + 1) % nk) for n in range(nk)])
+    yr = send(to_y, 0, 1, 0)
+    xr = send(to_x, 1, 0, 0)
+
     velocity = jnp.swapaxes(velocity, 3, 4).reshape(6, 2, 16, 32)
     vel, wxy, wzs, xsum, zsum = call(
         prep_kernel,
@@ -468,9 +470,9 @@
         bytes_accessed=10**6,
     )(velocity)
     zr, vel = lax.optimization_barrier((zr, vel))
-    xr = send(to_x, 1, 0, 0)
-    yr = send(to_y.at[:, 16].set(zr[:, 24:]), 0, 1, 0)
-    xyr = send(to_xy.at[:, 8].set(zr[:, 24:]), 1, 1, 0)
+    top = zr[:, 24:]
+    yzr = send(top, 0, 1, 0)
+    xyr = send(to_xy.at[:, 8].set(top), 1, 1, 0)
     xzr = send(zr, 1, 0, 0)
 
     def forces(upper, *arrays):
@@ -492,8 +494,8 @@
             bytes_accessed=10**6,
         )(*arrays, wxy, wzs, xsum, zsum)[0]
 
-    part = forces(True, images, zr, yr, vel)
-    part = forces(False, images, zr, yr, xr, xzr, xyr, part)
+    part = forces(True, images, zr, yr, yzr, vel)
+    part = forces(False, images, zr, yr, yzr, xr, xyr, xzr, part)
 
     swap = lambda v, axis, couples: lax.ppermute(v, axis, couples + [(b, a) for a, b in couples])
     chip = swap(part, "gz", [(1, 2), (3, 0)])
@@ -502,7 +504,7 @@
     far = swap(own, "gx", [(0, 2), (1, 3)])
     one = swap(own, "gx", [(0, 1), (2, 3)])
     two = swap(own, "gx", [(1, 2), (3, 0)])
-    (copies,) = call(across_kernel, [((8, 48, 128), f32)], [VMEM] * 4)(own, one, two, far)
+    (copies,) = call(across_kernel, [((8, 48, 128), f32)], [VMEM] * 4)(own, far, one, two)
     everything = lax.all_to_all(copies, "gy", 0, 0, tiled=True)
 
     nv, field = call(

time: 46.2 us -> 45.8 us (level)
  waiting for transfers between devices: 12.5 us -> 8.9 us
  starting transfers between devices: 15.2 us -> 17.6 us
    ppermute x1, waiting for transfers between devices: 2.26 us -> 0.76 us  [shards(): zr = lax.ppermute(pack, 'gz', [(n, (n + 1) % nk) for n in range(nk)])]
    ppermute x4 -> x5, starting transfers between devices: 8.44 us -> 9.9 us  [send(): return lax.ppermute(v, AXES, pairs(sizes, di, dj, dk))]
    ppermute x4 -> x5, waiting for transfers between devices: 3.82 us -> 2.61 us  [send(): return lax.ppermute(v, AXES, pairs(sizes, di, dj, dk))]
    ppermute x5, starting transfers between devices: 6.73 us -> 7.67 us  [shards(): lax.ppermute(v, axis, couples + [(b, a) for a, b in couples])]
    ppermute x5, waiting for transfers between devices: 6.39 us -> 5.53 us  [shards(): lax.ppermute(v, axis, couples + [(b, a) for a, b in couples])]
  transfers between devices with their start and end apart: 10 -> 11, of which waited for: 6 -> 7; matrix products, arithmetic and copies ran while one was open for 0% -> 0% of each run, Pallas kernels for 6% -> 6%
where the time goes in v6:
time: 45.8 us; the launch traced here: 45.2 us
  starting transfers between devices  17.6 us (38%)
  blocking collectives  9.87 us (22%)
  waiting for transfers between devices  8.9 us (19%)
  Pallas kernels  7.06 us (15%)
  local copies, waits for them, and re-layouts  1.06 us (2%)
  between operations  0.71 us (2%)
    ppermute x5, starting transfers between devices, send(): return lax.ppermute(v, AXES, pairs(sizes, di, dj, dk))  9.9 us
    all_to_all x1, blocking collectives, shards(): everything = lax.all_to_all(copies, 'gy', 0, 0, tiled=True)  9.87 us
    ppermute x5, starting transfers between devices, shards(): lax.ppermute(v, axis, couples + [(b, a) for a, b in couples])  7.67 us
    ppermute x5, waiting for transfers between devices, shards(): lax.ppermute(v, axis, couples + [(b, a) for a, b in couples])  5.53 us
    pallas_call x2, Pallas kernels, forces(): call(functools.partial(force_kernel, upper), [((40, 128), f32)], [VMEM] *...  4.17 us
    ppermute x5, waiting for transfers between devices, send(): return lax.ppermute(v, AXES, pairs(sizes, di, dj, dk))  2.61 us
    pallas_call x1, Pallas kernels, shards(): call(field_kernel, [((6, 2, 16, 32), f32), ((6, 512, 128), bf16)], [VMEM]...  2.1 us
    unnamed x10, local copies, waits for them, and re-layouts  1.06 us
  transfers between devices with their start and end apart: 11, of which 7 were waited for; matrix products, arithmetic and copies ran while one was open for 0% of the time, Pallas kernels for 6%

profile of v6, /device:TPU:0, one launch (start us, length us, event | category | flops | bytes accessed | tf_op | source)
XLA Modules:
  0.0 45.2 jit_solution(12370058350123114181)
XLA Ops:
  0.6 0.0 copy-start
  0.6 1.0 %copy-done = f32[2,16,32,128]{3,2,1,0:T(8,128)S(1)} copy-done((f32[2,16,32,128]{3,2,1,0:T(8,128)S(1)}, f32[2,16,32,128]{3,2,1,0:T(8,128)}, u32[]{:S(2)}) %copy-start) | copy-done | bytes 524312
  1.7 0.0 copy-start.1
  1.7 0.2 shard_map.59.after_ref
  1.9 0.0 copy-start.3
  1.9 0.1 collective-permute-start
  2.0 1.6 %collective-permute-start.1 = (f32[2,16,8,128]{3,2,1,0:T(8,128)S(1)}, f32[2,16,8,128]{3,2,1,0:T(8,128)S(1)}, u32[]{:S(2)}, u32[]{:S(2)}) collective-permute-start(f32[2,16,8,128]{3,2,1,0:T(8,128)S(1)} %get-tuple-element.28), channel_id=1, source_target_pairs={{0,4},{1,5},{2,6},{3,7},{4,8},{5,9},{6,10},{7,11},{8,12},{9,13},{1... | collective-permute-start | bytes 393224 | tf_op jit(solution)/shard_map/ppermute | solution.py:451
  3.6 1.9 %collective-permute-start.3 = (f32[2,8,32,128]{3,2,1,0:T(8,128)S(1)}, f32[2,8,32,128]{3,2,1,0:T(8,128)S(1)}, u32[]{:S(2)}, u32[]{:S(2)}) collective-permute-start(f32[2,8,32,128]{3,2,1,0:T(8,128)S(1)} %get-tuple-element.29), channel_id=1, source_target_pairs={{0,32},{1,33},{2,34},{3,35},{4,36},{5,37},{6,38},{7,39},{8,40},{9,... | collective-permute-start | bytes 786440 | tf_op jit(solution)/shard_map/ppermute | solution.py:451
  5.6 0.0 copy-done.3
  5.6 0.5 %shard_map.60 = (f32[16,128]{1,0:T(8,128)S(1)}, bf16[80,512]{1,0:T(8,128)(2,1)S(1)}, bf16[128,256]{1,0:T(8,128)(2,1)S(1)}, bf16[256,128]{1,0:T(8,128)(2,1)S(1)}, f32[256,128]{1,0:T(8,128)S(1)}) custom-call(f32[6,2,16,32]{3,2,1,0:T(8,128)S(1)} %bitcast.11), custom_call_target="tpu_custom_call" | custom-call | bytes 1000000 | tf_op jit(solution)/shard_map/pallas_call | solution.py:465
  6.0 0.8 %collective-permute-done.zr_ref = f32[2,32,128]{2,1,0:T(8,128)S(1)} collective-permute-done((f32[2,32,128]{2,1,0:T(8,128)S(1)}, f32[2,32,128]{2,1,0:T(8,128)S(1)}, u32[]{:S(2)}, u32[]{:S(2)}) %collective-permute-start) | collective-permute-done | bytes 32800 | tf_op jit(solution)/shard_map/ppermute | solution.py:460
  6.8 2.9 %collective-permute-start.4 = (f32[2,9,8,128]{3,2,1,0:T(8,128)S(1)}, f32[2,9,8,128]{3,2,1,0:T(8,128)S(1)}, u32[]{:S(2)}, u32[]{:S(2)}) collective-permute-start(f32[2,9,8,128]{3,2,1,0:T(8,128)S(1)} %bitcast_dynamic-update-slice_fusion), channel_id=1, source_target_pairs={{0,36},{1,37},{2,38},{3,39},{4,40},{5,41},{6,42},{7,43},{8,44},{9,... | collective-permute-start | bytes 221192 | tf_op jit(solution)/shard_map/ppermute | solution.py:451
  9.7 1.5 %collective-permute-start.2 = (f32[2,8,128]{2,1,0:T(8,128)S(1)}, f32[2,8,128]{2,1,0:T(8,128)S(1)}, u32[]{:S(2)}, u32[]{:S(2)}) collective-permute-start(f32[2,8,128]{2,1,0:T(8,128)S(1)} %slice.28), channel_id=1, source_target_pairs={{0,4},{1,5},{2,6},{3,7},{4,8},{5,9},{6,10},{7,11},{8,12},{9,13},{1... | collective-permute-start | bytes 24584 | tf_op jit(solution)/shard_map/ppermute | solution.py:451
  11.2 1.9 %collective-permute-start.5 = (f32[2,32,128]{2,1,0:T(8,128)S(1)}, f32[2,32,128]{2,1,0:T(8,128)S(1)}, u32[]{:S(2)}, u32[]{:S(2)}) collective-permute-start(f32[2,32,128]{2,1,0:T(8,128)S(1)} %collective-permute-done.zr_ref), channel_id=1, source_target_pairs={{0,32},{1,33},{2,34},{3,35},{4,36},{5,37},{6,38},{7,39},{8,40},{9,... | collective-permute-start | bytes 98312 | tf_op jit(solution)/shard_map/ppermute | solution.py:451
  13.1 2.4 %collective-permute-done.2.yzr_ref = f32[2,8,128]{2,1,0:T(8,128)S(1)} collective-permute-done((f32[2,8,128]{2,1,0:T(8,128)S(1)}, f32[2,8,128]{2,1,0:T(8,128)S(1)}, u32[]{:S(2)}, u32[]{:S(2)}) %collective-permute-start.2) | collective-permute-done | bytes 8224 | tf_op jit(solution)/shard_map/ppermute | solution.py:451
  15.5 0.0 collective-permute-done.1.yr_ref
  15.5 0.0 copy-done.1
  15.5 2.1 %shard_map.62.refs_3_ = f32[40,128]{1,0:T(8,128)S(1)} custom-call(f32[2,16,32,128]{3,2,1,0:T(8,128)S(1)} %copy-done.1, f32[2,32,128]{2,1,0:T(8,128)S(1)} %collective-permute-done.zr_ref, f32[2,16,8,128]{3,2,1,0:T(8,128)S(1)} %collective-permute-done.1.yr_ref, f32[2,8,128]{2,1,0:T(8,128)S(1)} %collective-permute-done.2.yzr_ref, ...), custom_call_target="tpu_custom_call" | custom-call | flops 500000000 | bytes 1000000 | tf_op jit(solution)/shard_map/pallas_call | solution.py:479
  17.6 0.2 collective-permute-done.5.refs_2_
  17.9 0.0 collective-permute-done.4.refs_1_
  17.9 0.0 collective-permute-done.3.refs_0_
  17.9 2.1 %shard_map.63.mine_ref = f32[40,128]{1,0:T(8,128)S(1)} custom-call(f32[2,16,32,128]{3,2,1,0:T(8,128)S(1)} %copy-done.1, f32[2,32,128]{2,1,0:T(8,128)S(1)} %collective-permute-done.zr_ref, f32[2,16,8,128]{3,2,1,0:T(8,128)S(1)} %collective-permute-done.1.yr_ref, f32[2,8,128]{2,1,0:T(8,128)S(1)} %collective-permute-done.2.yzr_ref, ...), custom_call_target="tpu_custom_call" | custom-call | flops 500000000 | bytes 1000000 | tf_op jit(solution)/shard_map/pallas_call | solution.py:479
  19.9 0.5 %collective-permute-start.6 = (f32[40,128]{1,0:T(8,128)S(1)}, f32[40,128]{1,0:T(8,128)S(1)}, u32[]{:S(2)}, u32[]{:S(2)}) collective-permute-start(f32[40,128]{1,0:T(8,128)S(1)} %shard_map.63.mine_ref), channel_id=1, source_target_pairs={{1,2},{3,0},{2,1},{0,3},{5,6},{7,4},{6,5},{4,7},{9,10},{11,8},{10,... | collective-permute-start | bytes 61448 | tf_op jit(solution)/shard_map/ppermute | solution.py:500
  20.4 2.7 %collective-permute-start.7 = (f32[40,128]{1,0:T(8,128)S(1)}, f32[40,128]{1,0:T(8,128)S(1)}, u32[]{:S(2)}, u32[]{:S(2)}) collective-permute-start(f32[40,128]{1,0:T(8,128)S(1)} %shard_map.63.mine_ref), channel_id=1, source_target_pairs={{0,1},{2,3},{1,0},{3,2},{4,5},{6,7},{5,4},{7,6},{8,9},{10,11},{9,8... | collective-permute-start | bytes 61448 | tf_op jit(solution)/shard_map/ppermute | solution.py:500
  23.1 1.6 %collective-permute-done.6.chip_ref = f32[40,128]{1,0:T(8,128)S(1)} collective-permute-done((f32[40,128]{1,0:T(8,128)S(1)}, f32[40,128]{1,0:T(8,128)S(1)}, u32[]{:S(2)}, u32[]{:S(2)}) %collective-permute-start.6) | collective-permute-done | bytes 20512 | tf_op jit(solution)/shard_map/ppermute | solution.py:500
  24.7 0.0 collective-permute-done.7.core_ref
  24.7 0.1 shard_map.64.own_ref
  24.8 3.4 %collective-permute-start.8 = (f32[40,128]{1,0:T(8,128)S(1)}, f32[40,128]{1,0:T(8,128)S(1)}, u32[]{:S(2)}, u32[]{:S(2)}) collective-permute-start(f32[40,128]{1,0:T(8,128)S(1)} %shard_map.64.own_ref), channel_id=1, source_target_pairs={{0,64},{32,96},{64,0},{96,32},{1,65},{33,97},{65,1},{97,33},{2,66}... | collective-permute-start | bytes 61448 | tf_op jit(solution)/shard_map/ppermute | solution.py:500
  28.2 0.0 collective-permute-start.9
  28.2 1.1 %collective-permute-start.10 = (f32[40,128]{1,0:T(8,128)S(1)}, f32[40,128]{1,0:T(8,128)S(1)}, u32[]{:S(2)}, u32[]{:S(2)}) collective-permute-start(f32[40,128]{1,0:T(8,128)S(1)} %shard_map.64.own_ref), channel_id=1, source_target_pairs={{32,64},{96,0},{64,32},{0,96},{33,65},{97,1},{65,33},{1,97},{34,66... | collective-permute-start | bytes 61448 | tf_op jit(solution)/shard_map/ppermute | solution.py:500
  29.3 0.8 %collective-permute-done.8.far_ref = f32[40,128]{1,0:T(8,128)S(1)} collective-permute-done((f32[40,128]{1,0:T(8,128)S(1)}, f32[40,128]{1,0:T(8,128)S(1)}, u32[]{:S(2)}, u32[]{:S(2)}) %collective-permute-start.8) | collective-permute-done | bytes 20512 | tf_op jit(solution)/shard_map/ppermute | solution.py:500
  30.1 1.8 %collective-permute-done.9.one_ref = f32[40,128]{1,0:T(8,128)S(1)} collective-permute-done((f32[40,128]{1,0:T(8,128)S(1)}, f32[40,128]{1,0:T(8,128)S(1)}, u32[]{:S(2)}, u32[]{:S(2)}) %collective-permute-start.9) | collective-permute-done | bytes 20512 | tf_op jit(solution)/shard_map/ppermute | solution.py:500
  32.0 1.2 %collective-permute-done.10.two_ref = f32[40,128]{1,0:T(8,128)S(1)} collective-permute-done((f32[40,128]{1,0:T(8,128)S(1)}, f32[40,128]{1,0:T(8,128)S(1)}, u32[]{:S(2)}, u32[]{:S(2)}) %collective-permute-start.10) | collective-permute-done | bytes 20512 | tf_op jit(solution)/shard_map/ppermute | solution.py:500
  33.2 0.0 copy-start.2
  33.2 0.0 copy-start.4
  33.3 9.9 %all_to_all.5.g_ref = f32[8,48,128]{2,1,0:T(8,128)S(1)} all-to-all(f32[8,48,128]{2,1,0:T(8,128)S(1)} %shard_map.65), channel_id=1, replica_groups=mesh['gx'=4,'gy'=8,'gz'=4] {'gy'}, dimensions={0} | all-to-all | bytes 393216 | tf_op jit(solution)/shard_map/all_to_all | solution.py:508
  43.1 0.0 copy-done.2
  43.1 0.0 copy-done.4
  43.1 2.1 %shard_map.66 = (f32[6,2,16,32]{3,2,1,0:T(8,128)}, bf16[6,512,128]{2,1,0:T(8,128)(2,1)}) custom-call(f32[8,48,128]{2,1,0:T(8,128)S(1)} %all_to_all.5.g_ref, bf16[512,144]{1,0:T(8,128)(2,1)S(1)} %copy-done.2, bf16[128,256]{1,0:T(8,128)(2,1)S(1)} %copy-done.4), custom_call_target="tpu_custom_call" | custom-call | flops 100000000 | bytes 1000000 | tf_op jit(solution)/shard_map/pallas_call | solution.py:510
  (4 shorter events, 0.1 us)
Async XLA Ops:
  0.6 1.0 %copy-start = (f32[2,16,32,128]{3,2,1,0:T(8,128)S(1)}, f32[2,16,32,128]{3,2,1,0:T(8,128)}, u32[]{:S(2)}) copy-start(f32[2,16,32,128]{3,2,1,0:T(8,128)} %own_ref.3) | copy-start | bytes 1572868
  1.7 13.8 %copy-start.1 = (f32[2,16,32,128]{3,2,1,0:T(8,128)S(1)}, f32[2,16,32,128]{3,2,1,0:T(8,128)}, u32[]{:S(2)}) copy-start(f32[2,16,32,128]{3,2,1,0:T(8,128)} %own_ref.3) | copy-start | bytes 1572868
  1.9 3.7 %copy-start.3 = (f32[2,3,2,32,16]{3,4,2,1,0:T(8,128)S(1)}, f32[2,3,2,32,16]{3,4,2,1,0:T(8,128)}, u32[]{:S(2)}) copy-start(f32[2,3,2,32,16]{3,4,2,1,0:T(8,128)} %param.7) | copy-start | bytes 73732
  1.9 4.9 %collective-permute-start = (f32[2,32,128]{2,1,0:T(8,128)S(1)}, f32[2,32,128]{2,1,0:T(8,128)S(1)}, u32[]{:S(2)}, u32[]{:S(2)}) collective-permute-start(f32[2,32,128]{2,1,0:T(8,128)S(1)} %shard_map.59.after_ref), channel_id=1, source_target_pairs={{0,1},{1,2},{2,3},{3,0},{4,5},{5,6},{6,7},{7,4},{8,9},{9,10},{10,1... | collective-permute-start | bytes 98312 | tf_op jit(solution)/shard_map/ppermute | solution.py:460
  2.0 13.5 %collective-permute-start.1 = (f32[2,16,8,128]{3,2,1,0:T(8,128)S(1)}, f32[2,16,8,128]{3,2,1,0:T(8,128)S(1)}, u32[]{:S(2)}, u32[]{:S(2)}) collective-permute-start(f32[2,16,8,128]{3,2,1,0:T(8,128)S(1)} %get-tuple-element.28), channel_id=1, source_target_pairs={{0,4},{1,5},{2,6},{3,7},{4,8},{5,9},{6,10},{7,11},{8,12},{9,13},{1... | collective-permute-start | bytes 393224 | tf_op jit(solution)/shard_map/ppermute | solution.py:451
  3.6 14.2 %collective-permute-start.3 = (f32[2,8,32,128]{3,2,1,0:T(8,128)S(1)}, f32[2,8,32,128]{3,2,1,0:T(8,128)S(1)}, u32[]{:S(2)}, u32[]{:S(2)}) collective-permute-start(f32[2,8,32,128]{3,2,1,0:T(8,128)S(1)} %get-tuple-element.29), channel_id=1, source_target_pairs={{0,32},{1,33},{2,34},{3,35},{4,36},{5,37},{6,38},{7,39},{8,40},{9,... | collective-permute-start | bytes 786440 | tf_op jit(solution)/shard_map/ppermute | solution.py:451
  6.8 11.1 %collective-permute-start.4 = (f32[2,9,8,128]{3,2,1,0:T(8,128)S(1)}, f32[2,9,8,128]{3,2,1,0:T(8,128)S(1)}, u32[]{:S(2)}, u32[]{:S(2)}) collective-permute-start(f32[2,9,8,128]{3,2,1,0:T(8,128)S(1)} %bitcast_dynamic-update-slice_fusion), channel_id=1, source_target_pairs={{0,36},{1,37},{2,38},{3,39},{4,40},{5,41},{6,42},{7,43},{8,44},{9,... | collective-permute-start | bytes 221192 | tf_op jit(solution)/shard_map/ppermute | solution.py:451
  9.7 5.8 %collective-permute-start.2 = (f32[2,8,128]{2,1,0:T(8,128)S(1)}, f32[2,8,128]{2,1,0:T(8,128)S(1)}, u32[]{:S(2)}, u32[]{:S(2)}) collective-permute-start(f32[2,8,128]{2,1,0:T(8,128)S(1)} %slice.28), channel_id=1, source_target_pairs={{0,4},{1,5},{2,6},{3,7},{4,8},{5,9},{6,10},{7,11},{8,12},{9,13},{1... | collective-permute-start | bytes 24584 | tf_op jit(solution)/shard_map/ppermute | solution.py:451
  11.2 6.6 %collective-permute-start.5 = (f32[2,32,128]{2,1,0:T(8,128)S(1)}, f32[2,32,128]{2,1,0:T(8,128)S(1)}, u32[]{:S(2)}, u32[]{:S(2)}) collective-permute-start(f32[2,32,128]{2,1,0:T(8,128)S(1)} %collective-permute-done.zr_ref), channel_id=1, source_target_pairs={{0,32},{1,33},{2,34},{3,35},{4,36},{5,37},{6,38},{7,39},{8,40},{9,... | collective-permute-start | bytes 98312 | tf_op jit(solution)/shard_map/ppermute | solution.py:451
  19.9 4.8 %collective-permute-start.6 = (f32[40,128]{1,0:T(8,128)S(1)}, f32[40,128]{1,0:T(8,128)S(1)}, u32[]{:S(2)}, u32[]{:S(2)}) collective-permute-start(f32[40,128]{1,0:T(8,128)S(1)} %shard_map.63.mine_ref), channel_id=1, source_target_pairs={{1,2},{3,0},{2,1},{0,3},{5,6},{7,4},{6,5},{4,7},{9,10},{11,8},{10,... | collective-permute-start | bytes 61448 | tf_op jit(solution)/shard_map/ppermute | solution.py:500
  20.4 4.3 %collective-permute-start.7 = (f32[40,128]{1,0:T(8,128)S(1)}, f32[40,128]{1,0:T(8,128)S(1)}, u32[]{:S(2)}, u32[]{:S(2)}) collective-permute-start(f32[40,128]{1,0:T(8,128)S(1)} %shard_map.63.mine_ref), channel_id=1, source_target_pairs={{0,1},{2,3},{1,0},{3,2},{4,5},{6,7},{5,4},{7,6},{8,9},{10,11},{9,8... | collective-permute-start | bytes 61448 | tf_op jit(solution)/shard_map/ppermute | solution.py:500
  24.8 5.3 %collective-permute-start.8 = (f32[40,128]{1,0:T(8,128)S(1)}, f32[40,128]{1,0:T(8,128)S(1)}, u32[]{:S(2)}, u32[]{:S(2)}) collective-permute-start(f32[40,128]{1,0:T(8,128)S(1)} %shard_map.64.own_ref), channel_id=1, source_target_pairs={{0,64},{32,96},{64,0},{96,32},{1,65},{33,97},{65,1},{97,33},{2,66}... | collective-permute-start | bytes 61448 | tf_op jit(solution)/shard_map/ppermute | solution.py:500
  28.2 3.8 %collective-permute-start.9 = (f32[40,128]{1,0:T(8,128)S(1)}, f32[40,128]{1,0:T(8,128)S(1)}, u32[]{:S(2)}, u32[]{:S(2)}) collective-permute-start(f32[40,128]{1,0:T(8,128)S(1)} %shard_map.64.own_ref), channel_id=1, source_target_pairs={{0,32},{64,96},{32,0},{96,64},{1,33},{65,97},{33,1},{97,65},{2,34}... | collective-permute-start | bytes 61448 | tf_op jit(solution)/shard_map/ppermute | solution.py:500
  28.2 5.0 %collective-permute-start.10 = (f32[40,128]{1,0:T(8,128)S(1)}, f32[40,128]{1,0:T(8,128)S(1)}, u32[]{:S(2)}, u32[]{:S(2)}) collective-permute-start(f32[40,128]{1,0:T(8,128)S(1)} %shard_map.64.own_ref), channel_id=1, source_target_pairs={{32,64},{96,0},{64,32},{0,96},{33,65},{97,1},{65,33},{1,97},{34,66... | collective-permute-start | bytes 61448 | tf_op jit(solution)/shard_map/ppermute | solution.py:500
  33.2 9.9 %copy-start.2 = (bf16[512,144]{1,0:T(8,128)(2,1)S(1)}, bf16[512,144]{1,0:T(8,128)(2,1)}, u32[]{:S(2)}) copy-start(bf16[512,144]{1,0:T(8,128)(2,1)} %constant.33.clone.wxy_ref) | copy-start | bytes 442372
  33.2 9.9 %copy-start.4 = (bf16[128,256]{1,0:T(8,128)(2,1)S(1)}, bf16[128,256]{1,0:T(8,128)(2,1)}, u32[]{:S(2)}) copy-start(bf16[128,256]{1,0:T(8,128)(2,1)} %constant.34.clone.wz_ref) | copy-start | bytes 196612

commit v7 on v6

--- a/solution.py
+++ b/solution.py
@@ -38,14 +38,12 @@
         out_ref[h] = packed
 
 
-def slab_kernel(after_ref, img_ref, x_ref, y_ref, xy_ref):
+def slab_kernel(after_ref, img_ref, x_ref, y_ref):
     for h in range(2):
         for t in range(16):
             y_ref[h, t] = img_ref[h, t, 24:32]
             if t >= 8:
                 x_ref[h, t - 8] = img_ref[h, t]
-                xy_ref[h, t - 8] = img_ref[h, t, 24:32]
-        xy_ref[h, 8] = jnp.zeros((8, 128), f32)
 
 
 def spline_at(t):
@@ -154,7 +152,7 @@
     return jnp.concatenate([top, w[8:32]], axis=0)
 
 
-def force_kernel(upper, own_ref, zr_ref, yr_ref, yzr_ref, *refs):
+def force_kernel(upper, own_ref, zr_ref, yr_ref, *refs):
     if upper:
         base_ref, *refs = refs
     else:
@@ -177,11 +175,9 @@
             else:
                 a_ref[h, n, 8:40] = xr_ref[h, n]
                 a_ref[h, n, 0:8] = xyr_ref[h, n]
-        h_ref[h, 0, 8:40] = zr_ref[h]
-        h_ref[h, 0, 0:8] = yzr_ref[h]
+        h_ref[h, 0] = zr_ref[h]
         if not upper:
-            h_ref[h, 1, 8:40] = xzr_ref[h]
-            h_ref[h, 1, 0:8] = xyr_ref[h, 8]
+            h_ref[h, 1] = xzr_ref[h]
 
     plus_z = jnp.where(lane40 == 127, ez, 1.0)
     minus_z = jnp.where(lane40 == 0, ez, 1.0)
@@ -451,9 +447,9 @@
         return lax.ppermute(v, AXES, pairs(sizes, di, dj, dk))
 
     (pack,) = call(pack_kernel, [((2, 32, 128), f32)], [VMEM], bytes_accessed=6 * 10**5)(images)
-    to_x, to_y, to_xy = call(
+    to_x, to_y = call(
         slab_kernel,
-        [((2, 8, 32, 128), f32), ((2, 16, 8, 128), f32), ((2, 9, 8, 128), f32)],
+        [((2, 8, 32, 128), f32), ((2, 16, 8, 128), f32)],
         [pl.BlockSpec(memory_space=pl.ANY), VMEM],
         bytes_accessed=10**6,
     )(pack, images)
@@ -470,10 +466,11 @@
         bytes_accessed=10**6,
     )(velocity)
     zr, vel = lax.optimization_barrier((zr, vel))
-    top = zr[:, 24:]
-    yzr = send(top, 0, 1, 0)
-    xyr = send(to_xy.at[:, 8].set(top), 1, 1, 0)
-    xzr = send(zr, 1, 0, 0)
+    zr, vel = lax.optimization_barrier((zr, vel))
+    yzr = send(zr[:, 24:], 0, 1, 0)
+    xyr = send(yr[:, 8:], 1, 0, 0)
+    below_z = jnp.concatenate([yzr, zr], axis=1)
+    xzr = send(below_z, 1, 0, 0)
 
     def forces(upper, *arrays):
         return call(
@@ -494,8 +491,8 @@
             bytes_accessed=10**6,
         )(*arrays, wxy, wzs, xsum, zsum)[0]
 
-    part = forces(True, images, zr, yr, yzr, vel)
-    part = forces(False, images, zr, yr, yzr, xr, xyr, xzr, part)
+    part = forces(True, images, below_z, yr, vel)
+    part = forces(False, images, below_z, yr, xr, xyr, xzr, part)
 
     swap = lambda v, axis, couples: lax.ppermute(v, axis, couples + [(b, a) for a, b in couples])
     chip = swap(part, "gz", [(1, 2), (3, 0)])

time: 45.8 us -> 48.9 us (1.068)
  waiting for transfers between devices: 8.9 us -> 13.6 us
  starting transfers between devices: 17.6 us -> 15.4 us
  blocking collectives: 9.87 us -> 10.8 us
    ppermute x5, waiting for transfers between devices: 2.61 us -> 4.71 us  [send(): return lax.ppermute(v, AXES, pairs(sizes, di, dj, dk))]
    ppermute x1, waiting for transfers between devices: 0.76 us -> 2.69 us  [shards(): zr = lax.ppermute(pack, 'gz', [(n, (n + 1) % nk) for n in range(nk)])]
    ppermute x5, starting transfers between devices: 7.67 us -> 6.25 us  [shards(): lax.ppermute(v, axis, couples + [(b, a) for a, b in couples])]
    all_to_all x1, blocking collectives: 9.87 us -> 10.8 us  [shards(): everything = lax.all_to_all(copies, 'gy', 0, 0, tiled=True)]
    ppermute x5, starting transfers between devices: 9.9 us -> 9.12 us  [send(): return lax.ppermute(v, AXES, pairs(sizes, di, dj, dk))]
    ppermute x5, waiting for transfers between devices: 5.53 us -> 6.18 us  [shards(): lax.ppermute(v, axis, couples + [(b, a) for a, b in couples])]
    unnamed x10 -> x11, local copies, waits for them, and re-layouts: 1.06 us -> 1.06 us
  transfers between devices with their start and end apart: 11 -> 11, of which waited for: 7 -> 6; matrix products, arithmetic and copies ran while one was open for 0% -> 0% of each run, Pallas kernels for 6% -> 5%
where the time goes in v7:
time: 48.9 us; the launch traced here: 48.7 us
  starting transfers between devices  15.4 us (31%)
  waiting for transfers between devices  13.6 us (28%)
  blocking collectives  10.8 us (22%)
  Pallas kernels  7.07 us (14%)
  local copies, waits for them, and re-layouts  1.07 us (2%)
  between operations  0.72 us (1%)
    all_to_all x1, blocking collectives, shards(): everything = lax.all_to_all(copies, 'gy', 0, 0, tiled=True)  10.8 us
    ppermute x5, starting transfers between devices, send(): return lax.ppermute(v, AXES, pairs(sizes, di, dj, dk))  9.12 us
    ppermute x5, starting transfers between devices, shards(): lax.ppermute(v, axis, couples + [(b, a) for a, b in couples])  6.25 us
    ppermute x5, waiting for transfers between devices, shards(): lax.ppermute(v, axis, couples + [(b, a) for a, b in couples])  6.18 us
    ppermute x5, waiting for transfers between devices, send(): return lax.ppermute(v, AXES, pairs(sizes, di, dj, dk))  4.71 us
    pallas_call x2, Pallas kernels, forces(): call(functools.partial(force_kernel, upper), [((40, 128), f32)], [VMEM] *...  4.19 us
    ppermute x1, waiting for transfers between devices, shards(): zr = lax.ppermute(pack, 'gz', [(n, (n + 1) % nk) for n in range(nk)])  2.69 us
    pallas_call x1, Pallas kernels, shards(): call(field_kernel, [((6, 2, 16, 32), f32), ((6, 512, 128), bf16)], [VMEM]...  2.1 us
  transfers between devices with their start and end apart: 11, of which 6 were waited for; matrix products, arithmetic and copies ran while one was open for 0% of the time, Pallas kernels for 5%

profile of v7, /device:TPU:0, one launch (start us, length us, event | category | flops | bytes accessed | tf_op | source)
XLA Modules:
  0.0 48.7 jit_solution(11201581951240409516)
XLA Ops:
  0.6 0.0 copy-start
  0.6 1.0 %copy-done = f32[2,16,32,128]{3,2,1,0:T(8,128)S(1)} copy-done((f32[2,16,32,128]{3,2,1,0:T(8,128)S(1)}, f32[2,16,32,128]{3,2,1,0:T(8,128)}, u32[]{:S(2)}) %copy-start) | copy-done | bytes 524312
  1.7 0.0 copy-start.3
  1.7 0.2 shard_map.59.after_ref
  1.9 0.0 copy-start.1
  1.9 0.1 collective-permute-start
  2.0 1.6 %collective-permute-start.2 = (f32[2,16,8,128]{3,2,1,0:T(8,128)S(1)}, f32[2,16,8,128]{3,2,1,0:T(8,128)S(1)}, u32[]{:S(2)}, u32[]{:S(2)}) collective-permute-start(f32[2,16,8,128]{3,2,1,0:T(8,128)S(1)} %get-tuple-element.15), channel_id=1, source_target_pairs={{0,4},{1,5},{2,6},{3,7},{4,8},{5,9},{6,10},{7,11},{8,12},{9,13},{1... | collective-permute-start | bytes 393224 | tf_op jit(solution)/shard_map/ppermute | solution.py:447
  3.6 0.0 copy-done.3
  3.6 0.5 shard_map.60
  4.1 2.7 %collective-permute-done = f32[2,32,128]{2,1,0:T(8,128)S(1)} collective-permute-done((f32[2,32,128]{2,1,0:T(8,128)S(1)}, f32[2,32,128]{2,1,0:T(8,128)S(1)}, u32[]{:S(2)}, u32[]{:S(2)}) %collective-permute-start) | collective-permute-done | bytes 32800 | tf_op jit(solution)/shard_map/ppermute | solution.py:456
  6.8 1.6 %collective-permute-start.1 = (f32[2,8,128]{2,1,0:T(8,128)S(1)}, f32[2,8,128]{2,1,0:T(8,128)S(1)}, u32[]{:S(2)}, u32[]{:S(2)}) collective-permute-start(f32[2,8,128]{2,1,0:T(8,128)S(1)} %slice.6), channel_id=1, source_target_pairs={{0,4},{1,5},{2,6},{3,7},{4,8},{5,9},{6,10},{7,11},{8,12},{9,13},{1... | collective-permute-start | bytes 24584 | tf_op jit(solution)/shard_map/ppermute | solution.py:447
  8.4 1.9 %collective-permute-start.3 = (f32[2,8,32,128]{3,2,1,0:T(8,128)S(1)}, f32[2,8,32,128]{3,2,1,0:T(8,128)S(1)}, u32[]{:S(2)}, u32[]{:S(2)}) collective-permute-start(f32[2,8,32,128]{3,2,1,0:T(8,128)S(1)} %get-tuple-element.16), channel_id=1, source_target_pairs={{0,32},{1,33},{2,34},{3,35},{4,36},{5,37},{6,38},{7,39},{8,40},{9,... | collective-permute-start | bytes 786440 | tf_op jit(solution)/shard_map/ppermute | solution.py:447
  10.3 2.3 %collective-permute-done.1 = f32[2,8,128]{2,1,0:T(8,128)S(1)} collective-permute-done((f32[2,8,128]{2,1,0:T(8,128)S(1)}, f32[2,8,128]{2,1,0:T(8,128)S(1)}, u32[]{:S(2)}, u32[]{:S(2)}) %collective-permute-start.1) | collective-permute-done | bytes 8224 | tf_op jit(solution)/shard_map/ppermute | solution.py:447
  12.6 0.0 collective-permute-done.2.yr_ref
  12.6 2.1 %collective-permute-start.4 = (f32[2,8,8,128]{3,2,1,0:T(8,128)S(1)}, f32[2,8,8,128]{3,2,1,0:T(8,128)S(1)}, u32[]{:S(2)}, u32[]{:S(2)}) collective-permute-start(f32[2,8,8,128]{3,2,1,0:T(8,128)S(1)} %slice.8), channel_id=1, source_target_pairs={{0,32},{1,33},{2,34},{3,35},{4,36},{5,37},{6,38},{7,39},{8,40},{9,... | collective-permute-start | bytes 196616 | tf_op jit(solution)/shard_map/ppermute | solution.py:447
  14.6 1.9 %collective-permute-start.5 = (f32[2,40,128]{2,1,0:T(8,128)S(1)}, f32[2,40,128]{2,1,0:T(8,128)S(1)}, u32[]{:S(2)}, u32[]{:S(2)}) collective-permute-start(f32[2,40,128]{2,1,0:T(8,128)S(1)} %constant_dynamic-update-slice_fusion.zr_ref), channel_id=1, source_target_pairs={{0,32},{1,33},{2,34},{3,35},{4,36},{5,37},{6,38},{7,39},{8,40},{9,... | collective-permute-start | bytes 122888 | tf_op jit(solution)/shard_map/ppermute | solution.py:447
  16.6 0.0 copy-done.1
  16.6 2.1 %shard_map.62.refs_3_ = f32[40,128]{1,0:T(8,128)S(1)} custom-call(f32[2,16,32,128]{3,2,1,0:T(8,128)S(1)} %copy-done.1, f32[2,40,128]{2,1,0:T(8,128)S(1)} %constant_dynamic-update-slice_fusion.zr_ref, f32[2,16,8,128]{3,2,1,0:T(8,128)S(1)} %collective-permute-done.2.yr_ref, f32[16,128]{1,0:T(8,128)S(1)} %get-tuple-element.17.refs_0_, ...), custom_call_target="tpu_custom_call" | custom-call | flops 500000000 | bytes 1000000 | tf_op jit(solution)/shard_map/pallas_call | solution.py:476
  18.7 2.4 %collective-permute-done.5.refs_2_ = f32[2,40,128]{2,1,0:T(8,128)S(1)} collective-permute-done((f32[2,40,128]{2,1,0:T(8,128)S(1)}, f32[2,40,128]{2,1,0:T(8,128)S(1)}, u32[]{:S(2)}, u32[]{:S(2)}) %collective-permute-start.5) | collective-permute-done | bytes 40992 | tf_op jit(solution)/shard_map/ppermute | solution.py:447
  21.1 0.0 collective-permute-done.4.refs_1_
  21.1 0.0 collective-permute-done.3.refs_0_
  21.1 2.1 %shard_map.63.mine_ref = f32[40,128]{1,0:T(8,128)S(1)} custom-call(f32[2,16,32,128]{3,2,1,0:T(8,128)S(1)} %copy-done.1, f32[2,40,128]{2,1,0:T(8,128)S(1)} %constant_dynamic-update-slice_fusion.zr_ref, f32[2,16,8,128]{3,2,1,0:T(8,128)S(1)} %collective-permute-done.2.yr_ref, f32[2,8,32,128]{3,2,1,0:T(8,128)S(1)} %collective-permute-done.3.refs_0_, ...), custom_call_target="tpu_custom_call" | custom-call | flops 500000000 | bytes 1000000 | tf_op jit(solution)/shard_map/pallas_call | solution.py:476
  23.2 0.1 collective-permute-start.6
  23.3 2.0 %collective-permute-start.7 = (f32[40,128]{1,0:T(8,128)S(1)}, f32[40,128]{1,0:T(8,128)S(1)}, u32[]{:S(2)}, u32[]{:S(2)}) collective-permute-start(f32[40,128]{1,0:T(8,128)S(1)} %shard_map.63.mine_ref), channel_id=1, source_target_pairs={{0,1},{2,3},{1,0},{3,2},{4,5},{6,7},{5,4},{7,6},{8,9},{10,11},{9,8... | collective-permute-start | bytes 61448 | tf_op jit(solution)/shard_map/ppermute | solution.py:497
  25.3 2.7 %collective-permute-done.6.chip_ref = f32[40,128]{1,0:T(8,128)S(1)} collective-permute-done((f32[40,128]{1,0:T(8,128)S(1)}, f32[40,128]{1,0:T(8,128)S(1)}, u32[]{:S(2)}, u32[]{:S(2)}) %collective-permute-start.6) | collective-permute-done | bytes 20512 | tf_op jit(solution)/shard_map/ppermute | solution.py:497
  28.0 0.0 collective-permute-done.7.core_ref
  28.0 0.1 shard_map.64.own_ref
  28.1 1.6 %collective-permute-start.8 = (f32[40,128]{1,0:T(8,128)S(1)}, f32[40,128]{1,0:T(8,128)S(1)}, u32[]{:S(2)}, u32[]{:S(2)}) collective-permute-start(f32[40,128]{1,0:T(8,128)S(1)} %shard_map.64.own_ref), channel_id=1, source_target_pairs={{0,64},{32,96},{64,0},{96,32},{1,65},{33,97},{65,1},{97,33},{2,66}... | collective-permute-start | bytes 61448 | tf_op jit(solution)/shard_map/ppermute | solution.py:497
  29.7 1.0 %collective-permute-start.9 = (f32[40,128]{1,0:T(8,128)S(1)}, f32[40,128]{1,0:T(8,128)S(1)}, u32[]{:S(2)}, u32[]{:S(2)}) collective-permute-start(f32[40,128]{1,0:T(8,128)S(1)} %shard_map.64.own_ref), channel_id=1, source_target_pairs={{0,32},{64,96},{32,0},{96,64},{1,33},{65,97},{33,1},{97,65},{2,34}... | collective-permute-start | bytes 61448 | tf_op jit(solution)/shard_map/ppermute | solution.py:497
  30.7 1.5 %collective-permute-start.10 = (f32[40,128]{1,0:T(8,128)S(1)}, f32[40,128]{1,0:T(8,128)S(1)}, u32[]{:S(2)}, u32[]{:S(2)}) collective-permute-start(f32[40,128]{1,0:T(8,128)S(1)} %shard_map.64.own_ref), channel_id=1, source_target_pairs={{32,64},{96,0},{64,32},{0,96},{33,65},{97,1},{65,33},{1,97},{34,66... | collective-permute-start | bytes 61448 | tf_op jit(solution)/shard_map/ppermute | solution.py:497
  32.2 1.3 %collective-permute-done.8.far_ref = f32[40,128]{1,0:T(8,128)S(1)} collective-permute-done((f32[40,128]{1,0:T(8,128)S(1)}, f32[40,128]{1,0:T(8,128)S(1)}, u32[]{:S(2)}, u32[]{:S(2)}) %collective-permute-start.8) | collective-permute-done | bytes 20512 | tf_op jit(solution)/shard_map/ppermute | solution.py:497
  33.5 0.0 collective-permute-done.9.one_ref
  33.5 2.2 %collective-permute-done.10.two_ref = f32[40,128]{1,0:T(8,128)S(1)} collective-permute-done((f32[40,128]{1,0:T(8,128)S(1)}, f32[40,128]{1,0:T(8,128)S(1)}, u32[]{:S(2)}, u32[]{:S(2)}) %collective-permute-start.10) | collective-permute-done | bytes 20512 | tf_op jit(solution)/shard_map/ppermute | solution.py:497
  35.8 0.0 copy-start.2
  35.8 0.0 copy-start.4
  35.8 10.8 %all_to_all.5.g_ref = f32[8,48,128]{2,1,0:T(8,128)S(1)} all-to-all(f32[8,48,128]{2,1,0:T(8,128)S(1)} %shard_map.65), channel_id=1, replica_groups=mesh['gx'=4,'gy'=8,'gz'=4] {'gy'}, dimensions={0} | all-to-all | bytes 393216 | tf_op jit(solution)/shard_map/all_to_all | solution.py:505
  46.6 0.0 copy-done.2
  46.6 0.0 copy-done.4
  46.6 2.1 %shard_map.66 = (f32[6,2,16,32]{3,2,1,0:T(8,128)}, bf16[6,512,128]{2,1,0:T(8,128)(2,1)}) custom-call(f32[8,48,128]{2,1,0:T(8,128)S(1)} %all_to_all.5.g_ref, bf16[512,144]{1,0:T(8,128)(2,1)S(1)} %copy-done.2, bf16[128,256]{1,0:T(8,128)(2,1)S(1)} %copy-done.4), custom_call_target="tpu_custom_call" | custom-call | flops 100000000 | bytes 1000000 | tf_op jit(solution)/shard_map/pallas_call | solution.py:507
  (6 shorter events, 0.1 us)
Async XLA Ops:
  0.6 1.0 %copy-start = (f32[2,16,32,128]{3,2,1,0:T(8,128)S(1)}, f32[2,16,32,128]{3,2,1,0:T(8,128)}, u32[]{:S(2)}) copy-start(f32[2,16,32,128]{3,2,1,0:T(8,128)} %own_ref.3) | copy-start | bytes 1572868
  1.7 2.0 %copy-start.3 = (f32[2,3,2,32,16]{3,4,2,1,0:T(8,128)S(1)}, f32[2,3,2,32,16]{3,4,2,1,0:T(8,128)}, u32[]{:S(2)}) copy-start(f32[2,3,2,32,16]{3,4,2,1,0:T(8,128)} %param.5) | copy-start | bytes 73732
  1.9 14.7 %copy-start.1 = (f32[2,16,32,128]{3,2,1,0:T(8,128)S(1)}, f32[2,16,32,128]{3,2,1,0:T(8,128)}, u32[]{:S(2)}) copy-start(f32[2,16,32,128]{3,2,1,0:T(8,128)} %own_ref.3) | copy-start | bytes 1572868
  1.9 4.9 %collective-permute-start = (f32[2,32,128]{2,1,0:T(8,128)S(1)}, f32[2,32,128]{2,1,0:T(8,128)S(1)}, u32[]{:S(2)}, u32[]{:S(2)}) collective-permute-start(f32[2,32,128]{2,1,0:T(8,128)S(1)} %shard_map.59.after_ref), channel_id=1, source_target_pairs={{0,1},{1,2},{2,3},{3,0},{4,5},{5,6},{6,7},{7,4},{8,9},{9,10},{10,1... | collective-permute-start | bytes 98312 | tf_op jit(solution)/shard_map/ppermute | solution.py:456
  2.0 10.6 %collective-permute-start.2 = (f32[2,16,8,128]{3,2,1,0:T(8,128)S(1)}, f32[2,16,8,128]{3,2,1,0:T(8,128)S(1)}, u32[]{:S(2)}, u32[]{:S(2)}) collective-permute-start(f32[2,16,8,128]{3,2,1,0:T(8,128)S(1)} %get-tuple-element.15), channel_id=1, source_target_pairs={{0,4},{1,5},{2,6},{3,7},{4,8},{5,9},{6,10},{7,11},{8,12},{9,13},{1... | collective-permute-start | bytes 393224 | tf_op jit(solution)/shard_map/ppermute | solution.py:447
  6.8 5.8 %collective-permute-start.1 = (f32[2,8,128]{2,1,0:T(8,128)S(1)}, f32[2,8,128]{2,1,0:T(8,128)S(1)}, u32[]{:S(2)}, u32[]{:S(2)}) collective-permute-start(f32[2,8,128]{2,1,0:T(8,128)S(1)} %slice.6), channel_id=1, source_target_pairs={{0,4},{1,5},{2,6},{3,7},{4,8},{5,9},{6,10},{7,11},{8,12},{9,13},{1... | collective-permute-start | bytes 24584 | tf_op jit(solution)/shard_map/ppermute | solution.py:447
  8.4 12.8 %collective-permute-start.3 = (f32[2,8,32,128]{3,2,1,0:T(8,128)S(1)}, f32[2,8,32,128]{3,2,1,0:T(8,128)S(1)}, u32[]{:S(2)}, u32[]{:S(2)}) collective-permute-start(f32[2,8,32,128]{3,2,1,0:T(8,128)S(1)} %get-tuple-element.16), channel_id=1, source_target_pairs={{0,32},{1,33},{2,34},{3,35},{4,36},{5,37},{6,38},{7,39},{8,40},{9,... | collective-permute-start | bytes 786440 | tf_op jit(solution)/shard_map/ppermute | solution.py:447
  12.6 8.6 %collective-permute-start.4 = (f32[2,8,8,128]{3,2,1,0:T(8,128)S(1)}, f32[2,8,8,128]{3,2,1,0:T(8,128)S(1)}, u32[]{:S(2)}, u32[]{:S(2)}) collective-permute-start(f32[2,8,8,128]{3,2,1,0:T(8,128)S(1)} %slice.8), channel_id=1, source_target_pairs={{0,32},{1,33},{2,34},{3,35},{4,36},{5,37},{6,38},{7,39},{8,40},{9,... | collective-permute-start | bytes 196616 | tf_op jit(solution)/shard_map/ppermute | solution.py:447
  14.6 6.5 %collective-permute-start.5 = (f32[2,40,128]{2,1,0:T(8,128)S(1)}, f32[2,40,128]{2,1,0:T(8,128)S(1)}, u32[]{:S(2)}, u32[]{:S(2)}) collective-permute-start(f32[2,40,128]{2,1,0:T(8,128)S(1)} %constant_dynamic-update-slice_fusion.zr_ref), channel_id=1, source_target_pairs={{0,32},{1,33},{2,34},{3,35},{4,36},{5,37},{6,38},{7,39},{8,40},{9,... | collective-permute-start | bytes 122888 | tf_op jit(solution)/shard_map/ppermute | solution.py:447
  23.2 4.8 %collective-permute-start.6 = (f32[40,128]{1,0:T(8,128)S(1)}, f32[40,128]{1,0:T(8,128)S(1)}, u32[]{:S(2)}, u32[]{:S(2)}) collective-permute-start(f32[40,128]{1,0:T(8,128)S(1)} %shard_map.63.mine_ref), channel_id=1, source_target_pairs={{1,2},{3,0},{2,1},{0,3},{5,6},{7,4},{6,5},{4,7},{9,10},{11,8},{10,... | collective-permute-start | bytes 61448 | tf_op jit(solution)/shard_map/ppermute | solution.py:497
  23.3 4.7 %collective-permute-start.7 = (f32[40,128]{1,0:T(8,128)S(1)}, f32[40,128]{1,0:T(8,128)S(1)}, u32[]{:S(2)}, u32[]{:S(2)}) collective-permute-start(f32[40,128]{1,0:T(8,128)S(1)} %shard_map.63.mine_ref), channel_id=1, source_target_pairs={{0,1},{2,3},{1,0},{3,2},{4,5},{6,7},{5,4},{7,6},{8,9},{10,11},{9,8... | collective-permute-start | bytes 61448 | tf_op jit(solution)/shard_map/ppermute | solution.py:497
  28.1 5.4 %collective-permute-start.8 = (f32[40,128]{1,0:T(8,128)S(1)}, f32[40,128]{1,0:T(8,128)S(1)}, u32[]{:S(2)}, u32[]{:S(2)}) collective-permute-start(f32[40,128]{1,0:T(8,128)S(1)} %shard_map.64.own_ref), channel_id=1, source_target_pairs={{0,64},{32,96},{64,0},{96,32},{1,65},{33,97},{65,1},{97,33},{2,66}... | collective-permute-start | bytes 61448 | tf_op jit(solution)/shard_map/ppermute | solution.py:497
  29.7 3.8 %collective-permute-start.9 = (f32[40,128]{1,0:T(8,128)S(1)}, f32[40,128]{1,0:T(8,128)S(1)}, u32[]{:S(2)}, u32[]{:S(2)}) collective-permute-start(f32[40,128]{1,0:T(8,128)S(1)} %shard_map.64.own_ref), channel_id=1, source_target_pairs={{0,32},{64,96},{32,0},{96,64},{1,33},{65,97},{33,1},{97,65},{2,34}... | collective-permute-start | bytes 61448 | tf_op jit(solution)/shard_map/ppermute | solution.py:497
  30.7 5.0 %collective-permute-start.10 = (f32[40,128]{1,0:T(8,128)S(1)}, f32[40,128]{1,0:T(8,128)S(1)}, u32[]{:S(2)}, u32[]{:S(2)}) collective-permute-start(f32[40,128]{1,0:T(8,128)S(1)} %shard_map.64.own_ref), channel_id=1, source_target_pairs={{32,64},{96,0},{64,32},{0,96},{33,65},{97,1},{65,33},{1,97},{34,66... | collective-permute-start | bytes 61448 | tf_op jit(solution)/shard_map/ppermute | solution.py:497
  35.8 10.8 %copy-start.2 = (bf16[512,144]{1,0:T(8,128)(2,1)S(1)}, bf16[512,144]{1,0:T(8,128)(2,1)}, u32[]{:S(2)}) copy-start(bf16[512,144]{1,0:T(8,128)(2,1)} %constant.4.clone.wxy_ref) | copy-start | bytes 442372
  35.8 10.8 %copy-start.4 = (bf16[128,256]{1,0:T(8,128)(2,1)S(1)}, bf16[128,256]{1,0:T(8,128)(2,1)}, u32[]{:S(2)}) copy-start(bf16[128,256]{1,0:T(8,128)(2,1)} %constant.5.clone.wz_ref) | copy-start | bytes 196612

commit v8 on v6

--- a/solution.py
+++ b/solution.py
@@ -178,7 +178,7 @@
                 a_ref[h, n, 8:40] = xr_ref[h, n]
                 a_ref[h, n, 0:8] = xyr_ref[h, n]
         h_ref[h, 0, 8:40] = zr_ref[h]
-        h_ref[h, 0, 0:8] = yzr_ref[h]
+        h_ref[h, 0, 0:8] = yzr_ref[h, 24:32]
         if not upper:
             h_ref[h, 1, 8:40] = xzr_ref[h]
             h_ref[h, 1, 0:8] = xyr_ref[h, 8]
@@ -471,7 +471,7 @@
     )(velocity)
     zr, vel = lax.optimization_barrier((zr, vel))
     top = zr[:, 24:]
-    yzr = send(top, 0, 1, 0)
+    yzr = send(zr, 0, 1, 0)
     xyr = send(to_xy.at[:, 8].set(top), 1, 1, 0)
     xzr = send(zr, 1, 0, 0)
 

time: 45.8 us -> 45.8 us (level)
  starting transfers between devices: 17.6 us -> 16.5 us
  waiting for transfers between devices: 8.9 us -> 9.46 us
    ppermute x5, starting transfers between devices: 7.67 us -> 6.5 us  [shards(): lax.ppermute(v, axis, couples + [(b, a) for a, b in couples])]
  transfers between devices with their start and end apart: 11 -> 11, of which waited for: 7 -> 6; matrix products, arithmetic and copies ran while one was open for 0% -> 0% of each run, Pallas kernels for 6% -> 6%
where the time goes in v8:
time: 45.8 us; the launch traced here: 44.9 us
  starting transfers between devices  16.5 us (36%)
  blocking collectives  10.1 us (22%)
  waiting for transfers between devices  9.46 us (21%)
  Pallas kernels  7.06 us (15%)
  local copies, waits for them, and re-layouts  1.06 us (2%)
  between operations  0.71 us (2%)
    all_to_all x1, blocking collectives, shards(): everything = lax.all_to_all(copies, 'gy', 0, 0, tiled=True)  10.1 us
    ppermute x5, starting transfers between devices, send(): return lax.ppermute(v, AXES, pairs(sizes, di, dj, dk))  9.9 us
    ppermute x5, starting transfers between devices, shards(): lax.ppermute(v, axis, couples + [(b, a) for a, b in couples])  6.5 us
    ppermute x5, waiting for transfers between devices, shards(): lax.ppermute(v, axis, couples + [(b, a) for a, b in couples])  5.76 us
    pallas_call x2, Pallas kernels, forces(): call(functools.partial(force_kernel, upper), [((40, 128), f32)], [VMEM] *...  4.17 us
    ppermute x5, waiting for transfers between devices, send(): return lax.ppermute(v, AXES, pairs(sizes, di, dj, dk))  2.94 us
    pallas_call x1, Pallas kernels, shards(): call(field_kernel, [((6, 2, 16, 32), f32), ((6, 512, 128), bf16)], [VMEM]...  2.1 us
    unnamed x10, local copies, waits for them, and re-layouts  1.06 us
  transfers between devices with their start and end apart: 11, of which 6 were waited for; matrix products, arithmetic and copies ran while one was open for 0% of the time, Pallas kernels for 6%

profile of v8, /device:TPU:0, one launch (start us, length us, event | category | flops | bytes accessed | tf_op | source)
XLA Modules:
  0.0 44.9 jit_solution(2657600871273407154)
XLA Ops:
  0.6 0.0 copy-start
  0.6 1.0 %copy-done = f32[2,16,32,128]{3,2,1,0:T(8,128)S(1)} copy-done((f32[2,16,32,128]{3,2,1,0:T(8,128)S(1)}, f32[2,16,32,128]{3,2,1,0:T(8,128)}, u32[]{:S(2)}) %copy-start) | copy-done | bytes 524312
  1.7 0.0 copy-start.1
  1.7 0.2 shard_map.59.after_ref
  1.9 0.0 copy-start.3
  1.9 0.1 collective-permute-start
  2.0 1.6 %collective-permute-start.1 = (f32[2,16,8,128]{3,2,1,0:T(8,128)S(1)}, f32[2,16,8,128]{3,2,1,0:T(8,128)S(1)}, u32[]{:S(2)}, u32[]{:S(2)}) collective-permute-start(f32[2,16,8,128]{3,2,1,0:T(8,128)S(1)} %get-tuple-element.28), channel_id=1, source_target_pairs={{0,4},{1,5},{2,6},{3,7},{4,8},{5,9},{6,10},{7,11},{8,12},{9,13},{1... | collective-permute-start | bytes 393224 | tf_op jit(solution)/shard_map/ppermute | solution.py:451
  3.6 1.9 %collective-permute-start.3 = (f32[2,8,32,128]{3,2,1,0:T(8,128)S(1)}, f32[2,8,32,128]{3,2,1,0:T(8,128)S(1)}, u32[]{:S(2)}, u32[]{:S(2)}) collective-permute-start(f32[2,8,32,128]{3,2,1,0:T(8,128)S(1)} %get-tuple-element.29), channel_id=1, source_target_pairs={{0,32},{1,33},{2,34},{3,35},{4,36},{5,37},{6,38},{7,39},{8,40},{9,... | collective-permute-start | bytes 786440 | tf_op jit(solution)/shard_map/ppermute | solution.py:451
  5.6 0.0 copy-done.3
  5.6 0.5 %shard_map.60 = (f32[16,128]{1,0:T(8,128)S(1)}, bf16[80,512]{1,0:T(8,128)(2,1)S(1)}, bf16[128,256]{1,0:T(8,128)(2,1)S(1)}, bf16[256,128]{1,0:T(8,128)(2,1)S(1)}, f32[256,128]{1,0:T(8,128)S(1)}) custom-call(f32[6,2,16,32]{3,2,1,0:T(8,128)S(1)} %bitcast.11), custom_call_target="tpu_custom_call" | custom-call | bytes 1000000 | tf_op jit(solution)/shard_map/pallas_call | solution.py:465
  6.0 0.8 %collective-permute-done.zr_ref = f32[2,32,128]{2,1,0:T(8,128)S(1)} collective-permute-done((f32[2,32,128]{2,1,0:T(8,128)S(1)}, f32[2,32,128]{2,1,0:T(8,128)S(1)}, u32[]{:S(2)}, u32[]{:S(2)}) %collective-permute-start) | collective-permute-done | bytes 32800 | tf_op jit(solution)/shard_map/ppermute | solution.py:460
  6.8 1.6 %collective-permute-start.2 = (f32[2,32,128]{2,1,0:T(8,128)S(1)}, f32[2,32,128]{2,1,0:T(8,128)S(1)}, u32[]{:S(2)}, u32[]{:S(2)}) collective-permute-start(f32[2,32,128]{2,1,0:T(8,128)S(1)} %collective-permute-done.zr_ref), channel_id=1, source_target_pairs={{0,4},{1,5},{2,6},{3,7},{4,8},{5,9},{6,10},{7,11},{8,12},{9,13},{1... | collective-permute-start | bytes 98312 | tf_op jit(solution)/shard_map/ppermute | solution.py:451
  8.4 2.8 %collective-permute-start.4 = (f32[2,9,8,128]{3,2,1,0:T(8,128)S(1)}, f32[2,9,8,128]{3,2,1,0:T(8,128)S(1)}, u32[]{:S(2)}, u32[]{:S(2)}) collective-permute-start(f32[2,9,8,128]{3,2,1,0:T(8,128)S(1)} %bitcast_dynamic-update-slice_fusion), channel_id=1, source_target_pairs={{0,36},{1,37},{2,38},{3,39},{4,40},{5,41},{6,42},{7,43},{8,44},{9,... | collective-permute-start | bytes 221192 | tf_op jit(solution)/shard_map/ppermute | solution.py:451
  11.2 1.9 %collective-permute-start.5 = (f32[2,32,128]{2,1,0:T(8,128)S(1)}, f32[2,32,128]{2,1,0:T(8,128)S(1)}, u32[]{:S(2)}, u32[]{:S(2)}) collective-permute-start(f32[2,32,128]{2,1,0:T(8,128)S(1)} %collective-permute-done.zr_ref), channel_id=1, source_target_pairs={{0,32},{1,33},{2,34},{3,35},{4,36},{5,37},{6,38},{7,39},{8,40},{9,... | collective-permute-start | bytes 98312 | tf_op jit(solution)/shard_map/ppermute | solution.py:451
  13.1 0.0 collective-permute-done.2.yzr_ref
  13.1 0.0 collective-permute-done.1.yr_ref
  13.1 0.0 copy-done.1
  13.1 2.1 %shard_map.62.refs_3_ = f32[40,128]{1,0:T(8,128)S(1)} custom-call(f32[2,16,32,128]{3,2,1,0:T(8,128)S(1)} %copy-done.1, f32[2,32,128]{2,1,0:T(8,128)S(1)} %collective-permute-done.zr_ref, f32[2,16,8,128]{3,2,1,0:T(8,128)S(1)} %collective-permute-done.1.yr_ref, f32[2,32,128]{2,1,0:T(8,128)S(1)} %collective-permute-done.2.yzr_ref, ...), custom_call_target="tpu_custom_call" | custom-call | flops 500000000 | bytes 1000000 | tf_op jit(solution)/shard_map/pallas_call | solution.py:479
  15.3 2.9 %collective-permute-done.5.refs_2_ = f32[2,32,128]{2,1,0:T(8,128)S(1)} collective-permute-done((f32[2,32,128]{2,1,0:T(8,128)S(1)}, f32[2,32,128]{2,1,0:T(8,128)S(1)}, u32[]{:S(2)}, u32[]{:S(2)}) %collective-permute-start.5) | collective-permute-done | bytes 32800 | tf_op jit(solution)/shard_map/ppermute | solution.py:451
  18.2 0.0 collective-permute-done.4.refs_1_
  18.2 0.0 collective-permute-done.3.refs_0_
  18.2 2.1 %shard_map.63.mine_ref = f32[40,128]{1,0:T(8,128)S(1)} custom-call(f32[2,16,32,128]{3,2,1,0:T(8,128)S(1)} %copy-done.1, f32[2,32,128]{2,1,0:T(8,128)S(1)} %collective-permute-done.zr_ref, f32[2,16,8,128]{3,2,1,0:T(8,128)S(1)} %collective-permute-done.1.yr_ref, f32[2,32,128]{2,1,0:T(8,128)S(1)} %collective-permute-done.2.yzr_ref, ...), custom_call_target="tpu_custom_call" | custom-call | flops 500000000 | bytes 1000000 | tf_op jit(solution)/shard_map/pallas_call | solution.py:479
  20.3 0.2 collective-permute-start.6
  20.4 2.2 %collective-permute-start.7 = (f32[40,128]{1,0:T(8,128)S(1)}, f32[40,128]{1,0:T(8,128)S(1)}, u32[]{:S(2)}, u32[]{:S(2)}) collective-permute-start(f32[40,128]{1,0:T(8,128)S(1)} %shard_map.63.mine_ref), channel_id=1, source_target_pairs={{0,1},{2,3},{1,0},{3,2},{4,5},{6,7},{5,4},{7,6},{8,9},{10,11},{9,8... | collective-permute-start | bytes 61448 | tf_op jit(solution)/shard_map/ppermute | solution.py:500
  22.6 2.4 %collective-permute-done.6.chip_ref = f32[40,128]{1,0:T(8,128)S(1)} collective-permute-done((f32[40,128]{1,0:T(8,128)S(1)}, f32[40,128]{1,0:T(8,128)S(1)}, u32[]{:S(2)}, u32[]{:S(2)}) %collective-permute-start.6) | collective-permute-done | bytes 20512 | tf_op jit(solution)/shard_map/ppermute | solution.py:500
  25.1 0.0 collective-permute-done.7.core_ref
  25.1 0.1 shard_map.64.own_ref
  25.1 2.0 %collective-permute-start.8 = (f32[40,128]{1,0:T(8,128)S(1)}, f32[40,128]{1,0:T(8,128)S(1)}, u32[]{:S(2)}, u32[]{:S(2)}) collective-permute-start(f32[40,128]{1,0:T(8,128)S(1)} %shard_map.64.own_ref), channel_id=1, source_target_pairs={{0,64},{32,96},{64,0},{96,32},{1,65},{33,97},{65,1},{97,33},{2,66}... | collective-permute-start | bytes 61448 | tf_op jit(solution)/shard_map/ppermute | solution.py:500
  27.1 0.5 %collective-permute-start.9 = (f32[40,128]{1,0:T(8,128)S(1)}, f32[40,128]{1,0:T(8,128)S(1)}, u32[]{:S(2)}, u32[]{:S(2)}) collective-permute-start(f32[40,128]{1,0:T(8,128)S(1)} %shard_map.64.own_ref), channel_id=1, source_target_pairs={{0,32},{64,96},{32,0},{96,64},{1,33},{65,97},{33,1},{97,65},{2,34}... | collective-permute-start | bytes 61448 | tf_op jit(solution)/shard_map/ppermute | solution.py:500
  27.6 1.7 %collective-permute-start.10 = (f32[40,128]{1,0:T(8,128)S(1)}, f32[40,128]{1,0:T(8,128)S(1)}, u32[]{:S(2)}, u32[]{:S(2)}) collective-permute-start(f32[40,128]{1,0:T(8,128)S(1)} %shard_map.64.own_ref), channel_id=1, source_target_pairs={{32,64},{96,0},{64,32},{0,96},{33,65},{97,1},{65,33},{1,97},{34,66... | collective-permute-start | bytes 61448 | tf_op jit(solution)/shard_map/ppermute | solution.py:500
  29.3 1.2 %collective-permute-done.8.far_ref = f32[40,128]{1,0:T(8,128)S(1)} collective-permute-done((f32[40,128]{1,0:T(8,128)S(1)}, f32[40,128]{1,0:T(8,128)S(1)}, u32[]{:S(2)}, u32[]{:S(2)}) %collective-permute-start.8) | collective-permute-done | bytes 20512 | tf_op jit(solution)/shard_map/ppermute | solution.py:500
  30.5 0.5 %collective-permute-done.9.one_ref = f32[40,128]{1,0:T(8,128)S(1)} collective-permute-done((f32[40,128]{1,0:T(8,128)S(1)}, f32[40,128]{1,0:T(8,128)S(1)}, u32[]{:S(2)}, u32[]{:S(2)}) %collective-permute-start.9) | collective-permute-done | bytes 20512 | tf_op jit(solution)/shard_map/ppermute | solution.py:500
  30.9 1.7 %collective-permute-done.10.two_ref = f32[40,128]{1,0:T(8,128)S(1)} collective-permute-done((f32[40,128]{1,0:T(8,128)S(1)}, f32[40,128]{1,0:T(8,128)S(1)}, u32[]{:S(2)}, u32[]{:S(2)}) %collective-permute-start.10) | collective-permute-done | bytes 20512 | tf_op jit(solution)/shard_map/ppermute | solution.py:500
  32.6 0.0 copy-start.2
  32.6 0.0 copy-start.4
  32.7 10.1 %all_to_all.5.g_ref = f32[8,48,128]{2,1,0:T(8,128)S(1)} all-to-all(f32[8,48,128]{2,1,0:T(8,128)S(1)} %shard_map.65), channel_id=1, replica_groups=mesh['gx'=4,'gy'=8,'gz'=4] {'gy'}, dimensions={0} | all-to-all | bytes 393216 | tf_op jit(solution)/shard_map/all_to_all | solution.py:508
  42.8 0.0 copy-done.2
  42.8 0.0 copy-done.4
  42.8 2.1 %shard_map.66 = (f32[6,2,16,32]{3,2,1,0:T(8,128)}, bf16[6,512,128]{2,1,0:T(8,128)(2,1)}) custom-call(f32[8,48,128]{2,1,0:T(8,128)S(1)} %all_to_all.5.g_ref, bf16[512,144]{1,0:T(8,128)(2,1)S(1)} %copy-done.2, bf16[128,256]{1,0:T(8,128)(2,1)S(1)} %copy-done.4), custom_call_target="tpu_custom_call" | custom-call | flops 100000000 | bytes 1000000 | tf_op jit(solution)/shard_map/pallas_call | solution.py:510
  (3 shorter events, 0.1 us)
Async XLA Ops:
  0.6 1.0 %copy-start = (f32[2,16,32,128]{3,2,1,0:T(8,128)S(1)}, f32[2,16,32,128]{3,2,1,0:T(8,128)}, u32[]{:S(2)}) copy-start(f32[2,16,32,128]{3,2,1,0:T(8,128)} %own_ref.3) | copy-start | bytes 1572868
  1.7 11.5 %copy-start.1 = (f32[2,16,32,128]{3,2,1,0:T(8,128)S(1)}, f32[2,16,32,128]{3,2,1,0:T(8,128)}, u32[]{:S(2)}) copy-start(f32[2,16,32,128]{3,2,1,0:T(8,128)} %own_ref.3) | copy-start | bytes 1572868
  1.9 3.7 %copy-start.3 = (f32[2,3,2,32,16]{3,4,2,1,0:T(8,128)S(1)}, f32[2,3,2,32,16]{3,4,2,1,0:T(8,128)}, u32[]{:S(2)}) copy-start(f32[2,3,2,32,16]{3,4,2,1,0:T(8,128)} %param.7) | copy-start | bytes 73732
  1.9 4.9 %collective-permute-start = (f32[2,32,128]{2,1,0:T(8,128)S(1)}, f32[2,32,128]{2,1,0:T(8,128)S(1)}, u32[]{:S(2)}, u32[]{:S(2)}) collective-permute-start(f32[2,32,128]{2,1,0:T(8,128)S(1)} %shard_map.59.after_ref), channel_id=1, source_target_pairs={{0,1},{1,2},{2,3},{3,0},{4,5},{5,6},{6,7},{7,4},{8,9},{9,10},{10,1... | collective-permute-start | bytes 98312 | tf_op jit(solution)/shard_map/ppermute | solution.py:460
  2.0 11.1 %collective-permute-start.1 = (f32[2,16,8,128]{3,2,1,0:T(8,128)S(1)}, f32[2,16,8,128]{3,2,1,0:T(8,128)S(1)}, u32[]{:S(2)}, u32[]{:S(2)}) collective-permute-start(f32[2,16,8,128]{3,2,1,0:T(8,128)S(1)} %get-tuple-element.28), channel_id=1, source_target_pairs={{0,4},{1,5},{2,6},{3,7},{4,8},{5,9},{6,10},{7,11},{8,12},{9,13},{1... | collective-permute-start | bytes 393224 | tf_op jit(solution)/shard_map/ppermute | solution.py:451
  3.6 14.6 %collective-permute-start.3 = (f32[2,8,32,128]{3,2,1,0:T(8,128)S(1)}, f32[2,8,32,128]{3,2,1,0:T(8,128)S(1)}, u32[]{:S(2)}, u32[]{:S(2)}) collective-permute-start(f32[2,8,32,128]{3,2,1,0:T(8,128)S(1)} %get-tuple-element.29), channel_id=1, source_target_pairs={{0,32},{1,33},{2,34},{3,35},{4,36},{5,37},{6,38},{7,39},{8,40},{9,... | collective-permute-start | bytes 786440 | tf_op jit(solution)/shard_map/ppermute | solution.py:451
  6.8 6.3 %collective-permute-start.2 = (f32[2,32,128]{2,1,0:T(8,128)S(1)}, f32[2,32,128]{2,1,0:T(8,128)S(1)}, u32[]{:S(2)}, u32[]{:S(2)}) collective-permute-start(f32[2,32,128]{2,1,0:T(8,128)S(1)} %collective-permute-done.zr_ref), channel_id=1, source_target_pairs={{0,4},{1,5},{2,6},{3,7},{4,8},{5,9},{6,10},{7,11},{8,12},{9,13},{1... | collective-permute-start | bytes 98312 | tf_op jit(solution)/shard_map/ppermute | solution.py:451
  8.4 9.8 %collective-permute-start.4 = (f32[2,9,8,128]{3,2,1,0:T(8,128)S(1)}, f32[2,9,8,128]{3,2,1,0:T(8,128)S(1)}, u32[]{:S(2)}, u32[]{:S(2)}) collective-permute-start(f32[2,9,8,128]{3,2,1,0:T(8,128)S(1)} %bitcast_dynamic-update-slice_fusion), channel_id=1, source_target_pairs={{0,36},{1,37},{2,38},{3,39},{4,40},{5,41},{6,42},{7,43},{8,44},{9,... | collective-permute-start | bytes 221192 | tf_op jit(solution)/shard_map/ppermute | solution.py:451
  11.2 7.0 %collective-permute-start.5 = (f32[2,32,128]{2,1,0:T(8,128)S(1)}, f32[2,32,128]{2,1,0:T(8,128)S(1)}, u32[]{:S(2)}, u32[]{:S(2)}) collective-permute-start(f32[2,32,128]{2,1,0:T(8,128)S(1)} %collective-permute-done.zr_ref), channel_id=1, source_target_pairs={{0,32},{1,33},{2,34},{3,35},{4,36},{5,37},{6,38},{7,39},{8,40},{9,... | collective-permute-start | bytes 98312 | tf_op jit(solution)/shard_map/ppermute | solution.py:451
  20.3 4.8 %collective-permute-start.6 = (f32[40,128]{1,0:T(8,128)S(1)}, f32[40,128]{1,0:T(8,128)S(1)}, u32[]{:S(2)}, u32[]{:S(2)}) collective-permute-start(f32[40,128]{1,0:T(8,128)S(1)} %shard_map.63.mine_ref), channel_id=1, source_target_pairs={{1,2},{3,0},{2,1},{0,3},{5,6},{7,4},{6,5},{4,7},{9,10},{11,8},{10,... | collective-permute-start | bytes 61448 | tf_op jit(solution)/shard_map/ppermute | solution.py:500
  20.4 4.6 %collective-permute-start.7 = (f32[40,128]{1,0:T(8,128)S(1)}, f32[40,128]{1,0:T(8,128)S(1)}, u32[]{:S(2)}, u32[]{:S(2)}) collective-permute-start(f32[40,128]{1,0:T(8,128)S(1)} %shard_map.63.mine_ref), channel_id=1, source_target_pairs={{0,1},{2,3},{1,0},{3,2},{4,5},{6,7},{5,4},{7,6},{8,9},{10,11},{9,8... | collective-permute-start | bytes 61448 | tf_op jit(solution)/shard_map/ppermute | solution.py:500
  25.1 5.3 %collective-permute-start.8 = (f32[40,128]{1,0:T(8,128)S(1)}, f32[40,128]{1,0:T(8,128)S(1)}, u32[]{:S(2)}, u32[]{:S(2)}) collective-permute-start(f32[40,128]{1,0:T(8,128)S(1)} %shard_map.64.own_ref), channel_id=1, source_target_pairs={{0,64},{32,96},{64,0},{96,32},{1,65},{33,97},{65,1},{97,33},{2,66}... | collective-permute-start | bytes 61448 | tf_op jit(solution)/shard_map/ppermute | solution.py:500
  27.1 3.8 %collective-permute-start.9 = (f32[40,128]{1,0:T(8,128)S(1)}, f32[40,128]{1,0:T(8,128)S(1)}, u32[]{:S(2)}, u32[]{:S(2)}) collective-permute-start(f32[40,128]{1,0:T(8,128)S(1)} %shard_map.64.own_ref), channel_id=1, source_target_pairs={{0,32},{64,96},{32,0},{96,64},{1,33},{65,97},{33,1},{97,65},{2,34}... | collective-permute-start | bytes 61448 | tf_op jit(solution)/shard_map/ppermute | solution.py:500
  27.6 5.0 %collective-permute-start.10 = (f32[40,128]{1,0:T(8,128)S(1)}, f32[40,128]{1,0:T(8,128)S(1)}, u32[]{:S(2)}, u32[]{:S(2)}) collective-permute-start(f32[40,128]{1,0:T(8,128)S(1)} %shard_map.64.own_ref), channel_id=1, source_target_pairs={{32,64},{96,0},{64,32},{0,96},{33,65},{97,1},{65,33},{1,97},{34,66... | collective-permute-start | bytes 61448 | tf_op jit(solution)/shard_map/ppermute | solution.py:500
  32.6 10.1 %copy-start.2 = (bf16[512,144]{1,0:T(8,128)(2,1)S(1)}, bf16[512,144]{1,0:T(8,128)(2,1)}, u32[]{:S(2)}) copy-start(bf16[512,144]{1,0:T(8,128)(2,1)} %constant.33.clone.wxy_ref) | copy-start | bytes 442372
  32.6 10.1 %copy-start.4 = (bf16[128,256]{1,0:T(8,128)(2,1)S(1)}, bf16[128,256]{1,0:T(8,128)(2,1)}, u32[]{:S(2)}) copy-start(bf16[128,256]{1,0:T(8,128)(2,1)} %constant.34.clone.wz_ref) | copy-start | bytes 196612

commit v9 on v8

--- a/solution.py
+++ b/solution.py
@@ -327,7 +327,7 @@
     out_ref[...] = total + jnp.where(live & (spot >= 16), high, 0.0)
 
 
-def across_kernel(own_ref, far_ref, one_ref, two_ref, out_ref):
+def across_kernel(own_ref, far_ref, one_ref, two_ref, out_ref, mine_ref):
     odd = (lax.axis_index("gx") & 1) == 1
     tiles = lambda ref: [ref[8 * p : 8 * p + 8] for p in range(5)]
     own, one, two, far = tiles(own_ref), tiles(one_ref), tiles(two_ref), tiles(far_ref)
@@ -341,21 +341,36 @@
         own[4] + above[2] + far[0],
         above[3] + far[1],
     ]
+    for w in range(6):
+        mine_ref[8 * w : 8 * w + 8] = window[w]
+    low_half = lax.broadcasted_iota(jnp.int32, (8, 128), 0) < 4
+    upper, lower = [], []
+    for w in (0, 4):
+        upper.append(jnp.where(low_half, pltpu.roll(window[w], 4, 0), window[w + 1]))
+        lower.append(jnp.where(low_half, window[w], pltpu.roll(window[w + 1], 4, 0)))
+    following = lax.rem(lax.axis_index("gy") + 1, 8)
     for n in range(8):
-        for w in range(6):
-            out_ref[n, 8 * w : 8 * w + 8] = window[w]
-
-
-def field_kernel(g_ref, wxy_ref, wz_ref, nv_ref, field_ref, rows_ref, buf_ref, sems):
+        out_ref[n, 0:8] = window[2]
+        out_ref[n, 8:16] = window[3]
+        for m in range(2):
+            out_ref[n, 16 + 8 * m : 24 + 8 * m] = jnp.where(following == n, upper[m], lower[m])
+
+
+def field_kernel(g_ref, mine_ref, wxy_ref, wz_ref, nv_ref, field_ref, rows_ref, buf_ref, sems):
     me_i, me_j, me_k = coords()
     ni, nj, nk = (lax.axis_size(a) for a in AXES)
     row8 = lax.broadcasted_iota(jnp.int32, (8, 128), 0)
 
     window = []
-    js = [lax.rem(me_j + 7, 8), me_j, lax.rem(me_j + 1, 8)]
+    before, after = lax.rem(me_j + 7, 8), lax.rem(me_j + 1, 8)
     for w in range(6):
-        before, own, after = (g_ref[j, 8 * w : 8 * w + 8] for j in js)
-        window.append(own + jnp.where(row8 < 4, pltpu.roll(before, 4, 0), pltpu.roll(after, 4, 0)))
+        at = 8 * (w - 2) if 2 <= w <= 3 else 16 + 8 * (w // 4)
+        lows, highs = g_ref[before, at : at + 8], g_ref[after, at : at + 8]
+        if w not in (0, 4):
+            lows = pltpu.roll(lows, 4, 0)
+        if w not in (1, 5):
+            highs = pltpu.roll(highs, 4, 0)
+        window.append(mine_ref[8 * w : 8 * w + 8] + jnp.where(row8 < 4, lows, highs))
     coefs = jnp.concatenate(window, axis=0)
     row = lax.broadcasted_iota(jnp.int32, (48, 128), 0)
     lane = lax.broadcasted_iota(jnp.int32, (48, 128), 1)
@@ -385,7 +400,7 @@
         copies.append(copy)
 
     for side in range(2):
-        cols = [g_ref[j, 16 + 8 * side : 24 + 8 * side] for j in range(8)]
+        cols = [g_ref[j, 8 * side : 8 * side + 8] for j in range(8)]
         turned = [pltpu.roll(c, 4, 0) for c in cols]
         tiles = []
         zero = jnp.zeros((8, 128), f32)
@@ -504,18 +519,18 @@
     far = swap(own, "gx", [(0, 2), (1, 3)])
     one = swap(own, "gx", [(0, 1), (2, 3)])
     two = swap(own, "gx", [(1, 2), (3, 0)])
-    (copies,) = call(across_kernel, [((8, 48, 128), f32)], [VMEM] * 4)(own, far, one, two)
+    copies, mine = call(across_kernel, [((8, 32, 128), f32), ((48, 128), f32)], [VMEM] * 4)(own, far, one, two)
     everything = lax.all_to_all(copies, "gy", 0, 0, tiled=True)
 
     nv, field = call(
         field_kernel,
         [((6, 2, 16, 32), f32), ((6, 512, 128), bf16)],
-        [VMEM] * 3,
+        [VMEM] * 4,
         [pltpu.VMEM((2, 40, 128), f32), pltpu.VMEM((6, 512, 128), bf16), pltpu.SemaphoreType.DMA((3,))],
         out_specs=[VMEM, HBM],
         flops=10**8,
         bytes_accessed=10**6,
-    )(everything, exy, ezs)
+    )(everything, mine, exy, ezs)
     nv = jnp.swapaxes(nv.reshape(2, 3, 2, 16, 32), 3, 4)
     return nv, field.reshape(2, 3, 16, 32, 128)
 

time: 45.8 us -> 45.5 us (level)
  the two profiles are of different devices: /device:TPU:0 before, /device:TPU:16 now
where the time goes in v9:
time: 45.5 us; the launch traced here: 45.2 us
  starting transfers between devices  15.5 us (34%)
  blocking collectives  10.6 us (23%)
  waiting for transfers between devices  10.3 us (23%)
  Pallas kernels  7.06 us (16%)
  local copies, waits for them, and re-layouts  1.06 us (2%)
  between operations  0.71 us (2%)
    all_to_all x1, blocking collectives, shards(): everything = lax.all_to_all(copies, 'gy', 0, 0, tiled=True)  10.6 us
    ppermute x5, starting transfers between devices, send(): return lax.ppermute(v, AXES, pairs(sizes, di, dj, dk))  9.73 us
    ppermute x5, waiting for transfers between devices, shards(): lax.ppermute(v, axis, couples + [(b, a) for a, b in couples])  7.59 us
    ppermute x5, starting transfers between devices, shards(): lax.ppermute(v, axis, couples + [(b, a) for a, b in couples])  5.71 us
    pallas_call x2, Pallas kernels, forces(): call(functools.partial(force_kernel, upper), [((40, 128), f32)], [VMEM] *...  4.17 us
    pallas_call x1, Pallas kernels, shards(): call(field_kernel, [((6, 2, 16, 32), f32), ((6, 512, 128), bf16)], [VMEM]...  2.1 us
    ppermute x5, waiting for transfers between devices, send(): return lax.ppermute(v, AXES, pairs(sizes, di, dj, dk))  1.9 us
    unnamed x10, local copies, waits for them, and re-layouts  1.06 us
  transfers between devices with their start and end apart: 11, of which 7 were waited for; matrix products, arithmetic and copies ran while one was open for 0% of the time, Pallas kernels for 6%

profile of v9, /device:TPU:16, one launch (start us, length us, event | category | flops | bytes accessed | tf_op | source)
XLA Modules:
  0.0 45.2 jit_solution(11161682905136902998)
XLA Ops:
  0.6 0.0 copy-start
  0.6 1.0 %copy-done = f32[2,16,32,128]{3,2,1,0:T(8,128)S(1)} copy-done((f32[2,16,32,128]{3,2,1,0:T(8,128)S(1)}, f32[2,16,32,128]{3,2,1,0:T(8,128)}, u32[]{:S(2)}) %copy-start) | copy-done | bytes 524312
  1.7 0.0 copy-start.1
  1.7 0.2 shard_map.59.after_ref
  1.9 0.0 copy-start.3
  1.9 0.1 collective-permute-start
  2.0 1.6 %collective-permute-start.1 = (f32[2,16,8,128]{3,2,1,0:T(8,128)S(1)}, f32[2,16,8,128]{3,2,1,0:T(8,128)S(1)}, u32[]{:S(2)}, u32[]{:S(2)}) collective-permute-start(f32[2,16,8,128]{3,2,1,0:T(8,128)S(1)} %get-tuple-element.30), channel_id=1, source_target_pairs={{0,4},{1,5},{2,6},{3,7},{4,8},{5,9},{6,10},{7,11},{8,12},{9,13},{1... | collective-permute-start | bytes 393224 | tf_op jit(solution)/shard_map/ppermute | solution.py:466
  3.6 1.9 %collective-permute-start.3 = (f32[2,8,32,128]{3,2,1,0:T(8,128)S(1)}, f32[2,8,32,128]{3,2,1,0:T(8,128)S(1)}, u32[]{:S(2)}, u32[]{:S(2)}) collective-permute-start(f32[2,8,32,128]{3,2,1,0:T(8,128)S(1)} %get-tuple-element.31), channel_id=1, source_target_pairs={{0,32},{1,33},{2,34},{3,35},{4,36},{5,37},{6,38},{7,39},{8,40},{9,... | collective-permute-start | bytes 786440 | tf_op jit(solution)/shard_map/ppermute | solution.py:466
  5.5 0.0 copy-done.3
  5.5 0.5 %shard_map.60 = (f32[16,128]{1,0:T(8,128)S(1)}, bf16[80,512]{1,0:T(8,128)(2,1)S(1)}, bf16[128,256]{1,0:T(8,128)(2,1)S(1)}, bf16[256,128]{1,0:T(8,128)(2,1)S(1)}, f32[256,128]{1,0:T(8,128)S(1)}) custom-call(f32[6,2,16,32]{3,2,1,0:T(8,128)S(1)} %bitcast.11), custom_call_target="tpu_custom_call" | custom-call | bytes 1000000 | tf_op jit(solution)/shard_map/pallas_call | solution.py:480
  5.9 0.8 %collective-permute-done.zr_ref = f32[2,32,128]{2,1,0:T(8,128)S(1)} collective-permute-done((f32[2,32,128]{2,1,0:T(8,128)S(1)}, f32[2,32,128]{2,1,0:T(8,128)S(1)}, u32[]{:S(2)}, u32[]{:S(2)}) %collective-permute-start) | collective-permute-done | bytes 32800 | tf_op jit(solution)/shard_map/ppermute | solution.py:475
  6.8 1.5 %collective-permute-start.2 = (f32[2,32,128]{2,1,0:T(8,128)S(1)}, f32[2,32,128]{2,1,0:T(8,128)S(1)}, u32[]{:S(2)}, u32[]{:S(2)}) collective-permute-start(f32[2,32,128]{2,1,0:T(8,128)S(1)} %collective-permute-done.zr_ref), channel_id=1, source_target_pairs={{0,4},{1,5},{2,6},{3,7},{4,8},{5,9},{6,10},{7,11},{8,12},{9,13},{1... | collective-permute-start | bytes 98312 | tf_op jit(solution)/shard_map/ppermute | solution.py:466
  8.3 2.8 %collective-permute-start.4 = (f32[2,9,8,128]{3,2,1,0:T(8,128)S(1)}, f32[2,9,8,128]{3,2,1,0:T(8,128)S(1)}, u32[]{:S(2)}, u32[]{:S(2)}) collective-permute-start(f32[2,9,8,128]{3,2,1,0:T(8,128)S(1)} %bitcast_dynamic-update-slice_fusion), channel_id=1, source_target_pairs={{0,36},{1,37},{2,38},{3,39},{4,40},{5,41},{6,42},{7,43},{8,44},{9,... | collective-permute-start | bytes 221192 | tf_op jit(solution)/shard_map/ppermute | solution.py:466
  11.1 1.9 %collective-permute-start.5 = (f32[2,32,128]{2,1,0:T(8,128)S(1)}, f32[2,32,128]{2,1,0:T(8,128)S(1)}, u32[]{:S(2)}, u32[]{:S(2)}) collective-permute-start(f32[2,32,128]{2,1,0:T(8,128)S(1)} %collective-permute-done.zr_ref), channel_id=1, source_target_pairs={{0,32},{1,33},{2,34},{3,35},{4,36},{5,37},{6,38},{7,39},{8,40},{9,... | collective-permute-start | bytes 98312 | tf_op jit(solution)/shard_map/ppermute | solution.py:466
  13.0 0.0 collective-permute-done.2.yzr_ref
  13.1 0.0 collective-permute-done.1.yr_ref
  13.1 0.0 copy-done.1
  13.1 2.1 %shard_map.62.refs_3_ = f32[40,128]{1,0:T(8,128)S(1)} custom-call(f32[2,16,32,128]{3,2,1,0:T(8,128)S(1)} %copy-done.1, f32[2,32,128]{2,1,0:T(8,128)S(1)} %collective-permute-done.zr_ref, f32[2,16,8,128]{3,2,1,0:T(8,128)S(1)} %collective-permute-done.1.yr_ref, f32[2,32,128]{2,1,0:T(8,128)S(1)} %collective-permute-done.2.yzr_ref, ...), custom_call_target="tpu_custom_call" | custom-call | flops 500000000 | bytes 1000000 | tf_op jit(solution)/shard_map/pallas_call | solution.py:494
  15.2 1.1 %collective-permute-done.5.refs_2_ = f32[2,32,128]{2,1,0:T(8,128)S(1)} collective-permute-done((f32[2,32,128]{2,1,0:T(8,128)S(1)}, f32[2,32,128]{2,1,0:T(8,128)S(1)}, u32[]{:S(2)}, u32[]{:S(2)}) %collective-permute-start.5) | collective-permute-done | bytes 32800 | tf_op jit(solution)/shard_map/ppermute | solution.py:466
  16.3 0.8 %collective-permute-done.4.refs_1_ = f32[2,9,8,128]{3,2,1,0:T(8,128)S(1)} collective-permute-done((f32[2,9,8,128]{3,2,1,0:T(8,128)S(1)}, f32[2,9,8,128]{3,2,1,0:T(8,128)S(1)}, u32[]{:S(2)}, u32[]{:S(2)}) %collective-permute-start.4) | collective-permute-done | bytes 73760 | tf_op jit(solution)/shard_map/ppermute | solution.py:466
  17.1 0.0 collective-permute-done.3.refs_0_
  17.1 2.0 %shard_map.63.mine_ref = f32[40,128]{1,0:T(8,128)S(1)} custom-call(f32[2,16,32,128]{3,2,1,0:T(8,128)S(1)} %copy-done.1, f32[2,32,128]{2,1,0:T(8,128)S(1)} %collective-permute-done.zr_ref, f32[2,16,8,128]{3,2,1,0:T(8,128)S(1)} %collective-permute-done.1.yr_ref, f32[2,32,128]{2,1,0:T(8,128)S(1)} %collective-permute-done.2.yzr_ref, ...), custom_call_target="tpu_custom_call" | custom-call | flops 500000000 | bytes 1000000 | tf_op jit(solution)/shard_map/pallas_call | solution.py:494
  19.1 0.0 copy-start.2
  19.2 1.2 %collective-permute-start.6 = (f32[40,128]{1,0:T(8,128)S(1)}, f32[40,128]{1,0:T(8,128)S(1)}, u32[]{:S(2)}, u32[]{:S(2)}) collective-permute-start(f32[40,128]{1,0:T(8,128)S(1)} %shard_map.63.mine_ref), channel_id=1, source_target_pairs={{1,2},{3,0},{2,1},{0,3},{5,6},{7,4},{6,5},{4,7},{9,10},{11,8},{10,... | collective-permute-start | bytes 61448 | tf_op jit(solution)/shard_map/ppermute | solution.py:515
  20.3 0.4 collective-permute-start.7
  20.7 3.2 %collective-permute-done.6.chip_ref = f32[40,128]{1,0:T(8,128)S(1)} collective-permute-done((f32[40,128]{1,0:T(8,128)S(1)}, f32[40,128]{1,0:T(8,128)S(1)}, u32[]{:S(2)}, u32[]{:S(2)}) %collective-permute-start.6) | collective-permute-done | bytes 20512 | tf_op jit(solution)/shard_map/ppermute | solution.py:515
  23.9 0.0 collective-permute-done.7.core_ref
  23.9 0.1 shard_map.64.own_ref
  24.0 2.5 %collective-permute-start.8 = (f32[40,128]{1,0:T(8,128)S(1)}, f32[40,128]{1,0:T(8,128)S(1)}, u32[]{:S(2)}, u32[]{:S(2)}) collective-permute-start(f32[40,128]{1,0:T(8,128)S(1)} %shard_map.64.own_ref), channel_id=1, source_target_pairs={{0,64},{32,96},{64,0},{96,32},{1,65},{33,97},{65,1},{97,33},{2,66}... | collective-permute-start | bytes 61448 | tf_op jit(solution)/shard_map/ppermute | solution.py:515
  26.5 1.0 %collective-permute-start.9 = (f32[40,128]{1,0:T(8,128)S(1)}, f32[40,128]{1,0:T(8,128)S(1)}, u32[]{:S(2)}, u32[]{:S(2)}) collective-permute-start(f32[40,128]{1,0:T(8,128)S(1)} %shard_map.64.own_ref), channel_id=1, source_target_pairs={{0,32},{64,96},{32,0},{96,64},{1,33},{65,97},{33,1},{97,65},{2,34}... | collective-permute-start | bytes 61448 | tf_op jit(solution)/shard_map/ppermute | solution.py:515
  27.5 0.6 %collective-permute-start.10 = (f32[40,128]{1,0:T(8,128)S(1)}, f32[40,128]{1,0:T(8,128)S(1)}, u32[]{:S(2)}, u32[]{:S(2)}) collective-permute-start(f32[40,128]{1,0:T(8,128)S(1)} %shard_map.64.own_ref), channel_id=1, source_target_pairs={{32,64},{96,0},{64,32},{0,96},{33,65},{97,1},{65,33},{1,97},{34,66... | collective-permute-start | bytes 61448 | tf_op jit(solution)/shard_map/ppermute | solution.py:515
  28.2 1.2 %collective-permute-done.8.far_ref = f32[40,128]{1,0:T(8,128)S(1)} collective-permute-done((f32[40,128]{1,0:T(8,128)S(1)}, f32[40,128]{1,0:T(8,128)S(1)}, u32[]{:S(2)}, u32[]{:S(2)}) %collective-permute-start.8) | collective-permute-done | bytes 20512 | tf_op jit(solution)/shard_map/ppermute | solution.py:515
  29.4 0.9 %collective-permute-done.9.one_ref = f32[40,128]{1,0:T(8,128)S(1)} collective-permute-done((f32[40,128]{1,0:T(8,128)S(1)}, f32[40,128]{1,0:T(8,128)S(1)}, u32[]{:S(2)}, u32[]{:S(2)}) %collective-permute-start.9) | collective-permute-done | bytes 20512 | tf_op jit(solution)/shard_map/ppermute | solution.py:515
  30.3 2.2 %collective-permute-done.10.two_ref = f32[40,128]{1,0:T(8,128)S(1)} collective-permute-done((f32[40,128]{1,0:T(8,128)S(1)}, f32[40,128]{1,0:T(8,128)S(1)}, u32[]{:S(2)}, u32[]{:S(2)}) %collective-permute-start.10) | collective-permute-done | bytes 20512 | tf_op jit(solution)/shard_map/ppermute | solution.py:515
  32.6 0.0 copy-start.4
  32.6 10.6 %all_to_all.5.g_ref = f32[8,32,128]{2,1,0:T(8,128)S(1)} all-to-all(f32[8,32,128]{2,1,0:T(8,128)S(1)} %get-tuple-element.38), channel_id=1, replica_groups=mesh['gx'=4,'gy'=8,'gz'=4] {'gy'}, dimensions={0} | all-to-all | bytes 262144 | tf_op jit(solution)/shard_map/all_to_all | solution.py:523
  43.1 0.0 copy-done.2
  43.1 0.0 copy-done.4
  43.1 2.1 %shard_map.66 = (f32[6,2,16,32]{3,2,1,0:T(8,128)}, bf16[6,512,128]{2,1,0:T(8,128)(2,1)}) custom-call(f32[8,32,128]{2,1,0:T(8,128)S(1)} %all_to_all.5.g_ref, f32[48,128]{1,0:T(8,128)S(1)} %get-tuple-element.39.mine_ref, bf16[512,144]{1,0:T(8,128)(2,1)S(1)} %copy-done.2, bf16[128,256]{1,0:T(8,128)(2,1)S(1)} %copy-done.4), custom_call_target="tpu_custom_call" | custom-call | flops 100000000 | bytes 1000000 | tf_op jit(solution)/shard_map/pallas_call | solution.py:525
  (3 shorter events, 0.1 us)
Async XLA Ops:
  0.6 1.0 %copy-start = (f32[2,16,32,128]{3,2,1,0:T(8,128)S(1)}, f32[2,16,32,128]{3,2,1,0:T(8,128)}, u32[]{:S(2)}) copy-start(f32[2,16,32,128]{3,2,1,0:T(8,128)} %own_ref.3) | copy-start | bytes 1572868
  1.7 11.4 %copy-start.1 = (f32[2,16,32,128]{3,2,1,0:T(8,128)S(1)}, f32[2,16,32,128]{3,2,1,0:T(8,128)}, u32[]{:S(2)}) copy-start(f32[2,16,32,128]{3,2,1,0:T(8,128)} %own_ref.3) | copy-start | bytes 1572868
  1.9 3.6 %copy-start.3 = (f32[2,3,2,32,16]{3,4,2,1,0:T(8,128)S(1)}, f32[2,3,2,32,16]{3,4,2,1,0:T(8,128)}, u32[]{:S(2)}) copy-start(f32[2,3,2,32,16]{3,4,2,1,0:T(8,128)} %param.7) | copy-start | bytes 73732
  1.9 4.9 %collective-permute-start = (f32[2,32,128]{2,1,0:T(8,128)S(1)}, f32[2,32,128]{2,1,0:T(8,128)S(1)}, u32[]{:S(2)}, u32[]{:S(2)}) collective-permute-start(f32[2,32,128]{2,1,0:T(8,128)S(1)} %shard_map.59.after_ref), channel_id=1, source_target_pairs={{0,1},{1,2},{2,3},{3,0},{4,5},{5,6},{6,7},{7,4},{8,9},{9,10},{10,1... | collective-permute-start | bytes 98312 | tf_op jit(solution)/shard_map/ppermute | solution.py:475
  2.0 11.1 %collective-permute-start.1 = (f32[2,16,8,128]{3,2,1,0:T(8,128)S(1)}, f32[2,16,8,128]{3,2,1,0:T(8,128)S(1)}, u32[]{:S(2)}, u32[]{:S(2)}) collective-permute-start(f32[2,16,8,128]{3,2,1,0:T(8,128)S(1)} %get-tuple-element.30), channel_id=1, source_target_pairs={{0,4},{1,5},{2,6},{3,7},{4,8},{5,9},{6,10},{7,11},{8,12},{9,13},{1... | collective-permute-start | bytes 393224 | tf_op jit(solution)/shard_map/ppermute | solution.py:466
  3.6 13.5 %collective-permute-start.3 = (f32[2,8,32,128]{3,2,1,0:T(8,128)S(1)}, f32[2,8,32,128]{3,2,1,0:T(8,128)S(1)}, u32[]{:S(2)}, u32[]{:S(2)}) collective-permute-start(f32[2,8,32,128]{3,2,1,0:T(8,128)S(1)} %get-tuple-element.31), channel_id=1, source_target_pairs={{0,32},{1,33},{2,34},{3,35},{4,36},{5,37},{6,38},{7,39},{8,40},{9,... | collective-permute-start | bytes 786440 | tf_op jit(solution)/shard_map/ppermute | solution.py:466
  6.8 6.3 %collective-permute-start.2 = (f32[2,32,128]{2,1,0:T(8,128)S(1)}, f32[2,32,128]{2,1,0:T(8,128)S(1)}, u32[]{:S(2)}, u32[]{:S(2)}) collective-permute-start(f32[2,32,128]{2,1,0:T(8,128)S(1)} %collective-permute-done.zr_ref), channel_id=1, source_target_pairs={{0,4},{1,5},{2,6},{3,7},{4,8},{5,9},{6,10},{7,11},{8,12},{9,13},{1... | collective-permute-start | bytes 98312 | tf_op jit(solution)/shard_map/ppermute | solution.py:466
  8.3 8.8 %collective-permute-start.4 = (f32[2,9,8,128]{3,2,1,0:T(8,128)S(1)}, f32[2,9,8,128]{3,2,1,0:T(8,128)S(1)}, u32[]{:S(2)}, u32[]{:S(2)}) collective-permute-start(f32[2,9,8,128]{3,2,1,0:T(8,128)S(1)} %bitcast_dynamic-update-slice_fusion), channel_id=1, source_target_pairs={{0,36},{1,37},{2,38},{3,39},{4,40},{5,41},{6,42},{7,43},{8,44},{9,... | collective-permute-start | bytes 221192 | tf_op jit(solution)/shard_map/ppermute | solution.py:466
  11.1 5.1 %collective-permute-start.5 = (f32[2,32,128]{2,1,0:T(8,128)S(1)}, f32[2,32,128]{2,1,0:T(8,128)S(1)}, u32[]{:S(2)}, u32[]{:S(2)}) collective-permute-start(f32[2,32,128]{2,1,0:T(8,128)S(1)} %collective-permute-done.zr_ref), channel_id=1, source_target_pairs={{0,32},{1,33},{2,34},{3,35},{4,36},{5,37},{6,38},{7,39},{8,40},{9,... | collective-permute-start | bytes 98312 | tf_op jit(solution)/shard_map/ppermute | solution.py:466
  19.1 24.0 %copy-start.2 = (bf16[512,144]{1,0:T(8,128)(2,1)S(1)}, bf16[512,144]{1,0:T(8,128)(2,1)}, u32[]{:S(2)}) copy-start(bf16[512,144]{1,0:T(8,128)(2,1)} %constant.33.clone.wxy_ref) | copy-start | bytes 442372
  19.2 4.8 %collective-permute-start.6 = (f32[40,128]{1,0:T(8,128)S(1)}, f32[40,128]{1,0:T(8,128)S(1)}, u32[]{:S(2)}, u32[]{:S(2)}) collective-permute-start(f32[40,128]{1,0:T(8,128)S(1)} %shard_map.63.mine_ref), channel_id=1, source_target_pairs={{1,2},{3,0},{2,1},{0,3},{5,6},{7,4},{6,5},{4,7},{9,10},{11,8},{10,... | collective-permute-start | bytes 61448 | tf_op jit(solution)/shard_map/ppermute | solution.py:515
  20.3 3.6 %collective-permute-start.7 = (f32[40,128]{1,0:T(8,128)S(1)}, f32[40,128]{1,0:T(8,128)S(1)}, u32[]{:S(2)}, u32[]{:S(2)}) collective-permute-start(f32[40,128]{1,0:T(8,128)S(1)} %shard_map.63.mine_ref), channel_id=1, source_target_pairs={{0,1},{2,3},{1,0},{3,2},{4,5},{6,7},{5,4},{7,6},{8,9},{10,11},{9,8... | collective-permute-start | bytes 61448 | tf_op jit(solution)/shard_map/ppermute | solution.py:515
  24.0 5.3 %collective-permute-start.8 = (f32[40,128]{1,0:T(8,128)S(1)}, f32[40,128]{1,0:T(8,128)S(1)}, u32[]{:S(2)}, u32[]{:S(2)}) collective-permute-start(f32[40,128]{1,0:T(8,128)S(1)} %shard_map.64.own_ref), channel_id=1, source_target_pairs={{0,64},{32,96},{64,0},{96,32},{1,65},{33,97},{65,1},{97,33},{2,66}... | collective-permute-start | bytes 61448 | tf_op jit(solution)/shard_map/ppermute | solution.py:515
  26.5 3.8 %collective-permute-start.9 = (f32[40,128]{1,0:T(8,128)S(1)}, f32[40,128]{1,0:T(8,128)S(1)}, u32[]{:S(2)}, u32[]{:S(2)}) collective-permute-start(f32[40,128]{1,0:T(8,128)S(1)} %shard_map.64.own_ref), channel_id=1, source_target_pairs={{0,32},{64,96},{32,0},{96,64},{1,33},{65,97},{33,1},{97,65},{2,34}... | collective-permute-start | bytes 61448 | tf_op jit(solution)/shard_map/ppermute | solution.py:515
  27.5 5.0 %collective-permute-start.10 = (f32[40,128]{1,0:T(8,128)S(1)}, f32[40,128]{1,0:T(8,128)S(1)}, u32[]{:S(2)}, u32[]{:S(2)}) collective-permute-start(f32[40,128]{1,0:T(8,128)S(1)} %shard_map.64.own_ref), channel_id=1, source_target_pairs={{32,64},{96,0},{64,32},{0,96},{33,65},{97,1},{65,33},{1,97},{34,66... | collective-permute-start | bytes 61448 | tf_op jit(solution)/shard_map/ppermute | solution.py:515
  32.6 10.6 %copy-start.4 = (bf16[128,256]{1,0:T(8,128)(2,1)S(1)}, bf16[128,256]{1,0:T(8,128)(2,1)}, u32[]{:S(2)}) copy-start(bf16[128,256]{1,0:T(8,128)(2,1)} %constant.34.clone.wz_ref) | copy-start | bytes 196612

commit v10 on v9

--- a/solution.py
+++ b/solution.py
@@ -356,7 +356,7 @@
             out_ref[n, 16 + 8 * m : 24 + 8 * m] = jnp.where(following == n, upper[m], lower[m])
 
 
-def field_kernel(g_ref, mine_ref, wxy_ref, wz_ref, nv_ref, field_ref, rows_ref, buf_ref, sems):
+def field_kernel(g_ref, mine_ref, wxy_ref, wz_ref, nv_ref, field_ref, rows_ref, buf_ref, own_ref, sems):
     me_i, me_j, me_k = coords()
     ni, nj, nk = (lax.axis_size(a) for a in AXES)
     row8 = lax.broadcasted_iota(jnp.int32, (8, 128), 0)
@@ -414,7 +414,10 @@
             rows_ref[side, 8 * n : 8 * n + 8] = tiles[n]
         block = jnp.transpose(rows_ref[side, 2:34])
         for c in range(6):
-            nv_ref[c, side] = block[20 * c + 2 : 20 * c + 18]
+            own_ref[c, side] = block[20 * c + 2 : 20 * c + 18]
+    copy = pltpu.make_async_copy(own_ref, nv_ref, sems.at[3])
+    copy.start()
+    copies.append(copy)
     for copy in copies:
         copy.wait()
 
@@ -526,8 +529,8 @@
         field_kernel,
         [((6, 2, 16, 32), f32), ((6, 512, 128), bf16)],
         [VMEM] * 4,
-        [pltpu.VMEM((2, 40, 128), f32), pltpu.VMEM((6, 512, 128), bf16), pltpu.SemaphoreType.DMA((3,))],
-        out_specs=[VMEM, HBM],
+        [pltpu.VMEM((2, 40, 128), f32), pltpu.VMEM((6, 512, 128), bf16), pltpu.VMEM((6, 2, 16, 32), f32), pltpu.SemaphoreType.DMA((4,))],
+        out_specs=[HBM, HBM],
         flops=10**8,
         bytes_accessed=10**6,
     )(everything, mine, exy, ezs)

time: 45.5 us -> 44.9 us (0.987)
  Pallas kernels: 7.06 us -> 6.45 us
    pallas_call x1, Pallas kernels: 2.1 us -> 1.49 us  [shards(): call(field_kernel, [((6, 2, 16, 32), f32), ((6, 512, 128), bf16)], [VMEM]...]
where the time goes in v10:
time: 44.9 us; the launch traced here: 44.6 us
  starting transfers between devices  15.5 us (35%)
  blocking collectives  10.6 us (24%)
  waiting for transfers between devices  10.3 us (23%)
  Pallas kernels  6.45 us (14%)
  local copies, waits for them, and re-layouts  1.06 us (2%)
  between operations  0.71 us (2%)
    all_to_all x1, blocking collectives, shards(): everything = lax.all_to_all(copies, 'gy', 0, 0, tiled=True)  10.6 us
    ppermute x5, starting transfers between devices, send(): return lax.ppermute(v, AXES, pairs(sizes, di, dj, dk))  9.73 us
    ppermute x5, waiting for transfers between devices, shards(): lax.ppermute(v, axis, couples + [(b, a) for a, b in couples])  7.59 us
    ppermute x5, starting transfers between devices, shards(): lax.ppermute(v, axis, couples + [(b, a) for a, b in couples])  5.71 us
    pallas_call x2, Pallas kernels, forces(): call(functools.partial(force_kernel, upper), [((40, 128), f32)], [VMEM] *...  4.17 us
    ppermute x5, waiting for transfers between devices, send(): return lax.ppermute(v, AXES, pairs(sizes, di, dj, dk))  1.9 us
    pallas_call x1, Pallas kernels, shards(): call(field_kernel, [((6, 2, 16, 32), f32), ((6, 512, 128), bf16)], [VMEM]...  1.49 us
    unnamed x10, local copies, waits for them, and re-layouts  1.06 us
  transfers between devices with their start and end apart: 11, of which 7 were waited for; matrix products, arithmetic and copies ran while one was open for 0% of the time, Pallas kernels for 6%

profile of v10, /device:TPU:16, one launch (start us, length us, event | category | flops | bytes accessed | tf_op | source)
XLA Modules:
  0.0 44.6 jit_solution(11426519824328633586)
XLA Ops:
  0.6 0.0 copy-start
  0.6 1.0 %copy-done = f32[2,16,32,128]{3,2,1,0:T(8,128)S(1)} copy-done((f32[2,16,32,128]{3,2,1,0:T(8,128)S(1)}, f32[2,16,32,128]{3,2,1,0:T(8,128)}, u32[]{:S(2)}) %copy-start) | copy-done | bytes 524312
  1.7 0.0 copy-start.1
  1.7 0.2 shard_map.59.after_ref
  1.9 0.0 copy-start.3
  1.9 0.1 collective-permute-start
  2.0 1.6 %collective-permute-start.1 = (f32[2,16,8,128]{3,2,1,0:T(8,128)S(1)}, f32[2,16,8,128]{3,2,1,0:T(8,128)S(1)}, u32[]{:S(2)}, u32[]{:S(2)}) collective-permute-start(f32[2,16,8,128]{3,2,1,0:T(8,128)S(1)} %get-tuple-element.30), channel_id=1, source_target_pairs={{0,4},{1,5},{2,6},{3,7},{4,8},{5,9},{6,10},{7,11},{8,12},{9,13},{1... | collective-permute-start | bytes 393224 | tf_op jit(solution)/shard_map/ppermute | solution.py:469
  3.6 1.9 %collective-permute-start.3 = (f32[2,8,32,128]{3,2,1,0:T(8,128)S(1)}, f32[2,8,32,128]{3,2,1,0:T(8,128)S(1)}, u32[]{:S(2)}, u32[]{:S(2)}) collective-permute-start(f32[2,8,32,128]{3,2,1,0:T(8,128)S(1)} %get-tuple-element.31), channel_id=1, source_target_pairs={{0,32},{1,33},{2,34},{3,35},{4,36},{5,37},{6,38},{7,39},{8,40},{9,... | collective-permute-start | bytes 786440 | tf_op jit(solution)/shard_map/ppermute | solution.py:469
  5.5 0.0 copy-done.3
  5.5 0.5 %shard_map.60 = (f32[16,128]{1,0:T(8,128)S(1)}, bf16[80,512]{1,0:T(8,128)(2,1)S(1)}, bf16[128,256]{1,0:T(8,128)(2,1)S(1)}, bf16[256,128]{1,0:T(8,128)(2,1)S(1)}, f32[256,128]{1,0:T(8,128)S(1)}) custom-call(f32[6,2,16,32]{3,2,1,0:T(8,128)S(1)} %bitcast.11), custom_call_target="tpu_custom_call" | custom-call | bytes 1000000 | tf_op jit(solution)/shard_map/pallas_call | solution.py:483
  5.9 0.8 %collective-permute-done.zr_ref = f32[2,32,128]{2,1,0:T(8,128)S(1)} collective-permute-done((f32[2,32,128]{2,1,0:T(8,128)S(1)}, f32[2,32,128]{2,1,0:T(8,128)S(1)}, u32[]{:S(2)}, u32[]{:S(2)}) %collective-permute-start) | collective-permute-done | bytes 32800 | tf_op jit(solution)/shard_map/ppermute | solution.py:478
  6.8 1.5 %collective-permute-start.2 = (f32[2,32,128]{2,1,0:T(8,128)S(1)}, f32[2,32,128]{2,1,0:T(8,128)S(1)}, u32[]{:S(2)}, u32[]{:S(2)}) collective-permute-start(f32[2,32,128]{2,1,0:T(8,128)S(1)} %collective-permute-done.zr_ref), channel_id=1, source_target_pairs={{0,4},{1,5},{2,6},{3,7},{4,8},{5,9},{6,10},{7,11},{8,12},{9,13},{1... | collective-permute-start | bytes 98312 | tf_op jit(solution)/shard_map/ppermute | solution.py:469
  8.3 2.8 %collective-permute-start.4 = (f32[2,9,8,128]{3,2,1,0:T(8,128)S(1)}, f32[2,9,8,128]{3,2,1,0:T(8,128)S(1)}, u32[]{:S(2)}, u32[]{:S(2)}) collective-permute-start(f32[2,9,8,128]{3,2,1,0:T(8,128)S(1)} %bitcast_dynamic-update-slice_fusion), channel_id=1, source_target_pairs={{0,36},{1,37},{2,38},{3,39},{4,40},{5,41},{6,42},{7,43},{8,44},{9,... | collective-permute-start | bytes 221192 | tf_op jit(solution)/shard_map/ppermute | solution.py:469
  11.1 1.9 %collective-permute-start.5 = (f32[2,32,128]{2,1,0:T(8,128)S(1)}, f32[2,32,128]{2,1,0:T(8,128)S(1)}, u32[]{:S(2)}, u32[]{:S(2)}) collective-permute-start(f32[2,32,128]{2,1,0:T(8,128)S(1)} %collective-permute-done.zr_ref), channel_id=1, source_target_pairs={{0,32},{1,33},{2,34},{3,35},{4,36},{5,37},{6,38},{7,39},{8,40},{9,... | collective-permute-start | bytes 98312 | tf_op jit(solution)/shard_map/ppermute | solution.py:469
  13.0 0.0 collective-permute-done.2.yzr_ref
  13.1 0.0 collective-permute-done.1.yr_ref
  13.1 0.0 copy-done.1
  13.1 2.1 %shard_map.62.refs_3_ = f32[40,128]{1,0:T(8,128)S(1)} custom-call(f32[2,16,32,128]{3,2,1,0:T(8,128)S(1)} %copy-done.1, f32[2,32,128]{2,1,0:T(8,128)S(1)} %collective-permute-done.zr_ref, f32[2,16,8,128]{3,2,1,0:T(8,128)S(1)} %collective-permute-done.1.yr_ref, f32[2,32,128]{2,1,0:T(8,128)S(1)} %collective-permute-done.2.yzr_ref, ...), custom_call_target="tpu_custom_call" | custom-call | flops 500000000 | bytes 1000000 | tf_op jit(solution)/shard_map/pallas_call | solution.py:497
  15.2 1.1 %collective-permute-done.5.refs_2_ = f32[2,32,128]{2,1,0:T(8,128)S(1)} collective-permute-done((f32[2,32,128]{2,1,0:T(8,128)S(1)}, f32[2,32,128]{2,1,0:T(8,128)S(1)}, u32[]{:S(2)}, u32[]{:S(2)}) %collective-permute-start.5) | collective-permute-done | bytes 32800 | tf_op jit(solution)/shard_map/ppermute | solution.py:469
  16.3 0.8 %collective-permute-done.4.refs_1_ = f32[2,9,8,128]{3,2,1,0:T(8,128)S(1)} collective-permute-done((f32[2,9,8,128]{3,2,1,0:T(8,128)S(1)}, f32[2,9,8,128]{3,2,1,0:T(8,128)S(1)}, u32[]{:S(2)}, u32[]{:S(2)}) %collective-permute-start.4) | collective-permute-done | bytes 73760 | tf_op jit(solution)/shard_map/ppermute | solution.py:469
  17.1 0.0 collective-permute-done.3.refs_0_
  17.1 2.0 %shard_map.63.mine_ref = f32[40,128]{1,0:T(8,128)S(1)} custom-call(f32[2,16,32,128]{3,2,1,0:T(8,128)S(1)} %copy-done.1, f32[2,32,128]{2,1,0:T(8,128)S(1)} %collective-permute-done.zr_ref, f32[2,16,8,128]{3,2,1,0:T(8,128)S(1)} %collective-permute-done.1.yr_ref, f32[2,32,128]{2,1,0:T(8,128)S(1)} %collective-permute-done.2.yzr_ref, ...), custom_call_target="tpu_custom_call" | custom-call | flops 500000000 | bytes 1000000 | tf_op jit(solution)/shard_map/pallas_call | solution.py:497
  19.1 0.0 copy-start.2
  19.2 1.2 %collective-permute-start.6 = (f32[40,128]{1,0:T(8,128)S(1)}, f32[40,128]{1,0:T(8,128)S(1)}, u32[]{:S(2)}, u32[]{:S(2)}) collective-permute-start(f32[40,128]{1,0:T(8,128)S(1)} %shard_map.63.mine_ref), channel_id=1, source_target_pairs={{1,2},{3,0},{2,1},{0,3},{5,6},{7,4},{6,5},{4,7},{9,10},{11,8},{10,... | collective-permute-start | bytes 61448 | tf_op jit(solution)/shard_map/ppermute | solution.py:518
  20.3 0.4 collective-permute-start.7
  20.7 3.2 %collective-permute-done.6.chip_ref = f32[40,128]{1,0:T(8,128)S(1)} collective-permute-done((f32[40,128]{1,0:T(8,128)S(1)}, f32[40,128]{1,0:T(8,128)S(1)}, u32[]{:S(2)}, u32[]{:S(2)}) %collective-permute-start.6) | collective-permute-done | bytes 20512 | tf_op jit(solution)/shard_map/ppermute | solution.py:518
  23.9 0.0 collective-permute-done.7.core_ref
  23.9 0.1 shard_map.64.own_ref
  24.0 2.5 %collective-permute-start.8 = (f32[40,128]{1,0:T(8,128)S(1)}, f32[40,128]{1,0:T(8,128)S(1)}, u32[]{:S(2)}, u32[]{:S(2)}) collective-permute-start(f32[40,128]{1,0:T(8,128)S(1)} %shard_map.64.own_ref), channel_id=1, source_target_pairs={{0,64},{32,96},{64,0},{96,32},{1,65},{33,97},{65,1},{97,33},{2,66}... | collective-permute-start | bytes 61448 | tf_op jit(solution)/shard_map/ppermute | solution.py:518
  26.5 1.0 %collective-permute-start.9 = (f32[40,128]{1,0:T(8,128)S(1)}, f32[40,128]{1,0:T(8,128)S(1)}, u32[]{:S(2)}, u32[]{:S(2)}) collective-permute-start(f32[40,128]{1,0:T(8,128)S(1)} %shard_map.64.own_ref), channel_id=1, source_target_pairs={{0,32},{64,96},{32,0},{96,64},{1,33},{65,97},{33,1},{97,65},{2,34}... | collective-permute-start | bytes 61448 | tf_op jit(solution)/shard_map/ppermute | solution.py:518
  27.5 0.6 %collective-permute-start.10 = (f32[40,128]{1,0:T(8,128)S(1)}, f32[40,128]{1,0:T(8,128)S(1)}, u32[]{:S(2)}, u32[]{:S(2)}) collective-permute-start(f32[40,128]{1,0:T(8,128)S(1)} %shard_map.64.own_ref), channel_id=1, source_target_pairs={{32,64},{96,0},{64,32},{0,96},{33,65},{97,1},{65,33},{1,97},{34,66... | collective-permute-start | bytes 61448 | tf_op jit(solution)/shard_map/ppermute | solution.py:518
  28.2 1.2 %collective-permute-done.8.far_ref = f32[40,128]{1,0:T(8,128)S(1)} collective-permute-done((f32[40,128]{1,0:T(8,128)S(1)}, f32[40,128]{1,0:T(8,128)S(1)}, u32[]{:S(2)}, u32[]{:S(2)}) %collective-permute-start.8) | collective-permute-done | bytes 20512 | tf_op jit(solution)/shard_map/ppermute | solution.py:518
  29.4 0.9 %collective-permute-done.9.one_ref = f32[40,128]{1,0:T(8,128)S(1)} collective-permute-done((f32[40,128]{1,0:T(8,128)S(1)}, f32[40,128]{1,0:T(8,128)S(1)}, u32[]{:S(2)}, u32[]{:S(2)}) %collective-permute-start.9) | collective-permute-done | bytes 20512 | tf_op jit(solution)/shard_map/ppermute | solution.py:518
  30.3 2.2 %collective-permute-done.10.two_ref = f32[40,128]{1,0:T(8,128)S(1)} collective-permute-done((f32[40,128]{1,0:T(8,128)S(1)}, f32[40,128]{1,0:T(8,128)S(1)}, u32[]{:S(2)}, u32[]{:S(2)}) %collective-permute-start.10) | collective-permute-done | bytes 20512 | tf_op jit(solution)/shard_map/ppermute | solution.py:518
  32.6 0.0 copy-start.4
  32.6 10.6 %all_to_all.5.g_ref = f32[8,32,128]{2,1,0:T(8,128)S(1)} all-to-all(f32[8,32,128]{2,1,0:T(8,128)S(1)} %get-tuple-element.38), channel_id=1, replica_groups=mesh['gx'=4,'gy'=8,'gz'=4] {'gy'}, dimensions={0} | all-to-all | bytes 262144 | tf_op jit(solution)/shard_map/all_to_all | solution.py:526
  43.1 0.0 copy-done.2
  43.1 0.0 copy-done.4
  43.1 1.5 %shard_map.66 = (f32[6,2,16,32]{3,2,1,0:T(8,128)}, bf16[6,512,128]{2,1,0:T(8,128)(2,1)}) custom-call(f32[8,32,128]{2,1,0:T(8,128)S(1)} %all_to_all.5.g_ref, f32[48,128]{1,0:T(8,128)S(1)} %get-tuple-element.39.mine_ref, bf16[512,144]{1,0:T(8,128)(2,1)S(1)} %copy-done.2, bf16[128,256]{1,0:T(8,128)(2,1)S(1)} %copy-done.4), custom_call_target="tpu_custom_call" | custom-call | flops 100000000 | bytes 1000000 | tf_op jit(solution)/shard_map/pallas_call | solution.py:528
  (3 shorter events, 0.1 us)
Async XLA Ops:
  0.6 1.0 %copy-start = (f32[2,16,32,128]{3,2,1,0:T(8,128)S(1)}, f32[2,16,32,128]{3,2,1,0:T(8,128)}, u32[]{:S(2)}) copy-start(f32[2,16,32,128]{3,2,1,0:T(8,128)} %own_ref.3) | copy-start | bytes 1572868
  1.7 11.4 %copy-start.1 = (f32[2,16,32,128]{3,2,1,0:T(8,128)S(1)}, f32[2,16,32,128]{3,2,1,0:T(8,128)}, u32[]{:S(2)}) copy-start(f32[2,16,32,128]{3,2,1,0:T(8,128)} %own_ref.3) | copy-start | bytes 1572868
  1.9 3.6 %copy-start.3 = (f32[2,3,2,32,16]{3,4,2,1,0:T(8,128)S(1)}, f32[2,3,2,32,16]{3,4,2,1,0:T(8,128)}, u32[]{:S(2)}) copy-start(f32[2,3,2,32,16]{3,4,2,1,0:T(8,128)} %param.7) | copy-start | bytes 73732
  1.9 4.9 %collective-permute-start = (f32[2,32,128]{2,1,0:T(8,128)S(1)}, f32[2,32,128]{2,1,0:T(8,128)S(1)}, u32[]{:S(2)}, u32[]{:S(2)}) collective-permute-start(f32[2,32,128]{2,1,0:T(8,128)S(1)} %shard_map.59.after_ref), channel_id=1, source_target_pairs={{0,1},{1,2},{2,3},{3,0},{4,5},{5,6},{6,7},{7,4},{8,9},{9,10},{10,1... | collective-permute-start | bytes 98312 | tf_op jit(solution)/shard_map/ppermute | solution.py:478
  2.0 11.1 %collective-permute-start.1 = (f32[2,16,8,128]{3,2,1,0:T(8,128)S(1)}, f32[2,16,8,128]{3,2,1,0:T(8,128)S(1)}, u32[]{:S(2)}, u32[]{:S(2)}) collective-permute-start(f32[2,16,8,128]{3,2,1,0:T(8,128)S(1)} %get-tuple-element.30), channel_id=1, source_target_pairs={{0,4},{1,5},{2,6},{3,7},{4,8},{5,9},{6,10},{7,11},{8,12},{9,13},{1... | collective-permute-start | bytes 393224 | tf_op jit(solution)/shard_map/ppermute | solution.py:469
  3.6 13.5 %collective-permute-start.3 = (f32[2,8,32,128]{3,2,1,0:T(8,128)S(1)}, f32[2,8,32,128]{3,2,1,0:T(8,128)S(1)}, u32[]{:S(2)}, u32[]{:S(2)}) collective-permute-start(f32[2,8,32,128]{3,2,1,0:T(8,128)S(1)} %get-tuple-element.31), channel_id=1, source_target_pairs={{0,32},{1,33},{2,34},{3,35},{4,36},{5,37},{6,38},{7,39},{8,40},{9,... | collective-permute-start | bytes 786440 | tf_op jit(solution)/shard_map/ppermute | solution.py:469
  6.8 6.3 %collective-permute-start.2 = (f32[2,32,128]{2,1,0:T(8,128)S(1)}, f32[2,32,128]{2,1,0:T(8,128)S(1)}, u32[]{:S(2)}, u32[]{:S(2)}) collective-permute-start(f32[2,32,128]{2,1,0:T(8,128)S(1)} %collective-permute-done.zr_ref), channel_id=1, source_target_pairs={{0,4},{1,5},{2,6},{3,7},{4,8},{5,9},{6,10},{7,11},{8,12},{9,13},{1... | collective-permute-start | bytes 98312 | tf_op jit(solution)/shard_map/ppermute | solution.py:469
  8.3 8.8 %collective-permute-start.4 = (f32[2,9,8,128]{3,2,1,0:T(8,128)S(1)}, f32[2,9,8,128]{3,2,1,0:T(8,128)S(1)}, u32[]{:S(2)}, u32[]{:S(2)}) collective-permute-start(f32[2,9,8,128]{3,2,1,0:T(8,128)S(1)} %bitcast_dynamic-update-slice_fusion), channel_id=1, source_target_pairs={{0,36},{1,37},{2,38},{3,39},{4,40},{5,41},{6,42},{7,43},{8,44},{9,... | collective-permute-start | bytes 221192 | tf_op jit(solution)/shard_map/ppermute | solution.py:469
  11.1 5.1 %collective-permute-start.5 = (f32[2,32,128]{2,1,0:T(8,128)S(1)}, f32[2,32,128]{2,1,0:T(8,128)S(1)}, u32[]{:S(2)}, u32[]{:S(2)}) collective-permute-start(f32[2,32,128]{2,1,0:T(8,128)S(1)} %collective-permute-done.zr_ref), channel_id=1, source_target_pairs={{0,32},{1,33},{2,34},{3,35},{4,36},{5,37},{6,38},{7,39},{8,40},{9,... | collective-permute-start | bytes 98312 | tf_op jit(solution)/shard_map/ppermute | solution.py:469
  19.1 24.0 %copy-start.2 = (bf16[512,144]{1,0:T(8,128)(2,1)S(1)}, bf16[512,144]{1,0:T(8,128)(2,1)}, u32[]{:S(2)}) copy-start(bf16[512,144]{1,0:T(8,128)(2,1)} %constant.33.clone.wxy_ref) | copy-start | bytes 442372
  19.2 4.8 %collective-permute-start.6 = (f32[40,128]{1,0:T(8,128)S(1)}, f32[40,128]{1,0:T(8,128)S(1)}, u32[]{:S(2)}, u32[]{:S(2)}) collective-permute-start(f32[40,128]{1,0:T(8,128)S(1)} %shard_map.63.mine_ref), channel_id=1, source_target_pairs={{1,2},{3,0},{2,1},{0,3},{5,6},{7,4},{6,5},{4,7},{9,10},{11,8},{10,... | collective-permute-start | bytes 61448 | tf_op jit(solution)/shard_map/ppermute | solution.py:518
  20.3 3.6 %collective-permute-start.7 = (f32[40,128]{1,0:T(8,128)S(1)}, f32[40,128]{1,0:T(8,128)S(1)}, u32[]{:S(2)}, u32[]{:S(2)}) collective-permute-start(f32[40,128]{1,0:T(8,128)S(1)} %shard_map.63.mine_ref), channel_id=1, source_target_pairs={{0,1},{2,3},{1,0},{3,2},{4,5},{6,7},{5,4},{7,6},{8,9},{10,11},{9,8... | collective-permute-start | bytes 61448 | tf_op jit(solution)/shard_map/ppermute | solution.py:518
  24.0 5.3 %collective-permute-start.8 = (f32[40,128]{1,0:T(8,128)S(1)}, f32[40,128]{1,0:T(8,128)S(1)}, u32[]{:S(2)}, u32[]{:S(2)}) collective-permute-start(f32[40,128]{1,0:T(8,128)S(1)} %shard_map.64.own_ref), channel_id=1, source_target_pairs={{0,64},{32,96},{64,0},{96,32},{1,65},{33,97},{65,1},{97,33},{2,66}... | collective-permute-start | bytes 61448 | tf_op jit(solution)/shard_map/ppermute | solution.py:518
  26.5 3.8 %collective-permute-start.9 = (f32[40,128]{1,0:T(8,128)S(1)}, f32[40,128]{1,0:T(8,128)S(1)}, u32[]{:S(2)}, u32[]{:S(2)}) collective-permute-start(f32[40,128]{1,0:T(8,128)S(1)} %shard_map.64.own_ref), channel_id=1, source_target_pairs={{0,32},{64,96},{32,0},{96,64},{1,33},{65,97},{33,1},{97,65},{2,34}... | collective-permute-start | bytes 61448 | tf_op jit(solution)/shard_map/ppermute | solution.py:518
  27.5 5.0 %collective-permute-start.10 = (f32[40,128]{1,0:T(8,128)S(1)}, f32[40,128]{1,0:T(8,128)S(1)}, u32[]{:S(2)}, u32[]{:S(2)}) collective-permute-start(f32[40,128]{1,0:T(8,128)S(1)} %shard_map.64.own_ref), channel_id=1, source_target_pairs={{32,64},{96,0},{64,32},{0,96},{33,65},{97,1},{65,33},{1,97},{34,66... | collective-permute-start | bytes 61448 | tf_op jit(solution)/shard_map/ppermute | solution.py:518
  32.6 10.6 %copy-start.4 = (bf16[128,256]{1,0:T(8,128)(2,1)S(1)}, bf16[128,256]{1,0:T(8,128)(2,1)}, u32[]{:S(2)}) copy-start(bf16[128,256]{1,0:T(8,128)(2,1)} %constant.34.clone.wz_ref) | copy-start | bytes 196612

commit v11 on v10

--- a/solution.py
+++ b/solution.py
@@ -157,9 +157,11 @@
 def force_kernel(upper, own_ref, zr_ref, yr_ref, yzr_ref, *refs):
     if upper:
         base_ref, *refs = refs
+        wxy_ref, wz_ref, xsum_ref, zsum_ref, out_ref, vown_ref, dzown_ref, xown_ref, hown_ref, *refs = refs
     else:
-        xr_ref, xyr_ref, xzr_ref, base_ref, *refs = refs
-    wxy_ref, wz_ref, xsum_ref, zsum_ref, out_ref, a_ref, h_ref, v_ref, dz_ref, xs_ref, hs_ref, fh_ref, fl_ref = refs
+        xr_ref, xyr_ref, xzr_ref, base_ref, vown_ref, dzown_ref, xown_ref, hown_ref, *refs = refs
+        wxy_ref, wz_ref, xsum_ref, zsum_ref, out_ref, *refs = refs
+    a_ref, h_ref, v_ref, dz_ref, xs_ref, hs_ref, fh_ref, fl_ref = refs
     first = 8 if upper else 0
     ex, ey, ez = (jnp.where(at == 0, 0.0, 1.0) for at in coords())
     row8 = lax.broadcasted_iota(jnp.int32, (8, 128), 0)
@@ -169,45 +171,56 @@
     tail = jnp.where(row8 < 4, ey, 1.0)
 
     for h in range(2):
-        for n in range(16):
-            if upper or n >= 8:
-                t = n if upper else n - 8
-                a_ref[h, n, 8:40] = own_ref[h, t]
-                a_ref[h, n, 0:8] = yr_ref[h, t]
-            else:
-                a_ref[h, n, 8:40] = xr_ref[h, n]
-                a_ref[h, n, 0:8] = xyr_ref[h, n]
-        h_ref[h, 0, 8:40] = zr_ref[h]
-        h_ref[h, 0, 0:8] = yzr_ref[h, 24:32]
-        if not upper:
+        for n in range(16 if upper else 8):
+            a_ref[h, n, 8:40] = own_ref[h, n] if upper else xr_ref[h, n]
+            a_ref[h, n, 0:8] = yr_ref[h, n] if upper else xyr_ref[h, n]
+        if upper:
+            h_ref[h, 0, 8:40] = zr_ref[h]
+            h_ref[h, 0, 0:8] = yzr_ref[h, 24:32]
+        else:
             h_ref[h, 1, 8:40] = xzr_ref[h]
             h_ref[h, 1, 0:8] = xyr_ref[h, 8]
 
     plus_z = jnp.where(lane40 == 127, ez, 1.0)
     minus_z = jnp.where(lane40 == 0, ez, 1.0)
+    def centre(h, n):
+        if upper:
+            return v_ref.at[h, n - 3]
+        return v_ref.at[h, n - 3] if n < 8 else vown_ref.at[h, n - 8]
+
+    def slope(h, n):
+        if upper:
+            return dz_ref.at[h, n - 4] if n >= 4 else dzown_ref.at[h, n]
+        return dz_ref.at[h, n - 4] if n < 8 else dzown_ref.at[h, n - 8]
+
+    planes = range(0, 13) if upper else range(3, 8)
+    sloped = range(0, 12) if upper else range(4, 8)
     for h in range(2):
-        for n in range(3, 13):
-            l = n + first
-            if l >= 8:
-                halo = pltpu.roll(h_ref[h, 0], (120 - 8 * (l - 8)) % 128, 1)
+        for n in planes:
+            if upper:
+                halo = pltpu.roll(h_ref[h, 0], (120 - 8 * n) % 128, 1)
             else:
-                halo = pltpu.roll(h_ref[h, 1], (120 - 8 * (l + 8)) % 128, 1)
-            v_ref[h, n - 3] = jnp.where(lane40 >= 124, halo, a_ref[h, n])
-            if 4 <= n < 12:
-                dz_ref[h, n - 4] = halo
+                halo = pltpu.roll(h_ref[h, 1], (120 - 8 * (n + 8)) % 128, 1)
+            value = jnp.where(lane40 >= 124, halo, a_ref[h, n])
+            if upper and n < 5:
+                vown_ref[h, n] = value
+            if not upper or n >= 3:
+                v_ref[h, n - 3] = value
+            if n in sloped:
+                slope(h, n)[...] = halo
     for h in range(2):
-        for n in range(4, 12):
+        for n in sloped:
             a = a_ref[h, n]
-            halo = dz_ref[h, n - 4]
+            halo = slope(h, n)[...]
             up = pltpu.roll(jnp.where(lane40 >= 125, halo, a), 127, 1)
             down = pltpu.roll(jnp.where(lane40 >= 123, halo, a), 1, 1)
-            dz_ref[h, n - 4] = plus_z * up - minus_z * down
+            slope(h, n)[...] = plus_z * up - minus_z * down
 
     def x_step(tile, carry):
         rows = pl.ds(pl.multiple_of(tile * 8, 8), 8)
         for q in range(5):
             p = []
-            for n in range(16):
+            for n in range(16 if upper else 8):
                 if q == 4:
                     p.append(a_ref[0, n, rows] * a_ref[1, n, rows])
                 else:
@@ -217,34 +230,35 @@
                 b = [p[n] + p[n + 1] for n in range(15)]
                 b = [b[n] + b[n + 2] for n in range(13)]
                 b = [b[n] + b[n + 4] for n in range(9)]
+                right = p[0]
                 for o in range(8):
                     xs_ref[q, o, rows] = b[o] + p[o + 8]
+                    if o > 0:
+                        right = right + p[o]
+                    xown_ref[q, o, rows] = right
                 continue
             left = [None] * 8
             left[7] = p[7]
             for o in range(6, -1, -1):
                 left[o] = left[o + 1] + p[o]
-            right = p[8]
             for o in range(8):
-                if o > 0:
-                    right = right + p[o + 8]
+                right = xown_ref[q, o, rows]
                 xs_ref[q, o, rows] = left[o] + ex * right if o < 4 else ex * left[o] + right
         return carry
 
     lax.fori_loop(0, 5, x_step, 0)
 
-    sides = 1 if upper else 2
-    x_sum = xsum_ref[0 : 128 * sides]
+    side = 0 if upper else 1
+    x_sum = xsum_ref[128 * side : 128 * side + 128]
     for q in range(5):
-        parts = []
-        for side in range(sides):
-            f = h_ref[0, side]
-            m = h_ref[1, side]
-            value = (f, m, f * f, m * m, f * m)[q]
-            parts.append(rows_window(value, head, tail, row8))
-        total = jnp.zeros((32, 128), f32)
-        for piece in split3(jnp.concatenate(parts, axis=1)):
+        f = h_ref[0, side]
+        m = h_ref[1, side]
+        value = (f, m, f * f, m * m, f * m)[q]
+        total = jnp.zeros((32, 128), f32) if upper else hown_ref[q]
+        for piece in split3(rows_window(value, head, tail, row8)):
             total = total + dot(piece, x_sum)
+        if upper:
+            hown_ref[q] = total
         for n, piece in enumerate(split3(total)):
             hs_ref[q, n] = piece
 
@@ -252,7 +266,7 @@
     plus_y = jnp.where(row32 == 3, ey, 1.0)
     minus_y = jnp.where(row32 == 4, ey, 1.0)
 
-    def o_step(o, carry):
+    for o in range(8):
         mine = (from_row < 128) | (lax.shift_right_logical(from_row - 128, 3) == o + first)
         z_sum = jnp.where(mine, zsum_ref[...], 0.0).astype(bf16)
         pieces = [[], [], []]
@@ -268,37 +282,34 @@
         var_f = sums[64:96] - mean_f * mean_f + epsilon_value
         var_m = sums[96:128] - mean_m * mean_m + epsilon_value
         cov = sums[128:160] - mean_f * mean_m
-        off_f = v_ref[0, o + 1, 4:36] - mean_f
-        off_m = v_ref[1, o + 1, 4:36] - mean_m
+        off_f = centre(0, o + 4)[4:36] - mean_f
+        off_m = centre(1, o + 4)[4:36] - mean_m
         inv = 1.0 / (var_f * var_m)
         factor = cov * inv
         pulls = (
             factor * (off_m - factor * var_m * off_f),
             factor * (off_f - factor * var_f * off_m),
         )
-        plus_x = jnp.where(o + first == 3, ex, 1.0)
-        minus_x = jnp.where(o + first == 4, ex, 1.0)
-        where_to = pl.ds(pl.multiple_of(o * 32, 32), 32)
+        plus_x = ex if o + first == 3 else 1.0
+        minus_x = ex if o + first == 4 else 1.0
+        where_to = slice(32 * o, 32 * o + 32)
         for h in range(2):
-            dx = plus_x * v_ref[h, o + 2, 4:36] - minus_x * v_ref[h, o, 4:36]
-            dy = plus_y * v_ref[h, o + 1, 5:37] - minus_y * v_ref[h, o + 1, 3:35]
-            dz = dz_ref[h, o, 4:36]
+            dx = plus_x * centre(h, o + 5)[4:36] - minus_x * centre(h, o + 3)[4:36]
+            dy = plus_y * centre(h, o + 4)[5:37] - minus_y * centre(h, o + 4)[3:35]
+            dz = slope(h, o + 4)[4:36]
             for c, d in enumerate((dx, dy, dz)):
                 hi, lo = split2(pulls[h] * d)
                 fh_ref[3 * h + c, where_to] = hi
                 fl_ref[3 * h + c, where_to] = lo
-        return carry
-
-    lax.fori_loop(0, 8, o_step, 0, unroll=8)
 
     cols = slice(32 * first, 32 * first + 256)
     wxy = wxy_ref[:, cols]
     wxy_hi = wxy_ref[0:40, cols]
-    planes = []
+    lattice = []
     for c in range(6):
         one = dot(wxy, fh_ref[c])
-        planes.append(one[0:40] + one[40:80] + dot(wxy_hi, fl_ref[c]))
-    hi, lo = split2(jnp.concatenate(planes, axis=0))
+        lattice.append(one[0:40] + one[40:80] + dot(wxy_hi, fl_ref[c]))
+    hi, lo = split2(jnp.concatenate(lattice, axis=0))
     along = dot(jnp.concatenate([hi, lo], axis=0), wz_ref[...])
     along = (along[0:240, 0:128] + along[0:240, 128:256]) + along[240:480, 0:128]
     which = lax.div(lax.broadcasted_iota(jnp.int32, (40, 128), 1), 20)
@@ -493,10 +504,10 @@
     xyr = send(to_xy.at[:, 8].set(top), 1, 1, 0)
     xzr = send(zr, 1, 0, 0)
 
-    def forces(upper, *arrays):
+    def forces(upper, more, *arrays):
         return call(
             functools.partial(force_kernel, upper),
-            [((40, 128), f32)],
+            [((40, 128), f32)] + [(shape, f32) for shape in more],
             [VMEM] * (len(arrays) + 4),
             [
                 pltpu.VMEM((2, 16, 40, 128), f32),
@@ -510,10 +521,11 @@
             ],
             flops=5 * 10**8,
             bytes_accessed=10**6,
-        )(*arrays, wxy, wzs, xsum, zsum)[0]
-
-    part = forces(True, images, zr, yr, yzr, vel)
-    part = forces(False, images, zr, yr, yzr, xr, xyr, xzr, part)
+        )(*arrays, wxy, wzs, xsum, zsum)
+
+    shared = [(2, 5, 40, 128), (2, 4, 40, 128), (5, 8, 40, 128), (5, 32, 128)]
+    part, *own_parts = forces(True, shared, images, zr, yr, yzr, vel)
+    (part,) = forces(False, (), images, zr, yr, yzr, xr, xyr, xzr, part, *own_parts)
 
     swap = lambda v, axis, couples: lax.ppermute(v, axis, couples + [(b, a) for a, b in couples])
     chip = swap(part, "gz", [(1, 2), (3, 0)])

time: 44.9 us -> 44.5 us (level)
  the two profiles are of different devices: /device:TPU:16 before, /device:TPU:0 now
where the time goes in v11:
time: 44.5 us; the launch traced here: 44.2 us
  starting transfers between devices  17.1 us (38%)
  blocking collectives  10.3 us (23%)
  waiting for transfers between devices  8.57 us (19%)
  Pallas kernels  6.51 us (15%)
  local copies, waits for them, and re-layouts  1.06 us (2%)
  between operations  0.71 us (2%)
    all_to_all x1, blocking collectives, shards(): everything = lax.all_to_all(copies, 'gy', 0, 0, tiled=True)  10.3 us
    ppermute x5, starting transfers between devices, send(): return lax.ppermute(v, AXES, pairs(sizes, di, dj, dk))  9.9 us
    ppermute x5, starting transfers between devices, shards(): lax.ppermute(v, axis, couples + [(b, a) for a, b in couples])  7.13 us
    ppermute x5, waiting for transfers between devices, shards(): lax.ppermute(v, axis, couples + [(b, a) for a, b in couples])  5.03 us
    pallas_call x2, Pallas kernels, forces(): call(functools.partial(force_kernel, upper), [((40, 128), f32)] + [(shape...  4.23 us
    ppermute x5, waiting for transfers between devices, send(): return lax.ppermute(v, AXES, pairs(sizes, di, dj, dk))  2.78 us
    pallas_call x1, Pallas kernels, shards(): call(field_kernel, [((6, 2, 16, 32), f32), ((6, 512, 128), bf16)], [VMEM]...  1.49 us
    unnamed x10, local copies, waits for them, and re-layouts  1.06 us
  transfers between devices with their start and end apart: 11, of which 6 were waited for; matrix products, arithmetic and copies ran while one was open for 0% of the time, Pallas kernels for 6%

profile of v11, /device:TPU:0, one launch (start us, length us, event | category | flops | bytes accessed | tf_op | source)
XLA Modules:
  0.0 44.2 jit_solution(5598110701798841821)
XLA Ops:
  0.6 0.0 copy-start
  0.6 1.0 %copy-done = f32[2,16,32,128]{3,2,1,0:T(8,128)S(1)} copy-done((f32[2,16,32,128]{3,2,1,0:T(8,128)S(1)}, f32[2,16,32,128]{3,2,1,0:T(8,128)}, u32[]{:S(2)}) %copy-start) | copy-done | bytes 524312
  1.7 0.0 copy-start.1
  1.7 0.2 shard_map.59.after_ref
  1.9 0.0 copy-start.3
  1.9 0.1 collective-permute-start
  2.0 1.6 %collective-permute-start.1 = (f32[2,16,8,128]{3,2,1,0:T(8,128)S(1)}, f32[2,16,8,128]{3,2,1,0:T(8,128)S(1)}, u32[]{:S(2)}, u32[]{:S(2)}) collective-permute-start(f32[2,16,8,128]{3,2,1,0:T(8,128)S(1)} %get-tuple-element.35), channel_id=1, source_target_pairs={{0,4},{1,5},{2,6},{3,7},{4,8},{5,9},{6,10},{7,11},{8,12},{9,13},{1... | collective-permute-start | bytes 393224 | tf_op jit(solution)/shard_map/ppermute | solution.py:480
  3.6 1.9 %collective-permute-start.3 = (f32[2,8,32,128]{3,2,1,0:T(8,128)S(1)}, f32[2,8,32,128]{3,2,1,0:T(8,128)S(1)}, u32[]{:S(2)}, u32[]{:S(2)}) collective-permute-start(f32[2,8,32,128]{3,2,1,0:T(8,128)S(1)} %get-tuple-element.36), channel_id=1, source_target_pairs={{0,32},{1,33},{2,34},{3,35},{4,36},{5,37},{6,38},{7,39},{8,40},{9,... | collective-permute-start | bytes 786440 | tf_op jit(solution)/shard_map/ppermute | solution.py:480
  5.6 0.0 copy-done.3
  5.6 0.5 %shard_map.60 = (f32[16,128]{1,0:T(8,128)S(1)}, bf16[80,512]{1,0:T(8,128)(2,1)S(1)}, bf16[128,256]{1,0:T(8,128)(2,1)S(1)}, bf16[256,128]{1,0:T(8,128)(2,1)S(1)}, f32[256,128]{1,0:T(8,128)S(1)}) custom-call(f32[6,2,16,32]{3,2,1,0:T(8,128)S(1)} %bitcast.11), custom_call_target="tpu_custom_call" | custom-call | bytes 1000000 | tf_op jit(solution)/shard_map/pallas_call | solution.py:494
  6.0 0.8 %collective-permute-done.zr_ref = f32[2,32,128]{2,1,0:T(8,128)S(1)} collective-permute-done((f32[2,32,128]{2,1,0:T(8,128)S(1)}, f32[2,32,128]{2,1,0:T(8,128)S(1)}, u32[]{:S(2)}, u32[]{:S(2)}) %collective-permute-start) | collective-permute-done | bytes 32800 | tf_op jit(solution)/shard_map/ppermute | solution.py:489
  6.8 1.6 %collective-permute-start.2 = (f32[2,32,128]{2,1,0:T(8,128)S(1)}, f32[2,32,128]{2,1,0:T(8,128)S(1)}, u32[]{:S(2)}, u32[]{:S(2)}) collective-permute-start(f32[2,32,128]{2,1,0:T(8,128)S(1)} %collective-permute-done.zr_ref), channel_id=1, source_target_pairs={{0,4},{1,5},{2,6},{3,7},{4,8},{5,9},{6,10},{7,11},{8,12},{9,13},{1... | collective-permute-start | bytes 98312 | tf_op jit(solution)/shard_map/ppermute | solution.py:480
  8.4 2.8 %collective-permute-start.4 = (f32[2,9,8,128]{3,2,1,0:T(8,128)S(1)}, f32[2,9,8,128]{3,2,1,0:T(8,128)S(1)}, u32[]{:S(2)}, u32[]{:S(2)}) collective-permute-start(f32[2,9,8,128]{3,2,1,0:T(8,128)S(1)} %bitcast_dynamic-update-slice_fusion), channel_id=1, source_target_pairs={{0,36},{1,37},{2,38},{3,39},{4,40},{5,41},{6,42},{7,43},{8,44},{9,... | collective-permute-start | bytes 221192 | tf_op jit(solution)/shard_map/ppermute | solution.py:480
  11.2 1.9 %collective-permute-start.5 = (f32[2,32,128]{2,1,0:T(8,128)S(1)}, f32[2,32,128]{2,1,0:T(8,128)S(1)}, u32[]{:S(2)}, u32[]{:S(2)}) collective-permute-start(f32[2,32,128]{2,1,0:T(8,128)S(1)} %collective-permute-done.zr_ref), channel_id=1, source_target_pairs={{0,32},{1,33},{2,34},{3,35},{4,36},{5,37},{6,38},{7,39},{8,40},{9,... | collective-permute-start | bytes 98312 | tf_op jit(solution)/shard_map/ppermute | solution.py:480
  13.1 0.0 collective-permute-done.2.yzr_ref
  13.1 0.0 collective-permute-done.1.yr_ref
  13.1 0.0 copy-done.1
  13.1 2.3 %shard_map.62 = (f32[40,128]{1,0:T(8,128)S(1)}, f32[2,5,40,128]{3,2,1,0:T(8,128)S(1)}, f32[2,4,40,128]{3,2,1,0:T(8,128)S(1)}, f32[5,8,40,128]{3,2,1,0:T(8,128)S(1)}, f32[5,32,128]{2,1,0:T(8,128)S(1)}) custom-call(f32[2,16,32,128]{3,2,1,0:T(8,128)S(1)} %copy-done.1, f32[2,32,128]{2,1,0:T(8,128)S(1)} %collective-permute-done.zr_ref, ...), custom_call_target="tpu_custom_call" | custom-call | flops 500000000 | bytes 1000000 | tf_op jit(solution)/shard_map/pallas_call | solution.py:508
  15.4 2.8 %collective-permute-done.5.refs_2_ = f32[2,32,128]{2,1,0:T(8,128)S(1)} collective-permute-done((f32[2,32,128]{2,1,0:T(8,128)S(1)}, f32[2,32,128]{2,1,0:T(8,128)S(1)}, u32[]{:S(2)}, u32[]{:S(2)}) %collective-permute-start.5) | collective-permute-done | bytes 32800 | tf_op jit(solution)/shard_map/ppermute | solution.py:480
  18.2 0.0 collective-permute-done.4.refs_1_
  18.2 0.0 collective-permute-done.3.refs_0_
  18.2 2.0 %shard_map.63.mine_ref = f32[40,128]{1,0:T(8,128)S(1)} custom-call(f32[2,16,32,128]{3,2,1,0:T(8,128)S(1)} %copy-done.1, f32[2,32,128]{2,1,0:T(8,128)S(1)} %collective-permute-done.zr_ref, f32[2,16,8,128]{3,2,1,0:T(8,128)S(1)} %collective-permute-done.1.yr_ref, f32[2,32,128]{2,1,0:T(8,128)S(1)} %collective-permute-done.2.yzr_ref, ...), custom_call_target="tpu_custom_call" | custom-call | flops 500000000 | bytes 1000000 | tf_op jit(solution)/shard_map/pallas_call | solution.py:508
  20.2 0.0 copy-start.2
  20.2 0.2 collective-permute-start.7
  20.4 2.2 %collective-permute-start.6 = (f32[40,128]{1,0:T(8,128)S(1)}, f32[40,128]{1,0:T(8,128)S(1)}, u32[]{:S(2)}, u32[]{:S(2)}) collective-permute-start(f32[40,128]{1,0:T(8,128)S(1)} %shard_map.63.mine_ref), channel_id=1, source_target_pairs={{1,2},{3,0},{2,1},{0,3},{5,6},{7,4},{6,5},{4,7},{9,10},{11,8},{10,... | collective-permute-start | bytes 61448 | tf_op jit(solution)/shard_map/ppermute | solution.py:530
  22.5 0.0 collective-permute-done.7.core_ref
  22.6 2.5 %collective-permute-done.6.chip_ref = f32[40,128]{1,0:T(8,128)S(1)} collective-permute-done((f32[40,128]{1,0:T(8,128)S(1)}, f32[40,128]{1,0:T(8,128)S(1)}, u32[]{:S(2)}, u32[]{:S(2)}) %collective-permute-start.6) | collective-permute-done | bytes 20512 | tf_op jit(solution)/shard_map/ppermute | solution.py:530
  25.1 0.1 shard_map.64.own_ref
  25.2 1.6 %collective-permute-start.10 = (f32[40,128]{1,0:T(8,128)S(1)}, f32[40,128]{1,0:T(8,128)S(1)}, u32[]{:S(2)}, u32[]{:S(2)}) collective-permute-start(f32[40,128]{1,0:T(8,128)S(1)} %shard_map.64.own_ref), channel_id=1, source_target_pairs={{32,64},{96,0},{64,32},{0,96},{33,65},{97,1},{65,33},{1,97},{34,66... | collective-permute-start | bytes 61448 | tf_op jit(solution)/shard_map/ppermute | solution.py:530
  26.8 0.4 collective-permute-start.9
  27.1 2.8 %collective-permute-start.8 = (f32[40,128]{1,0:T(8,128)S(1)}, f32[40,128]{1,0:T(8,128)S(1)}, u32[]{:S(2)}, u32[]{:S(2)}) collective-permute-start(f32[40,128]{1,0:T(8,128)S(1)} %shard_map.64.own_ref), channel_id=1, source_target_pairs={{0,64},{32,96},{64,0},{96,32},{1,65},{33,97},{65,1},{97,33},{2,66}... | collective-permute-start | bytes 61448 | tf_op jit(solution)/shard_map/ppermute | solution.py:530
  29.9 0.3 collective-permute-done.10.two_ref
  30.2 0.3 collective-permute-done.9.one_ref
  30.6 1.9 %collective-permute-done.8.far_ref = f32[40,128]{1,0:T(8,128)S(1)} collective-permute-done((f32[40,128]{1,0:T(8,128)S(1)}, f32[40,128]{1,0:T(8,128)S(1)}, u32[]{:S(2)}, u32[]{:S(2)}) %collective-permute-start.8) | collective-permute-done | bytes 20512 | tf_op jit(solution)/shard_map/ppermute | solution.py:530
  32.4 0.0 copy-start.4
  32.5 10.3 %all_to_all.5.g_ref = f32[8,32,128]{2,1,0:T(8,128)S(1)} all-to-all(f32[8,32,128]{2,1,0:T(8,128)S(1)} %get-tuple-element.48), channel_id=1, replica_groups=mesh['gx'=4,'gy'=8,'gz'=4] {'gy'}, dimensions={0} | all-to-all | bytes 262144 | tf_op jit(solution)/shard_map/all_to_all | solution.py:538
  42.7 0.0 copy-done.2
  42.8 0.0 copy-done.4
  42.8 1.5 %shard_map.66 = (f32[6,2,16,32]{3,2,1,0:T(8,128)}, bf16[6,512,128]{2,1,0:T(8,128)(2,1)}) custom-call(f32[8,32,128]{2,1,0:T(8,128)S(1)} %all_to_all.5.g_ref, f32[48,128]{1,0:T(8,128)S(1)} %get-tuple-element.49.mine_ref, bf16[512,144]{1,0:T(8,128)(2,1)S(1)} %copy-done.2, bf16[128,256]{1,0:T(8,128)(2,1)S(1)} %copy-done.4), custom_call_target="tpu_custom_call" | custom-call | flops 100000000 | bytes 1000000 | tf_op jit(solution)/shard_map/pallas_call | solution.py:540
  (3 shorter events, 0.1 us)
Async XLA Ops:
  0.6 1.0 %copy-start = (f32[2,16,32,128]{3,2,1,0:T(8,128)S(1)}, f32[2,16,32,128]{3,2,1,0:T(8,128)}, u32[]{:S(2)}) copy-start(f32[2,16,32,128]{3,2,1,0:T(8,128)} %own_ref.3) | copy-start | bytes 1572868
  1.7 11.5 %copy-start.1 = (f32[2,16,32,128]{3,2,1,0:T(8,128)S(1)}, f32[2,16,32,128]{3,2,1,0:T(8,128)}, u32[]{:S(2)}) copy-start(f32[2,16,32,128]{3,2,1,0:T(8,128)} %own_ref.3) | copy-start | bytes 1572868
  1.9 3.7 %copy-start.3 = (f32[2,3,2,32,16]{3,4,2,1,0:T(8,128)S(1)}, f32[2,3,2,32,16]{3,4,2,1,0:T(8,128)}, u32[]{:S(2)}) copy-start(f32[2,3,2,32,16]{3,4,2,1,0:T(8,128)} %param.7) | copy-start | bytes 73732
  1.9 4.9 %collective-permute-start = (f32[2,32,128]{2,1,0:T(8,128)S(1)}, f32[2,32,128]{2,1,0:T(8,128)S(1)}, u32[]{:S(2)}, u32[]{:S(2)}) collective-permute-start(f32[2,32,128]{2,1,0:T(8,128)S(1)} %shard_map.59.after_ref), channel_id=1, source_target_pairs={{0,1},{1,2},{2,3},{3,0},{4,5},{5,6},{6,7},{7,4},{8,9},{9,10},{10,1... | collective-permute-start | bytes 98312 | tf_op jit(solution)/shard_map/ppermute | solution.py:489
  2.0 11.1 %collective-permute-start.1 = (f32[2,16,8,128]{3,2,1,0:T(8,128)S(1)}, f32[2,16,8,128]{3,2,1,0:T(8,128)S(1)}, u32[]{:S(2)}, u32[]{:S(2)}) collective-permute-start(f32[2,16,8,128]{3,2,1,0:T(8,128)S(1)} %get-tuple-element.35), channel_id=1, source_target_pairs={{0,4},{1,5},{2,6},{3,7},{4,8},{5,9},{6,10},{7,11},{8,12},{9,13},{1... | collective-permute-start | bytes 393224 | tf_op jit(solution)/shard_map/ppermute | solution.py:480
  3.6 14.6 %collective-permute-start.3 = (f32[2,8,32,128]{3,2,1,0:T(8,128)S(1)}, f32[2,8,32,128]{3,2,1,0:T(8,128)S(1)}, u32[]{:S(2)}, u32[]{:S(2)}) collective-permute-start(f32[2,8,32,128]{3,2,1,0:T(8,128)S(1)} %get-tuple-element.36), channel_id=1, source_target_pairs={{0,32},{1,33},{2,34},{3,35},{4,36},{5,37},{6,38},{7,39},{8,40},{9,... | collective-permute-start | bytes 786440 | tf_op jit(solution)/shard_map/ppermute | solution.py:480
  6.8 6.3 %collective-permute-start.2 = (f32[2,32,128]{2,1,0:T(8,128)S(1)}, f32[2,32,128]{2,1,0:T(8,128)S(1)}, u32[]{:S(2)}, u32[]{:S(2)}) collective-permute-start(f32[2,32,128]{2,1,0:T(8,128)S(1)} %collective-permute-done.zr_ref), channel_id=1, source_target_pairs={{0,4},{1,5},{2,6},{3,7},{4,8},{5,9},{6,10},{7,11},{8,12},{9,13},{1... | collective-permute-start | bytes 98312 | tf_op jit(solution)/shard_map/ppermute | solution.py:480
  8.4 9.8 %collective-permute-start.4 = (f32[2,9,8,128]{3,2,1,0:T(8,128)S(1)}, f32[2,9,8,128]{3,2,1,0:T(8,128)S(1)}, u32[]{:S(2)}, u32[]{:S(2)}) collective-permute-start(f32[2,9,8,128]{3,2,1,0:T(8,128)S(1)} %bitcast_dynamic-update-slice_fusion), channel_id=1, source_target_pairs={{0,36},{1,37},{2,38},{3,39},{4,40},{5,41},{6,42},{7,43},{8,44},{9,... | collective-permute-start | bytes 221192 | tf_op jit(solution)/shard_map/ppermute | solution.py:480
  11.2 7.0 %collective-permute-start.5 = (f32[2,32,128]{2,1,0:T(8,128)S(1)}, f32[2,32,128]{2,1,0:T(8,128)S(1)}, u32[]{:S(2)}, u32[]{:S(2)}) collective-permute-start(f32[2,32,128]{2,1,0:T(8,128)S(1)} %collective-permute-done.zr_ref), channel_id=1, source_target_pairs={{0,32},{1,33},{2,34},{3,35},{4,36},{5,37},{6,38},{7,39},{8,40},{9,... | collective-permute-start | bytes 98312 | tf_op jit(solution)/shard_map/ppermute | solution.py:480
  20.2 22.6 %copy-start.2 = (bf16[512,144]{1,0:T(8,128)(2,1)S(1)}, bf16[512,144]{1,0:T(8,128)(2,1)}, u32[]{:S(2)}) copy-start(bf16[512,144]{1,0:T(8,128)(2,1)} %constant.33.clone.wxy_ref) | copy-start | bytes 442372
  20.2 2.4 %collective-permute-start.7 = (f32[40,128]{1,0:T(8,128)S(1)}, f32[40,128]{1,0:T(8,128)S(1)}, u32[]{:S(2)}, u32[]{:S(2)}) collective-permute-start(f32[40,128]{1,0:T(8,128)S(1)} %shard_map.63.mine_ref), channel_id=1, source_target_pairs={{0,1},{2,3},{1,0},{3,2},{4,5},{6,7},{5,4},{7,6},{8,9},{10,11},{9,8... | collective-permute-start | bytes 61448 | tf_op jit(solution)/shard_map/ppermute | solution.py:530
  20.4 4.7 %collective-permute-start.6 = (f32[40,128]{1,0:T(8,128)S(1)}, f32[40,128]{1,0:T(8,128)S(1)}, u32[]{:S(2)}, u32[]{:S(2)}) collective-permute-start(f32[40,128]{1,0:T(8,128)S(1)} %shard_map.63.mine_ref), channel_id=1, source_target_pairs={{1,2},{3,0},{2,1},{0,3},{5,6},{7,4},{6,5},{4,7},{9,10},{11,8},{10,... | collective-permute-start | bytes 61448 | tf_op jit(solution)/shard_map/ppermute | solution.py:530
  25.2 5.0 %collective-permute-start.10 = (f32[40,128]{1,0:T(8,128)S(1)}, f32[40,128]{1,0:T(8,128)S(1)}, u32[]{:S(2)}, u32[]{:S(2)}) collective-permute-start(f32[40,128]{1,0:T(8,128)S(1)} %shard_map.64.own_ref), channel_id=1, source_target_pairs={{32,64},{96,0},{64,32},{0,96},{33,65},{97,1},{65,33},{1,97},{34,66... | collective-permute-start | bytes 61448 | tf_op jit(solution)/shard_map/ppermute | solution.py:530
  26.8 3.8 %collective-permute-start.9 = (f32[40,128]{1,0:T(8,128)S(1)}, f32[40,128]{1,0:T(8,128)S(1)}, u32[]{:S(2)}, u32[]{:S(2)}) collective-permute-start(f32[40,128]{1,0:T(8,128)S(1)} %shard_map.64.own_ref), channel_id=1, source_target_pairs={{0,32},{64,96},{32,0},{96,64},{1,33},{65,97},{33,1},{97,65},{2,34}... | collective-permute-start | bytes 61448 | tf_op jit(solution)/shard_map/ppermute | solution.py:530
  27.1 5.3 %collective-permute-start.8 = (f32[40,128]{1,0:T(8,128)S(1)}, f32[40,128]{1,0:T(8,128)S(1)}, u32[]{:S(2)}, u32[]{:S(2)}) collective-permute-start(f32[40,128]{1,0:T(8,128)S(1)} %shard_map.64.own_ref), channel_id=1, source_target_pairs={{0,64},{32,96},{64,0},{96,32},{1,65},{33,97},{65,1},{97,33},{2,66}... | collective-permute-start | bytes 61448 | tf_op jit(solution)/shard_map/ppermute | solution.py:530
  32.4 10.3 %copy-start.4 = (bf16[128,256]{1,0:T(8,128)(2,1)S(1)}, bf16[128,256]{1,0:T(8,128)(2,1)}, u32[]{:S(2)}) copy-start(bf16[128,256]{1,0:T(8,128)(2,1)} %constant.34.clone.wz_ref) | copy-start | bytes 196612

commit v12 on v11

--- a/solution.py
+++ b/solution.py
@@ -325,7 +325,7 @@
         out_ref[...] = total + base_ref[...]
 
 
-def fold_kernel(mine_ref, chip_ref, core_ref, out_ref):
+def fold_kernel(mine_ref, core_ref, chip_ref, out_ref):
     lane = lax.broadcasted_iota(jnp.int32, (40, 128), 1)
     spot = lax.rem(lane, 20)
     live = lane < 120
@@ -338,7 +338,7 @@
     out_ref[...] = total + jnp.where(live & (spot >= 16), high, 0.0)
 
 
-def across_kernel(own_ref, far_ref, one_ref, two_ref, out_ref, mine_ref):
+def across_kernel(own_ref, one_ref, two_ref, far_ref, out_ref, mine_ref):
     odd = (lax.axis_index("gx") & 1) == 1
     tiles = lambda ref: [ref[8 * p : 8 * p + 8] for p in range(5)]
     own, one, two, far = tiles(own_ref), tiles(one_ref), tiles(two_ref), tiles(far_ref)
@@ -530,11 +530,11 @@
     swap = lambda v, axis, couples: lax.ppermute(v, axis, couples + [(b, a) for a, b in couples])
     chip = swap(part, "gz", [(1, 2), (3, 0)])
     core = swap(part, "gz", [(0, 1), (2, 3)])
-    (own,) = call(fold_kernel, [((40, 128), f32)], [VMEM] * 3)(part, chip, core)
+    (own,) = call(fold_kernel, [((40, 128), f32)], [VMEM] * 3)(part, core, chip)
     far = swap(own, "gx", [(0, 2), (1, 3)])
     one = swap(own, "gx", [(0, 1), (2, 3)])
     two = swap(own, "gx", [(1, 2), (3, 0)])
-    copies, mine = call(across_kernel, [((8, 32, 128), f32), ((48, 128), f32)], [VMEM] * 4)(own, far, one, two)
+    copies, mine = call(across_kernel, [((8, 32, 128), f32), ((48, 128), f32)], [VMEM] * 4)(own, one, two, far)
     everything = lax.all_to_all(copies, "gy", 0, 0, tiled=True)
 
     nv, field = call(

time: 44.5 us -> 43.7 us (0.982)
  starting transfers between devices: 17.1 us -> 15.9 us
  waiting for transfers between devices: 8.57 us -> 9.51 us
  blocking collectives: 10.3 us -> 9.72 us
    ppermute x5, starting transfers between devices: 7.13 us -> 5.9 us  [shards(): lax.ppermute(v, axis, couples + [(b, a) for a, b in couples])]
    ppermute x5, waiting for transfers between devices: 5.03 us -> 5.97 us  [shards(): lax.ppermute(v, axis, couples + [(b, a) for a, b in couples])]
    all_to_all x1, blocking collectives: 10.3 us -> 9.72 us  [shards(): everything = lax.all_to_all(copies, 'gy', 0, 0, tiled=True)]
where the time goes in v12:
time: 43.7 us; the launch traced here: 43.4 us
  starting transfers between devices  15.9 us (36%)
  blocking collectives  9.72 us (22%)
  waiting for transfers between devices  9.51 us (22%)
  Pallas kernels  6.51 us (15%)
  local copies, waits for them, and re-layouts  1.06 us (2%)
  between operations  0.71 us (2%)
    ppermute x5, starting transfers between devices, send(): return lax.ppermute(v, AXES, pairs(sizes, di, dj, dk))  9.9 us
    all_to_all x1, blocking collectives, shards(): everything = lax.all_to_all(copies, 'gy', 0, 0, tiled=True)  9.72 us
    ppermute x5, waiting for transfers between devices, shards(): lax.ppermute(v, axis, couples + [(b, a) for a, b in couples])  5.97 us
    ppermute x5, starting transfers between devices, shards(): lax.ppermute(v, axis, couples + [(b, a) for a, b in couples])  5.9 us
    pallas_call x2, Pallas kernels, forces(): call(functools.partial(force_kernel, upper), [((40, 128), f32)] + [(shape...  4.23 us
    ppermute x5, waiting for transfers between devices, send(): return lax.ppermute(v, AXES, pairs(sizes, di, dj, dk))  2.78 us
    pallas_call x1, Pallas kernels, shards(): call(field_kernel, [((6, 2, 16, 32), f32), ((6, 512, 128), bf16)], [VMEM]...  1.49 us
    unnamed x10, local copies, waits for them, and re-layouts  1.06 us
  transfers between devices with their start and end apart: 11, of which 6 were waited for; matrix products, arithmetic and copies ran while one was open for 0% of the time, Pallas kernels for 6%

profile of v12, /device:TPU:0, one launch (start us, length us, event | category | flops | bytes accessed | tf_op | source)
XLA Modules:
  0.0 43.4 jit_solution(15056943782111634705)
XLA Ops:
  0.6 0.0 copy-start
  0.6 1.0 %copy-done = f32[2,16,32,128]{3,2,1,0:T(8,128)S(1)} copy-done((f32[2,16,32,128]{3,2,1,0:T(8,128)S(1)}, f32[2,16,32,128]{3,2,1,0:T(8,128)}, u32[]{:S(2)}) %copy-start) | copy-done | bytes 524312
  1.7 0.0 copy-start.1
  1.7 0.2 shard_map.59.after_ref
  1.9 0.0 copy-start.3
  1.9 0.1 collective-permute-start
  2.0 1.6 %collective-permute-start.1 = (f32[2,16,8,128]{3,2,1,0:T(8,128)S(1)}, f32[2,16,8,128]{3,2,1,0:T(8,128)S(1)}, u32[]{:S(2)}, u32[]{:S(2)}) collective-permute-start(f32[2,16,8,128]{3,2,1,0:T(8,128)S(1)} %get-tuple-element.35), channel_id=1, source_target_pairs={{0,4},{1,5},{2,6},{3,7},{4,8},{5,9},{6,10},{7,11},{8,12},{9,13},{1... | collective-permute-start | bytes 393224 | tf_op jit(solution)/shard_map/ppermute | solution.py:480
  3.6 1.9 %collective-permute-start.3 = (f32[2,8,32,128]{3,2,1,0:T(8,128)S(1)}, f32[2,8,32,128]{3,2,1,0:T(8,128)S(1)}, u32[]{:S(2)}, u32[]{:S(2)}) collective-permute-start(f32[2,8,32,128]{3,2,1,0:T(8,128)S(1)} %get-tuple-element.36), channel_id=1, source_target_pairs={{0,32},{1,33},{2,34},{3,35},{4,36},{5,37},{6,38},{7,39},{8,40},{9,... | collective-permute-start | bytes 786440 | tf_op jit(solution)/shard_map/ppermute | solution.py:480
  5.6 0.0 copy-done.3
  5.6 0.5 %shard_map.60 = (f32[16,128]{1,0:T(8,128)S(1)}, bf16[80,512]{1,0:T(8,128)(2,1)S(1)}, bf16[128,256]{1,0:T(8,128)(2,1)S(1)}, bf16[256,128]{1,0:T(8,128)(2,1)S(1)}, f32[256,128]{1,0:T(8,128)S(1)}) custom-call(f32[6,2,16,32]{3,2,1,0:T(8,128)S(1)} %bitcast.11), custom_call_target="tpu_custom_call" | custom-call | bytes 1000000 | tf_op jit(solution)/shard_map/pallas_call | solution.py:494
  6.0 0.8 %collective-permute-done.zr_ref = f32[2,32,128]{2,1,0:T(8,128)S(1)} collective-permute-done((f32[2,32,128]{2,1,0:T(8,128)S(1)}, f32[2,32,128]{2,1,0:T(8,128)S(1)}, u32[]{:S(2)}, u32[]{:S(2)}) %collective-permute-start) | collective-permute-done | bytes 32800 | tf_op jit(solution)/shard_map/ppermute | solution.py:489
  6.8 1.6 %collective-permute-start.2 = (f32[2,32,128]{2,1,0:T(8,128)S(1)}, f32[2,32,128]{2,1,0:T(8,128)S(1)}, u32[]{:S(2)}, u32[]{:S(2)}) collective-permute-start(f32[2,32,128]{2,1,0:T(8,128)S(1)} %collective-permute-done.zr_ref), channel_id=1, source_target_pairs={{0,4},{1,5},{2,6},{3,7},{4,8},{5,9},{6,10},{7,11},{8,12},{9,13},{1... | collective-permute-start | bytes 98312 | tf_op jit(solution)/shard_map/ppermute | solution.py:480
  8.4 2.8 %collective-permute-start.4 = (f32[2,9,8,128]{3,2,1,0:T(8,128)S(1)}, f32[2,9,8,128]{3,2,1,0:T(8,128)S(1)}, u32[]{:S(2)}, u32[]{:S(2)}) collective-permute-start(f32[2,9,8,128]{3,2,1,0:T(8,128)S(1)} %bitcast_dynamic-update-slice_fusion), channel_id=1, source_target_pairs={{0,36},{1,37},{2,38},{3,39},{4,40},{5,41},{6,42},{7,43},{8,44},{9,... | collective-permute-start | bytes 221192 | tf_op jit(solution)/shard_map/ppermute | solution.py:480
  11.2 1.9 %collective-permute-start.5 = (f32[2,32,128]{2,1,0:T(8,128)S(1)}, f32[2,32,128]{2,1,0:T(8,128)S(1)}, u32[]{:S(2)}, u32[]{:S(2)}) collective-permute-start(f32[2,32,128]{2,1,0:T(8,128)S(1)} %collective-permute-done.zr_ref), channel_id=1, source_target_pairs={{0,32},{1,33},{2,34},{3,35},{4,36},{5,37},{6,38},{7,39},{8,40},{9,... | collective-permute-start | bytes 98312 | tf_op jit(solution)/shard_map/ppermute | solution.py:480
  13.1 0.0 collective-permute-done.2.yzr_ref
  13.1 0.0 collective-permute-done.1.yr_ref
  13.1 0.0 copy-done.1
  13.1 2.3 %shard_map.62 = (f32[40,128]{1,0:T(8,128)S(1)}, f32[2,5,40,128]{3,2,1,0:T(8,128)S(1)}, f32[2,4,40,128]{3,2,1,0:T(8,128)S(1)}, f32[5,8,40,128]{3,2,1,0:T(8,128)S(1)}, f32[5,32,128]{2,1,0:T(8,128)S(1)}) custom-call(f32[2,16,32,128]{3,2,1,0:T(8,128)S(1)} %copy-done.1, f32[2,32,128]{2,1,0:T(8,128)S(1)} %collective-permute-done.zr_ref, ...), custom_call_target="tpu_custom_call" | custom-call | flops 500000000 | bytes 1000000 | tf_op jit(solution)/shard_map/pallas_call | solution.py:508
  15.4 2.8 %collective-permute-done.5.refs_2_ = f32[2,32,128]{2,1,0:T(8,128)S(1)} collective-permute-done((f32[2,32,128]{2,1,0:T(8,128)S(1)}, f32[2,32,128]{2,1,0:T(8,128)S(1)}, u32[]{:S(2)}, u32[]{:S(2)}) %collective-permute-start.5) | collective-permute-done | bytes 32800 | tf_op jit(solution)/shard_map/ppermute | solution.py:480
  18.2 0.0 collective-permute-done.4.refs_1_
  18.2 0.0 collective-permute-done.3.refs_0_
  18.2 2.0 %shard_map.63.mine_ref = f32[40,128]{1,0:T(8,128)S(1)} custom-call(f32[2,16,32,128]{3,2,1,0:T(8,128)S(1)} %copy-done.1, f32[2,32,128]{2,1,0:T(8,128)S(1)} %collective-permute-done.zr_ref, f32[2,16,8,128]{3,2,1,0:T(8,128)S(1)} %collective-permute-done.1.yr_ref, f32[2,32,128]{2,1,0:T(8,128)S(1)} %collective-permute-done.2.yzr_ref, ...), custom_call_target="tpu_custom_call" | custom-call | flops 500000000 | bytes 1000000 | tf_op jit(solution)/shard_map/pallas_call | solution.py:508
  20.2 0.0 copy-start.2
  20.2 0.2 collective-permute-start.7
  20.3 2.2 %collective-permute-start.6 = (f32[40,128]{1,0:T(8,128)S(1)}, f32[40,128]{1,0:T(8,128)S(1)}, u32[]{:S(2)}, u32[]{:S(2)}) collective-permute-start(f32[40,128]{1,0:T(8,128)S(1)} %shard_map.63.mine_ref), channel_id=1, source_target_pairs={{0,1},{2,3},{1,0},{3,2},{4,5},{6,7},{5,4},{7,6},{8,9},{10,11},{9,8... | collective-permute-start | bytes 61448 | tf_op jit(solution)/shard_map/ppermute | solution.py:530
  22.5 2.4 %collective-permute-done.7.chip_ref = f32[40,128]{1,0:T(8,128)S(1)} collective-permute-done((f32[40,128]{1,0:T(8,128)S(1)}, f32[40,128]{1,0:T(8,128)S(1)}, u32[]{:S(2)}, u32[]{:S(2)}) %collective-permute-start.7) | collective-permute-done | bytes 20512 | tf_op jit(solution)/shard_map/ppermute | solution.py:530
  25.0 0.0 collective-permute-done.6.core_ref
  25.0 0.1 shard_map.64.own_ref
  25.0 2.0 %collective-permute-start.10 = (f32[40,128]{1,0:T(8,128)S(1)}, f32[40,128]{1,0:T(8,128)S(1)}, u32[]{:S(2)}, u32[]{:S(2)}) collective-permute-start(f32[40,128]{1,0:T(8,128)S(1)} %shard_map.64.own_ref), channel_id=1, source_target_pairs={{0,64},{32,96},{64,0},{96,32},{1,65},{33,97},{65,1},{97,33},{2,66}... | collective-permute-start | bytes 61448 | tf_op jit(solution)/shard_map/ppermute | solution.py:530
  27.1 1.3 %collective-permute-start.9 = (f32[40,128]{1,0:T(8,128)S(1)}, f32[40,128]{1,0:T(8,128)S(1)}, u32[]{:S(2)}, u32[]{:S(2)}) collective-permute-start(f32[40,128]{1,0:T(8,128)S(1)} %shard_map.64.own_ref), channel_id=1, source_target_pairs={{32,64},{96,0},{64,32},{0,96},{33,65},{97,1},{65,33},{1,97},{34,66... | collective-permute-start | bytes 61448 | tf_op jit(solution)/shard_map/ppermute | solution.py:530
  28.3 0.2 collective-permute-start.8
  28.6 1.8 %collective-permute-done.10.far_ref = f32[40,128]{1,0:T(8,128)S(1)} collective-permute-done((f32[40,128]{1,0:T(8,128)S(1)}, f32[40,128]{1,0:T(8,128)S(1)}, u32[]{:S(2)}, u32[]{:S(2)}) %collective-permute-start.10) | collective-permute-done | bytes 20512 | tf_op jit(solution)/shard_map/ppermute | solution.py:530
  30.4 1.7 %collective-permute-done.9.two_ref = f32[40,128]{1,0:T(8,128)S(1)} collective-permute-done((f32[40,128]{1,0:T(8,128)S(1)}, f32[40,128]{1,0:T(8,128)S(1)}, u32[]{:S(2)}, u32[]{:S(2)}) %collective-permute-start.9) | collective-permute-done | bytes 20512 | tf_op jit(solution)/shard_map/ppermute | solution.py:530
  32.1 0.1 collective-permute-done.8.one_ref
  32.2 0.0 copy-start.4
  32.2 9.7 %all_to_all.5.g_ref = f32[8,32,128]{2,1,0:T(8,128)S(1)} all-to-all(f32[8,32,128]{2,1,0:T(8,128)S(1)} %get-tuple-element.48), channel_id=1, replica_groups=mesh['gx'=4,'gy'=8,'gz'=4] {'gy'}, dimensions={0} | all-to-all | bytes 262144 | tf_op jit(solution)/shard_map/all_to_all | solution.py:538
  41.9 0.0 copy-done.2
  41.9 0.0 copy-done.4
  41.9 1.5 %shard_map.66 = (f32[6,2,16,32]{3,2,1,0:T(8,128)}, bf16[6,512,128]{2,1,0:T(8,128)(2,1)}) custom-call(f32[8,32,128]{2,1,0:T(8,128)S(1)} %all_to_all.5.g_ref, f32[48,128]{1,0:T(8,128)S(1)} %get-tuple-element.49.mine_ref, bf16[512,144]{1,0:T(8,128)(2,1)S(1)} %copy-done.2, bf16[128,256]{1,0:T(8,128)(2,1)S(1)} %copy-done.4), custom_call_target="tpu_custom_call" | custom-call | flops 100000000 | bytes 1000000 | tf_op jit(solution)/shard_map/pallas_call | solution.py:540
  (3 shorter events, 0.1 us)
Async XLA Ops:
  0.6 1.0 %copy-start = (f32[2,16,32,128]{3,2,1,0:T(8,128)S(1)}, f32[2,16,32,128]{3,2,1,0:T(8,128)}, u32[]{:S(2)}) copy-start(f32[2,16,32,128]{3,2,1,0:T(8,128)} %own_ref.3) | copy-start | bytes 1572868
  1.7 11.5 %copy-start.1 = (f32[2,16,32,128]{3,2,1,0:T(8,128)S(1)}, f32[2,16,32,128]{3,2,1,0:T(8,128)}, u32[]{:S(2)}) copy-start(f32[2,16,32,128]{3,2,1,0:T(8,128)} %own_ref.3) | copy-start | bytes 1572868
  1.9 3.7 %copy-start.3 = (f32[2,3,2,32,16]{3,4,2,1,0:T(8,128)S(1)}, f32[2,3,2,32,16]{3,4,2,1,0:T(8,128)}, u32[]{:S(2)}) copy-start(f32[2,3,2,32,16]{3,4,2,1,0:T(8,128)} %param.7) | copy-start | bytes 73732
  1.9 4.9 %collective-permute-start = (f32[2,32,128]{2,1,0:T(8,128)S(1)}, f32[2,32,128]{2,1,0:T(8,128)S(1)}, u32[]{:S(2)}, u32[]{:S(2)}) collective-permute-start(f32[2,32,128]{2,1,0:T(8,128)S(1)} %shard_map.59.after_ref), channel_id=1, source_target_pairs={{0,1},{1,2},{2,3},{3,0},{4,5},{5,6},{6,7},{7,4},{8,9},{9,10},{10,1... | collective-permute-start | bytes 98312 | tf_op jit(solution)/shard_map/ppermute | solution.py:489
  2.0 11.1 %collective-permute-start.1 = (f32[2,16,8,128]{3,2,1,0:T(8,128)S(1)}, f32[2,16,8,128]{3,2,1,0:T(8,128)S(1)}, u32[]{:S(2)}, u32[]{:S(2)}) collective-permute-start(f32[2,16,8,128]{3,2,1,0:T(8,128)S(1)} %get-tuple-element.35), channel_id=1, source_target_pairs={{0,4},{1,5},{2,6},{3,7},{4,8},{5,9},{6,10},{7,11},{8,12},{9,13},{1... | collective-permute-start | bytes 393224 | tf_op jit(solution)/shard_map/ppermute | solution.py:480
  3.6 14.6 %collective-permute-start.3 = (f32[2,8,32,128]{3,2,1,0:T(8,128)S(1)}, f32[2,8,32,128]{3,2,1,0:T(8,128)S(1)}, u32[]{:S(2)}, u32[]{:S(2)}) collective-permute-start(f32[2,8,32,128]{3,2,1,0:T(8,128)S(1)} %get-tuple-element.36), channel_id=1, source_target_pairs={{0,32},{1,33},{2,34},{3,35},{4,36},{5,37},{6,38},{7,39},{8,40},{9,... | collective-permute-start | bytes 786440 | tf_op jit(solution)/shard_map/ppermute | solution.py:480
  6.8 6.3 %collective-permute-start.2 = (f32[2,32,128]{2,1,0:T(8,128)S(1)}, f32[2,32,128]{2,1,0:T(8,128)S(1)}, u32[]{:S(2)}, u32[]{:S(2)}) collective-permute-start(f32[2,32,128]{2,1,0:T(8,128)S(1)} %collective-permute-done.zr_ref), channel_id=1, source_target_pairs={{0,4},{1,5},{2,6},{3,7},{4,8},{5,9},{6,10},{7,11},{8,12},{9,13},{1... | collective-permute-start | bytes 98312 | tf_op jit(solution)/shard_map/ppermute | solution.py:480
  8.4 9.8 %collective-permute-start.4 = (f32[2,9,8,128]{3,2,1,0:T(8,128)S(1)}, f32[2,9,8,128]{3,2,1,0:T(8,128)S(1)}, u32[]{:S(2)}, u32[]{:S(2)}) collective-permute-start(f32[2,9,8,128]{3,2,1,0:T(8,128)S(1)} %bitcast_dynamic-update-slice_fusion), channel_id=1, source_target_pairs={{0,36},{1,37},{2,38},{3,39},{4,40},{5,41},{6,42},{7,43},{8,44},{9,... | collective-permute-start | bytes 221192 | tf_op jit(solution)/shard_map/ppermute | solution.py:480
  11.2 7.0 %collective-permute-start.5 = (f32[2,32,128]{2,1,0:T(8,128)S(1)}, f32[2,32,128]{2,1,0:T(8,128)S(1)}, u32[]{:S(2)}, u32[]{:S(2)}) collective-permute-start(f32[2,32,128]{2,1,0:T(8,128)S(1)} %collective-permute-done.zr_ref), channel_id=1, source_target_pairs={{0,32},{1,33},{2,34},{3,35},{4,36},{5,37},{6,38},{7,39},{8,40},{9,... | collective-permute-start | bytes 98312 | tf_op jit(solution)/shard_map/ppermute | solution.py:480
  20.2 21.7 %copy-start.2 = (bf16[512,144]{1,0:T(8,128)(2,1)S(1)}, bf16[512,144]{1,0:T(8,128)(2,1)}, u32[]{:S(2)}) copy-start(bf16[512,144]{1,0:T(8,128)(2,1)} %constant.33.clone.wxy_ref) | copy-start | bytes 442372
  20.2 4.8 %collective-permute-start.7 = (f32[40,128]{1,0:T(8,128)S(1)}, f32[40,128]{1,0:T(8,128)S(1)}, u32[]{:S(2)}, u32[]{:S(2)}) collective-permute-start(f32[40,128]{1,0:T(8,128)S(1)} %shard_map.63.mine_ref), channel_id=1, source_target_pairs={{1,2},{3,0},{2,1},{0,3},{5,6},{7,4},{6,5},{4,7},{9,10},{11,8},{10,... | collective-permute-start | bytes 61448 | tf_op jit(solution)/shard_map/ppermute | solution.py:530
  20.3 4.6 %collective-permute-start.6 = (f32[40,128]{1,0:T(8,128)S(1)}, f32[40,128]{1,0:T(8,128)S(1)}, u32[]{:S(2)}, u32[]{:S(2)}) collective-permute-start(f32[40,128]{1,0:T(8,128)S(1)} %shard_map.63.mine_ref), channel_id=1, source_target_pairs={{0,1},{2,3},{1,0},{3,2},{4,5},{6,7},{5,4},{7,6},{8,9},{10,11},{9,8... | collective-permute-start | bytes 61448 | tf_op jit(solution)/shard_map/ppermute | solution.py:530
  25.0 5.3 %collective-permute-start.10 = (f32[40,128]{1,0:T(8,128)S(1)}, f32[40,128]{1,0:T(8,128)S(1)}, u32[]{:S(2)}, u32[]{:S(2)}) collective-permute-start(f32[40,128]{1,0:T(8,128)S(1)} %shard_map.64.own_ref), channel_id=1, source_target_pairs={{0,64},{32,96},{64,0},{96,32},{1,65},{33,97},{65,1},{97,33},{2,66}... | collective-permute-start | bytes 61448 | tf_op jit(solution)/shard_map/ppermute | solution.py:530
  27.1 5.0 %collective-permute-start.9 = (f32[40,128]{1,0:T(8,128)S(1)}, f32[40,128]{1,0:T(8,128)S(1)}, u32[]{:S(2)}, u32[]{:S(2)}) collective-permute-start(f32[40,128]{1,0:T(8,128)S(1)} %shard_map.64.own_ref), channel_id=1, source_target_pairs={{32,64},{96,0},{64,32},{0,96},{33,65},{97,1},{65,33},{1,97},{34,66... | collective-permute-start | bytes 61448 | tf_op jit(solution)/shard_map/ppermute | solution.py:530
  28.3 3.8 %collective-permute-start.8 = (f32[40,128]{1,0:T(8,128)S(1)}, f32[40,128]{1,0:T(8,128)S(1)}, u32[]{:S(2)}, u32[]{:S(2)}) collective-permute-start(f32[40,128]{1,0:T(8,128)S(1)} %shard_map.64.own_ref), channel_id=1, source_target_pairs={{0,32},{64,96},{32,0},{96,64},{1,33},{65,97},{33,1},{97,65},{2,34}... | collective-permute-start | bytes 61448 | tf_op jit(solution)/shard_map/ppermute | solution.py:530
  32.2 9.7 %copy-start.4 = (bf16[128,256]{1,0:T(8,128)(2,1)S(1)}, bf16[128,256]{1,0:T(8,128)(2,1)}, u32[]{:S(2)}) copy-start(bf16[128,256]{1,0:T(8,128)(2,1)} %constant.34.clone.wz_ref) | copy-start | bytes 196612

commit v13 on v12

--- a/solution.py
+++ b/solution.py
@@ -216,8 +216,8 @@
             down = pltpu.roll(jnp.where(lane40 >= 123, halo, a), 1, 1)
             slope(h, n)[...] = plus_z * up - minus_z * down
 
-    def x_step(tile, carry):
-        rows = pl.ds(pl.multiple_of(tile * 8, 8), 8)
+    for tile in range(5):
+        rows = slice(8 * tile, 8 * tile + 8)
         for q in range(5):
             p = []
             for n in range(16 if upper else 8):
@@ -244,9 +244,6 @@
             for o in range(8):
                 right = xown_ref[q, o, rows]
                 xs_ref[q, o, rows] = left[o] + ex * right if o < 4 else ex * left[o] + right
-        return carry
-
-    lax.fori_loop(0, 5, x_step, 0)
 
     side = 0 if upper else 1
     x_sum = xsum_ref[128 * side : 128 * side + 128]
@@ -262,13 +259,14 @@
         for n, piece in enumerate(split3(total)):
             hs_ref[q, n] = piece
 
-    from_row = lax.broadcasted_iota(jnp.int32, (256, 128), 0)
+    group = lax.shift_right_logical(lax.broadcasted_iota(jnp.int32, (128, 128), 0), 3)
+    z_own = zsum_ref[0:128].astype(bf16)
+    z_halo = zsum_ref[128:256]
     plus_y = jnp.where(row32 == 3, ey, 1.0)
     minus_y = jnp.where(row32 == 4, ey, 1.0)
 
     for o in range(8):
-        mine = (from_row < 128) | (lax.shift_right_logical(from_row - 128, 3) == o + first)
-        z_sum = jnp.where(mine, zsum_ref[...], 0.0).astype(bf16)
+        z_sum = jnp.concatenate([z_own, jnp.where(group == o + first, z_halo, 0.0).astype(bf16)], axis=0)
         pieces = [[], [], []]
         for q in range(5):
             y = rows_window(xs_ref[q, o], head, tail, row8)

time: 43.7 us -> 43.5 us (level)
  Pallas kernels: 6.51 us -> 5.94 us
    pallas_call x2, Pallas kernels: 4.23 us -> 3.66 us  [forces(): call(functools.partial(force_kernel, upper), [((40, 128), f32)] + [(shape...]
where the time goes in v13:
time: 43.5 us; the launch traced here: 43.1 us
  starting transfers between devices  15.9 us (37%)
  waiting for transfers between devices  9.84 us (23%)
  blocking collectives  9.7 us (22%)
  Pallas kernels  5.94 us (14%)
  local copies, waits for them, and re-layouts  1.06 us (2%)
  between operations  0.71 us (2%)
    ppermute x5, starting transfers between devices, send(): return lax.ppermute(v, AXES, pairs(sizes, di, dj, dk))  9.9 us
    all_to_all x1, blocking collectives, shards(): everything = lax.all_to_all(copies, 'gy', 0, 0, tiled=True)  9.7 us
    ppermute x5, waiting for transfers between devices, shards(): lax.ppermute(v, axis, couples + [(b, a) for a, b in couples])  5.97 us
    ppermute x5, starting transfers between devices, shards(): lax.ppermute(v, axis, couples + [(b, a) for a, b in couples])  5.89 us
    pallas_call x2, Pallas kernels, forces(): call(functools.partial(force_kernel, upper), [((40, 128), f32)] + [(shape...  3.66 us
    ppermute x5, waiting for transfers between devices, send(): return lax.ppermute(v, AXES, pairs(sizes, di, dj, dk))  3.11 us
    pallas_call x1, Pallas kernels, shards(): call(field_kernel, [((6, 2, 16, 32), f32), ((6, 512, 128), bf16)], [VMEM]...  1.49 us
    unnamed x10, local copies, waits for them, and re-layouts  1.06 us
  transfers between devices with their start and end apart: 11, of which 6 were waited for; matrix products, arithmetic and copies ran while one was open for 0% of the time, Pallas kernels for 6%

profile of v13, /device:TPU:0, one launch (start us, length us, event | category | flops | bytes accessed | tf_op | source)
XLA Modules:
  0.0 43.1 jit_solution(2884059122669570384)
XLA Ops:
  0.6 0.0 copy-start
  0.6 1.0 %copy-done = f32[2,16,32,128]{3,2,1,0:T(8,128)S(1)} copy-done((f32[2,16,32,128]{3,2,1,0:T(8,128)S(1)}, f32[2,16,32,128]{3,2,1,0:T(8,128)}, u32[]{:S(2)}) %copy-start) | copy-done | bytes 524312
  1.7 0.0 copy-start.1
  1.7 0.2 shard_map.59.after_ref
  1.9 0.0 copy-start.3
  1.9 0.1 collective-permute-start
  2.0 1.6 %collective-permute-start.1 = (f32[2,16,8,128]{3,2,1,0:T(8,128)S(1)}, f32[2,16,8,128]{3,2,1,0:T(8,128)S(1)}, u32[]{:S(2)}, u32[]{:S(2)}) collective-permute-start(f32[2,16,8,128]{3,2,1,0:T(8,128)S(1)} %get-tuple-element.35), channel_id=1, source_target_pairs={{0,4},{1,5},{2,6},{3,7},{4,8},{5,9},{6,10},{7,11},{8,12},{9,13},{1... | collective-permute-start | bytes 393224 | tf_op jit(solution)/shard_map/ppermute | solution.py:478
  3.6 1.9 %collective-permute-start.3 = (f32[2,8,32,128]{3,2,1,0:T(8,128)S(1)}, f32[2,8,32,128]{3,2,1,0:T(8,128)S(1)}, u32[]{:S(2)}, u32[]{:S(2)}) collective-permute-start(f32[2,8,32,128]{3,2,1,0:T(8,128)S(1)} %get-tuple-element.36), channel_id=1, source_target_pairs={{0,32},{1,33},{2,34},{3,35},{4,36},{5,37},{6,38},{7,39},{8,40},{9,... | collective-permute-start | bytes 786440 | tf_op jit(solution)/shard_map/ppermute | solution.py:478
  5.6 0.0 copy-done.3
  5.6 0.5 %shard_map.60 = (f32[16,128]{1,0:T(8,128)S(1)}, bf16[80,512]{1,0:T(8,128)(2,1)S(1)}, bf16[128,256]{1,0:T(8,128)(2,1)S(1)}, bf16[256,128]{1,0:T(8,128)(2,1)S(1)}, f32[256,128]{1,0:T(8,128)S(1)}) custom-call(f32[6,2,16,32]{3,2,1,0:T(8,128)S(1)} %bitcast.11), custom_call_target="tpu_custom_call" | custom-call | bytes 1000000 | tf_op jit(solution)/shard_map/pallas_call | solution.py:492
  6.0 0.8 %collective-permute-done.zr_ref = f32[2,32,128]{2,1,0:T(8,128)S(1)} collective-permute-done((f32[2,32,128]{2,1,0:T(8,128)S(1)}, f32[2,32,128]{2,1,0:T(8,128)S(1)}, u32[]{:S(2)}, u32[]{:S(2)}) %collective-permute-start) | collective-permute-done | bytes 32800 | tf_op jit(solution)/shard_map/ppermute | solution.py:487
  6.8 1.6 %collective-permute-start.2 = (f32[2,32,128]{2,1,0:T(8,128)S(1)}, f32[2,32,128]{2,1,0:T(8,128)S(1)}, u32[]{:S(2)}, u32[]{:S(2)}) collective-permute-start(f32[2,32,128]{2,1,0:T(8,128)S(1)} %collective-permute-done.zr_ref), channel_id=1, source_target_pairs={{0,4},{1,5},{2,6},{3,7},{4,8},{5,9},{6,10},{7,11},{8,12},{9,13},{1... | collective-permute-start | bytes 98312 | tf_op jit(solution)/shard_map/ppermute | solution.py:478
  8.4 2.8 %collective-permute-start.4 = (f32[2,9,8,128]{3,2,1,0:T(8,128)S(1)}, f32[2,9,8,128]{3,2,1,0:T(8,128)S(1)}, u32[]{:S(2)}, u32[]{:S(2)}) collective-permute-start(f32[2,9,8,128]{3,2,1,0:T(8,128)S(1)} %bitcast_dynamic-update-slice_fusion), channel_id=1, source_target_pairs={{0,36},{1,37},{2,38},{3,39},{4,40},{5,41},{6,42},{7,43},{8,44},{9,... | collective-permute-start | bytes 221192 | tf_op jit(solution)/shard_map/ppermute | solution.py:478
  11.2 1.9 %collective-permute-start.5 = (f32[2,32,128]{2,1,0:T(8,128)S(1)}, f32[2,32,128]{2,1,0:T(8,128)S(1)}, u32[]{:S(2)}, u32[]{:S(2)}) collective-permute-start(f32[2,32,128]{2,1,0:T(8,128)S(1)} %collective-permute-done.zr_ref), channel_id=1, source_target_pairs={{0,32},{1,33},{2,34},{3,35},{4,36},{5,37},{6,38},{7,39},{8,40},{9,... | collective-permute-start | bytes 98312 | tf_op jit(solution)/shard_map/ppermute | solution.py:478
  13.1 0.0 collective-permute-done.2.yzr_ref
  13.1 0.0 collective-permute-done.1.yr_ref
  13.1 0.0 copy-done.1
  13.1 1.9 %shard_map.62 = (f32[40,128]{1,0:T(8,128)S(1)}, f32[2,5,40,128]{3,2,1,0:T(8,128)S(1)}, f32[2,4,40,128]{3,2,1,0:T(8,128)S(1)}, f32[5,8,40,128]{3,2,1,0:T(8,128)S(1)}, f32[5,32,128]{2,1,0:T(8,128)S(1)}) custom-call(f32[2,16,32,128]{3,2,1,0:T(8,128)S(1)} %copy-done.1, f32[2,32,128]{2,1,0:T(8,128)S(1)} %collective-permute-done.zr_ref, ...), custom_call_target="tpu_custom_call" | custom-call | flops 500000000 | bytes 1000000 | tf_op jit(solution)/shard_map/pallas_call | solution.py:506
  15.1 3.1 %collective-permute-done.5.refs_2_ = f32[2,32,128]{2,1,0:T(8,128)S(1)} collective-permute-done((f32[2,32,128]{2,1,0:T(8,128)S(1)}, f32[2,32,128]{2,1,0:T(8,128)S(1)}, u32[]{:S(2)}, u32[]{:S(2)}) %collective-permute-start.5) | collective-permute-done | bytes 32800 | tf_op jit(solution)/shard_map/ppermute | solution.py:478
  18.2 0.0 collective-permute-done.4.refs_1_
  18.2 0.0 collective-permute-done.3.refs_0_
  18.2 1.7 %shard_map.63.mine_ref = f32[40,128]{1,0:T(8,128)S(1)} custom-call(f32[2,16,32,128]{3,2,1,0:T(8,128)S(1)} %copy-done.1, f32[2,32,128]{2,1,0:T(8,128)S(1)} %collective-permute-done.zr_ref, f32[2,16,8,128]{3,2,1,0:T(8,128)S(1)} %collective-permute-done.1.yr_ref, f32[2,32,128]{2,1,0:T(8,128)S(1)} %collective-permute-done.2.yzr_ref, ...), custom_call_target="tpu_custom_call" | custom-call | flops 500000000 | bytes 1000000 | tf_op jit(solution)/shard_map/pallas_call | solution.py:506
  19.9 0.0 copy-start.2
  19.9 0.1 collective-permute-start.7
  20.1 2.2 %collective-permute-start.6 = (f32[40,128]{1,0:T(8,128)S(1)}, f32[40,128]{1,0:T(8,128)S(1)}, u32[]{:S(2)}, u32[]{:S(2)}) collective-permute-start(f32[40,128]{1,0:T(8,128)S(1)} %shard_map.63.mine_ref), channel_id=1, source_target_pairs={{0,1},{2,3},{1,0},{3,2},{4,5},{6,7},{5,4},{7,6},{8,9},{10,11},{9,8... | collective-permute-start | bytes 61448 | tf_op jit(solution)/shard_map/ppermute | solution.py:528
  22.3 2.4 %collective-permute-done.7.chip_ref = f32[40,128]{1,0:T(8,128)S(1)} collective-permute-done((f32[40,128]{1,0:T(8,128)S(1)}, f32[40,128]{1,0:T(8,128)S(1)}, u32[]{:S(2)}, u32[]{:S(2)}) %collective-permute-start.7) | collective-permute-done | bytes 20512 | tf_op jit(solution)/shard_map/ppermute | solution.py:528
  24.7 0.0 collective-permute-done.6.core_ref
  24.7 0.1 shard_map.64.own_ref
  24.8 2.0 %collective-permute-start.10 = (f32[40,128]{1,0:T(8,128)S(1)}, f32[40,128]{1,0:T(8,128)S(1)}, u32[]{:S(2)}, u32[]{:S(2)}) collective-permute-start(f32[40,128]{1,0:T(8,128)S(1)} %shard_map.64.own_ref), channel_id=1, source_target_pairs={{0,64},{32,96},{64,0},{96,32},{1,65},{33,97},{65,1},{97,33},{2,66}... | collective-permute-start | bytes 61448 | tf_op jit(solution)/shard_map/ppermute | solution.py:528
  26.8 1.3 %collective-permute-start.9 = (f32[40,128]{1,0:T(8,128)S(1)}, f32[40,128]{1,0:T(8,128)S(1)}, u32[]{:S(2)}, u32[]{:S(2)}) collective-permute-start(f32[40,128]{1,0:T(8,128)S(1)} %shard_map.64.own_ref), channel_id=1, source_target_pairs={{32,64},{96,0},{64,32},{0,96},{33,65},{97,1},{65,33},{1,97},{34,66... | collective-permute-start | bytes 61448 | tf_op jit(solution)/shard_map/ppermute | solution.py:528
  28.1 0.3 collective-permute-start.8
  28.4 1.8 %collective-permute-done.10.far_ref = f32[40,128]{1,0:T(8,128)S(1)} collective-permute-done((f32[40,128]{1,0:T(8,128)S(1)}, f32[40,128]{1,0:T(8,128)S(1)}, u32[]{:S(2)}, u32[]{:S(2)}) %collective-permute-start.10) | collective-permute-done | bytes 20512 | tf_op jit(solution)/shard_map/ppermute | solution.py:528
  30.2 1.6 %collective-permute-done.9.two_ref = f32[40,128]{1,0:T(8,128)S(1)} collective-permute-done((f32[40,128]{1,0:T(8,128)S(1)}, f32[40,128]{1,0:T(8,128)S(1)}, u32[]{:S(2)}, u32[]{:S(2)}) %collective-permute-start.9) | collective-permute-done | bytes 20512 | tf_op jit(solution)/shard_map/ppermute | solution.py:528
  31.8 0.1 collective-permute-done.8.one_ref
  31.9 0.0 copy-start.4
  31.9 9.7 %all_to_all.5.g_ref = f32[8,32,128]{2,1,0:T(8,128)S(1)} all-to-all(f32[8,32,128]{2,1,0:T(8,128)S(1)} %get-tuple-element.48), channel_id=1, replica_groups=mesh['gx'=4,'gy'=8,'gz'=4] {'gy'}, dimensions={0} | all-to-all | bytes 262144 | tf_op jit(solution)/shard_map/all_to_all | solution.py:536
  41.6 0.0 copy-done.2
  41.6 0.0 copy-done.4
  41.6 1.5 %shard_map.66 = (f32[6,2,16,32]{3,2,1,0:T(8,128)}, bf16[6,512,128]{2,1,0:T(8,128)(2,1)}) custom-call(f32[8,32,128]{2,1,0:T(8,128)S(1)} %all_to_all.5.g_ref, f32[48,128]{1,0:T(8,128)S(1)} %get-tuple-element.49.mine_ref, bf16[512,144]{1,0:T(8,128)(2,1)S(1)} %copy-done.2, bf16[128,256]{1,0:T(8,128)(2,1)S(1)} %copy-done.4), custom_call_target="tpu_custom_call" | custom-call | flops 100000000 | bytes 1000000 | tf_op jit(solution)/shard_map/pallas_call | solution.py:538
  (3 shorter events, 0.1 us)
Async XLA Ops:
  0.6 1.0 %copy-start = (f32[2,16,32,128]{3,2,1,0:T(8,128)S(1)}, f32[2,16,32,128]{3,2,1,0:T(8,128)}, u32[]{:S(2)}) copy-start(f32[2,16,32,128]{3,2,1,0:T(8,128)} %own_ref.3) | copy-start | bytes 1572868
  1.7 11.5 %copy-start.1 = (f32[2,16,32,128]{3,2,1,0:T(8,128)S(1)}, f32[2,16,32,128]{3,2,1,0:T(8,128)}, u32[]{:S(2)}) copy-start(f32[2,16,32,128]{3,2,1,0:T(8,128)} %own_ref.3) | copy-start | bytes 1572868
  1.9 3.7 %copy-start.3 = (f32[2,3,2,32,16]{3,4,2,1,0:T(8,128)S(1)}, f32[2,3,2,32,16]{3,4,2,1,0:T(8,128)}, u32[]{:S(2)}) copy-start(f32[2,3,2,32,16]{3,4,2,1,0:T(8,128)} %param.7) | copy-start | bytes 73732
  1.9 4.9 %collective-permute-start = (f32[2,32,128]{2,1,0:T(8,128)S(1)}, f32[2,32,128]{2,1,0:T(8,128)S(1)}, u32[]{:S(2)}, u32[]{:S(2)}) collective-permute-start(f32[2,32,128]{2,1,0:T(8,128)S(1)} %shard_map.59.after_ref), channel_id=1, source_target_pairs={{0,1},{1,2},{2,3},{3,0},{4,5},{5,6},{6,7},{7,4},{8,9},{9,10},{10,1... | collective-permute-start | bytes 98312 | tf_op jit(solution)/shard_map/ppermute | solution.py:487
  2.0 11.1 %collective-permute-start.1 = (f32[2,16,8,128]{3,2,1,0:T(8,128)S(1)}, f32[2,16,8,128]{3,2,1,0:T(8,128)S(1)}, u32[]{:S(2)}, u32[]{:S(2)}) collective-permute-start(f32[2,16,8,128]{3,2,1,0:T(8,128)S(1)} %get-tuple-element.35), channel_id=1, source_target_pairs={{0,4},{1,5},{2,6},{3,7},{4,8},{5,9},{6,10},{7,11},{8,12},{9,13},{1... | collective-permute-start | bytes 393224 | tf_op jit(solution)/shard_map/ppermute | solution.py:478
  3.6 14.6 %collective-permute-start.3 = (f32[2,8,32,128]{3,2,1,0:T(8,128)S(1)}, f32[2,8,32,128]{3,2,1,0:T(8,128)S(1)}, u32[]{:S(2)}, u32[]{:S(2)}) collective-permute-start(f32[2,8,32,128]{3,2,1,0:T(8,128)S(1)} %get-tuple-element.36), channel_id=1, source_target_pairs={{0,32},{1,33},{2,34},{3,35},{4,36},{5,37},{6,38},{7,39},{8,40},{9,... | collective-permute-start | bytes 786440 | tf_op jit(solution)/shard_map/ppermute | solution.py:478
  6.8 6.3 %collective-permute-start.2 = (f32[2,32,128]{2,1,0:T(8,128)S(1)}, f32[2,32,128]{2,1,0:T(8,128)S(1)}, u32[]{:S(2)}, u32[]{:S(2)}) collective-permute-start(f32[2,32,128]{2,1,0:T(8,128)S(1)} %collective-permute-done.zr_ref), channel_id=1, source_target_pairs={{0,4},{1,5},{2,6},{3,7},{4,8},{5,9},{6,10},{7,11},{8,12},{9,13},{1... | collective-permute-start | bytes 98312 | tf_op jit(solution)/shard_map/ppermute | solution.py:478
  8.4 9.8 %collective-permute-start.4 = (f32[2,9,8,128]{3,2,1,0:T(8,128)S(1)}, f32[2,9,8,128]{3,2,1,0:T(8,128)S(1)}, u32[]{:S(2)}, u32[]{:S(2)}) collective-permute-start(f32[2,9,8,128]{3,2,1,0:T(8,128)S(1)} %bitcast_dynamic-update-slice_fusion), channel_id=1, source_target_pairs={{0,36},{1,37},{2,38},{3,39},{4,40},{5,41},{6,42},{7,43},{8,44},{9,... | collective-permute-start | bytes 221192 | tf_op jit(solution)/shard_map/ppermute | solution.py:478
  11.2 7.0 %collective-permute-start.5 = (f32[2,32,128]{2,1,0:T(8,128)S(1)}, f32[2,32,128]{2,1,0:T(8,128)S(1)}, u32[]{:S(2)}, u32[]{:S(2)}) collective-permute-start(f32[2,32,128]{2,1,0:T(8,128)S(1)} %collective-permute-done.zr_ref), channel_id=1, source_target_pairs={{0,32},{1,33},{2,34},{3,35},{4,36},{5,37},{6,38},{7,39},{8,40},{9,... | collective-permute-start | bytes 98312 | tf_op jit(solution)/shard_map/ppermute | solution.py:478
  19.9 21.7 %copy-start.2 = (bf16[512,144]{1,0:T(8,128)(2,1)S(1)}, bf16[512,144]{1,0:T(8,128)(2,1)}, u32[]{:S(2)}) copy-start(bf16[512,144]{1,0:T(8,128)(2,1)} %constant.33.clone.wxy_ref) | copy-start | bytes 442372
  19.9 4.8 %collective-permute-start.7 = (f32[40,128]{1,0:T(8,128)S(1)}, f32[40,128]{1,0:T(8,128)S(1)}, u32[]{:S(2)}, u32[]{:S(2)}) collective-permute-start(f32[40,128]{1,0:T(8,128)S(1)} %shard_map.63.mine_ref), channel_id=1, source_target_pairs={{1,2},{3,0},{2,1},{0,3},{5,6},{7,4},{6,5},{4,7},{9,10},{11,8},{10,... | collective-permute-start | bytes 61448 | tf_op jit(solution)/shard_map/ppermute | solution.py:528
  20.1 4.6 %collective-permute-start.6 = (f32[40,128]{1,0:T(8,128)S(1)}, f32[40,128]{1,0:T(8,128)S(1)}, u32[]{:S(2)}, u32[]{:S(2)}) collective-permute-start(f32[40,128]{1,0:T(8,128)S(1)} %shard_map.63.mine_ref), channel_id=1, source_target_pairs={{0,1},{2,3},{1,0},{3,2},{4,5},{6,7},{5,4},{7,6},{8,9},{10,11},{9,8... | collective-permute-start | bytes 61448 | tf_op jit(solution)/shard_map/ppermute | solution.py:528
  24.8 5.3 %collective-permute-start.10 = (f32[40,128]{1,0:T(8,128)S(1)}, f32[40,128]{1,0:T(8,128)S(1)}, u32[]{:S(2)}, u32[]{:S(2)}) collective-permute-start(f32[40,128]{1,0:T(8,128)S(1)} %shard_map.64.own_ref), channel_id=1, source_target_pairs={{0,64},{32,96},{64,0},{96,32},{1,65},{33,97},{65,1},{97,33},{2,66}... | collective-permute-start | bytes 61448 | tf_op jit(solution)/shard_map/ppermute | solution.py:528
  26.8 5.0 %collective-permute-start.9 = (f32[40,128]{1,0:T(8,128)S(1)}, f32[40,128]{1,0:T(8,128)S(1)}, u32[]{:S(2)}, u32[]{:S(2)}) collective-permute-start(f32[40,128]{1,0:T(8,128)S(1)} %shard_map.64.own_ref), channel_id=1, source_target_pairs={{32,64},{96,0},{64,32},{0,96},{33,65},{97,1},{65,33},{1,97},{34,66... | collective-permute-start | bytes 61448 | tf_op jit(solution)/shard_map/ppermute | solution.py:528
  28.1 3.8 %collective-permute-start.8 = (f32[40,128]{1,0:T(8,128)S(1)}, f32[40,128]{1,0:T(8,128)S(1)}, u32[]{:S(2)}, u32[]{:S(2)}) collective-permute-start(f32[40,128]{1,0:T(8,128)S(1)} %shard_map.64.own_ref), channel_id=1, source_target_pairs={{0,32},{64,96},{32,0},{96,64},{1,33},{65,97},{33,1},{97,65},{2,34}... | collective-permute-start | bytes 61448 | tf_op jit(solution)/shard_map/ppermute | solution.py:528
  31.9 9.7 %copy-start.4 = (bf16[128,256]{1,0:T(8,128)(2,1)S(1)}, bf16[128,256]{1,0:T(8,128)(2,1)}, u32[]{:S(2)}) copy-start(bf16[128,256]{1,0:T(8,128)(2,1)} %constant.34.clone.wz_ref) | copy-start | bytes 196612

commit v14 on v13

--- a/solution.py
+++ b/solution.py
@@ -297,16 +297,18 @@
             dz = slope(h, o + 4)[4:36]
             for c, d in enumerate((dx, dy, dz)):
                 hi, lo = split2(pulls[h] * d)
-                fh_ref[3 * h + c, where_to] = hi
-                fl_ref[3 * h + c, where_to] = lo
+                pair, lanes = divmod(3 * h + c, 2)
+                fh_ref[pair, where_to, 128 * lanes : 128 * lanes + 128] = hi
+                fl_ref[pair, where_to, 128 * lanes : 128 * lanes + 128] = lo
 
     cols = slice(32 * first, 32 * first + 256)
     wxy = wxy_ref[:, cols]
     wxy_hi = wxy_ref[0:40, cols]
     lattice = []
-    for c in range(6):
-        one = dot(wxy, fh_ref[c])
-        lattice.append(one[0:40] + one[40:80] + dot(wxy_hi, fl_ref[c]))
+    for pair in range(3):
+        one = dot(wxy, fh_ref[pair])
+        both = one[0:40] + one[40:80] + dot(wxy_hi, fl_ref[pair])
+        lattice += [both[:, 0:128], both[:, 128:256]]
     hi, lo = split2(jnp.concatenate(lattice, axis=0))
     along = dot(jnp.concatenate([hi, lo], axis=0), wz_ref[...])
     along = (along[0:240, 0:128] + along[0:240, 128:256]) + along[240:480, 0:128]
@@ -400,13 +402,16 @@
         for c in (2 * pair, 2 * pair + 1):
             rows = slice(48 * c, 48 * c + 48)
             rhs.append(jnp.concatenate([ch[rows], cl[rows], ch[rows]], axis=0))
-        both = dot(wxy_ref[...], jnp.concatenate(rhs, axis=1)).astype(bf16)
-        for n in range(2):
-            buf_ref[2 * pair + n] = both[:, 128 * n : 128 * n + 128]
-        there = pl.ds(2 * pair, 2)
-        copy = pltpu.make_async_copy(buf_ref.at[there], field_ref.at[there], sems.at[pair])
-        copy.start()
-        copies.append(copy)
+        rhs = jnp.concatenate(rhs, axis=1)
+        for half in range(2):
+            rows = pl.ds(256 * half, 256)
+            both = dot(wxy_ref[rows], rhs).astype(bf16)
+            for n in range(2):
+                buf_ref[2 * pair + n, rows] = both[:, 128 * n : 128 * n + 128]
+            there = pl.ds(2 * pair, 2)
+            copy = pltpu.make_async_copy(buf_ref.at[there, rows], field_ref.at[there, rows], sems.at[2 * pair + half])
+            copy.start()
+            copies.append(copy)
 
     for side in range(2):
         cols = [g_ref[j, 8 * side : 8 * side + 8] for j in range(8)]
@@ -424,7 +429,7 @@
         block = jnp.transpose(rows_ref[side, 2:34])
         for c in range(6):
             own_ref[c, side] = block[20 * c + 2 : 20 * c + 18]
-    copy = pltpu.make_async_copy(own_ref, nv_ref, sems.at[3])
+    copy = pltpu.make_async_copy(own_ref, nv_ref, sems.at[6])
     copy.start()
     copies.append(copy)
     for copy in copies:
@@ -514,8 +519,8 @@
                 pltpu.VMEM((2, 8, 40, 128), f32),
                 pltpu.VMEM((5, 8, 40, 128), f32),
                 pltpu.VMEM((5, 3, 32, 128), bf16),
-                pltpu.VMEM((6, 256, 128), bf16),
-                pltpu.VMEM((6, 256, 128), bf16),
+                pltpu.VMEM((3, 256, 256), bf16),
+                pltpu.VMEM((3, 256, 256), bf16),
             ],
             flops=5 * 10**8,
             bytes_accessed=10**6,
@@ -539,7 +544,7 @@
         field_kernel,
         [((6, 2, 16, 32), f32), ((6, 512, 128), bf16)],
         [VMEM] * 4,
-        [pltpu.VMEM((2, 40, 128), f32), pltpu.VMEM((6, 512, 128), bf16), pltpu.VMEM((6, 2, 16, 32), f32), pltpu.SemaphoreType.DMA((4,))],
+        [pltpu.VMEM((2, 40, 128), f32), pltpu.VMEM((6, 512, 128), bf16), pltpu.VMEM((6, 2, 16, 32), f32), pltpu.SemaphoreType.DMA((7,))],
         out_specs=[HBM, HBM],
         flops=10**8,
         bytes_accessed=10**6,

time: 43.5 us -> 43.5 us (level)
  no operation moved by 1% of the time
where the time goes in v14:
time: 43.5 us; the launch traced here: 43.1 us
  starting transfers between devices  15.9 us (37%)
  waiting for transfers between devices  9.88 us (23%)
  blocking collectives  9.69 us (22%)
  Pallas kernels  5.88 us (14%)
  local copies, waits for them, and re-layouts  1.06 us (2%)
  between operations  0.71 us (2%)
    ppermute x5, starting transfers between devices, send(): return lax.ppermute(v, AXES, pairs(sizes, di, dj, dk))  9.9 us
    all_to_all x1, blocking collectives, shards(): everything = lax.all_to_all(copies, 'gy', 0, 0, tiled=True)  9.69 us
    ppermute x5, waiting for transfers between devices, shards(): lax.ppermute(v, axis, couples + [(b, a) for a, b in couples])  5.98 us
    ppermute x5, starting transfers between devices, shards(): lax.ppermute(v, axis, couples + [(b, a) for a, b in couples])  5.89 us
    pallas_call x2, Pallas kernels, forces(): call(functools.partial(force_kernel, upper), [((40, 128), f32)] + [(shape...  3.62 us
    ppermute x5, waiting for transfers between devices, send(): return lax.ppermute(v, AXES, pairs(sizes, di, dj, dk))  3.14 us
    pallas_call x1, Pallas kernels, shards(): call(field_kernel, [((6, 2, 16, 32), f32), ((6, 512, 128), bf16)], [VMEM]...  1.46 us
    unnamed x10, local copies, waits for them, and re-layouts  1.06 us
  transfers between devices with their start and end apart: 11, of which 6 were waited for; matrix products, arithmetic and copies ran while one was open for 0% of the time, Pallas kernels for 6%

profile of v14, /device:TPU:0, one launch (start us, length us, event | category | flops | bytes accessed | tf_op | source)
XLA Modules:
  0.0 43.1 jit_solution(15159783419711043621)
XLA Ops:
  0.6 0.0 copy-start
  0.6 1.0 %copy-done = f32[2,16,32,128]{3,2,1,0:T(8,128)S(1)} copy-done((f32[2,16,32,128]{3,2,1,0:T(8,128)S(1)}, f32[2,16,32,128]{3,2,1,0:T(8,128)}, u32[]{:S(2)}) %copy-start) | copy-done | bytes 524312
  1.7 0.0 copy-start.1
  1.7 0.2 shard_map.59.after_ref
  1.9 0.0 copy-start.3
  1.9 0.1 collective-permute-start
  2.0 1.6 %collective-permute-start.1 = (f32[2,16,8,128]{3,2,1,0:T(8,128)S(1)}, f32[2,16,8,128]{3,2,1,0:T(8,128)S(1)}, u32[]{:S(2)}, u32[]{:S(2)}) collective-permute-start(f32[2,16,8,128]{3,2,1,0:T(8,128)S(1)} %get-tuple-element.35), channel_id=1, source_target_pairs={{0,4},{1,5},{2,6},{3,7},{4,8},{5,9},{6,10},{7,11},{8,12},{9,13},{1... | collective-permute-start | bytes 393224 | tf_op jit(solution)/shard_map/ppermute | solution.py:483
  3.6 1.9 %collective-permute-start.3 = (f32[2,8,32,128]{3,2,1,0:T(8,128)S(1)}, f32[2,8,32,128]{3,2,1,0:T(8,128)S(1)}, u32[]{:S(2)}, u32[]{:S(2)}) collective-permute-start(f32[2,8,32,128]{3,2,1,0:T(8,128)S(1)} %get-tuple-element.36), channel_id=1, source_target_pairs={{0,32},{1,33},{2,34},{3,35},{4,36},{5,37},{6,38},{7,39},{8,40},{9,... | collective-permute-start | bytes 786440 | tf_op jit(solution)/shard_map/ppermute | solution.py:483
  5.6 0.0 copy-done.3
  5.6 0.5 %shard_map.60 = (f32[16,128]{1,0:T(8,128)S(1)}, bf16[80,512]{1,0:T(8,128)(2,1)S(1)}, bf16[128,256]{1,0:T(8,128)(2,1)S(1)}, bf16[256,128]{1,0:T(8,128)(2,1)S(1)}, f32[256,128]{1,0:T(8,128)S(1)}) custom-call(f32[6,2,16,32]{3,2,1,0:T(8,128)S(1)} %bitcast.11), custom_call_target="tpu_custom_call" | custom-call | bytes 1000000 | tf_op jit(solution)/shard_map/pallas_call | solution.py:497
  6.0 0.8 %collective-permute-done.zr_ref = f32[2,32,128]{2,1,0:T(8,128)S(1)} collective-permute-done((f32[2,32,128]{2,1,0:T(8,128)S(1)}, f32[2,32,128]{2,1,0:T(8,128)S(1)}, u32[]{:S(2)}, u32[]{:S(2)}) %collective-permute-start) | collective-permute-done | bytes 32800 | tf_op jit(solution)/shard_map/ppermute | solution.py:492
  6.8 1.6 %collective-permute-start.2 = (f32[2,32,128]{2,1,0:T(8,128)S(1)}, f32[2,32,128]{2,1,0:T(8,128)S(1)}, u32[]{:S(2)}, u32[]{:S(2)}) collective-permute-start(f32[2,32,128]{2,1,0:T(8,128)S(1)} %collective-permute-done.zr_ref), channel_id=1, source_target_pairs={{0,4},{1,5},{2,6},{3,7},{4,8},{5,9},{6,10},{7,11},{8,12},{9,13},{1... | collective-permute-start | bytes 98312 | tf_op jit(solution)/shard_map/ppermute | solution.py:483
  8.4 2.8 %collective-permute-start.4 = (f32[2,9,8,128]{3,2,1,0:T(8,128)S(1)}, f32[2,9,8,128]{3,2,1,0:T(8,128)S(1)}, u32[]{:S(2)}, u32[]{:S(2)}) collective-permute-start(f32[2,9,8,128]{3,2,1,0:T(8,128)S(1)} %bitcast_dynamic-update-slice_fusion), channel_id=1, source_target_pairs={{0,36},{1,37},{2,38},{3,39},{4,40},{5,41},{6,42},{7,43},{8,44},{9,... | collective-permute-start | bytes 221192 | tf_op jit(solution)/shard_map/ppermute | solution.py:483
  11.2 1.9 %collective-permute-start.5 = (f32[2,32,128]{2,1,0:T(8,128)S(1)}, f32[2,32,128]{2,1,0:T(8,128)S(1)}, u32[]{:S(2)}, u32[]{:S(2)}) collective-permute-start(f32[2,32,128]{2,1,0:T(8,128)S(1)} %collective-permute-done.zr_ref), channel_id=1, source_target_pairs={{0,32},{1,33},{2,34},{3,35},{4,36},{5,37},{6,38},{7,39},{8,40},{9,... | collective-permute-start | bytes 98312 | tf_op jit(solution)/shard_map/ppermute | solution.py:483
  13.1 0.0 collective-permute-done.2.yzr_ref
  13.1 0.0 collective-permute-done.1.yr_ref
  13.1 0.0 copy-done.1
  13.1 1.9 %shard_map.62 = (f32[40,128]{1,0:T(8,128)S(1)}, f32[2,5,40,128]{3,2,1,0:T(8,128)S(1)}, f32[2,4,40,128]{3,2,1,0:T(8,128)S(1)}, f32[5,8,40,128]{3,2,1,0:T(8,128)S(1)}, f32[5,32,128]{2,1,0:T(8,128)S(1)}) custom-call(f32[2,16,32,128]{3,2,1,0:T(8,128)S(1)} %copy-done.1, f32[2,32,128]{2,1,0:T(8,128)S(1)} %collective-permute-done.zr_ref, ...), custom_call_target="tpu_custom_call" | custom-call | flops 500000000 | bytes 1000000 | tf_op jit(solution)/shard_map/pallas_call | solution.py:511
  15.1 3.1 %collective-permute-done.5.refs_2_ = f32[2,32,128]{2,1,0:T(8,128)S(1)} collective-permute-done((f32[2,32,128]{2,1,0:T(8,128)S(1)}, f32[2,32,128]{2,1,0:T(8,128)S(1)}, u32[]{:S(2)}, u32[]{:S(2)}) %collective-permute-start.5) | collective-permute-done | bytes 32800 | tf_op jit(solution)/shard_map/ppermute | solution.py:483
  18.2 0.0 collective-permute-done.4.refs_1_
  18.2 0.0 collective-permute-done.3.refs_0_
  18.2 1.7 %shard_map.63.mine_ref = f32[40,128]{1,0:T(8,128)S(1)} custom-call(f32[2,16,32,128]{3,2,1,0:T(8,128)S(1)} %copy-done.1, f32[2,32,128]{2,1,0:T(8,128)S(1)} %collective-permute-done.zr_ref, f32[2,16,8,128]{3,2,1,0:T(8,128)S(1)} %collective-permute-done.1.yr_ref, f32[2,32,128]{2,1,0:T(8,128)S(1)} %collective-permute-done.2.yzr_ref, ...), custom_call_target="tpu_custom_call" | custom-call | flops 500000000 | bytes 1000000 | tf_op jit(solution)/shard_map/pallas_call | solution.py:511
  19.9 0.0 copy-start.2
  19.9 0.1 collective-permute-start.7
  20.1 2.2 %collective-permute-start.6 = (f32[40,128]{1,0:T(8,128)S(1)}, f32[40,128]{1,0:T(8,128)S(1)}, u32[]{:S(2)}, u32[]{:S(2)}) collective-permute-start(f32[40,128]{1,0:T(8,128)S(1)} %shard_map.63.mine_ref), channel_id=1, source_target_pairs={{0,1},{2,3},{1,0},{3,2},{4,5},{6,7},{5,4},{7,6},{8,9},{10,11},{9,8... | collective-permute-start | bytes 61448 | tf_op jit(solution)/shard_map/ppermute | solution.py:533
  22.3 2.4 %collective-permute-done.7.chip_ref = f32[40,128]{1,0:T(8,128)S(1)} collective-permute-done((f32[40,128]{1,0:T(8,128)S(1)}, f32[40,128]{1,0:T(8,128)S(1)}, u32[]{:S(2)}, u32[]{:S(2)}) %collective-permute-start.7) | collective-permute-done | bytes 20512 | tf_op jit(solution)/shard_map/ppermute | solution.py:533
  24.7 0.0 collective-permute-done.6.core_ref
  24.7 0.1 shard_map.64.own_ref
  24.8 2.0 %collective-permute-start.10 = (f32[40,128]{1,0:T(8,128)S(1)}, f32[40,128]{1,0:T(8,128)S(1)}, u32[]{:S(2)}, u32[]{:S(2)}) collective-permute-start(f32[40,128]{1,0:T(8,128)S(1)} %shard_map.64.own_ref), channel_id=1, source_target_pairs={{0,64},{32,96},{64,0},{96,32},{1,65},{33,97},{65,1},{97,33},{2,66}... | collective-permute-start | bytes 61448 | tf_op jit(solution)/shard_map/ppermute | solution.py:533
  26.8 1.3 %collective-permute-start.9 = (f32[40,128]{1,0:T(8,128)S(1)}, f32[40,128]{1,0:T(8,128)S(1)}, u32[]{:S(2)}, u32[]{:S(2)}) collective-permute-start(f32[40,128]{1,0:T(8,128)S(1)} %shard_map.64.own_ref), channel_id=1, source_target_pairs={{32,64},{96,0},{64,32},{0,96},{33,65},{97,1},{65,33},{1,97},{34,66... | collective-permute-start | bytes 61448 | tf_op jit(solution)/shard_map/ppermute | solution.py:533
  28.1 0.2 collective-permute-start.8
  28.3 1.8 %collective-permute-done.10.far_ref = f32[40,128]{1,0:T(8,128)S(1)} collective-permute-done((f32[40,128]{1,0:T(8,128)S(1)}, f32[40,128]{1,0:T(8,128)S(1)}, u32[]{:S(2)}, u32[]{:S(2)}) %collective-permute-start.10) | collective-permute-done | bytes 20512 | tf_op jit(solution)/shard_map/ppermute | solution.py:533
  30.1 1.6 %collective-permute-done.9.two_ref = f32[40,128]{1,0:T(8,128)S(1)} collective-permute-done((f32[40,128]{1,0:T(8,128)S(1)}, f32[40,128]{1,0:T(8,128)S(1)}, u32[]{:S(2)}, u32[]{:S(2)}) %collective-permute-start.9) | collective-permute-done | bytes 20512 | tf_op jit(solution)/shard_map/ppermute | solution.py:533
  31.8 0.1 collective-permute-done.8.one_ref
  31.9 0.0 copy-start.4
  31.9 9.7 %all_to_all.5.g_ref = f32[8,32,128]{2,1,0:T(8,128)S(1)} all-to-all(f32[8,32,128]{2,1,0:T(8,128)S(1)} %get-tuple-element.48), channel_id=1, replica_groups=mesh['gx'=4,'gy'=8,'gz'=4] {'gy'}, dimensions={0} | all-to-all | bytes 262144 | tf_op jit(solution)/shard_map/all_to_all | solution.py:541
  41.6 0.0 copy-done.2
  41.6 0.0 copy-done.4
  41.6 1.5 %shard_map.66 = (f32[6,2,16,32]{3,2,1,0:T(8,128)}, bf16[6,512,128]{2,1,0:T(8,128)(2,1)}) custom-call(f32[8,32,128]{2,1,0:T(8,128)S(1)} %all_to_all.5.g_ref, f32[48,128]{1,0:T(8,128)S(1)} %get-tuple-element.49.mine_ref, bf16[512,144]{1,0:T(8,128)(2,1)S(1)} %copy-done.2, bf16[128,256]{1,0:T(8,128)(2,1)S(1)} %copy-done.4), custom_call_target="tpu_custom_call" | custom-call | flops 100000000 | bytes 1000000 | tf_op jit(solution)/shard_map/pallas_call | solution.py:543
  (3 shorter events, 0.1 us)
Async XLA Ops:
  0.6 1.0 %copy-start = (f32[2,16,32,128]{3,2,1,0:T(8,128)S(1)}, f32[2,16,32,128]{3,2,1,0:T(8,128)}, u32[]{:S(2)}) copy-start(f32[2,16,32,128]{3,2,1,0:T(8,128)} %own_ref.3) | copy-start | bytes 1572868
  1.7 11.5 %copy-start.1 = (f32[2,16,32,128]{3,2,1,0:T(8,128)S(1)}, f32[2,16,32,128]{3,2,1,0:T(8,128)}, u32[]{:S(2)}) copy-start(f32[2,16,32,128]{3,2,1,0:T(8,128)} %own_ref.3) | copy-start | bytes 1572868
  1.9 3.7 %copy-start.3 = (f32[2,3,2,32,16]{3,4,2,1,0:T(8,128)S(1)}, f32[2,3,2,32,16]{3,4,2,1,0:T(8,128)}, u32[]{:S(2)}) copy-start(f32[2,3,2,32,16]{3,4,2,1,0:T(8,128)} %param.7) | copy-start | bytes 73732
  1.9 4.9 %collective-permute-start = (f32[2,32,128]{2,1,0:T(8,128)S(1)}, f32[2,32,128]{2,1,0:T(8,128)S(1)}, u32[]{:S(2)}, u32[]{:S(2)}) collective-permute-start(f32[2,32,128]{2,1,0:T(8,128)S(1)} %shard_map.59.after_ref), channel_id=1, source_target_pairs={{0,1},{1,2},{2,3},{3,0},{4,5},{5,6},{6,7},{7,4},{8,9},{9,10},{10,1... | collective-permute-start | bytes 98312 | tf_op jit(solution)/shard_map/ppermute | solution.py:492
  2.0 11.1 %collective-permute-start.1 = (f32[2,16,8,128]{3,2,1,0:T(8,128)S(1)}, f32[2,16,8,128]{3,2,1,0:T(8,128)S(1)}, u32[]{:S(2)}, u32[]{:S(2)}) collective-permute-start(f32[2,16,8,128]{3,2,1,0:T(8,128)S(1)} %get-tuple-element.35), channel_id=1, source_target_pairs={{0,4},{1,5},{2,6},{3,7},{4,8},{5,9},{6,10},{7,11},{8,12},{9,13},{1... | collective-permute-start | bytes 393224 | tf_op jit(solution)/shard_map/ppermute | solution.py:483
  3.6 14.6 %collective-permute-start.3 = (f32[2,8,32,128]{3,2,1,0:T(8,128)S(1)}, f32[2,8,32,128]{3,2,1,0:T(8,128)S(1)}, u32[]{:S(2)}, u32[]{:S(2)}) collective-permute-start(f32[2,8,32,128]{3,2,1,0:T(8,128)S(1)} %get-tuple-element.36), channel_id=1, source_target_pairs={{0,32},{1,33},{2,34},{3,35},{4,36},{5,37},{6,38},{7,39},{8,40},{9,... | collective-permute-start | bytes 786440 | tf_op jit(solution)/shard_map/ppermute | solution.py:483
  6.8 6.3 %collective-permute-start.2 = (f32[2,32,128]{2,1,0:T(8,128)S(1)}, f32[2,32,128]{2,1,0:T(8,128)S(1)}, u32[]{:S(2)}, u32[]{:S(2)}) collective-permute-start(f32[2,32,128]{2,1,0:T(8,128)S(1)} %collective-permute-done.zr_ref), channel_id=1, source_target_pairs={{0,4},{1,5},{2,6},{3,7},{4,8},{5,9},{6,10},{7,11},{8,12},{9,13},{1... | collective-permute-start | bytes 98312 | tf_op jit(solution)/shard_map/ppermute | solution.py:483
  8.4 9.8 %collective-permute-start.4 = (f32[2,9,8,128]{3,2,1,0:T(8,128)S(1)}, f32[2,9,8,128]{3,2,1,0:T(8,128)S(1)}, u32[]{:S(2)}, u32[]{:S(2)}) collective-permute-start(f32[2,9,8,128]{3,2,1,0:T(8,128)S(1)} %bitcast_dynamic-update-slice_fusion), channel_id=1, source_target_pairs={{0,36},{1,37},{2,38},{3,39},{4,40},{5,41},{6,42},{7,43},{8,44},{9,... | collective-permute-start | bytes 221192 | tf_op jit(solution)/shard_map/ppermute | solution.py:483
  11.2 7.0 %collective-permute-start.5 = (f32[2,32,128]{2,1,0:T(8,128)S(1)}, f32[2,32,128]{2,1,0:T(8,128)S(1)}, u32[]{:S(2)}, u32[]{:S(2)}) collective-permute-start(f32[2,32,128]{2,1,0:T(8,128)S(1)} %collective-permute-done.zr_ref), channel_id=1, source_target_pairs={{0,32},{1,33},{2,34},{3,35},{4,36},{5,37},{6,38},{7,39},{8,40},{9,... | collective-permute-start | bytes 98312 | tf_op jit(solution)/shard_map/ppermute | solution.py:483
  19.9 21.7 %copy-start.2 = (bf16[512,144]{1,0:T(8,128)(2,1)S(1)}, bf16[512,144]{1,0:T(8,128)(2,1)}, u32[]{:S(2)}) copy-start(bf16[512,144]{1,0:T(8,128)(2,1)} %constant.33.clone.wxy_ref) | copy-start | bytes 442372
  19.9 4.8 %collective-permute-start.7 = (f32[40,128]{1,0:T(8,128)S(1)}, f32[40,128]{1,0:T(8,128)S(1)}, u32[]{:S(2)}, u32[]{:S(2)}) collective-permute-start(f32[40,128]{1,0:T(8,128)S(1)} %shard_map.63.mine_ref), channel_id=1, source_target_pairs={{1,2},{3,0},{2,1},{0,3},{5,6},{7,4},{6,5},{4,7},{9,10},{11,8},{10,... | collective-permute-start | bytes 61448 | tf_op jit(solution)/shard_map/ppermute | solution.py:533
  20.1 4.6 %collective-permute-start.6 = (f32[40,128]{1,0:T(8,128)S(1)}, f32[40,128]{1,0:T(8,128)S(1)}, u32[]{:S(2)}, u32[]{:S(2)}) collective-permute-start(f32[40,128]{1,0:T(8,128)S(1)} %shard_map.63.mine_ref), channel_id=1, source_target_pairs={{0,1},{2,3},{1,0},{3,2},{4,5},{6,7},{5,4},{7,6},{8,9},{10,11},{9,8... | collective-permute-start | bytes 61448 | tf_op jit(solution)/shard_map/ppermute | solution.py:533
  24.8 5.3 %collective-permute-start.10 = (f32[40,128]{1,0:T(8,128)S(1)}, f32[40,128]{1,0:T(8,128)S(1)}, u32[]{:S(2)}, u32[]{:S(2)}) collective-permute-start(f32[40,128]{1,0:T(8,128)S(1)} %shard_map.64.own_ref), channel_id=1, source_target_pairs={{0,64},{32,96},{64,0},{96,32},{1,65},{33,97},{65,1},{97,33},{2,66}... | collective-permute-start | bytes 61448 | tf_op jit(solution)/shard_map/ppermute | solution.py:533
  26.8 5.0 %collective-permute-start.9 = (f32[40,128]{1,0:T(8,128)S(1)}, f32[40,128]{1,0:T(8,128)S(1)}, u32[]{:S(2)}, u32[]{:S(2)}) collective-permute-start(f32[40,128]{1,0:T(8,128)S(1)} %shard_map.64.own_ref), channel_id=1, source_target_pairs={{32,64},{96,0},{64,32},{0,96},{33,65},{97,1},{65,33},{1,97},{34,66... | collective-permute-start | bytes 61448 | tf_op jit(solution)/shard_map/ppermute | solution.py:533
  28.1 3.8 %collective-permute-start.8 = (f32[40,128]{1,0:T(8,128)S(1)}, f32[40,128]{1,0:T(8,128)S(1)}, u32[]{:S(2)}, u32[]{:S(2)}) collective-permute-start(f32[40,128]{1,0:T(8,128)S(1)} %shard_map.64.own_ref), channel_id=1, source_target_pairs={{0,32},{64,96},{32,0},{96,64},{1,33},{65,97},{33,1},{97,65},{2,34}... | collective-permute-start | bytes 61448 | tf_op jit(solution)/shard_map/ppermute | solution.py:533
  31.9 9.7 %copy-start.4 = (bf16[128,256]{1,0:T(8,128)(2,1)S(1)}, bf16[128,256]{1,0:T(8,128)(2,1)}, u32[]{:S(2)}) copy-start(bf16[128,256]{1,0:T(8,128)(2,1)} %constant.34.clone.wz_ref) | copy-start | bytes 196612

commit v15 on v13

--- a/solution.py
+++ b/solution.py
@@ -323,7 +323,7 @@
         out_ref[...] = total + base_ref[...]
 
 
-def fold_kernel(mine_ref, core_ref, chip_ref, out_ref):
+def fold_kernel(mine_ref, core_ref, chip_ref, out_ref, one_ref, two_ref):
     lane = lax.broadcasted_iota(jnp.int32, (40, 128), 1)
     spot = lax.rem(lane, 20)
     live = lane < 120
@@ -333,14 +333,19 @@
     high = pltpu.roll(jnp.where(odd, chip, core), 16, 1)
     total = mine_ref[...]
     total = total + jnp.where(live & (spot < 3), low, 0.0)
-    out_ref[...] = total + jnp.where(live & (spot >= 16), high, 0.0)
+    total = total + jnp.where(live & (spot >= 16), high, 0.0)
+    out_ref[...] = total
+    before, after = total[0:32], total[8:40]
+    odd_x = (lax.axis_index("gx") & 1) == 1
+    one_ref[...] = jnp.where(odd_x, before, after)
+    two_ref[...] = jnp.where(odd_x, after, before)
 
 
 def across_kernel(own_ref, one_ref, two_ref, far_ref, out_ref, mine_ref):
     odd = (lax.axis_index("gx") & 1) == 1
-    tiles = lambda ref: [ref[8 * p : 8 * p + 8] for p in range(5)]
+    tiles = lambda ref: [ref[8 * p : 8 * p + 8] for p in range(ref.shape[0] // 8)]
     own, one, two, far = tiles(own_ref), tiles(one_ref), tiles(two_ref), tiles(far_ref)
-    below = [jnp.where(odd, a, b) for a, b in zip(one, two)]
+    below = [None] + [jnp.where(odd, a, b) for a, b in zip(one, two)]
     above = [jnp.where(odd, b, a) for a, b in zip(one, two)]
     window = [
         own[0] + below[2] + far[4],
@@ -528,10 +533,10 @@
     swap = lambda v, axis, couples: lax.ppermute(v, axis, couples + [(b, a) for a, b in couples])
     chip = swap(part, "gz", [(1, 2), (3, 0)])
     core = swap(part, "gz", [(0, 1), (2, 3)])
-    (own,) = call(fold_kernel, [((40, 128), f32)], [VMEM] * 3)(part, core, chip)
+    own, to_one, to_two = call(fold_kernel, [((40, 128), f32), ((32, 128), f32), ((32, 128), f32)], [VMEM] * 3)(part, core, chip)
     far = swap(own, "gx", [(0, 2), (1, 3)])
-    one = swap(own, "gx", [(0, 1), (2, 3)])
-    two = swap(own, "gx", [(1, 2), (3, 0)])
+    one = swap(to_one, "gx", [(0, 1), (2, 3)])
+    two = swap(to_two, "gx", [(1, 2), (3, 0)])
     copies, mine = call(across_kernel, [((8, 32, 128), f32), ((48, 128), f32)], [VMEM] * 4)(own, one, two, far)
     everything = lax.all_to_all(copies, "gy", 0, 0, tiled=True)
 

time: 43.5 us -> 44.5 us (1.023)
  the two profiles are of different devices: /device:TPU:0 before, /device:TPU:16 now
where the time goes in v15:
time: 44.5 us; the launch traced here: 44.3 us
  starting transfers between devices  15.5 us (35%)
  waiting for transfers between devices  10.5 us (24%)
  blocking collectives  10.5 us (24%)
  Pallas kernels  5.94 us (13%)
  local copies, waits for them, and re-layouts  1.06 us (2%)
  between operations  0.71 us (2%)
    all_to_all x1, blocking collectives, shards(): everything = lax.all_to_all(copies, 'gy', 0, 0, tiled=True)  10.5 us
    ppermute x5, starting transfers between devices, send(): return lax.ppermute(v, AXES, pairs(sizes, di, dj, dk))  9.73 us
    ppermute x5, waiting for transfers between devices, shards(): lax.ppermute(v, axis, couples + [(b, a) for a, b in couples])  7.55 us
    ppermute x5, starting transfers between devices, shards(): lax.ppermute(v, axis, couples + [(b, a) for a, b in couples])  5.74 us
    pallas_call x2, Pallas kernels, forces(): call(functools.partial(force_kernel, upper), [((40, 128), f32)] + [(shape...  3.66 us
    ppermute x5, waiting for transfers between devices, send(): return lax.ppermute(v, AXES, pairs(sizes, di, dj, dk))  2.07 us
    pallas_call x1, Pallas kernels, shards(): call(field_kernel, [((6, 2, 16, 32), f32), ((6, 512, 128), bf16)], [VMEM]...  1.49 us
    unnamed x10, local copies, waits for them, and re-layouts  1.06 us
  transfers between devices with their start and end apart: 11, of which 6 were waited for; matrix products, arithmetic and copies ran while one was open for 0% of the time, Pallas kernels for 6%

profile of v15, /device:TPU:16, one launch (start us, length us, event | category | flops | bytes accessed | tf_op | source)
XLA Modules:
  0.0 44.3 jit_solution(8888297395097509465)
XLA Ops:
  0.6 0.0 copy-start
  0.6 1.0 %copy-done = f32[2,16,32,128]{3,2,1,0:T(8,128)S(1)} copy-done((f32[2,16,32,128]{3,2,1,0:T(8,128)S(1)}, f32[2,16,32,128]{3,2,1,0:T(8,128)}, u32[]{:S(2)}) %copy-start) | copy-done | bytes 524312
  1.7 0.0 copy-start.1
  1.7 0.2 shard_map.59.after_ref
  1.9 0.0 copy-start.3
  1.9 0.1 collective-permute-start
  2.0 1.6 %collective-permute-start.1 = (f32[2,16,8,128]{3,2,1,0:T(8,128)S(1)}, f32[2,16,8,128]{3,2,1,0:T(8,128)S(1)}, u32[]{:S(2)}, u32[]{:S(2)}) collective-permute-start(f32[2,16,8,128]{3,2,1,0:T(8,128)S(1)} %get-tuple-element.38), channel_id=1, source_target_pairs={{0,4},{1,5},{2,6},{3,7},{4,8},{5,9},{6,10},{7,11},{8,12},{9,13},{1... | collective-permute-start | bytes 393224 | tf_op jit(solution)/shard_map/ppermute | solution.py:483
  3.6 1.9 %collective-permute-start.3 = (f32[2,8,32,128]{3,2,1,0:T(8,128)S(1)}, f32[2,8,32,128]{3,2,1,0:T(8,128)S(1)}, u32[]{:S(2)}, u32[]{:S(2)}) collective-permute-start(f32[2,8,32,128]{3,2,1,0:T(8,128)S(1)} %get-tuple-element.39), channel_id=1, source_target_pairs={{0,32},{1,33},{2,34},{3,35},{4,36},{5,37},{6,38},{7,39},{8,40},{9,... | collective-permute-start | bytes 786440 | tf_op jit(solution)/shard_map/ppermute | solution.py:483
  5.5 0.0 copy-done.3
  5.5 0.5 %shard_map.60 = (f32[16,128]{1,0:T(8,128)S(1)}, bf16[80,512]{1,0:T(8,128)(2,1)S(1)}, bf16[128,256]{1,0:T(8,128)(2,1)S(1)}, bf16[256,128]{1,0:T(8,128)(2,1)S(1)}, f32[256,128]{1,0:T(8,128)S(1)}) custom-call(f32[6,2,16,32]{3,2,1,0:T(8,128)S(1)} %bitcast.11), custom_call_target="tpu_custom_call" | custom-call | bytes 1000000 | tf_op jit(solution)/shard_map/pallas_call | solution.py:497
  5.9 0.8 %collective-permute-done.zr_ref = f32[2,32,128]{2,1,0:T(8,128)S(1)} collective-permute-done((f32[2,32,128]{2,1,0:T(8,128)S(1)}, f32[2,32,128]{2,1,0:T(8,128)S(1)}, u32[]{:S(2)}, u32[]{:S(2)}) %collective-permute-start) | collective-permute-done | bytes 32800 | tf_op jit(solution)/shard_map/ppermute | solution.py:492
  6.8 1.5 %collective-permute-start.2 = (f32[2,32,128]{2,1,0:T(8,128)S(1)}, f32[2,32,128]{2,1,0:T(8,128)S(1)}, u32[]{:S(2)}, u32[]{:S(2)}) collective-permute-start(f32[2,32,128]{2,1,0:T(8,128)S(1)} %collective-permute-done.zr_ref), channel_id=1, source_target_pairs={{0,4},{1,5},{2,6},{3,7},{4,8},{5,9},{6,10},{7,11},{8,12},{9,13},{1... | collective-permute-start | bytes 98312 | tf_op jit(solution)/shard_map/ppermute | solution.py:483
  8.3 2.8 %collective-permute-start.4 = (f32[2,9,8,128]{3,2,1,0:T(8,128)S(1)}, f32[2,9,8,128]{3,2,1,0:T(8,128)S(1)}, u32[]{:S(2)}, u32[]{:S(2)}) collective-permute-start(f32[2,9,8,128]{3,2,1,0:T(8,128)S(1)} %bitcast_dynamic-update-slice_fusion), channel_id=1, source_target_pairs={{0,36},{1,37},{2,38},{3,39},{4,40},{5,41},{6,42},{7,43},{8,44},{9,... | collective-permute-start | bytes 221192 | tf_op jit(solution)/shard_map/ppermute | solution.py:483
  11.1 1.9 %collective-permute-start.5 = (f32[2,32,128]{2,1,0:T(8,128)S(1)}, f32[2,32,128]{2,1,0:T(8,128)S(1)}, u32[]{:S(2)}, u32[]{:S(2)}) collective-permute-start(f32[2,32,128]{2,1,0:T(8,128)S(1)} %collective-permute-done.zr_ref), channel_id=1, source_target_pairs={{0,32},{1,33},{2,34},{3,35},{4,36},{5,37},{6,38},{7,39},{8,40},{9,... | collective-permute-start | bytes 98312 | tf_op jit(solution)/shard_map/ppermute | solution.py:483
  13.0 0.0 collective-permute-done.2.yzr_ref
  13.1 0.0 collective-permute-done.1.yr_ref
  13.1 0.0 copy-done.1
  13.1 1.9 %shard_map.62 = (f32[40,128]{1,0:T(8,128)S(1)}, f32[2,5,40,128]{3,2,1,0:T(8,128)S(1)}, f32[2,4,40,128]{3,2,1,0:T(8,128)S(1)}, f32[5,8,40,128]{3,2,1,0:T(8,128)S(1)}, f32[5,32,128]{2,1,0:T(8,128)S(1)}) custom-call(f32[2,16,32,128]{3,2,1,0:T(8,128)S(1)} %copy-done.1, f32[2,32,128]{2,1,0:T(8,128)S(1)} %collective-permute-done.zr_ref, ...), custom_call_target="tpu_custom_call" | custom-call | flops 500000000 | bytes 1000000 | tf_op jit(solution)/shard_map/pallas_call | solution.py:511
  15.0 1.2 %collective-permute-done.5.refs_2_ = f32[2,32,128]{2,1,0:T(8,128)S(1)} collective-permute-done((f32[2,32,128]{2,1,0:T(8,128)S(1)}, f32[2,32,128]{2,1,0:T(8,128)S(1)}, u32[]{:S(2)}, u32[]{:S(2)}) %collective-permute-start.5) | collective-permute-done | bytes 32800 | tf_op jit(solution)/shard_map/ppermute | solution.py:483
  16.3 0.8 %collective-permute-done.4.refs_1_ = f32[2,9,8,128]{3,2,1,0:T(8,128)S(1)} collective-permute-done((f32[2,9,8,128]{3,2,1,0:T(8,128)S(1)}, f32[2,9,8,128]{3,2,1,0:T(8,128)S(1)}, u32[]{:S(2)}, u32[]{:S(2)}) %collective-permute-start.4) | collective-permute-done | bytes 73760 | tf_op jit(solution)/shard_map/ppermute | solution.py:483
  17.1 0.0 collective-permute-done.3.refs_0_
  17.1 1.7 %shard_map.63.mine_ref = f32[40,128]{1,0:T(8,128)S(1)} custom-call(f32[2,16,32,128]{3,2,1,0:T(8,128)S(1)} %copy-done.1, f32[2,32,128]{2,1,0:T(8,128)S(1)} %collective-permute-done.zr_ref, f32[2,16,8,128]{3,2,1,0:T(8,128)S(1)} %collective-permute-done.1.yr_ref, f32[2,32,128]{2,1,0:T(8,128)S(1)} %collective-permute-done.2.yzr_ref, ...), custom_call_target="tpu_custom_call" | custom-call | flops 500000000 | bytes 1000000 | tf_op jit(solution)/shard_map/pallas_call | solution.py:511
  18.8 0.0 copy-start.2
  18.8 1.2 %collective-permute-start.7 = (f32[40,128]{1,0:T(8,128)S(1)}, f32[40,128]{1,0:T(8,128)S(1)}, u32[]{:S(2)}, u32[]{:S(2)}) collective-permute-start(f32[40,128]{1,0:T(8,128)S(1)} %shard_map.63.mine_ref), channel_id=1, source_target_pairs={{1,2},{3,0},{2,1},{0,3},{5,6},{7,4},{6,5},{4,7},{9,10},{11,8},{10,... | collective-permute-start | bytes 61448 | tf_op jit(solution)/shard_map/ppermute | solution.py:533
  20.0 0.4 collective-permute-start.6
  20.4 3.2 %collective-permute-done.7.chip_ref = f32[40,128]{1,0:T(8,128)S(1)} collective-permute-done((f32[40,128]{1,0:T(8,128)S(1)}, f32[40,128]{1,0:T(8,128)S(1)}, u32[]{:S(2)}, u32[]{:S(2)}) %collective-permute-start.7) | collective-permute-done | bytes 20512 | tf_op jit(solution)/shard_map/ppermute | solution.py:533
  23.6 0.0 collective-permute-done.6.core_ref
  23.6 0.1 shard_map.64
  23.7 2.5 %collective-permute-start.10 = (f32[40,128]{1,0:T(8,128)S(1)}, f32[40,128]{1,0:T(8,128)S(1)}, u32[]{:S(2)}, u32[]{:S(2)}) collective-permute-start(f32[40,128]{1,0:T(8,128)S(1)} %get-tuple-element.51.own_ref), channel_id=1, source_target_pairs={{0,64},{32,96},{64,0},{96,32},{1,65},{33,97},{65,1},{97,33},{2,66}... | collective-permute-start | bytes 61448 | tf_op jit(solution)/shard_map/ppermute | solution.py:533
  26.2 1.0 %collective-permute-start.8 = (f32[32,128]{1,0:T(8,128)S(1)}, f32[32,128]{1,0:T(8,128)S(1)}, u32[]{:S(2)}, u32[]{:S(2)}) collective-permute-start(f32[32,128]{1,0:T(8,128)S(1)} %get-tuple-element.52), channel_id=1, source_target_pairs={{0,32},{64,96},{32,0},{96,64},{1,33},{65,97},{33,1},{97,65},{2,34}... | collective-permute-start | bytes 49160 | tf_op jit(solution)/shard_map/ppermute | solution.py:533
  27.2 0.6 %collective-permute-start.9 = (f32[32,128]{1,0:T(8,128)S(1)}, f32[32,128]{1,0:T(8,128)S(1)}, u32[]{:S(2)}, u32[]{:S(2)}) collective-permute-start(f32[32,128]{1,0:T(8,128)S(1)} %get-tuple-element.53), channel_id=1, source_target_pairs={{32,64},{96,0},{64,32},{0,96},{33,65},{97,1},{65,33},{1,97},{34,66... | collective-permute-start | bytes 49160 | tf_op jit(solution)/shard_map/ppermute | solution.py:533
  27.9 2.1 %collective-permute-done.8.one_ref = f32[32,128]{1,0:T(8,128)S(1)} collective-permute-done((f32[32,128]{1,0:T(8,128)S(1)}, f32[32,128]{1,0:T(8,128)S(1)}, u32[]{:S(2)}, u32[]{:S(2)}) %collective-permute-start.8) | collective-permute-done | bytes 16416 | tf_op jit(solution)/shard_map/ppermute | solution.py:533
  30.0 2.2 %collective-permute-done.9.two_ref = f32[32,128]{1,0:T(8,128)S(1)} collective-permute-done((f32[32,128]{1,0:T(8,128)S(1)}, f32[32,128]{1,0:T(8,128)S(1)}, u32[]{:S(2)}, u32[]{:S(2)}) %collective-permute-start.9) | collective-permute-done | bytes 16416 | tf_op jit(solution)/shard_map/ppermute | solution.py:533
  32.2 0.0 collective-permute-done.10.far_ref
  32.2 0.0 copy-start.4
  32.2 10.5 %all_to_all.5.g_ref = f32[8,32,128]{2,1,0:T(8,128)S(1)} all-to-all(f32[8,32,128]{2,1,0:T(8,128)S(1)} %get-tuple-element.54), channel_id=1, replica_groups=mesh['gx'=4,'gy'=8,'gz'=4] {'gy'}, dimensions={0} | all-to-all | bytes 262144 | tf_op jit(solution)/shard_map/all_to_all | solution.py:541
  42.8 0.0 copy-done.2
  42.8 0.0 copy-done.4
  42.8 1.5 %shard_map.66 = (f32[6,2,16,32]{3,2,1,0:T(8,128)}, bf16[6,512,128]{2,1,0:T(8,128)(2,1)}) custom-call(f32[8,32,128]{2,1,0:T(8,128)S(1)} %all_to_all.5.g_ref, f32[48,128]{1,0:T(8,128)S(1)} %get-tuple-element.55.mine_ref, bf16[512,144]{1,0:T(8,128)(2,1)S(1)} %copy-done.2, bf16[128,256]{1,0:T(8,128)(2,1)S(1)} %copy-done.4), custom_call_target="tpu_custom_call" | custom-call | flops 100000000 | bytes 1000000 | tf_op jit(solution)/shard_map/pallas_call | solution.py:543
  (3 shorter events, 0.1 us)
Async XLA Ops:
  0.6 1.0 %copy-start = (f32[2,16,32,128]{3,2,1,0:T(8,128)S(1)}, f32[2,16,32,128]{3,2,1,0:T(8,128)}, u32[]{:S(2)}) copy-start(f32[2,16,32,128]{3,2,1,0:T(8,128)} %own_ref.3) | copy-start | bytes 1572868
  1.7 11.4 %copy-start.1 = (f32[2,16,32,128]{3,2,1,0:T(8,128)S(1)}, f32[2,16,32,128]{3,2,1,0:T(8,128)}, u32[]{:S(2)}) copy-start(f32[2,16,32,128]{3,2,1,0:T(8,128)} %own_ref.3) | copy-start | bytes 1572868
  1.9 3.6 %copy-start.3 = (f32[2,3,2,32,16]{3,4,2,1,0:T(8,128)S(1)}, f32[2,3,2,32,16]{3,4,2,1,0:T(8,128)}, u32[]{:S(2)}) copy-start(f32[2,3,2,32,16]{3,4,2,1,0:T(8,128)} %param.7) | copy-start | bytes 73732
  1.9 4.9 %collective-permute-start = (f32[2,32,128]{2,1,0:T(8,128)S(1)}, f32[2,32,128]{2,1,0:T(8,128)S(1)}, u32[]{:S(2)}, u32[]{:S(2)}) collective-permute-start(f32[2,32,128]{2,1,0:T(8,128)S(1)} %shard_map.59.after_ref), channel_id=1, source_target_pairs={{0,1},{1,2},{2,3},{3,0},{4,5},{5,6},{6,7},{7,4},{8,9},{9,10},{10,1... | collective-permute-start | bytes 98312 | tf_op jit(solution)/shard_map/ppermute | solution.py:492
  2.0 11.1 %collective-permute-start.1 = (f32[2,16,8,128]{3,2,1,0:T(8,128)S(1)}, f32[2,16,8,128]{3,2,1,0:T(8,128)S(1)}, u32[]{:S(2)}, u32[]{:S(2)}) collective-permute-start(f32[2,16,8,128]{3,2,1,0:T(8,128)S(1)} %get-tuple-element.38), channel_id=1, source_target_pairs={{0,4},{1,5},{2,6},{3,7},{4,8},{5,9},{6,10},{7,11},{8,12},{9,13},{1... | collective-permute-start | bytes 393224 | tf_op jit(solution)/shard_map/ppermute | solution.py:483
  3.6 13.5 %collective-permute-start.3 = (f32[2,8,32,128]{3,2,1,0:T(8,128)S(1)}, f32[2,8,32,128]{3,2,1,0:T(8,128)S(1)}, u32[]{:S(2)}, u32[]{:S(2)}) collective-permute-start(f32[2,8,32,128]{3,2,1,0:T(8,128)S(1)} %get-tuple-element.39), channel_id=1, source_target_pairs={{0,32},{1,33},{2,34},{3,35},{4,36},{5,37},{6,38},{7,39},{8,40},{9,... | collective-permute-start | bytes 786440 | tf_op jit(solution)/shard_map/ppermute | solution.py:483
  6.8 6.3 %collective-permute-start.2 = (f32[2,32,128]{2,1,0:T(8,128)S(1)}, f32[2,32,128]{2,1,0:T(8,128)S(1)}, u32[]{:S(2)}, u32[]{:S(2)}) collective-permute-start(f32[2,32,128]{2,1,0:T(8,128)S(1)} %collective-permute-done.zr_ref), channel_id=1, source_target_pairs={{0,4},{1,5},{2,6},{3,7},{4,8},{5,9},{6,10},{7,11},{8,12},{9,13},{1... | collective-permute-start | bytes 98312 | tf_op jit(solution)/shard_map/ppermute | solution.py:483
  8.3 8.8 %collective-permute-start.4 = (f32[2,9,8,128]{3,2,1,0:T(8,128)S(1)}, f32[2,9,8,128]{3,2,1,0:T(8,128)S(1)}, u32[]{:S(2)}, u32[]{:S(2)}) collective-permute-start(f32[2,9,8,128]{3,2,1,0:T(8,128)S(1)} %bitcast_dynamic-update-slice_fusion), channel_id=1, source_target_pairs={{0,36},{1,37},{2,38},{3,39},{4,40},{5,41},{6,42},{7,43},{8,44},{9,... | collective-permute-start | bytes 221192 | tf_op jit(solution)/shard_map/ppermute | solution.py:483
  11.1 5.1 %collective-permute-start.5 = (f32[2,32,128]{2,1,0:T(8,128)S(1)}, f32[2,32,128]{2,1,0:T(8,128)S(1)}, u32[]{:S(2)}, u32[]{:S(2)}) collective-permute-start(f32[2,32,128]{2,1,0:T(8,128)S(1)} %collective-permute-done.zr_ref), channel_id=1, source_target_pairs={{0,32},{1,33},{2,34},{3,35},{4,36},{5,37},{6,38},{7,39},{8,40},{9,... | collective-permute-start | bytes 98312 | tf_op jit(solution)/shard_map/ppermute | solution.py:483
  18.8 24.0 %copy-start.2 = (bf16[512,144]{1,0:T(8,128)(2,1)S(1)}, bf16[512,144]{1,0:T(8,128)(2,1)}, u32[]{:S(2)}) copy-start(bf16[512,144]{1,0:T(8,128)(2,1)} %constant.33.clone.wxy_ref) | copy-start | bytes 442372
  18.8 4.8 %collective-permute-start.7 = (f32[40,128]{1,0:T(8,128)S(1)}, f32[40,128]{1,0:T(8,128)S(1)}, u32[]{:S(2)}, u32[]{:S(2)}) collective-permute-start(f32[40,128]{1,0:T(8,128)S(1)} %shard_map.63.mine_ref), channel_id=1, source_target_pairs={{1,2},{3,0},{2,1},{0,3},{5,6},{7,4},{6,5},{4,7},{9,10},{11,8},{10,... | collective-permute-start | bytes 61448 | tf_op jit(solution)/shard_map/ppermute | solution.py:533
  20.0 3.6 %collective-permute-start.6 = (f32[40,128]{1,0:T(8,128)S(1)}, f32[40,128]{1,0:T(8,128)S(1)}, u32[]{:S(2)}, u32[]{:S(2)}) collective-permute-start(f32[40,128]{1,0:T(8,128)S(1)} %shard_map.63.mine_ref), channel_id=1, source_target_pairs={{0,1},{2,3},{1,0},{3,2},{4,5},{6,7},{5,4},{7,6},{8,9},{10,11},{9,8... | collective-permute-start | bytes 61448 | tf_op jit(solution)/shard_map/ppermute | solution.py:533
  23.7 8.5 %collective-permute-start.10 = (f32[40,128]{1,0:T(8,128)S(1)}, f32[40,128]{1,0:T(8,128)S(1)}, u32[]{:S(2)}, u32[]{:S(2)}) collective-permute-start(f32[40,128]{1,0:T(8,128)S(1)} %get-tuple-element.51.own_ref), channel_id=1, source_target_pairs={{0,64},{32,96},{64,0},{96,32},{1,65},{33,97},{65,1},{97,33},{2,66}... | collective-permute-start | bytes 61448 | tf_op jit(solution)/shard_map/ppermute | solution.py:533
  26.2 3.7 %collective-permute-start.8 = (f32[32,128]{1,0:T(8,128)S(1)}, f32[32,128]{1,0:T(8,128)S(1)}, u32[]{:S(2)}, u32[]{:S(2)}) collective-permute-start(f32[32,128]{1,0:T(8,128)S(1)} %get-tuple-element.52), channel_id=1, source_target_pairs={{0,32},{64,96},{32,0},{96,64},{1,33},{65,97},{33,1},{97,65},{2,34}... | collective-permute-start | bytes 49160 | tf_op jit(solution)/shard_map/ppermute | solution.py:533
  27.2 4.9 %collective-permute-start.9 = (f32[32,128]{1,0:T(8,128)S(1)}, f32[32,128]{1,0:T(8,128)S(1)}, u32[]{:S(2)}, u32[]{:S(2)}) collective-permute-start(f32[32,128]{1,0:T(8,128)S(1)} %get-tuple-element.53), channel_id=1, source_target_pairs={{32,64},{96,0},{64,32},{0,96},{33,65},{97,1},{65,33},{1,97},{34,66... | collective-permute-start | bytes 49160 | tf_op jit(solution)/shard_map/ppermute | solution.py:533
  32.2 10.6 %copy-start.4 = (bf16[128,256]{1,0:T(8,128)(2,1)S(1)}, bf16[128,256]{1,0:T(8,128)(2,1)}, u32[]{:S(2)}) copy-start(bf16[128,256]{1,0:T(8,128)(2,1)} %constant.34.clone.wz_ref) | copy-start | bytes 196612
